TPU v7x, 32 devices: a whole 2x2x4 slice. The times are simulated.
32 devices in a mesh: shard: 2 (over core), context: 4 (over z), tensor: 4 (over y, x).
Axes of the slice: x: 2, y: 2, z: 4, core: 2. Of those that a mesh axis runs over, the one named last changes fastest.
Arguments:
- tokens: bfloat16 [2, 4096, 2048], P('shard', 'context'), may hold values from -6 to 6
- ln1_gain: bfloat16 [2048], replicated, may hold values from 0.099609375 to 1.8984375
- ln1_shift: bfloat16 [2048], replicated, may hold values from -1.25 to 1.25
- q_weight: bfloat16 [2048, 2048], P('shard', 'tensor'), may hold values from -0.125 to 0.125
- k_weight: bfloat16 [2048, 2048], P('shard', 'tensor'), may hold values from -0.125 to 0.125
- v_weight: bfloat16 [2048, 2048], P('shard', 'tensor'), may hold values from -0.125 to 0.125
- q_bias: bfloat16 [2048], P('tensor'), may hold values from -1.75 to 1.75
- k_bias: bfloat16 [512], P('tensor'), may hold values from -3 to 3
- v_bias: bfloat16 [2048], P('tensor'), may hold values from -1.75 to 1.75
- o_weight: bfloat16 [2048, 2048], P('tensor', 'shard'), may hold values from -0.25 to 0.25
- ln2_gain: bfloat16 [2048], replicated, may hold values from 0.099609375 to 1.8984375
- ln2_shift: bfloat16 [2048], replicated, may hold values from -1.25 to 1.25
- gate_weight: bfloat16 [2048, 5632], P('shard', 'tensor'), may hold values from -0.125 to 0.125
- up_weight: bfloat16 [2048, 5632], P('shard', 'tensor'), may hold values from -0.125 to 0.125
- down_weight: bfloat16 [5632, 2048], P('tensor', 'shard'), may hold values from -0.109375 to 0.109375
- cotangent: bfloat16 [2, 4096, 2048], P('shard', 'context'), may hold values from -6 to 6
- doc_lengths: int32 [2, 4], P('shard'), may hold values from 1 to 2560, 4096 in all within a row
- picture_starts: int32 [2, 4], P('shard'), may hold values from 0 to 3840
Outputs:
- output: bfloat16 [2, 4096, 2048], P('shard', ('context', 'tensor'))
- tokens_grad: float32 [2, 4096, 2048], P('shard', ('context', 'tensor'))
- ln1_gain_grad: float32 [2048], replicated
- ln1_shift_grad: float32 [2048], replicated
- q_weight_grad: float32 [2048, 2048], P(('shard', 'context'), 'tensor')
- k_weight_grad: float32 [2048, 2048], P(('shard', 'context'), 'tensor')
- v_weight_grad: float32 [2048, 2048], P(('shard', 'context'), 'tensor')
- q_bias_grad: float32 [2048], P('tensor')
- k_bias_grad: float32 [512], P('tensor')
- v_bias_grad: float32 [2048], P('tensor')
- o_weight_grad: float32 [2048, 2048], P('tensor', ('shard', 'context'))
- ln2_gain_grad: float32 [2048], replicated
- ln2_shift_grad: float32 [2048], replicated
- gate_weight_grad: float32 [2048, 5632], P(('shard', 'context'), 'tensor')
- up_weight_grad: float32 [2048, 5632], P(('shard', 'context'), 'tensor')
- down_weight_grad: float32 [5632, 2048], P('tensor', ('shard', 'context'))
Inputs may be any that keep to these rules, and one draw needn't show every extreme that they name: `doc_lengths`: each row of 4 document lengths sums to 4096; the documents follow one another from position 0. `picture_starts`: each picture span [s, s + 256) lies within its sequence; spans may share positions and may cross a document's bound.
All inputs are finite; a program needn't handle non-finite values.
Results may differ from a plain program's by a relative error of at most 0.03.
Values may be sent and summed in bfloat16 or wider, within the bound.
No kernel may reach another device: no remote copies, remote signals or barrier semaphores. Data moves between devices by JAX's collectives and lax.ppermute only.
A program may use at most 256 MiB of HBM per device.

v0:
```python
import functools

import jax
import jax.numpy as jnp
from jax import lax
from jax.experimental import pallas as pl
from jax.experimental.pallas import tpu as pltpu
from jax.sharding import PartitionSpec as P

HEAD_DIM = 64
ROT = 16
SPAN = 256
PAIR = 128
EPS = 1e-05
LOW = -1e30
LOWER = -2e30
SCALE = HEAD_DIM ** (-0.5)

f32 = jnp.float32
bf16 = jnp.bfloat16


NT = (((1,), (1,)), ((), ()))
NN = (((1,), (0,)), ((), ()))
TN = (((0,), (0,)), ((), ()))


def dot(a, b, dims=NN):
    return lax.dot_general(a, b, dims, preferred_element_type=f32)


def swap_with(x, axis, bit):
    size = lax.axis_size(axis)
    return lax.ppermute(x, axis, [(i, i ^ bit) for i in range(size)])


def sum_over(x, axis):
    size = lax.axis_size(axis)
    bit = 1
    while bit < size:
        x = x + swap_with(x, axis, bit)
        bit *= 2
    return x


def rotary_tables(positions):
    half = ROT // 2
    freq = 10000.0 ** (-(2.0 * jnp.arange(half).astype(f32)) / ROT)
    angles = freq[:, None] * positions.astype(f32)[None, :]
    parts = jnp.concatenate([jnp.cos(angles), jnp.sin(angles)], axis=0)
    lane = jnp.arange(PAIR) % HEAD_DIM
    row = jnp.arange(half)[:, None]
    hit = (lane[None, :] % half == row) & (lane[None, :] < ROT)
    spread_cos = jnp.concatenate([hit, jnp.zeros_like(hit)], axis=0).astype(f32)
    sign = jnp.where(lane < half, -1.0, 1.0)[None, :]
    spread_sin = jnp.concatenate([jnp.zeros_like(hit), hit], axis=0).astype(f32) * sign
    expand = functools.partial(
        lax.dot_general,
        dimension_numbers=TN,
        precision=lax.Precision.HIGHEST,
        preferred_element_type=f32,
    )
    rest = jnp.where(lane < ROT, 0.0, 1.0).astype(f32)
    return expand(parts, spread_cos) + rest[None, :], expand(parts, spread_sin)


def swap_halves(x):
    lane = lax.broadcasted_iota(jnp.int32, x.shape, 1) % HEAD_DIM
    return jnp.where(lane < ROT // 2, pltpu.roll(x, PAIR - ROT // 2, 1), pltpu.roll(x, ROT // 2, 1))


def project_kernel(
    groups,
    ids,
    x_own,
    x_oth,
    gain_own,
    gain_oth,
    shift_own,
    shift_oth,
    wq_own,
    wk_own,
    wv_own,
    wq_oth,
    wk_oth,
    wv_oth,
    q_bias,
    k_bias,
    v_bias,
    cos_ref,
    sin_ref,
    *rest,
):
    h_ref, pieces, (qs, ks, vs) = rest[0], rest[1 : 1 + groups], rest[1 + groups :]
    half = x_own.shape[1]
    a = x_own[...].astype(f32)
    b = x_oth[...].astype(f32)
    count = 1.0 / (2 * half)
    mean = (jnp.sum(a, axis=1, keepdims=True) + jnp.sum(b, axis=1, keepdims=True)) * count
    a = a - mean
    b = b - mean
    var = (jnp.sum(a * a, axis=1, keepdims=True) + jnp.sum(b * b, axis=1, keepdims=True)) * count
    inv = lax.rsqrt(var + EPS)
    ha = (a * inv * gain_own[...].astype(f32) + shift_own[...].astype(f32)).astype(bf16)
    hb = (b * inv * gain_oth[...].astype(f32) + shift_oth[...].astype(f32)).astype(bf16)
    h_ref[:, :half] = ha
    h_ref[:, half:] = hb
    qs[...] = dot(ha, wq_own[...]) + dot(hb, wq_oth[...]) + q_bias[...]
    ks[...] = dot(ha, wk_own[...]) + dot(hb, wk_oth[...]) + k_bias[...]
    vs[...] = dot(ha, wv_own[...]) + dot(hb, wv_oth[...]) + v_bias[...]
    cos = cos_ref[...]
    sin = sin_ref[...]
    for s in range(groups):
        group = (ids[1] & (groups - 1)) ^ s
        cols = pl.ds(pl.multiple_of(group * PAIR, PAIR), PAIR)
        q = qs[:, cols]
        k = ks[:, cols]
        pieces[s][:, :PAIR] = (q * cos + swap_halves(q) * sin).astype(bf16)
        pieces[s][:, PAIR : 2 * PAIR] = (k * cos + swap_halves(k) * sin).astype(bf16)
        pieces[s][:, 2 * PAIR :] = vs[:, cols].astype(bf16)


def project(ids, tokens, gain, shift, own, other, biases, tables, groups, slots):
    rows, width = tokens.shape
    half = width // 2
    share = rows // slots
    inner = own[0].shape[1]

    def row_block(i, ids):
        return ids[2] ^ i

    whole = lambda i, ids: (0, 0)
    weight = pl.BlockSpec((half, inner), whole)
    bias = pl.BlockSpec((1, inner), whole)
    in_specs = [
        pl.BlockSpec((share, half), lambda i, ids: (row_block(i, ids), ids[0])),
        pl.BlockSpec((share, half), lambda i, ids: (row_block(i, ids), 1 - ids[0])),
        pl.BlockSpec((1, half), lambda i, ids: (0, ids[0])),
        pl.BlockSpec((1, half), lambda i, ids: (0, 1 - ids[0])),
        pl.BlockSpec((1, half), lambda i, ids: (0, ids[0])),
        pl.BlockSpec((1, half), lambda i, ids: (0, 1 - ids[0])),
    ]
    in_specs += [weight] * 6 + [bias] * 3
    in_specs += [pl.BlockSpec((share, PAIR), lambda i, ids: (row_block(i, ids), 0))] * 2
    out = pl.pallas_call(
        functools.partial(project_kernel, groups),
        grid_spec=pltpu.PrefetchScalarGridSpec(
            num_scalar_prefetch=1,
            grid=(slots,),
            in_specs=in_specs,
            out_specs=[pl.BlockSpec((share, width), lambda i, ids: (i, 0))]
            + [pl.BlockSpec((share, 3 * PAIR), lambda i, ids: (i, 0))] * groups,
            scratch_shapes=[pltpu.VMEM((share, inner), f32)] * 3,
        ),
        out_shape=[jax.ShapeDtypeStruct((rows, width), bf16)]
        + [jax.ShapeDtypeStruct((rows, 3 * PAIR), bf16)] * groups,
        compiler_params=pltpu.CompilerParams(vmem_limit_bytes=56 << 20),
        cost_estimate=pl.CostEstimate(
            flops=2 * rows * width * inner * 3,
            bytes_accessed=rows * width * 4 + 3 * width * inner * 2 + rows * inner * 6,
            transcendentals=rows,
        ),
        name="project",
    )(ids, tokens, tokens, gain, gain, shift, shift, *own, *other, *biases, *tables)
    return out[0], out[1:]


def reach(ids, p, docs, pics, length):
    start = jnp.zeros_like(p)
    end = jnp.full_like(p, length)
    for j in range(docs):
        e = ids[4 + j]
        start = jnp.where(p >= e, jnp.maximum(start, e), start)
        end = jnp.where(p < e, jnp.minimum(end, e), end)
    far = p + 1
    for j in range(pics):
        b = ids[4 + docs + j]
        inside = (p >= b) & (p < b + SPAN)
        far = jnp.where(inside, jnp.maximum(far, jnp.minimum(b + SPAN, end)), far)
    return start, far


def block_ranges(ids, first, bq, bk, docs, pics, length):
    lo_a, hi_a = reach(ids, first, docs, pics, length)
    lo_b, hi_b = reach(ids, first + (bq - 1), docs, pics, length)
    begin = lo_a // bk
    stop = (hi_b + (bk - 1)) // bk
    full_begin = jnp.clip((lo_b + (bk - 1)) // bk, begin, stop)
    full_stop = jnp.clip(hi_a // bk, full_begin, stop)
    return begin, full_begin, full_stop, stop


def piece_copies(ids, pieces, whole, sems, slots, share, outward=False):
    copies = []
    for s, piece in enumerate(pieces):
        for i in range(slots):
            first = ((ids[1] ^ s) * slots + (ids[2] ^ i)) * share
            there = whole.at[pl.ds(pl.multiple_of(first, share), share)]
            here = piece.at[pl.ds(i * share, share)]
            src, dst = (there, here) if outward else (here, there)
            copies.append(pltpu.make_async_copy(src, dst, sems.at[s * slots + i]))
    return copies


def attend_kernel(dims, ids, *refs):
    pieces, groups, slots, share, length, docs, pics, bq, bk = dims
    ins = refs[:pieces]
    outs = refs[pieces : pieces + groups]
    o_t, lse = refs[pieces + groups : pieces + groups + 2]
    qkv, vx, ob, acc, m_ref, sem_in, sem_out = refs[pieces + groups + 2 :]
    loads = piece_copies(ids, ins, qkv, sem_in, slots, share)
    for c in loads:
        c.start()
    for c in loads:
        c.wait()

    def prepare(j, _):
        rows = pl.ds(pl.multiple_of(j * bk, bk), bk)
        v_t = qkv[rows, 2 * PAIR :].astype(f32).T
        ones = jnp.ones((16, bk), bf16)
        for h in range(2):
            vx[h, :HEAD_DIM, rows] = v_t[h * HEAD_DIM : (h + 1) * HEAD_DIM].astype(bf16)
            vx[h, HEAD_DIM:, rows] = ones
        return 0

    lax.fori_loop(0, length // bk, prepare, 0)
    lane = lax.broadcasted_iota(jnp.int32, (bq, PAIR), 1)

    def query_block(i, _):
        first = i * bq
        rows = pl.ds(pl.multiple_of(first, bq), bq)
        q = qkv[rows, :PAIR].astype(f32) * SCALE
        heads = [
            jnp.where((lane < HEAD_DIM) == (h == 0), q, 0.0).astype(bf16) for h in range(2)
        ]
        for h in range(2):
            acc[h] = jnp.zeros_like(acc[h])
            m_ref[h] = jnp.full_like(m_ref[h], LOW)
        lo, hi = reach(
            ids, first + lax.broadcasted_iota(jnp.int32, (1, bq), 1), docs, pics, length
        )
        begin, full_begin, full_stop, stop = block_ranges(
            ids, first, bq, bk, docs, pics, length
        )

        def visit(masked, j, _):
            keys = pl.ds(pl.multiple_of(j * bk, bk), bk)
            k = qkv[keys, PAIR : 2 * PAIR]
            if masked:
                p = j * bk + lax.broadcasted_iota(jnp.int32, (bk, bq), 0)
                ok = (p >= lo) & (p < hi)
            for h in range(2):
                s = dot(k, heads[h], NT)
                if masked:
                    s = jnp.where(ok, s, LOWER)
                old = m_ref[h, 0:1]
                new = jnp.maximum(old, jnp.max(s, axis=0, keepdims=True))
                w = jnp.exp(s - new).astype(bf16)
                acc[h] = acc[h] * jnp.exp(old - new) + dot(vx[h, :, keys], w)
                m_ref[h, 0:1] = new
            return 0

        lax.fori_loop(begin, full_begin, functools.partial(visit, True), 0)
        lax.fori_loop(full_begin, full_stop, functools.partial(visit, False), 0)
        lax.fori_loop(full_stop, stop, functools.partial(visit, True), 0)
        for h in range(2):
            total = acc[h, HEAD_DIM : HEAD_DIM + 1]
            o_t[h * HEAD_DIM : (h + 1) * HEAD_DIM, rows] = acc[h, :HEAD_DIM] / total
            lse[h : h + 1, rows] = m_ref[h, 0:1] + jnp.log(total)
        ob[rows] = o_t[:, rows].T.astype(bf16)
        return 0

    lax.fori_loop(0, length // bq, query_block, 0)
    stores = piece_copies(ids, outs, ob, sem_out, slots, share, outward=True)
    for c in stores:
        c.start()
    for c in stores:
        c.wait()


def attend_cost(length, matmuls):
    pairs = length * length // 2
    return pl.CostEstimate(
        flops=2 * pairs * 256 * 2 * matmuls,
        bytes_accessed=length * PAIR * 2 * 8,
        transcendentals=2 * pairs,
    )


def attend(ids, pieces, groups, slots, docs, pics, bq, bk):
    rows = pieces[0].shape[0]
    n = len(pieces)
    length = rows * n
    share = rows // slots
    dims = (n, groups, slots, share, length, docs, pics, bq, bk)
    anywhere = pl.BlockSpec(memory_space=pl.ANY)
    out = pl.pallas_call(
        functools.partial(attend_kernel, dims),
        grid_spec=pltpu.PrefetchScalarGridSpec(
            num_scalar_prefetch=1,
            grid=(1,),
            in_specs=[anywhere] * n,
            out_specs=[anywhere] * groups
            + [
                pl.BlockSpec((PAIR, length), lambda i, ids: (0, 0)),
                pl.BlockSpec((8, length), lambda i, ids: (0, 0)),
            ],
            scratch_shapes=[
                pltpu.VMEM((length, 3 * PAIR), bf16),
                pltpu.VMEM((2, HEAD_DIM + 16, length), bf16),
                pltpu.VMEM((length, PAIR), bf16),
                pltpu.VMEM((2, HEAD_DIM + 16, bq), f32),
                pltpu.VMEM((2, 8, bq), f32),
                pltpu.SemaphoreType.DMA((n * slots,)),
                pltpu.SemaphoreType.DMA((groups * slots,)),
            ],
        ),
        out_shape=[jax.ShapeDtypeStruct((rows, PAIR), bf16)] * groups
        + [
            jax.ShapeDtypeStruct((PAIR, length), f32),
            jax.ShapeDtypeStruct((8, length), f32),
        ],
        compiler_params=pltpu.CompilerParams(vmem_limit_bytes=56 << 20),
        cost_estimate=attend_cost(length, 2),
        name="attend",
    )(ids, *pieces)
    return out[:groups], out[groups], out[groups + 1]


def attend_back_kernel(dims, ids, *refs):
    pieces, groups, slots, share, length, docs, pics, bq, bk = dims
    ins = refs[:pieces]
    grads = refs[pieces : 2 * pieces]
    o_t, lse, cos_ref, sin_ref = refs[2 * pieces : 2 * pieces + 4]
    outs = refs[2 * pieces + 4 : 2 * pieces + 4 + groups]
    qkv, dob, kt, dq_t, dk, dv, sem_in, sem_grad, sem_out = refs[2 * pieces + 4 + groups :]
    loads = piece_copies(ids, ins, qkv, sem_in, slots, share)
    loads += piece_copies(ids, grads, dob, sem_grad, slots, share)
    for c in loads:
        c.start()
    for c in loads:
        c.wait()

    def prepare(j, _):
        rows = pl.ds(pl.multiple_of(j * bk, bk), bk)
        kt[:, rows] = qkv[rows, PAIR : 2 * PAIR].astype(f32).T.astype(bf16)
        dk[rows] = jnp.zeros((bk, PAIR), f32)
        dv[rows] = jnp.zeros((bk, PAIR), f32)
        return 0

    lax.fori_loop(0, length // bk, prepare, 0)
    lane = lax.broadcasted_iota(jnp.int32, (bq, PAIR), 1)

    def turn_back(x, rows):
        return x * cos_ref[rows] - swap_halves(x) * sin_ref[rows]

    def query_block(i, _):
        first = i * bq
        rows = pl.ds(pl.multiple_of(first, bq), bq)
        q = qkv[rows, :PAIR].astype(f32) * SCALE
        do = dob[rows].astype(f32)
        q_of = []
        do_of = []
        for h in range(2):
            mine = (lane < HEAD_DIM) == (h == 0)
            q_of.append(jnp.where(mine, q, 0.0).astype(bf16))
            do_of.append(jnp.where(mine, do, 0.0).astype(bf16))
        prod = do.T * o_t[:, rows]
        delta = [
            jnp.sum(prod[h * HEAD_DIM : (h + 1) * HEAD_DIM], axis=0, keepdims=True)
            for h in range(2)
        ]
        dq_t[...] = jnp.zeros_like(dq_t)
        lo, hi = reach(
            ids, first + lax.broadcasted_iota(jnp.int32, (1, bq), 1), docs, pics, length
        )
        begin, full_begin, full_stop, stop = block_ranges(
            ids, first, bq, bk, docs, pics, length
        )

        def visit(masked, j, _):
            keys = pl.ds(pl.multiple_of(j * bk, bk), bk)
            k = qkv[keys, PAIR : 2 * PAIR]
            v = qkv[keys, 2 * PAIR :]
            if masked:
                p = j * bk + lax.broadcasted_iota(jnp.int32, (bk, bq), 0)
                ok = (p >= lo) & (p < hi)
            dk_sum = dk[keys]
            dv_sum = dv[keys]
            for h in range(2):
                feats = slice(h * HEAD_DIM, (h + 1) * HEAD_DIM)
                s = dot(k, q_of[h], NT)
                if masked:
                    s = jnp.where(ok, s, LOWER)
                w = jnp.exp(s - lse[h : h + 1, rows])
                dw = dot(v, do_of[h], NT)
                ds = (w * (dw - delta[h])).astype(bf16)
                dv_sum = dv_sum + dot(w.astype(bf16), do_of[h])
                dk_sum = dk_sum + dot(ds, q_of[h])
                dq_t[feats] += dot(kt[feats, keys], ds)
            dk[keys] = dk_sum
            dv[keys] = dv_sum
            return 0

        lax.fori_loop(begin, full_begin, functools.partial(visit, True), 0)
        lax.fori_loop(full_begin, full_stop, functools.partial(visit, False), 0)
        lax.fori_loop(full_stop, stop, functools.partial(visit, True), 0)
        dq = dq_t[...].T * SCALE
        qkv[rows, :PAIR] = turn_back(dq, rows).astype(bf16)
        return 0

    lax.fori_loop(0, length // bq, query_block, 0)

    def finish(j, _):
        rows = pl.ds(pl.multiple_of(j * bk, bk), bk)
        qkv[rows, PAIR : 2 * PAIR] = turn_back(dk[rows], rows).astype(bf16)
        qkv[rows, 2 * PAIR :] = dv[rows].astype(bf16)
        return 0

    lax.fori_loop(0, length // bk, finish, 0)
    stores = piece_copies(ids, outs, qkv, sem_out, slots, share, outward=True)
    for c in stores:
        c.start()
    for c in stores:
        c.wait()


def attend_back(ids, pieces, grads, o_t, lse, tables, groups, slots, docs, pics, bq, bk):
    rows = pieces[0].shape[0]
    n = len(pieces)
    length = rows * n
    share = rows // slots
    dims = (n, groups, slots, share, length, docs, pics, bq, bk)
    anywhere = pl.BlockSpec(memory_space=pl.ANY)
    once = dict(pipeline_mode=pl.Buffered(1))
    return pl.pallas_call(
        functools.partial(attend_back_kernel, dims),
        grid_spec=pltpu.PrefetchScalarGridSpec(
            num_scalar_prefetch=1,
            grid=(1,),
            in_specs=[anywhere] * (2 * n)
            + [
                pl.BlockSpec((PAIR, length), lambda i, ids: (0, 0), **once),
                pl.BlockSpec((8, length), lambda i, ids: (0, 0), **once),
                pl.BlockSpec((length, PAIR), lambda i, ids: (0, 0), **once),
                pl.BlockSpec((length, PAIR), lambda i, ids: (0, 0), **once),
            ],
            out_specs=[anywhere] * groups,
            scratch_shapes=[
                pltpu.VMEM((length, 3 * PAIR), bf16),
                pltpu.VMEM((length, PAIR), bf16),
                pltpu.VMEM((PAIR, length), bf16),
                pltpu.VMEM((PAIR, bq), f32),
                pltpu.VMEM((length, PAIR), f32),
                pltpu.VMEM((length, PAIR), f32),
                pltpu.SemaphoreType.DMA((n * slots,)),
                pltpu.SemaphoreType.DMA((n * slots,)),
                pltpu.SemaphoreType.DMA((groups * slots,)),
            ],
        ),
        out_shape=[jax.ShapeDtypeStruct((rows, 3 * PAIR), bf16)] * groups,
        compiler_params=pltpu.CompilerParams(vmem_limit_bytes=56 << 20),
        cost_estimate=attend_cost(length, 5),
        name="attend_back",
    )(ids, *pieces, *grads, o_t, lse, *tables)


def join_kernel(groups, kinds, slots, dims, ids, *refs):
    pieces = refs[:groups]
    own = refs[groups : groups + kinds]
    oth = refs[groups + kinds : groups + 2 * kinds]
    joined = refs[groups + 2 * kinds]
    parts = refs[groups + 2 * kinds + 1 :]
    inner = groups * PAIR
    half = parts[0].shape[1] // 2
    for s in range(groups):
        group = (ids[1] & (groups - 1)) ^ s
        for j in range(kinds):
            cols = pl.ds(pl.multiple_of(j * inner + group * PAIR, PAIR), PAIR)
            joined[:, cols] = pieces[s][:, j * PAIR : (j + 1) * PAIR]
    for side, weights in enumerate((own, oth)):
        total = None
        for j, w in enumerate(weights):
            term = dot(joined[:, j * inner : (j + 1) * inner], w[...], dims)
            total = term if total is None else total + term
        for i in range(slots):

            @pl.when(pl.program_id(0) == i)
            def _():
                parts[i][:, side * half : (side + 1) * half] = total.astype(parts[i].dtype)


def join(ids, pieces, own, oth, slots, dims):
    groups = len(pieces)
    kinds = len(own)
    rows = pieces[0].shape[0]
    share = rows // slots
    inner = groups * PAIR
    width = 2 * (own[0].shape[0] if dims == NT else own[0].shape[1])
    whole = lambda i, ids: (0, 0)
    by_row = lambda i, ids: (i, 0)
    out = pl.pallas_call(
        functools.partial(join_kernel, groups, kinds, slots, dims),
        grid_spec=pltpu.PrefetchScalarGridSpec(
            num_scalar_prefetch=1,
            grid=(slots,),
            in_specs=[pl.BlockSpec((share, kinds * PAIR), by_row)] * groups
            + [pl.BlockSpec(own[0].shape, whole)] * (2 * kinds),
            out_specs=[pl.BlockSpec((share, kinds * inner), by_row)]
            + [pl.BlockSpec((share, width), whole)] * slots,
        ),
        out_shape=[jax.ShapeDtypeStruct((rows, kinds * inner), bf16)]
        + [jax.ShapeDtypeStruct((share, width), f32 if i == 0 else bf16) for i in range(slots)],
        compiler_params=pltpu.CompilerParams(vmem_limit_bytes=44 << 20),
        cost_estimate=pl.CostEstimate(
            flops=2 * rows * width * inner * kinds,
            bytes_accessed=rows * width * 3 + kinds * (width * inner * 2 + rows * inner * 4),
            transcendentals=0,
        ),
    )(ids, *pieces, *own, *oth)
    return out[0], out[1:]


def fill(blocks, axis, origin):
    shape = list(blocks[0].shape)
    size = shape[axis]
    shape[axis] = size * len(blocks)
    out = jnp.zeros(shape, blocks[0].dtype)
    for i, block in enumerate(blocks):
        out = lax.dynamic_update_slice_in_dim(out, block, origin + i * size, axis)
    return out


def hold(*groups):
    return lax.optimization_barrier(groups)


def local(
    tokens,
    ln1_gain,
    ln1_shift,
    q_weight,
    k_weight,
    v_weight,
    q_bias,
    k_bias,
    v_bias,
    o_weight,
    ln2_gain,
    ln2_shift,
    gate_weight,
    up_weight,
    down_weight,
    cotangent,
    doc_lengths,
    picture_starts,
):
    me = lax.axis_index("shard")
    ctx = lax.axis_index("context")
    ctxs = lax.axis_size("context")
    ten = lax.axis_index("tensor")
    slots = lax.axis_size("tensor")
    rows, width = tokens.shape[1:]
    half = width // 2
    share = rows // slots
    inner = q_weight.shape[1]
    groups = inner // PAIR
    heads_here = inner // HEAD_DIM
    docs = doc_lengths.shape[1]
    pics = picture_starts.shape[1]
    length = ctxs * rows
    quarter = half // ctxs
    bq = min(512, rows)
    bk = min(512, rows)
    assert ctxs % groups == 0 and ctxs & (ctxs - 1) == 0 and slots & (slots - 1) == 0

    def by_shard(x):
        turned = jnp.concatenate([x[..., half:], x[..., :half]], axis=-1)
        return jnp.where(me == 0, x, turned)

    def slot_rows(x, i):
        return lax.dynamic_slice_in_dim(x, (ten ^ i) * share, share, 0)

    def other_half(x):
        return swap_with(x, "shard", 1)

    origin = jnp.minimum(me, 0)

    own_qkv = (q_weight, k_weight, v_weight)
    oth_qkv = tuple(other_half(w) for w in own_qkv)
    doc_ends = jnp.cumsum(doc_lengths[0])
    ids = jnp.concatenate(
        [
            jnp.stack([me, ctx, ten, ctx * 0]).astype(jnp.int32),
            doc_ends.astype(jnp.int32),
            picture_starts[0].astype(jnp.int32),
        ]
    )
    local_tables = rotary_tables(ctx * rows + jnp.arange(rows, dtype=jnp.int32))
    k_bias_wide = jnp.pad(
        k_bias.astype(f32).reshape(heads_here, ROT), ((0, 0), (0, HEAD_DIM - ROT))
    ).reshape(1, inner)
    h1, send = project(
        ids,
        tokens[0],
        ln1_gain.reshape(1, width),
        ln1_shift.reshape(1, width),
        own_qkv,
        oth_qkv,
        (q_bias.astype(f32).reshape(1, inner), k_bias_wide, v_bias.astype(f32).reshape(1, inner)),
        local_tables,
        groups,
        slots,
    )

    (send, later) = hold(
        send,
        (
            o_weight,
            gate_weight,
            up_weight,
            down_weight,
            cotangent[0],
            tokens[0],
            jnp.arange(length, dtype=jnp.int32),
        ),
    )
    o_weight, gate_weight, up_weight, down_weight, cot_rows, x_rows, positions = later
    pieces = [send[0]] + [swap_with(send[s % groups], "context", s) for s in range(1, ctxs)]
    down_oth, o_oth, gate_oth, up_oth = map(
        other_half, (down_weight, o_weight, gate_weight, up_weight)
    )
    full_tables = rotary_tables(positions)
    cot_all = by_shard(fill([slot_rows(cot_rows, i) for i in range(slots)], 0, origin))
    x_share = by_shard(slot_rows(x_rows, 0)).astype(f32)
    down_full = fill([down_weight, down_oth], 1, origin)
    o_full = fill([o_weight, o_oth], 1, origin)
    dm_all = dot(cot_all, down_full, NT)
    gate_full = fill([gate_weight, gate_oth], 0, origin)
    up_full = fill([up_weight, up_oth], 0, origin)
    gain_two = by_shard(ln2_gain.astype(f32))
    shift_two = by_shard(ln2_shift.astype(f32))
    gain_one = by_shard(ln1_gain.astype(f32))
    pieces, ready = hold(
        pieces, (down_full, o_full, gate_full, up_full, cot_all, dm_all, full_tables, x_share)
    )
    down_full, o_full, gate_full, up_full, cot_all, dm_all, full_tables, x_share = ready

    attn_send, o_t, lse = attend(ids, pieces, groups, slots, docs, pics, bq, bk)
    attn, attn_parts = join(
        ids,
        [attn_send[0]] + [swap_with(attn_send[s], "context", s) for s in range(1, groups)],
        (o_weight,),
        (o_oth,),
        slots,
        NN,
    )

    def send_rows(parts):
        return [swap_with(parts[i].astype(bf16), "tensor", i) for i in range(1, slots)]

    def add_rows(own, received):
        for part in received:
            own = own + part.astype(f32)
        return own

    def gather_rows(block):
        return [block] + [swap_with(block, "tensor", i) for i in range(1, slots)]

    def slot_of(x, i):
        return x[i * share : (i + 1) * share]

    x1 = x_share + add_rows(attn_parts[0], send_rows(attn_parts))
    mean2 = jnp.mean(x1, axis=-1, keepdims=True)
    cent2 = x1 - mean2
    inv2 = lax.rsqrt(jnp.mean(cent2 * cent2, axis=-1, keepdims=True) + EPS)
    unit2 = cent2 * inv2
    h2 = gather_rows((unit2 * gain_two + shift_two).astype(bf16))

    hidden = []
    gate_grad = []
    up_grad = []
    norm2_parts = []
    dh2_received = []
    for i in range(slots):
        dm = slot_of(dm_all, i)
        g = dot(h2[i], gate_full)
        u = dot(h2[i], up_full)
        sig = jax.nn.sigmoid(g)
        act = g * sig
        hidden.append((act * u).astype(bf16))
        gate_grad.append((dm * u * sig * (1.0 + g * (1.0 - sig))).astype(bf16))
        up_grad.append((dm * act).astype(bf16))
        part = dot(gate_grad[i], gate_full, NT) + dot(up_grad[i], up_full, NT)
        norm2_parts.append(part if i == 0 else part.astype(bf16))
        if i + 1 < slots:
            norm2_parts[i], h2[i + 1] = hold(norm2_parts[i], h2[i + 1])
        if i > 0:
            dh2_received.append(swap_with(norm2_parts[i], "tensor", i))

    def blocks_of(mine, theirs, axis):
        def block(x, d):
            return lax.dynamic_slice_in_dim(x, (ctx ^ d) * quarter, quarter, axis).astype(f32)

        return {d: block(mine, d) + block(theirs, d) for d in range(ctxs)}

    def scatter_step(parts, bit):
        parts = dict(parts)
        for d in sorted((d for d in parts if d & bit), reverse=True):
            parts[d ^ bit] += swap_with(parts.pop(d).astype(bf16), "context", bit).astype(f32)
        return parts

    def scatter_rest(parts):
        bit = 2
        while bit < ctxs:
            parts = scatter_step(parts, bit)
            bit *= 2
        return parts[0]

    h2_all, gate_all, up_all, hidden_all = (
        fill(blocks, 0, origin) for blocks in (h2, gate_grad, up_grad, hidden)
    )

    norm2_parts, h2_all, gate_all, up_all = hold(norm2_parts, h2_all, gate_all, up_all)
    gate_theirs = dot(h2_all[:, half:], gate_all, TN).astype(bf16)
    up_theirs = dot(h2_all[:, half:], up_all, TN).astype(bf16)
    h2_all, gate_theirs, up_theirs = hold(h2_all, gate_theirs, up_theirs)
    gate_theirs = other_half(gate_theirs)
    up_theirs = other_half(up_theirs)
    gate_mine = dot(h2_all[:, :half], gate_all, TN).astype(bf16)
    up_mine = dot(h2_all[:, :half], up_all, TN).astype(bf16)
    dh2_received, norm2_own, gate_mine, up_mine, gate_theirs, up_theirs = hold(
        dh2_received, norm2_parts[0], gate_mine, up_mine, gate_theirs, up_theirs
    )
    gate_parts = scatter_step(blocks_of(gate_mine, gate_theirs, 0), 1)
    up_parts = scatter_step(blocks_of(up_mine, up_theirs, 0), 1)
    dh2 = add_rows(norm2_own, dh2_received)
    cot_share = slot_of(cot_all, 0).astype(f32)
    e2 = dh2 * gain_two
    dx1 = cot_share + inv2 * (
        e2
        - jnp.mean(e2, axis=-1, keepdims=True)
        - unit2 * jnp.mean(e2 * unit2, axis=-1, keepdims=True)
    )
    dx1_slots = gather_rows(dx1.astype(bf16))

    hidden_all, cot_all, dx1_own = hold(hidden_all, cot_all, dx1_slots[0])
    down_theirs = dot(hidden_all, cot_all[:, half:], TN).astype(bf16)
    down_mine = dot(hidden_all, cot_all[:, :half], TN).astype(bf16)
    out_all = dot(hidden_all, down_full).astype(bf16)
    down_theirs = other_half(down_theirs)
    dx1_rest, dx1_own, out_all, down_mine = hold(dx1_slots[1:], dx1_own, out_all, down_mine)
    dx1b = fill([dx1_own] + dx1_rest, 0, origin)
    d_attn = dot(dx1b, o_full, NT).astype(bf16)
    d_send = [
        lax.dynamic_slice_in_dim(d_attn, ((ctx & (groups - 1)) ^ s) * PAIR, PAIR, 1)
        for s in range(groups)
    ]
    d_send, dx1b = hold(d_send, dx1b)
    d_pieces = [d_send[0]] + [swap_with(d_send[s % groups], "context", s) for s in range(1, ctxs)]

    o_theirs = dot(attn, dx1b[:, half:], TN).astype(bf16)
    o_mine = dot(attn, dx1b[:, :half], TN).astype(bf16)
    o_theirs = other_half(o_theirs)

    d_pieces, out_all, o_mine, o_theirs, down_mine, down_theirs, gate_parts, up_parts = hold(
        d_pieces, out_all, o_mine, o_theirs, down_mine, down_theirs, gate_parts, up_parts
    )
    out_received = send_rows([slot_of(out_all, i) for i in range(slots)])
    gate_out = scatter_rest(gate_parts)
    up_out = scatter_rest(up_parts)
    down_parts = scatter_step(blocks_of(down_mine, down_theirs, 1), 1)
    back = attend_back(
        ids, pieces, d_pieces, o_t, lse, full_tables, groups, slots, docs, pics, bq, bk
    )
    back_rest = [swap_with(back[s], "context", s) for s in range(1, groups)]

    back_own, out_received, down_parts, o_mine = hold(back[0], out_received, down_parts, o_mine)
    output = by_shard((x1 + add_rows(slot_of(out_all, 0).astype(f32), out_received)).astype(bf16))[None]
    o_parts = scatter_step(blocks_of(o_mine, o_theirs, 1), 1)
    down_grad = scatter_rest(down_parts)
    o_grad = scatter_rest(o_parts)
    back_rest, output = hold(back_rest, output)

    d_qkv, norm1_parts = join(ids, [back_own] + back_rest, own_qkv, oth_qkv, slots, NT)
    norm1_parts, d_qkv = hold(norm1_parts, d_qkv)
    dh1_received = send_rows(norm1_parts)
    qkv_theirs = other_half(dot(h1[:, half:], d_qkv, TN).astype(bf16))
    qkv_mine = dot(h1[:, :half], d_qkv, TN).astype(bf16)
    qkv_grad = scatter_rest(scatter_step(blocks_of(qkv_mine, qkv_theirs, 0), 1))
    bias = jnp.sum(d_qkv.astype(f32), axis=0, keepdims=True)
    bias = sum_over(sum_over(bias, "shard"), "context")[0]
    dh1_received, qkv_mine = hold(dh1_received, qkv_mine)
    dh1 = add_rows(norm1_parts[0], dh1_received)

    mean1 = jnp.mean(x_share, axis=-1, keepdims=True)
    cent1 = x_share - mean1
    inv1 = lax.rsqrt(jnp.mean(cent1 * cent1, axis=-1, keepdims=True) + EPS)
    unit1 = cent1 * inv1
    e1 = dh1 * gain_one
    tokens_grad = dx1 + inv1 * (
        e1
        - jnp.mean(e1, axis=-1, keepdims=True)
        - unit1 * jnp.mean(e1 * unit1, axis=-1, keepdims=True)
    )
    tokens_grad = by_shard(tokens_grad)[None]

    k_bias_grad = bias[inner : 2 * inner].reshape(heads_here, HEAD_DIM)[:, :ROT]
    norms = jnp.stack(
        [
            jnp.sum(dh1 * unit1, axis=0),
            jnp.sum(dh1, axis=0),
            jnp.sum(dh2 * unit2, axis=0),
            jnp.sum(dh2, axis=0),
        ]
    )
    norms = by_shard(norms)
    for axis in ("shard", "context", "tensor"):
        norms = sum_over(norms, axis)
    return (
        output,
        tokens_grad,
        norms[0],
        norms[1],
        qkv_grad[:, :inner],
        qkv_grad[:, inner : 2 * inner],
        qkv_grad[:, 2 * inner :],
        bias[:inner],
        k_bias_grad.reshape(heads_here * ROT),
        bias[2 * inner :],
        o_grad,
        norms[2],
        norms[3],
        gate_out,
        up_out,
        down_grad,
    )


def solution(mesh):
    tokens = P("shard", "context", None)
    inward = P("shard", "tensor")
    outward = P("tensor", "shard")
    vector = P("tensor")
    placed = (
        tokens,
        P(),
        P(),
        inward,
        inward,
        inward,
        vector,
        vector,
        vector,
        outward,
        P(),
        P(),
        inward,
        inward,
        outward,
        tokens,
        P("shard", None),
        P("shard", None),
    )
    share = P("shard", ("context", "tensor"), None)
    grad_in = P(("shard", "context"), "tensor")
    grad_out = P("tensor", ("shard", "context"))

    return jax.shard_map(
        local,
        mesh=mesh,
        in_specs=placed,
        out_specs=(
            share,
            share,
            P(),
            P(),
            grad_in,
            grad_in,
            grad_in,
            vector,
            vector,
            vector,
            grad_out,
            P(),
            P(),
            grad_in,
            grad_in,
            grad_out,
        ),
        check_vma=False,
    )
```

profile of v0, /device:TPU:0, one launch (start us, length us, event | category | flops | bytes accessed | tf_op | source)
XLA Modules:
  0.0 1039.3 jit_solution(12767584876228860654)
XLA Ops:
  15.1 16.7 %project.1 = (bf16[1024,2048]{1,0:T(8,128)(2,1)}, bf16[1024,384]{1,0:T(8,128)(2,1)}, bf16[1024,384]{1,0:T(8,128)(2,1)}, bf16[1024,384]{1,0:T(8,128)(2,1)}, bf16[1024,384]{1,0:T(8,128)(2,1)}) custom-call(s32[12]{0:T(128)} %concatenate.41.ids, bf16[1024,2048]{1,0:T(8,128)(2,1)} %bitcast.88, bf16[1024,2048]{1,0:T(8,128)(2,1)} %bitcast.89, ...), custom_call_target="tpu_custom_call" | custom-call | flops 6442450944 | bytes 17825792 | tf_op jit(solution)/shard_map/project/pallas_call | solution.py:145
  39.8 6.3 dynamic_update_slice.104
  46.1 6.4 dynamic_update_slice.105
  52.5 6.3 dynamic_update_slice.106
  58.8 5.5 dynamic_update_slice.107
  81.5 26.3 %dynamic_update_slice.96 = bf16[1408,2048]{1,0:T(8,128)(2,1)} dynamic-update-slice(bf16[1408,2048]{1,0:T(8,128)(2,1)} %broadcast_in_dim.29, bf16[1408,1024]{1,0:T(8,128)(2,1)} %param.32, s32[]{:T(128)} %constant.93.clone.1, s32[]{:T(128)S(6)} %select_n.235) | dynamic-update-slice | bytes 5767172 | tf_op jit(solution)/shard_map/dynamic_update_slice | solution.py:530
  110.8 14.7 %dynamic_update_slice.100 = bf16[2048,1408]{1,0:T(8,128)(2,1)} dynamic-update-slice(bf16[2048,1408]{1,0:T(8,128)(2,1)} %broadcast.240.clone, bf16[1024,1408]{1,0:T(8,128)(2,1)} %param.30, s32[]{:T(128)S(6)} %select_n.235, s32[]{:T(128)} %constant.93.clone.1) | dynamic-update-slice | bytes 5767172 | tf_op jit(solution)/shard_map/dynamic_update_slice | solution.py:530
  128.4 14.3 %dynamic_update_slice.102 = bf16[2048,1408]{1,0:T(8,128)(2,1)} dynamic-update-slice(bf16[2048,1408]{1,0:T(8,128)(2,1)} %broadcast.240.clone.1, bf16[1024,1408]{1,0:T(8,128)(2,1)} %param.31, s32[]{:T(128)S(6)} %select_n.235, s32[]{:T(128)} %constant.93.clone.1) | dynamic-update-slice | bytes 5767172 | tf_op jit(solution)/shard_map/dynamic_update_slice | solution.py:530
  144.3 10.0 dynamic_update_slice.98
  154.3 5.6 maximum_select_fusion
  162.6 9.1 dynamic_update_slice.99
  171.7 25.3 %dynamic_update_slice.97 = bf16[1408,2048]{1,0:T(8,128)(2,1)} dynamic-update-slice(bf16[1408,2048]{1,0:T(8,128)(2,1)} %dynamic_update_slice.96, bf16[1408,1024]{1,0:T(8,128)(2,1)} %collective-permute-done.6, s32[]{:T(128)} %constant.93.clone.1, s32[]{:T(128)S(6)} %select_n.236) | dynamic-update-slice | bytes 5767172 | tf_op jit(solution)/shard_map/dynamic_update_slice | solution.py:530
  197.0 11.7 %fusion.66 = f32[1024,1408]{1,0:T(8,128)} fusion(bf16[1024,2048]{1,0:T(8,128)(2,1)} %maximum_select_fusion, bf16[1408,2048]{1,0:T(8,128)(2,1)} %dynamic_update_slice.97), kind=kOutput, calls=%fused_computation.179 | convolution fusion | flops 5905580032 | bytes 15728640 | tf_op jit(solution)/shard_map/dot_general | solution.py:29
  208.7 14.3 %dynamic_update_slice.101 = bf16[2048,1408]{1,0:T(8,128)(2,1)} dynamic-update-slice(bf16[2048,1408]{1,0:T(8,128)(2,1)} %dynamic_update_slice.100, bf16[1024,1408]{1,0:T(8,128)(2,1)} %collective-permute-done.8, s32[]{:T(128)S(6)} %select_n.236, s32[]{:T(128)} %constant.93.clone.1) | dynamic-update-slice | bytes 5767172 | tf_op jit(solution)/shard_map/dynamic_update_slice | solution.py:530
  223.0 14.3 %dynamic_update_slice.103 = bf16[2048,1408]{1,0:T(8,128)(2,1)} dynamic-update-slice(bf16[2048,1408]{1,0:T(8,128)(2,1)} %dynamic_update_slice.102, bf16[1024,1408]{1,0:T(8,128)(2,1)} %collective-permute-done.9, s32[]{:T(128)S(6)} %select_n.236, s32[]{:T(128)} %constant.93.clone.1) | dynamic-update-slice | bytes 5767172 | tf_op jit(solution)/shard_map/dynamic_update_slice | solution.py:530
  238.2 33.5 %attend.1 = (bf16[1024,128]{1,0:T(8,128)(2,1)}, bf16[1024,128]{1,0:T(8,128)(2,1)}, bf16[1024,128]{1,0:T(8,128)(2,1)}, bf16[1024,128]{1,0:T(8,128)(2,1)}, f32[128,4096]{1,0:T(8,128)}, /*index=5*/f32[8,4096]{1,0:T(8,128)}) custom-call(s32[12]{0:T(128)} %concatenate.41.ids, bf16[1024,384]{1,0:T(8,128)(2,1)} %get-tuple-element.147.refs_0_, ...), custom_call_target="tpu_custom_call" | custom-call | flops 17179869184 | bytes 8388608 | tf_op jit(solution)/shard_map/attend/pallas_call | solution.py:297
  283.2 7.5 collective-permute-done.12.refs_3_
  291.7 6.3 shard_map.297
  304.2 15.6 %collective-permute-done.13 = bf16[256,2048]{1,0:T(8,128)(2,1)S(1)} collective-permute-done((bf16[256,2048]{1,0:T(8,128)(2,1)}, bf16[256,2048]{1,0:T(8,128)(2,1)S(1)}, u32[]{:S(2)}, u32[]{:S(2)}) %collective-permute-start.13) | collective-permute-done | bytes 1048608 | tf_op jit(solution)/shard_map/ppermute | solution.py:34
  322.5 21.0 %collective-permute-done.15 = bf16[256,2048]{1,0:T(8,128)(2,1)} collective-permute-done((bf16[256,2048]{1,0:T(8,128)(2,1)}, bf16[256,2048]{1,0:T(8,128)(2,1)}, u32[]{:S(2)}, u32[]{:S(2)}) %collective-permute-start.15) | collective-permute-done | bytes 1048608 | tf_op jit(solution)/shard_map/ppermute | solution.py:34
  351.3 5.5 fusion.67
  359.3 6.1 dynamic_update_slice.108
  365.4 6.6 multiply_convert_fusion.11
  395.8 5.2 multiply_convert_fusion.9
  401.0 5.0 dynamic_update_slice.117
  410.8 5.6 fusion
  419.7 4.9 multiply_convert_fusion.7
  434.1 5.6 fusion.1
  442.9 5.3 multiply_convert_fusion.5
  466.5 6.4 dynamic_update_slice.109
  472.8 6.4 dynamic_update_slice.110
  479.2 5.8 dynamic_update_slice.111
  489.7 6.4 fusion.2
  501.0 5.2 convolution_convert_fusion.8
  521.5 6.5 convolution_convert_fusion.5
  541.8 6.1 convolution_convert_fusion.6
  547.9 19.4 %collective-permute-done.20 = bf16[256,2048]{1,0:T(8,128)(2,1)} collective-permute-done((bf16[256,2048]{1,0:T(8,128)(2,1)}, bf16[256,2048]{1,0:T(8,128)(2,1)}, u32[]{:S(2)}, u32[]{:S(2)}) %collective-permute-start.20) | collective-permute-done | bytes 1048608 | tf_op jit(solution)/shard_map/ppermute | solution.py:34
  578.7 8.1 collective-permute-start.35
  586.9 6.8 convolution_convert_fusion.3
  593.7 10.1 convolution_convert_fusion
  603.8 6.4 convolution_convert_fusion.4
  627.9 6.4 dynamic_update_slice.124
  634.3 6.4 dynamic_update_slice.125
  640.6 6.4 dynamic_update_slice.126
  647.0 6.0 dynamic_update_slice.127
  653.1 5.4 convolution_convert_fusion.9
  665.6 6.2 collective-permute-start.27
  676.6 6.7 collective-permute-done.27.refs_5_
  683.3 9.8 collective-permute-done.28.refs_6_
  696.3 5.0 collective-permute-start.43
  707.3 47.6 %attend_back.1 = (bf16[1024,384]{1,0:T(8,128)(2,1)}, bf16[1024,384]{1,0:T(8,128)(2,1)}, bf16[1024,384]{1,0:T(8,128)(2,1)}, bf16[1024,384]{1,0:T(8,128)(2,1)}) custom-call(s32[12]{0:T(128)} %concatenate.41.ids, bf16[1024,384]{1,0:T(8,128)(2,1)} %get-tuple-element.147.refs_0_, bf16[1024,384]{1,0:T(8,128)(2,1)} %collective-permute-done.3.refs_1_, ...), custom_call_target="tpu_custom_call" | custom-call | flops 42949672960 | bytes 8388608 | tf_op jit(solution)/shard_map/attend_back/pallas_call | solution.py:436
  767.1 27.6 %collective-permute-done.62 = bf16[256,1408]{1,0:T(8,128)(2,1)S(1)} collective-permute-done((bf16[256,1408]{1,0:T(8,128)(2,1)S(1)}, bf16[256,1408]{1,0:T(8,128)(2,1)S(1)}, u32[]{:S(2)}, u32[]{:S(2)}) %collective-permute-start.62) | collective-permute-done | bytes 720928 | tf_op jit(solution)/shard_map/ppermute | solution.py:34
  803.6 59.5 %collective-permute-done.37.refs_2_ = bf16[1024,384]{1,0:T(8,128)(2,1)S(1)} collective-permute-done((bf16[1024,384]{1,0:T(8,128)(2,1)S(1)}, bf16[1024,384]{1,0:T(8,128)(2,1)S(1)}, u32[]{:S(2)}, u32[]{:S(2)}) %collective-permute-start.37) | collective-permute-done | bytes 786464 | tf_op jit(solution)/shard_map/ppermute | solution.py:34
  863.2 13.2 %shard_map.298 = (bf16[1024,1536]{1,0:T(8,128)(2,1)}, f32[256,2048]{1,0:T(8,128)}, bf16[256,2048]{1,0:T(8,128)(2,1)S(1)}, bf16[256,2048]{1,0:T(8,128)(2,1)S(1)}, bf16[256,2048]{1,0:T(8,128)(2,1)S(1)}) custom-call(s32[12]{0:T(128)S(1)} %copy-done.4, bf16[1024,384]{1,0:T(8,128)(2,1)S(1)} %copy-done.11, bf16[1024,384]{1,0:T(8,128)(2,1)S(1)} %collective-permute-done.36.refs_1_, ...), custom_call_target="tpu_custom_call" | custom-call | flops 6442450944 | bytes 18874368 | tf_op jit(solution)/shard_map/pallas_call | solution.py:502
  880.3 17.5 %collective-permute-start.60 = (bf16[512,256]{1,0:T(8,128)(2,1)S(1)}, bf16[512,256]{1,0:T(8,128)(2,1)S(1)}, u32[]{:S(2)}, u32[]{:S(2)}) collective-permute-start(bf16[512,256]{1,0:T(8,128)(2,1)S(1)} %get-tuple-element.294), channel_id=1, source_target_pairs={{0,4},{4,0},{8,12},{12,8},{1,5},{5,1},{9,13},{13,9},{2,6},{6,2},{1... | collective-permute-start | bytes 786440 | tf_op jit(solution)/shard_map/ppermute | solution.py:34
  899.8 4.9 convolution_convert_fusion.1
  904.7 5.7 collective-permute-done.57
  914.6 5.2 convolution_convert_fusion.2
  921.7 6.7 collective-permute-done.61
  935.1 10.9 %collective-permute-done.44 = bf16[256,2048]{1,0:T(8,128)(2,1)} collective-permute-done((bf16[256,2048]{1,0:T(8,128)(2,1)S(1)}, bf16[256,2048]{1,0:T(8,128)(2,1)}, u32[]{:S(2)}, u32[]{:S(2)}) %collective-permute-start.44) | collective-permute-done | bytes 1048608 | tf_op jit(solution)/shard_map/ppermute | solution.py:34
  946.0 21.7 %collective-permute-done.45 = bf16[256,2048]{1,0:T(8,128)(2,1)} collective-permute-done((bf16[256,2048]{1,0:T(8,128)(2,1)S(1)}, bf16[256,2048]{1,0:T(8,128)(2,1)}, u32[]{:S(2)}, u32[]{:S(2)}) %collective-permute-start.45) | collective-permute-done | bytes 1048608 | tf_op jit(solution)/shard_map/ppermute | solution.py:34
  988.9 12.9 %collective-permute-done.54 = bf16[256,1536]{1,0:T(8,128)(2,1)S(1)} collective-permute-done((bf16[256,1536]{1,0:T(8,128)(2,1)S(1)}, bf16[256,1536]{1,0:T(8,128)(2,1)S(1)}, u32[]{:S(2)}, u32[]{:S(2)}) %collective-permute-start.54) | collective-permute-done | bytes 786464 | tf_op jit(solution)/shard_map/ppermute | solution.py:34
  1006.1 24.5 %collective-permute-done.53 = bf16[256,1536]{1,0:T(8,128)(2,1)S(1)} collective-permute-done((bf16[256,1536]{1,0:T(8,128)(2,1)S(1)}, bf16[256,1536]{1,0:T(8,128)(2,1)S(1)}, u32[]{:S(2)}, u32[]{:S(2)}) %collective-permute-start.53) | collective-permute-done | bytes 786464 | tf_op jit(solution)/shard_map/ppermute | solution.py:34
  1030.5 5.6 collective-permute-done.55
  (393 shorter events, 301.5 us)
Async XLA Ops:
  0.6 13.1 %collective-permute-start = (bf16[1024,512]{1,0:T(8,128)(2,1)}, bf16[1024,512]{1,0:T(8,128)(2,1)S(1)}, u32[]{:S(2)}, u32[]{:S(2)}) collective-permute-start(bf16[1024,512]{1,0:T(8,128)(2,1)} %refs_4_.2), channel_id=1, source_target_pairs={{0,16},{16,0},{1,17},{17,1},{2,18},{18,2},{3,19},{19,3},{4,20},{20... | collective-permute-start | bytes 3145736 | tf_op jit(solution)/shard_map/ppermute | solution.py:34
  1.2 12.6 %collective-permute-start.1 = (bf16[1024,512]{1,0:T(8,128)(2,1)}, bf16[1024,512]{1,0:T(8,128)(2,1)S(1)}, u32[]{:S(2)}, u32[]{:S(2)}) collective-permute-start(bf16[1024,512]{1,0:T(8,128)(2,1)} %refs_5_.1), channel_id=1, source_target_pairs={{0,16},{16,0},{1,17},{17,1},{2,18},{18,2},{3,19},{19,3},{4,20},{20... | collective-permute-start | bytes 3145736 | tf_op jit(solution)/shard_map/ppermute | solution.py:34
  1.3 12.5 %collective-permute-start.2 = (bf16[1024,512]{1,0:T(8,128)(2,1)}, bf16[1024,512]{1,0:T(8,128)(2,1)}, u32[]{:S(2)}, u32[]{:S(2)}) collective-permute-start(bf16[1024,512]{1,0:T(8,128)(2,1)} %refs_6_.1), channel_id=1, source_target_pairs={{0,16},{16,0},{1,17},{17,1},{2,18},{18,2},{3,19},{19,3},{4,20},{20... | collective-permute-start | bytes 3145736 | tf_op jit(solution)/shard_map/ppermute | solution.py:34
  31.8 139.8 %collective-permute-start.6 = (bf16[1408,1024]{1,0:T(8,128)(2,1)}, bf16[1408,1024]{1,0:T(8,128)(2,1)}, u32[]{:S(2)}, u32[]{:S(2)}) collective-permute-start(bf16[1408,1024]{1,0:T(8,128)(2,1)} %param.32), channel_id=1, source_target_pairs={{0,16},{16,0},{1,17},{17,1},{2,18},{18,2},{3,19},{19,3},{4,20},{20... | collective-permute-start | bytes 8650760 | tf_op jit(solution)/shard_map/ppermute | solution.py:34
  32.0 176.7 %collective-permute-start.8 = (bf16[1024,1408]{1,0:T(8,128)(2,1)}, bf16[1024,1408]{1,0:T(8,128)(2,1)}, u32[]{:S(2)}, u32[]{:S(2)}) collective-permute-start(bf16[1024,1408]{1,0:T(8,128)(2,1)} %param.30), channel_id=1, source_target_pairs={{0,16},{16,0},{1,17},{17,1},{2,18},{18,2},{3,19},{19,3},{4,20},{20... | collective-permute-start | bytes 8650760 | tf_op jit(solution)/shard_map/ppermute | solution.py:34
  32.4 190.6 %collective-permute-start.9 = (bf16[1024,1408]{1,0:T(8,128)(2,1)}, bf16[1024,1408]{1,0:T(8,128)(2,1)}, u32[]{:S(2)}, u32[]{:S(2)}) collective-permute-start(bf16[1024,1408]{1,0:T(8,128)(2,1)} %param.31), channel_id=1, source_target_pairs={{0,16},{16,0},{1,17},{17,1},{2,18},{18,2},{3,19},{19,3},{4,20},{20... | collective-permute-start | bytes 8650760 | tf_op jit(solution)/shard_map/ppermute | solution.py:34
  32.5 127.4 %collective-permute-start.7 = (bf16[512,1024]{1,0:T(8,128)(2,1)S(1)}, bf16[512,1024]{1,0:T(8,128)(2,1)S(1)}, u32[]{:S(2)}, u32[]{:S(2)}) collective-permute-start(bf16[512,1024]{1,0:T(8,128)(2,1)S(1)} %copy-done), channel_id=1, source_target_pairs={{0,16},{16,0},{1,17},{17,1},{2,18},{18,2},{3,19},{19,3},{4,20},{20... | collective-permute-start | bytes 3145736 | tf_op jit(solution)/shard_map/ppermute | solution.py:34
  32.9 204.3 %collective-permute-start.3 = (bf16[1024,384]{1,0:T(8,128)(2,1)}, bf16[1024,384]{1,0:T(8,128)(2,1)}, u32[]{:S(2)}, u32[]{:S(2)}) collective-permute-start(bf16[1024,384]{1,0:T(8,128)(2,1)} %get-tuple-element.137), channel_id=1, source_target_pairs={{0,4},{4,0},{8,12},{12,8},{1,5},{5,1},{9,13},{13,9},{2,6},{6,2},{1... | collective-permute-start | bytes 2359304 | tf_op jit(solution)/shard_map/ppermute | solution.py:34
  159.9 77.4 %collective-permute-start.4 = (bf16[1024,384]{1,0:T(8,128)(2,1)}, bf16[1024,384]{1,0:T(8,128)(2,1)S(1)}, u32[]{:S(2)}, u32[]{:S(2)}) collective-permute-start(bf16[1024,384]{1,0:T(8,128)(2,1)} %get-tuple-element.138), channel_id=1, source_target_pairs={{0,8},{4,12},{8,0},{12,4},{1,9},{5,13},{9,1},{13,5},{2,10},{6,14},... | collective-permute-start | bytes 2359304 | tf_op jit(solution)/shard_map/ppermute | solution.py:34
  171.7 65.6 %collective-permute-start.5 = (bf16[1024,384]{1,0:T(8,128)(2,1)}, bf16[1024,384]{1,0:T(8,128)(2,1)}, u32[]{:S(2)}, u32[]{:S(2)}) collective-permute-start(bf16[1024,384]{1,0:T(8,128)(2,1)} %get-tuple-element.139), channel_id=1, source_target_pairs={{0,12},{4,8},{8,4},{12,0},{1,13},{5,9},{9,5},{13,1},{2,14},{6,10},... | collective-permute-start | bytes 2359304 | tf_op jit(solution)/shard_map/ppermute | solution.py:34
  271.7 9.3 collective-permute-start.10
  272.7 10.5 %collective-permute-start.11 = (bf16[1024,128]{1,0:T(8,128)(2,1)}, bf16[1024,128]{1,0:T(8,128)(2,1)S(1)}, u32[]{:S(2)}, u32[]{:S(2)}) collective-permute-start(bf16[1024,128]{1,0:T(8,128)(2,1)} %get-tuple-element.155), channel_id=1, source_target_pairs={{0,8},{4,12},{8,0},{12,4},{1,9},{5,13},{9,1},{13,5},{2,10},{6,14},... | collective-permute-start | bytes 786440 | tf_op jit(solution)/shard_map/ppermute | solution.py:34
  276.2 14.6 %collective-permute-start.12 = (bf16[1024,128]{1,0:T(8,128)(2,1)}, bf16[1024,128]{1,0:T(8,128)(2,1)S(1)}, u32[]{:S(2)}, u32[]{:S(2)}) collective-permute-start(bf16[1024,128]{1,0:T(8,128)(2,1)} %get-tuple-element.156), channel_id=1, source_target_pairs={{0,12},{4,8},{8,4},{12,0},{1,13},{5,9},{9,5},{13,1},{2,14},{6,10},... | collective-permute-start | bytes 786440 | tf_op jit(solution)/shard_map/ppermute | solution.py:34
  298.9 21.0 %collective-permute-start.13 = (bf16[256,2048]{1,0:T(8,128)(2,1)}, bf16[256,2048]{1,0:T(8,128)(2,1)S(1)}, u32[]{:S(2)}, u32[]{:S(2)}) collective-permute-start(bf16[256,2048]{1,0:T(8,128)(2,1)} %get-tuple-element.158), channel_id=1, source_target_pairs={{0,1},{1,0},{2,3},{3,2},{4,5},{5,4},{6,7},{7,6},{8,9},{9,8},{10,11... | collective-permute-start | bytes 3145736 | tf_op jit(solution)/shard_map/ppermute | solution.py:34
  300.4 22.1 %collective-permute-start.14 = (bf16[256,2048]{1,0:T(8,128)(2,1)}, bf16[256,2048]{1,0:T(8,128)(2,1)}, u32[]{:S(2)}, u32[]{:S(2)}) collective-permute-start(bf16[256,2048]{1,0:T(8,128)(2,1)} %get-tuple-element.159), channel_id=1, source_target_pairs={{0,2},{1,3},{2,0},{3,1},{4,6},{5,7},{6,4},{7,5},{8,10},{9,11},{10,... | collective-permute-start | bytes 3145736 | tf_op jit(solution)/shard_map/ppermute | solution.py:34
  301.9 41.6 %collective-permute-start.15 = (bf16[256,2048]{1,0:T(8,128)(2,1)}, bf16[256,2048]{1,0:T(8,128)(2,1)}, u32[]{:S(2)}, u32[]{:S(2)}) collective-permute-start(bf16[256,2048]{1,0:T(8,128)(2,1)} %get-tuple-element.160), channel_id=1, source_target_pairs={{0,3},{1,2},{2,1},{3,0},{4,7},{5,6},{6,5},{7,4},{8,11},{9,10},{10,... | collective-permute-start | bytes 3145736 | tf_op jit(solution)/shard_map/ppermute | solution.py:34
  347.8 44.9 %collective-permute-start.16 = (bf16[256,2048]{1,0:T(8,128)(2,1)S(1)}, bf16[256,2048]{1,0:T(8,128)(2,1)}, u32[]{:S(2)}, u32[]{:S(2)}) collective-permute-start(bf16[256,2048]{1,0:T(8,128)(2,1)S(1)} %add_convert_fusion.1), channel_id=1, source_target_pairs={{0,1},{1,0},{2,3},{3,2},{4,5},{5,4},{6,7},{7,6},{8,9},{9,8},{10,11... | collective-permute-start | bytes 3145736 | tf_op jit(solution)/shard_map/ppermute | solution.py:34
  349.2 67.2 %collective-permute-start.17 = (bf16[256,2048]{1,0:T(8,128)(2,1)S(1)}, bf16[256,2048]{1,0:T(8,128)(2,1)}, u32[]{:S(2)}, u32[]{:S(2)}) collective-permute-start(bf16[256,2048]{1,0:T(8,128)(2,1)S(1)} %add_convert_fusion.1), channel_id=1, source_target_pairs={{0,2},{1,3},{2,0},{3,1},{4,6},{5,7},{6,4},{7,5},{8,10},{9,11},{10,... | collective-permute-start | bytes 3145736 | tf_op jit(solution)/shard_map/ppermute | solution.py:34
  349.8 89.9 %collective-permute-start.19 = (bf16[256,2048]{1,0:T(8,128)(2,1)S(1)}, bf16[256,2048]{1,0:T(8,128)(2,1)}, u32[]{:S(2)}, u32[]{:S(2)}) collective-permute-start(bf16[256,2048]{1,0:T(8,128)(2,1)S(1)} %add_convert_fusion.1), channel_id=1, source_target_pairs={{0,3},{1,2},{2,1},{3,0},{4,7},{5,6},{6,5},{7,4},{8,11},{9,10},{10,... | collective-permute-start | bytes 3145736 | tf_op jit(solution)/shard_map/ppermute | solution.py:34
  506.1 61.2 %collective-permute-start.22 = (bf16[1024,1408]{1,0:T(8,128)(2,1)}, bf16[1024,1408]{1,0:T(8,128)(2,1)}, u32[]{:S(2)}, u32[]{:S(2)}) collective-permute-start(bf16[1024,1408]{1,0:T(8,128)(2,1)} %convolution_convert_fusion.8), channel_id=1, source_target_pairs={{0,16},{16,0},{1,17},{17,1},{2,18},{18,2},{3,19},{19,3},{4,20},{20... | collective-permute-start | bytes 8650760 | tf_op jit(solution)/shard_map/ppermute | solution.py:34
  510.9 56.5 %collective-permute-start.23 = (bf16[1024,1408]{1,0:T(8,128)(2,1)}, bf16[1024,1408]{1,0:T(8,128)(2,1)}, u32[]{:S(2)}, u32[]{:S(2)}) collective-permute-start(bf16[1024,1408]{1,0:T(8,128)(2,1)} %convolution_convert_fusion.7), channel_id=1, source_target_pairs={{0,16},{16,0},{1,17},{17,1},{2,18},{18,2},{3,19},{19,3},{4,20},{20... | collective-permute-start | bytes 8650760 | tf_op jit(solution)/shard_map/ppermute | solution.py:34
  518.0 29.9 %collective-permute-start.21 = (bf16[256,2048]{1,0:T(8,128)(2,1)}, bf16[256,2048]{1,0:T(8,128)(2,1)}, u32[]{:S(2)}, u32[]{:S(2)}) collective-permute-start(bf16[256,2048]{1,0:T(8,128)(2,1)} %fusion.2), channel_id=1, source_target_pairs={{0,3},{1,2},{2,1},{3,0},{4,7},{5,6},{6,5},{7,4},{8,11},{9,10},{10,... | collective-permute-start | bytes 3145736 | tf_op jit(solution)/shard_map/ppermute | solution.py:34
  519.5 47.8 %collective-permute-start.20 = (bf16[256,2048]{1,0:T(8,128)(2,1)}, bf16[256,2048]{1,0:T(8,128)(2,1)}, u32[]{:S(2)}, u32[]{:S(2)}) collective-permute-start(bf16[256,2048]{1,0:T(8,128)(2,1)} %fusion.1), channel_id=1, source_target_pairs={{0,2},{1,3},{2,0},{3,1},{4,6},{5,7},{6,4},{7,5},{8,10},{9,11},{10,... | collective-permute-start | bytes 3145736 | tf_op jit(solution)/shard_map/ppermute | solution.py:34
  520.4 46.9 %collective-permute-start.18 = (bf16[256,2048]{1,0:T(8,128)(2,1)}, bf16[256,2048]{1,0:T(8,128)(2,1)}, u32[]{:S(2)}, u32[]{:S(2)}) collective-permute-start(bf16[256,2048]{1,0:T(8,128)(2,1)} %fusion), channel_id=1, source_target_pairs={{0,1},{1,0},{2,3},{3,2},{4,5},{5,4},{6,7},{7,6},{8,9},{9,8},{10,11... | collective-permute-start | bytes 3145736 | tf_op jit(solution)/shard_map/ppermute | solution.py:34
  573.5 49.5 %collective-permute-start.24 = (bf16[256,2048]{1,0:T(8,128)(2,1)S(1)}, bf16[256,2048]{1,0:T(8,128)(2,1)S(1)}, u32[]{:S(2)}, u32[]{:S(2)}) collective-permute-start(bf16[256,2048]{1,0:T(8,128)(2,1)S(1)} %get-tuple-element.185), channel_id=1, source_target_pairs={{0,1},{1,0},{2,3},{3,2},{4,5},{5,4},{6,7},{7,6},{8,9},{9,8},{10,11... | collective-permute-start | bytes 3145736 | tf_op jit(solution)/shard_map/ppermute | solution.py:34
  574.4 49.0 %collective-permute-start.25 = (bf16[256,2048]{1,0:T(8,128)(2,1)S(1)}, bf16[256,2048]{1,0:T(8,128)(2,1)S(1)}, u32[]{:S(2)}, u32[]{:S(2)}) collective-permute-start(bf16[256,2048]{1,0:T(8,128)(2,1)S(1)} %get-tuple-element.185), channel_id=1, source_target_pairs={{0,2},{1,3},{2,0},{3,1},{4,6},{5,7},{6,4},{7,5},{8,10},{9,11},{10,... | collective-permute-start | bytes 3145736 | tf_op jit(solution)/shard_map/ppermute | solution.py:34
  575.5 47.9 %collective-permute-start.26 = (bf16[256,2048]{1,0:T(8,128)(2,1)S(1)}, bf16[256,2048]{1,0:T(8,128)(2,1)S(1)}, u32[]{:S(2)}, u32[]{:S(2)}) collective-permute-start(bf16[256,2048]{1,0:T(8,128)(2,1)S(1)} %get-tuple-element.185), channel_id=1, source_target_pairs={{0,3},{1,2},{2,1},{3,0},{4,7},{5,6},{6,5},{7,4},{8,11},{9,10},{10,... | collective-permute-start | bytes 3145736 | tf_op jit(solution)/shard_map/ppermute | solution.py:34
  578.7 41.9 %collective-permute-start.35 = (bf16[256,1408]{1,0:T(8,128)(2,1)S(1)}, bf16[256,1408]{1,0:T(8,128)(2,1)S(1)}, u32[]{:S(2)}, u32[]{:S(2)}) collective-permute-start(bf16[256,1408]{1,0:T(8,128)(2,1)S(1)} %get-tuple-element.274), channel_id=1, source_target_pairs={{0,4},{4,0},{8,12},{12,8},{1,5},{5,1},{9,13},{13,9},{2,6},{6,2},{1... | collective-permute-start | bytes 2162696 | tf_op jit(solution)/shard_map/ppermute | solution.py:34
  586.8 30.7 %collective-permute-start.34 = (bf16[256,1408]{1,0:T(8,128)(2,1)S(1)}, bf16[256,1408]{1,0:T(8,128)(2,1)S(1)}, u32[]{:S(2)}, u32[]{:S(2)}) collective-permute-start(bf16[256,1408]{1,0:T(8,128)(2,1)S(1)} %get-tuple-element.275), channel_id=1, source_target_pairs={{0,4},{4,0},{8,12},{12,8},{1,5},{5,1},{9,13},{13,9},{2,6},{6,2},{1... | collective-permute-start | bytes 2162696 | tf_op jit(solution)/shard_map/ppermute | solution.py:34
  617.6 44.0 %collective-permute-start.33 = (bf16[256,1408]{1,0:T(8,128)(2,1)}, bf16[256,1408]{1,0:T(8,128)(2,1)}, u32[]{:S(2)}, u32[]{:S(2)}) collective-permute-start(bf16[256,1408]{1,0:T(8,128)(2,1)} %get-tuple-element.276), channel_id=1, source_target_pairs={{0,4},{4,0},{8,12},{12,8},{1,5},{5,1},{9,13},{13,9},{2,6},{6,2},{1... | collective-permute-start | bytes 2162696 | tf_op jit(solution)/shard_map/ppermute | solution.py:34
  620.7 72.5 %collective-permute-start.31 = (bf16[1408,1024]{1,0:T(8,128)(2,1)}, bf16[1408,1024]{1,0:T(8,128)(2,1)}, u32[]{:S(2)}, u32[]{:S(2)}) collective-permute-start(bf16[1408,1024]{1,0:T(8,128)(2,1)} %convolution_convert_fusion.3), channel_id=1, source_target_pairs={{0,16},{16,0},{1,17},{17,1},{2,18},{18,2},{3,19},{19,3},{4,20},{20... | collective-permute-start | bytes 8650760 | tf_op jit(solution)/shard_map/ppermute | solution.py:34
  623.1 41.0 %collective-permute-start.32 = (bf16[256,1408]{1,0:T(8,128)(2,1)}, bf16[256,1408]{1,0:T(8,128)(2,1)}, u32[]{:S(2)}, u32[]{:S(2)}) collective-permute-start(bf16[256,1408]{1,0:T(8,128)(2,1)} %get-tuple-element.277), channel_id=1, source_target_pairs={{0,4},{4,0},{8,12},{12,8},{1,5},{5,1},{9,13},{13,9},{2,6},{6,2},{1... | collective-permute-start | bytes 2162696 | tf_op jit(solution)/shard_map/ppermute | solution.py:34
  661.0 32.1 %collective-permute-start.30 = (bf16[512,1024]{1,0:T(8,128)(2,1)S(1)}, bf16[512,1024]{1,0:T(8,128)(2,1)}, u32[]{:S(2)}, u32[]{:S(2)}) collective-permute-start(bf16[512,1024]{1,0:T(8,128)(2,1)S(1)} %fusion.19), channel_id=1, source_target_pairs={{0,16},{16,0},{1,17},{17,1},{2,18},{18,2},{3,19},{19,3},{4,20},{20... | collective-permute-start | bytes 3145736 | tf_op jit(solution)/shard_map/ppermute | solution.py:34
  665.6 17.7 %collective-permute-start.27 = (bf16[1024,128]{1,0:T(8,128)(2,1)S(1)}, bf16[1024,128]{1,0:T(8,128)(2,1)S(1)}, u32[]{:S(2)}, u32[]{:S(2)}) collective-permute-start(bf16[1024,128]{1,0:T(8,128)(2,1)S(1)} %get-tuple-element.191), channel_id=1, source_target_pairs={{0,4},{4,0},{8,12},{12,8},{1,5},{5,1},{9,13},{13,9},{2,6},{6,2},{1... | collective-permute-start | bytes 786440 | tf_op jit(solution)/shard_map/ppermute | solution.py:34
  671.8 21.3 %collective-permute-start.28 = (bf16[1024,128]{1,0:T(8,128)(2,1)S(1)}, bf16[1024,128]{1,0:T(8,128)(2,1)S(1)}, u32[]{:S(2)}, u32[]{:S(2)}) collective-permute-start(bf16[1024,128]{1,0:T(8,128)(2,1)S(1)} %get-tuple-element.192), channel_id=1, source_target_pairs={{0,8},{4,12},{8,0},{12,4},{1,9},{5,13},{9,1},{13,5},{2,10},{6,14},... | collective-permute-start | bytes 786440 | tf_op jit(solution)/shard_map/ppermute | solution.py:34
  673.0 20.2 %collective-permute-start.29 = (bf16[1024,128]{1,0:T(8,128)(2,1)S(1)}, bf16[1024,128]{1,0:T(8,128)(2,1)S(1)}, u32[]{:S(2)}, u32[]{:S(2)}) collective-permute-start(bf16[1024,128]{1,0:T(8,128)(2,1)S(1)} %get-tuple-element.193), channel_id=1, source_target_pairs={{0,12},{4,8},{8,4},{12,0},{1,13},{5,9},{9,5},{13,1},{2,14},{6,10},... | collective-permute-start | bytes 786440 | tf_op jit(solution)/shard_map/ppermute | solution.py:34
  696.3 66.3 %collective-permute-start.43 = (bf16[1408,256]{1,0:T(8,128)(2,1)}, bf16[1408,256]{1,0:T(8,128)(2,1)}, u32[]{:S(2)}, u32[]{:S(2)}) collective-permute-start(bf16[1408,256]{1,0:T(8,128)(2,1)} %get-tuple-element.272), channel_id=1, source_target_pairs={{0,4},{4,0},{8,12},{12,8},{1,5},{5,1},{9,13},{13,9},{2,6},{6,2},{1... | collective-permute-start | bytes 2162696 | tf_op jit(solution)/shard_map/ppermute | solution.py:34
  701.3 58.5 %collective-permute-start.42 = (bf16[1408,256]{1,0:T(8,128)(2,1)}, bf16[1408,256]{1,0:T(8,128)(2,1)}, u32[]{:S(2)}, u32[]{:S(2)}) collective-permute-start(bf16[1408,256]{1,0:T(8,128)(2,1)} %get-tuple-element.273), channel_id=1, source_target_pairs={{0,4},{4,0},{8,12},{12,8},{1,5},{5,1},{9,13},{13,9},{2,6},{6,2},{1... | collective-permute-start | bytes 2162696 | tf_op jit(solution)/shard_map/ppermute | solution.py:34
  703.2 92.7 %collective-permute-start.39 = (bf16[256,2048]{1,0:T(8,128)(2,1)}, bf16[256,2048]{1,0:T(8,128)(2,1)}, u32[]{:S(2)}, u32[]{:S(2)}) collective-permute-start(bf16[256,2048]{1,0:T(8,128)(2,1)} %get-tuple-element.280), channel_id=1, source_target_pairs={{0,1},{1,0},{2,3},{3,2},{4,5},{5,4},{6,7},{7,6},{8,9},{9,8},{10,11... | collective-permute-start | bytes 3145736 | tf_op jit(solution)/shard_map/ppermute | solution.py:34
  704.3 93.0 %collective-permute-start.40 = (bf16[256,2048]{1,0:T(8,128)(2,1)}, bf16[256,2048]{1,0:T(8,128)(2,1)}, u32[]{:S(2)}, u32[]{:S(2)}) collective-permute-start(bf16[256,2048]{1,0:T(8,128)(2,1)} %get-tuple-element.279), channel_id=1, source_target_pairs={{0,2},{1,3},{2,0},{3,1},{4,6},{5,7},{6,4},{7,5},{8,10},{9,11},{10,... | collective-permute-start | bytes 3145736 | tf_op jit(solution)/shard_map/ppermute | solution.py:34
  705.1 49.9 %collective-permute-start.63 = (bf16[256,1408]{1,0:T(8,128)(2,1)}, bf16[256,1408]{1,0:T(8,128)(2,1)}, u32[]{:S(2)}, u32[]{:S(2)}) collective-permute-start(bf16[256,1408]{1,0:T(8,128)(2,1)} %convert_add_fusion.8), channel_id=1, source_target_pairs={{0,8},{4,12},{8,0},{12,4},{1,9},{5,13},{9,1},{13,5},{2,10},{6,14},... | collective-permute-start | bytes 2162696 | tf_op jit(solution)/shard_map/ppermute | solution.py:34
  755.0 42.4 %collective-permute-start.41 = (bf16[256,2048]{1,0:T(8,128)(2,1)}, bf16[256,2048]{1,0:T(8,128)(2,1)S(1)}, u32[]{:S(2)}, u32[]{:S(2)}) collective-permute-start(bf16[256,2048]{1,0:T(8,128)(2,1)} %get-tuple-element.278), channel_id=1, source_target_pairs={{0,3},{1,2},{2,1},{3,0},{4,7},{5,6},{6,5},{7,4},{8,11},{9,10},{10,... | collective-permute-start | bytes 3145736 | tf_op jit(solution)/shard_map/ppermute | solution.py:34
  759.8 34.9 %collective-permute-start.62 = (bf16[256,1408]{1,0:T(8,128)(2,1)S(1)}, bf16[256,1408]{1,0:T(8,128)(2,1)S(1)}, u32[]{:S(2)}, u32[]{:S(2)}) collective-permute-start(bf16[256,1408]{1,0:T(8,128)(2,1)S(1)} %copy-done.43), channel_id=1, source_target_pairs={{0,8},{4,12},{8,0},{12,4},{1,9},{5,13},{9,1},{13,5},{2,10},{6,14},... | collective-permute-start | bytes 2162696 | tf_op jit(solution)/shard_map/ppermute | solution.py:34
  762.6 41.0 %collective-permute-start.36 = (bf16[1024,384]{1,0:T(8,128)(2,1)S(1)}, bf16[1024,384]{1,0:T(8,128)(2,1)S(1)}, u32[]{:S(2)}, u32[]{:S(2)}) collective-permute-start(bf16[1024,384]{1,0:T(8,128)(2,1)S(1)} %copy-done.57), channel_id=1, source_target_pairs={{0,4},{4,0},{8,12},{12,8},{1,5},{5,1},{9,13},{13,9},{2,6},{6,2},{1... | collective-permute-start | bytes 2359304 | tf_op jit(solution)/shard_map/ppermute | solution.py:34
  794.7 68.4 %collective-permute-start.37 = (bf16[1024,384]{1,0:T(8,128)(2,1)S(1)}, bf16[1024,384]{1,0:T(8,128)(2,1)S(1)}, u32[]{:S(2)}, u32[]{:S(2)}) collective-permute-start(bf16[1024,384]{1,0:T(8,128)(2,1)S(1)} %copy-done.56), channel_id=1, source_target_pairs={{0,8},{4,12},{8,0},{12,4},{1,9},{5,13},{9,1},{13,5},{2,10},{6,14},... | collective-permute-start | bytes 2359304 | tf_op jit(solution)/shard_map/ppermute | solution.py:34
  795.9 67.2 %collective-permute-start.38 = (bf16[1024,384]{1,0:T(8,128)(2,1)S(1)}, bf16[1024,384]{1,0:T(8,128)(2,1)S(1)}, u32[]{:S(2)}, u32[]{:S(2)}) collective-permute-start(bf16[1024,384]{1,0:T(8,128)(2,1)S(1)} %copy-done.55), channel_id=1, source_target_pairs={{0,12},{4,8},{8,4},{12,0},{1,13},{5,9},{9,5},{13,1},{2,14},{6,10},... | collective-permute-start | bytes 2359304 | tf_op jit(solution)/shard_map/ppermute | solution.py:34
  797.3 135.2 %collective-permute-start.64 = (bf16[1408,256]{1,0:T(8,128)(2,1)}, bf16[1408,256]{1,0:T(8,128)(2,1)}, u32[]{:S(2)}, u32[]{:S(2)}) collective-permute-start(bf16[1408,256]{1,0:T(8,128)(2,1)} %convert_add_fusion.6), channel_id=1, source_target_pairs={{0,8},{4,12},{8,0},{12,4},{1,9},{5,13},{9,1},{13,5},{2,10},{6,14},... | collective-permute-start | bytes 2162696 | tf_op jit(solution)/shard_map/ppermute | solution.py:34
  878.9 18.9 %collective-permute-start.56 = (f32[1,1536]{1,0:T(1,128)S(1)}, f32[1,1536]{1,0:T(1,128)S(1)}, u32[]{:S(2)}, u32[]{:S(2)}) collective-permute-start(f32[1,1536]{1,0:T(1,128)S(1)} %broadcast_in_dim.33), channel_id=1, source_target_pairs={{0,16},{16,0},{1,17},{17,1},{2,18},{18,2},{3,19},{19,3},{4,20},{20... | collective-permute-start | bytes 18440 | tf_op jit(solution)/shard_map/ppermute | solution.py:34
  880.3 33.0 %collective-permute-start.60 = (bf16[512,256]{1,0:T(8,128)(2,1)S(1)}, bf16[512,256]{1,0:T(8,128)(2,1)S(1)}, u32[]{:S(2)}, u32[]{:S(2)}) collective-permute-start(bf16[512,256]{1,0:T(8,128)(2,1)S(1)} %get-tuple-element.294), channel_id=1, source_target_pairs={{0,4},{4,0},{8,12},{12,8},{1,5},{5,1},{9,13},{13,9},{2,6},{6,2},{1... | collective-permute-start | bytes 786440 | tf_op jit(solution)/shard_map/ppermute | solution.py:34
  897.7 23.2 %collective-permute-start.59 = (bf16[512,256]{1,0:T(8,128)(2,1)S(1)}, bf16[512,256]{1,0:T(8,128)(2,1)S(1)}, u32[]{:S(2)}, u32[]{:S(2)}) collective-permute-start(bf16[512,256]{1,0:T(8,128)(2,1)S(1)} %get-tuple-element.293), channel_id=1, source_target_pairs={{0,4},{4,0},{8,12},{12,8},{1,5},{5,1},{9,13},{13,9},{2,6},{6,2},{1... | collective-permute-start | bytes 786440 | tf_op jit(solution)/shard_map/ppermute | solution.py:34
  897.8 12.6 %collective-permute-start.57 = (f32[1,1536]{1,0:T(1,128)S(1)}, f32[1,1536]{1,0:T(1,128)S(1)}, u32[]{:S(2)}, u32[]{:S(2)}) collective-permute-start(f32[1,1536]{1,0:T(1,128)S(1)} %reshape_add_fusion), channel_id=1, source_target_pairs={{0,4},{4,0},{8,12},{12,8},{1,5},{5,1},{9,13},{13,9},{2,6},{6,2},{1... | collective-permute-start | bytes 18440 | tf_op jit(solution)/shard_map/ppermute | solution.py:34
  904.7 74.8 %collective-permute-start.52 = (bf16[1024,1536]{1,0:T(8,128)(2,1)}, bf16[1024,1536]{1,0:T(8,128)(2,1)}, u32[]{:S(2)}, u32[]{:S(2)}) collective-permute-start(bf16[1024,1536]{1,0:T(8,128)(2,1)} %convolution_convert_fusion.1), channel_id=1, source_target_pairs={{0,16},{16,0},{1,17},{17,1},{2,18},{18,2},{3,19},{19,3},{4,20},{20... | collective-permute-start | bytes 9437192 | tf_op jit(solution)/shard_map/ppermute | solution.py:34
  910.4 9.3 collective-permute-start.58
  914.3 14.1 %collective-permute-start.61 = (bf16[512,256]{1,0:T(8,128)(2,1)S(1)}, bf16[512,256]{1,0:T(8,128)(2,1)S(1)}, u32[]{:S(2)}, u32[]{:S(2)}) collective-permute-start(bf16[512,256]{1,0:T(8,128)(2,1)S(1)} %add_convert_fusion.11), channel_id=1, source_target_pairs={{0,8},{4,12},{8,0},{12,4},{1,9},{5,13},{9,1},{13,5},{2,10},{6,14},... | collective-permute-start | bytes 786440 | tf_op jit(solution)/shard_map/ppermute | solution.py:34
  919.8 26.2 %collective-permute-start.44 = (bf16[256,2048]{1,0:T(8,128)(2,1)S(1)}, bf16[256,2048]{1,0:T(8,128)(2,1)}, u32[]{:S(2)}, u32[]{:S(2)}) collective-permute-start(bf16[256,2048]{1,0:T(8,128)(2,1)S(1)} %get-tuple-element.232), channel_id=1, source_target_pairs={{0,1},{1,0},{2,3},{3,2},{4,5},{5,4},{6,7},{7,6},{8,9},{9,8},{10,11... | collective-permute-start | bytes 3145736 | tf_op jit(solution)/shard_map/ppermute | solution.py:34
  920.9 46.8 %collective-permute-start.45 = (bf16[256,2048]{1,0:T(8,128)(2,1)S(1)}, bf16[256,2048]{1,0:T(8,128)(2,1)}, u32[]{:S(2)}, u32[]{:S(2)}) collective-permute-start(bf16[256,2048]{1,0:T(8,128)(2,1)S(1)} %get-tuple-element.233), channel_id=1, source_target_pairs={{0,2},{1,3},{2,0},{3,1},{4,6},{5,7},{6,4},{7,5},{8,10},{9,11},{10,... | collective-permute-start | bytes 3145736 | tf_op jit(solution)/shard_map/ppermute | solution.py:34
  928.4 39.3 %collective-permute-start.46 = (bf16[256,2048]{1,0:T(8,128)(2,1)S(1)}, bf16[256,2048]{1,0:T(8,128)(2,1)}, u32[]{:S(2)}, u32[]{:S(2)}) collective-permute-start(bf16[256,2048]{1,0:T(8,128)(2,1)S(1)} %get-tuple-element.234), channel_id=1, source_target_pairs={{0,3},{1,2},{2,1},{3,0},{4,7},{5,6},{6,5},{7,4},{8,11},{9,10},{10,... | collective-permute-start | bytes 3145736 | tf_op jit(solution)/shard_map/ppermute | solution.py:34
  973.0 4.0 collective-permute-start.48
  977.0 5.8 collective-permute-start.49
  981.3 20.5 %collective-permute-start.54 = (bf16[256,1536]{1,0:T(8,128)(2,1)S(1)}, bf16[256,1536]{1,0:T(8,128)(2,1)S(1)}, u32[]{:S(2)}, u32[]{:S(2)}) collective-permute-start(bf16[256,1536]{1,0:T(8,128)(2,1)S(1)} %get-tuple-element.271), channel_id=1, source_target_pairs={{0,4},{4,0},{8,12},{12,8},{1,5},{5,1},{9,13},{13,9},{2,6},{6,2},{1... | collective-permute-start | bytes 2359304 | tf_op jit(solution)/shard_map/ppermute | solution.py:34
  982.8 4.0 collective-permute-start.50
  986.8 18.7 %collective-permute-start.51 = (f32[4,2048]{1,0:T(4,128)S(1)}, f32[4,2048]{1,0:T(4,128)S(1)}, u32[]{:S(2)}, u32[]{:S(2)}) collective-permute-start(f32[4,2048]{1,0:T(4,128)S(1)} %add.544), channel_id=1, source_target_pairs={{0,2},{1,3},{2,0},{3,1},{4,6},{5,7},{6,4},{7,5},{8,10},{9,11},{10,... | collective-permute-start | bytes 98312 | tf_op jit(solution)/shard_map/ppermute | solution.py:34
  987.4 43.1 %collective-permute-start.53 = (bf16[256,1536]{1,0:T(8,128)(2,1)S(1)}, bf16[256,1536]{1,0:T(8,128)(2,1)S(1)}, u32[]{:S(2)}, u32[]{:S(2)}) collective-permute-start(bf16[256,1536]{1,0:T(8,128)(2,1)S(1)} %get-tuple-element.270), channel_id=1, source_target_pairs={{0,4},{4,0},{8,12},{12,8},{1,5},{5,1},{9,13},{13,9},{2,6},{6,2},{1... | collective-permute-start | bytes 2359304 | tf_op jit(solution)/shard_map/ppermute | solution.py:34
  1003.2 33.0 %collective-permute-start.55 = (bf16[256,1536]{1,0:T(8,128)(2,1)S(1)}, bf16[256,1536]{1,0:T(8,128)(2,1)S(1)}, u32[]{:S(2)}, u32[]{:S(2)}) collective-permute-start(bf16[256,1536]{1,0:T(8,128)(2,1)S(1)} %add_convert_fusion.2), channel_id=1, source_target_pairs={{0,8},{4,12},{8,0},{12,4},{1,9},{5,13},{9,1},{13,5},{2,10},{6,14},... | collective-permute-start | bytes 2359304 | tf_op jit(solution)/shard_map/ppermute | solution.py:34
  (77 other events, 1284.5 us)
where the time goes:
time: 1060 us; the launch traced here: 1040 us
  local copies, waits for them, and re-layouts  308 us (29%)
  waiting for transfers between devices  276 us (26%)
  matrix products  163 us (15%)
  Pallas kernels  117 us (11%)
  starting transfers between devices  101 us (10%)
  other arithmetic  72.7 us (7%)
    ppermute x65, waiting for transfers between devices, swap_with(): return lax.ppermute(x, axis, [(i, i ^ bit) for i in range(size)])  276 us
    dynamic_update_slice x32, local copies, waits for them, and re-layouts, fill(): out = lax.dynamic_update_slice_in_dim(out, block, origin + i * size, axis)  259 us
    dot_general x29, matrix products, dot(): return lax.dot_general(a, b, dims, preferred_element_type=f32)  151 us
    ppermute x65, starting transfers between devices, swap_with(): return lax.ppermute(x, axis, [(i, i ^ bit) for i in range(size)])  101 us
    pallas_call x1, Pallas kernels, attend_back(): pl.pallas_call(functools.partial(attend_back_kernel, dims), grid_spec=plt...  47.6 us
    pallas_call x1, Pallas kernels, attend(): pl.pallas_call(functools.partial(attend_kernel, dims), grid_spec=pltpu.Pr...  33.5 us
    add x11, other arithmetic, scatter_step(): parts[d ^ bit]  22.8 us
  transfers between devices with their start and end apart: 65, of which 23 were waited for; matrix products, arithmetic and copies ran while one was open for 44% of the time, Pallas kernels for 6%

commit v1 on v0

--- a/solution.py
+++ b/solution.py
@@ -521,16 +521,6 @@
     return out[0], out[1:]
 
 
-def fill(blocks, axis, origin):
-    shape = list(blocks[0].shape)
-    size = shape[axis]
-    shape[axis] = size * len(blocks)
-    out = jnp.zeros(shape, blocks[0].dtype)
-    for i, block in enumerate(blocks):
-        out = lax.dynamic_update_slice_in_dim(out, block, origin + i * size, axis)
-    return out
-
-
 def hold(*groups):
     return lax.optimization_barrier(groups)
 
@@ -584,8 +574,6 @@
     def other_half(x):
         return swap_with(x, "shard", 1)
 
-    origin = jnp.minimum(me, 0)
-
     own_qkv = (q_weight, k_weight, v_weight)
     oth_qkv = tuple(other_half(w) for w in own_qkv)
     doc_ends = jnp.cumsum(doc_lengths[0])
@@ -631,13 +619,13 @@
         other_half, (down_weight, o_weight, gate_weight, up_weight)
     )
     full_tables = rotary_tables(positions)
-    cot_all = by_shard(fill([slot_rows(cot_rows, i) for i in range(slots)], 0, origin))
+    cot_all = by_shard(jnp.concatenate([slot_rows(cot_rows, i) for i in range(slots)], axis=0))
     x_share = by_shard(slot_rows(x_rows, 0)).astype(f32)
-    down_full = fill([down_weight, down_oth], 1, origin)
-    o_full = fill([o_weight, o_oth], 1, origin)
+    down_full = jnp.concatenate([down_weight, down_oth], axis=1)
+    o_full = jnp.concatenate([o_weight, o_oth], axis=1)
     dm_all = dot(cot_all, down_full, NT)
-    gate_full = fill([gate_weight, gate_oth], 0, origin)
-    up_full = fill([up_weight, up_oth], 0, origin)
+    gate_full = jnp.concatenate([gate_weight, gate_oth], axis=0)
+    up_full = jnp.concatenate([up_weight, up_oth], axis=0)
     gain_two = by_shard(ln2_gain.astype(f32))
     shift_two = by_shard(ln2_shift.astype(f32))
     gain_one = by_shard(ln1_gain.astype(f32))
@@ -718,7 +706,7 @@
         return parts[0]
 
     h2_all, gate_all, up_all, hidden_all = (
-        fill(blocks, 0, origin) for blocks in (h2, gate_grad, up_grad, hidden)
+        jnp.concatenate(blocks, axis=0) for blocks in (h2, gate_grad, up_grad, hidden)
     )
 
     norm2_parts, h2_all, gate_all, up_all = hold(norm2_parts, h2_all, gate_all, up_all)
@@ -750,7 +738,7 @@
     out_all = dot(hidden_all, down_full).astype(bf16)
     down_theirs = other_half(down_theirs)
     dx1_rest, dx1_own, out_all, down_mine = hold(dx1_slots[1:], dx1_own, out_all, down_mine)
-    dx1b = fill([dx1_own] + dx1_rest, 0, origin)
+    dx1b = jnp.concatenate([dx1_own] + dx1_rest, axis=0)
     d_attn = dot(dx1b, o_full, NT).astype(bf16)
     d_send = [
         lax.dynamic_slice_in_dim(d_attn, ((ctx & (groups - 1)) ^ s) * PAIR, PAIR, 1)
@@ -787,7 +775,8 @@
     dh1_received = send_rows(norm1_parts)
     qkv_theirs = other_half(dot(h1[:, half:], d_qkv, TN).astype(bf16))
     qkv_mine = dot(h1[:, :half], d_qkv, TN).astype(bf16)
-    qkv_grad = scatter_rest(scatter_step(blocks_of(qkv_mine, qkv_theirs, 0), 1))
+    qkv_parts = scatter_step(blocks_of(qkv_mine, qkv_theirs, 0), 1)
+    qkv_grad = scatter_rest(qkv_parts)
     bias = jnp.sum(d_qkv.astype(f32), axis=0, keepdims=True)
     bias = sum_over(sum_over(bias, "shard"), "context")[0]
     dh1_received, qkv_mine = hold(dh1_received, qkv_mine)

time: 1060 us -> 844 us (0.80); the launches traced: 1040 us -> 834 us
  local copies, waits for them, and re-layouts: 308 us -> 24.1 us
  waiting for transfers between devices: 276 us -> 346 us
  matrix products: 163 us -> 117 us
  other arithmetic: 72.7 us -> 100 us
  starting transfers between devices: 101 us -> 128 us
    dynamic_update_slice x32 -> x0, local copies, waits for them, and re-layouts: 259 us -> none  [fill(): out = lax.dynamic_update_slice_in_dim(out, block, origin + i * size, axis)]
    ppermute x65, waiting for transfers between devices: 276 us -> 346 us  [swap_with(): return lax.ppermute(x, axis, [(i, i ^ bit) for i in range(size)])]
    dot_general x29, matrix products: 151 us -> 105 us  [dot(): return lax.dot_general(a, b, dims, preferred_element_type=f32)]
    ppermute x65, starting transfers between devices: 101 us -> 128 us  [swap_with(): return lax.ppermute(x, axis, [(i, i ^ bit) for i in range(size)])]
    concatenate x0 -> x8, other arithmetic: none -> 27.1 us  [the longest x4 15.4 us: local(): jnp.concatenate(blocks, axis=0)]
    another operation x8 -> x0, local copies, waits for them, and re-layouts: 18.9 us -> none
  transfers between devices with their start and end apart: 65 -> 65, of which waited for: 23 -> 28; matrix products, arithmetic and copies ran while one was open for 44% -> 22% of each run, Pallas kernels for 6% -> 7%
where the time goes in v1:
time: 844 us; the launch traced here: 834 us
  waiting for transfers between devices  346 us (41%)
  starting transfers between devices  128 us (15%)
  matrix products  117 us (14%)
  Pallas kernels  117 us (14%)
  other arithmetic  100 us (12%)
  local copies, waits for them, and re-layouts  24.1 us (3%)
    ppermute x65, waiting for transfers between devices, swap_with(): return lax.ppermute(x, axis, [(i, i ^ bit) for i in range(size)])  346 us
    ppermute x65, starting transfers between devices, swap_with(): return lax.ppermute(x, axis, [(i, i ^ bit) for i in range(size)])  128 us
    dot_general x29, matrix products, dot(): return lax.dot_general(a, b, dims, preferred_element_type=f32)  105 us
    pallas_call x1, Pallas kernels, attend_back(): pl.pallas_call(functools.partial(attend_back_kernel, dims), grid_spec=plt...  47.8 us
    pallas_call x1, Pallas kernels, attend(): pl.pallas_call(functools.partial(attend_kernel, dims), grid_spec=pltpu.Pr...  33.6 us
    add x11, other arithmetic, scatter_step(): parts[d ^ bit]  22.1 us
    pallas_call x2, Pallas kernels, join(): pl.pallas_call(functools.partial(join_kernel, groups, kinds, slots, dims)...  19.4 us
  transfers between devices with their start and end apart: 65, of which 28 were waited for; matrix products, arithmetic and copies ran while one was open for 22% of the time, Pallas kernels for 7%

profile of v1, /device:TPU:0, one launch (start us, length us, event | category | flops | bytes accessed | tf_op | source)
XLA Modules:
  0.0 834.3 jit_solution(14136188160867013159)
XLA Ops:
  15.0 16.3 %project.1 = (bf16[1024,2048]{1,0:T(8,128)(2,1)}, bf16[1024,384]{1,0:T(8,128)(2,1)}, bf16[1024,384]{1,0:T(8,128)(2,1)}, bf16[1024,384]{1,0:T(8,128)(2,1)}, bf16[1024,384]{1,0:T(8,128)(2,1)}) custom-call(s32[12]{0:T(128)} %concatenate.71.ids, bf16[1024,2048]{1,0:T(8,128)(2,1)} %bitcast.80, bf16[1024,2048]{1,0:T(8,128)(2,1)} %bitcast.81, ...), custom_call_target="tpu_custom_call" | custom-call | flops 6442450944 | bytes 17825792 | tf_op jit(solution)/shard_map/project/pallas_call | solution.py:145
  34.4 3.2 convolution_add_fusion.refs_10_
  39.1 4.8 fusion.28.refs_11_
  48.2 9.4 %maximum_select_fusion = bf16[1024,2048]{1,0:T(8,128)(2,1)S(1)} fusion(bf16[1024,1024]{1,0:T(8,128)(2,1)S(1)} %get-tuple-element.284, bf16[1024,1024]{1,0:T(8,128)(2,1)S(1)} %get-tuple-element.283, pred[]{:T(512)S(6)} %eq.23, bf16[256,2048]{1,0:T(8,128)(2,1)S(1)} %get-tuple-element.286, bf16[256,2048]{1,0:T(8,128)(2,1)S(1)} %get-tuple-element.287, ...), kind=kLoop, calls=%fused_computation.5 | loop fusion | flops 27262976 | bytes 12582913 | tf_op jit(solution)/shard_map/jit(_where)/select_n | solution.py:569
  57.6 3.8 fusion.26
  67.5 10.5 %fusion.66 = f32[1024,1408]{1,0:T(8,128)} fusion(bf16[1024,2048]{1,0:T(8,128)(2,1)S(1)} %maximum_select_fusion, bf16[1408,2048]{1,0:T(8,128)(2,1)} %constant_dynamic-update-slice_fusion), kind=kOutput, calls=%fused_computation.193 | convolution fusion | flops 5905580032 | bytes 15728640 | tf_op jit(solution)/shard_map/dot_general | solution.py:29
  78.0 4.7 pad_maximum_fusion
  82.7 4.8 pad_maximum_fusion.1
  87.5 29.1 %collective-permute-done.4.refs_2_ = bf16[1024,384]{1,0:T(8,128)(2,1)} collective-permute-done((bf16[1024,384]{1,0:T(8,128)(2,1)S(1)}, bf16[1024,384]{1,0:T(8,128)(2,1)}, u32[]{:S(2)}, u32[]{:S(2)}) %collective-permute-start.4) | collective-permute-done | bytes 786464 | tf_op jit(solution)/shard_map/ppermute | solution.py:34
  117.5 33.6 %attend.1 = (bf16[1024,128]{1,0:T(8,128)(2,1)}, bf16[1024,128]{1,0:T(8,128)(2,1)}, bf16[1024,128]{1,0:T(8,128)(2,1)}, bf16[1024,128]{1,0:T(8,128)(2,1)}, f32[128,4096]{1,0:T(8,128)}, /*index=5*/f32[8,4096]{1,0:T(8,128)}) custom-call(s32[12]{0:T(128)} %concatenate.71.ids, bf16[1024,384]{1,0:T(8,128)(2,1)} %get-tuple-element.147.refs_0_, ...), custom_call_target="tpu_custom_call" | custom-call | flops 17179869184 | bytes 8388608 | tf_op jit(solution)/shard_map/attend/pallas_call | solution.py:297
  151.0 16.6 %collective-permute-start.10 = (bf16[1024,128]{1,0:T(8,128)(2,1)}, bf16[1024,128]{1,0:T(8,128)(2,1)S(1)}, u32[]{:S(2)}, u32[]{:S(2)}) collective-permute-start(bf16[1024,128]{1,0:T(8,128)(2,1)} %get-tuple-element.154), channel_id=1, source_target_pairs={{0,4},{4,0},{8,12},{12,8},{1,5},{5,1},{9,13},{13,9},{2,6},{6,2},{1... | collective-permute-start | bytes 786440 | tf_op jit(solution)/shard_map/ppermute | solution.py:34
  172.2 5.0 collective-permute-done.11.refs_2_
  177.2 7.7 collective-permute-done.12.refs_3_
  185.8 6.1 shard_map.297
  198.2 15.4 %collective-permute-done.13 = bf16[256,2048]{1,0:T(8,128)(2,1)} collective-permute-done((bf16[256,2048]{1,0:T(8,128)(2,1)}, bf16[256,2048]{1,0:T(8,128)(2,1)}, u32[]{:S(2)}, u32[]{:S(2)}) %collective-permute-start.13) | collective-permute-done | bytes 1048608 | tf_op jit(solution)/shard_map/ppermute | solution.py:34
  216.1 21.0 %collective-permute-done.15 = bf16[256,2048]{1,0:T(8,128)(2,1)} collective-permute-done((bf16[256,2048]{1,0:T(8,128)(2,1)S(1)}, bf16[256,2048]{1,0:T(8,128)(2,1)}, u32[]{:S(2)}, u32[]{:S(2)}) %collective-permute-start.15) | collective-permute-done | bytes 1048608 | tf_op jit(solution)/shard_map/ppermute | solution.py:34
  237.1 3.3 fusion.53
  245.3 4.6 fusion.67
  250.0 3.3 multiply_convert_fusion.11
  255.1 3.2 convolution_add_fusion.4
  258.3 4.7 collective-permute-done.16
  264.8 3.3 multiply_convert_fusion.9
  270.1 2.8 fusion
  274.7 3.2 multiply_convert_fusion.7
  279.8 2.8 fusion.1
  287.3 5.7 multiply_convert_fusion.5
  293.0 5.2 pad_maximum_fusion.5
  300.0 4.8 pad_maximum_fusion.4
  307.5 4.9 convolution_convert_fusion.7
  312.4 5.0 convolution_convert_fusion.8
  317.4 16.5 %collective-permute-start.22 = (bf16[1024,1408]{1,0:T(8,128)(2,1)}, bf16[1024,1408]{1,0:T(8,128)(2,1)}, u32[]{:S(2)}, u32[]{:S(2)}) collective-permute-start(bf16[1024,1408]{1,0:T(8,128)(2,1)} %convolution_convert_fusion.8), channel_id=1, source_target_pairs={{0,16},{16,0},{1,17},{17,1},{2,18},{18,2},{3,19},{19,3},{4,20},{20... | collective-permute-start | bytes 8650760 | tf_op jit(solution)/shard_map/ppermute | solution.py:34
  337.6 5.9 convolution_convert_fusion.5
  343.6 4.8 pad_maximum_fusion.6
  348.4 3.8 convolution_convert_fusion.6
  352.2 9.1 %collective-permute-done.21 = bf16[256,2048]{1,0:T(8,128)(2,1)S(1)} collective-permute-done((bf16[256,2048]{1,0:T(8,128)(2,1)}, bf16[256,2048]{1,0:T(8,128)(2,1)S(1)}, u32[]{:S(2)}, u32[]{:S(2)}) %collective-permute-start.21) | collective-permute-done | bytes 1048608 | tf_op jit(solution)/shard_map/ppermute | solution.py:34
  361.3 21.1 %collective-permute-done.20 = bf16[256,2048]{1,0:T(8,128)(2,1)S(1)} collective-permute-done((bf16[256,2048]{1,0:T(8,128)(2,1)}, bf16[256,2048]{1,0:T(8,128)(2,1)S(1)}, u32[]{:S(2)}, u32[]{:S(2)}) %collective-permute-start.20) | collective-permute-done | bytes 1048608 | tf_op jit(solution)/shard_map/ppermute | solution.py:34
  391.3 12.7 %collective-permute-start.35 = (bf16[256,1408]{1,0:T(8,128)(2,1)S(1)}, bf16[256,1408]{1,0:T(8,128)(2,1)S(1)}, u32[]{:S(2)}, u32[]{:S(2)}) collective-permute-start(bf16[256,1408]{1,0:T(8,128)(2,1)S(1)} %get-tuple-element.274), channel_id=1, source_target_pairs={{0,4},{4,0},{8,12},{12,8},{1,5},{5,1},{9,13},{13,9},{2,6},{6,2},{1... | collective-permute-start | bytes 2162696 | tf_op jit(solution)/shard_map/ppermute | solution.py:34
  404.1 4.7 convolution_convert_fusion.3
  408.8 7.0 convolution_convert_fusion
  415.8 3.5 convolution_convert_fusion.4
  425.3 11.2 %collective-permute-done.34 = bf16[256,1408]{1,0:T(8,128)(2,1)S(1)} collective-permute-done((bf16[256,1408]{1,0:T(8,128)(2,1)S(1)}, bf16[256,1408]{1,0:T(8,128)(2,1)S(1)}, u32[]{:S(2)}, u32[]{:S(2)}) %collective-permute-start.34) | collective-permute-done | bytes 720928 | tf_op jit(solution)/shard_map/ppermute | solution.py:34
  447.3 4.6 collective-permute-done.33
  454.2 11.7 %collective-permute-done.32 = bf16[256,1408]{1,0:T(8,128)(2,1)S(1)} collective-permute-done((bf16[256,1408]{1,0:T(8,128)(2,1)S(1)}, bf16[256,1408]{1,0:T(8,128)(2,1)S(1)}, u32[]{:S(2)}, u32[]{:S(2)}) %collective-permute-start.32) | collective-permute-done | bytes 720928 | tf_op jit(solution)/shard_map/ppermute | solution.py:34
  474.3 3.7 collective-permute-done.27.refs_5_
  478.0 12.3 %collective-permute-done.28.refs_6_ = bf16[1024,128]{1,0:T(8,128)(2,1)S(1)} collective-permute-done((bf16[1024,128]{1,0:T(8,128)(2,1)S(1)}, bf16[1024,128]{1,0:T(8,128)(2,1)S(1)}, u32[]{:S(2)}, u32[]{:S(2)}) %collective-permute-start.28) | collective-permute-done | bytes 262176 | tf_op jit(solution)/shard_map/ppermute | solution.py:34
  492.6 3.4 collective-permute-start.43
  499.2 3.7 collective-permute-start.63
  502.9 47.8 %attend_back.1 = (bf16[1024,384]{1,0:T(8,128)(2,1)}, bf16[1024,384]{1,0:T(8,128)(2,1)}, bf16[1024,384]{1,0:T(8,128)(2,1)}, bf16[1024,384]{1,0:T(8,128)(2,1)}) custom-call(s32[12]{0:T(128)} %concatenate.71.ids, bf16[1024,384]{1,0:T(8,128)(2,1)} %get-tuple-element.147.refs_0_, bf16[1024,384]{1,0:T(8,128)(2,1)} %collective-permute-done.3.refs_1_, ...), custom_call_target="tpu_custom_call" | custom-call | flops 42949672960 | bytes 8388608 | tf_op jit(solution)/shard_map/attend_back/pallas_call | solution.py:436
  561.5 28.0 %collective-permute-done.62 = bf16[256,1408]{1,0:T(8,128)(2,1)S(1)} collective-permute-done((bf16[256,1408]{1,0:T(8,128)(2,1)S(1)}, bf16[256,1408]{1,0:T(8,128)(2,1)S(1)}, u32[]{:S(2)}, u32[]{:S(2)}) %collective-permute-start.62) | collective-permute-done | bytes 720928 | tf_op jit(solution)/shard_map/ppermute | solution.py:34
  598.5 59.5 %collective-permute-done.37.refs_2_ = bf16[1024,384]{1,0:T(8,128)(2,1)S(1)} collective-permute-done((bf16[1024,384]{1,0:T(8,128)(2,1)S(1)}, bf16[1024,384]{1,0:T(8,128)(2,1)S(1)}, u32[]{:S(2)}, u32[]{:S(2)}) %collective-permute-start.37) | collective-permute-done | bytes 786464 | tf_op jit(solution)/shard_map/ppermute | solution.py:34
  658.0 13.3 %shard_map.298 = (bf16[1024,1536]{1,0:T(8,128)(2,1)}, f32[256,2048]{1,0:T(8,128)}, bf16[256,2048]{1,0:T(8,128)(2,1)S(1)}, bf16[256,2048]{1,0:T(8,128)(2,1)S(1)}, bf16[256,2048]{1,0:T(8,128)(2,1)S(1)}) custom-call(s32[12]{0:T(128)S(1)} %copy-done.2, bf16[1024,384]{1,0:T(8,128)(2,1)S(1)} %copy-done.9, bf16[1024,384]{1,0:T(8,128)(2,1)S(1)} %collective-permute-done.36.refs_1_, ...), custom_call_target="tpu_custom_call" | custom-call | flops 6442450944 | bytes 18874368 | tf_op jit(solution)/shard_map/pallas_call | solution.py:502
  675.2 17.5 %collective-permute-start.60 = (bf16[512,256]{1,0:T(8,128)(2,1)S(1)}, bf16[512,256]{1,0:T(8,128)(2,1)S(1)}, u32[]{:S(2)}, u32[]{:S(2)}) collective-permute-start(bf16[512,256]{1,0:T(8,128)(2,1)S(1)} %get-tuple-element.294), channel_id=1, source_target_pairs={{0,4},{4,0},{8,12},{12,8},{1,5},{5,1},{9,13},{13,9},{2,6},{6,2},{1... | collective-permute-start | bytes 786440 | tf_op jit(solution)/shard_map/ppermute | solution.py:34
  694.8 5.0 convolution_convert_fusion.1
  699.9 5.5 collective-permute-done.57
  709.5 4.8 convolution_convert_fusion.2
  716.3 7.1 collective-permute-done.61
  730.8 9.8 %collective-permute-done.44 = bf16[256,2048]{1,0:T(8,128)(2,1)} collective-permute-done((bf16[256,2048]{1,0:T(8,128)(2,1)S(1)}, bf16[256,2048]{1,0:T(8,128)(2,1)}, u32[]{:S(2)}, u32[]{:S(2)}) %collective-permute-start.44) | collective-permute-done | bytes 1048608 | tf_op jit(solution)/shard_map/ppermute | solution.py:34
  740.5 22.3 %collective-permute-done.45 = bf16[256,2048]{1,0:T(8,128)(2,1)} collective-permute-done((bf16[256,2048]{1,0:T(8,128)(2,1)S(1)}, bf16[256,2048]{1,0:T(8,128)(2,1)}, u32[]{:S(2)}, u32[]{:S(2)}) %collective-permute-start.45) | collective-permute-done | bytes 1048608 | tf_op jit(solution)/shard_map/ppermute | solution.py:34
  762.9 3.9 multiply_reduce_fusion.1
  769.2 2.9 collective-permute-done.48
  778.7 3.3 collective-permute-done.50
  784.0 13.1 %collective-permute-done.54 = bf16[256,1536]{1,0:T(8,128)(2,1)S(1)} collective-permute-done((bf16[256,1536]{1,0:T(8,128)(2,1)S(1)}, bf16[256,1536]{1,0:T(8,128)(2,1)S(1)}, u32[]{:S(2)}, u32[]{:S(2)}) %collective-permute-start.54) | collective-permute-done | bytes 786464 | tf_op jit(solution)/shard_map/ppermute | solution.py:34
  801.3 24.3 %collective-permute-done.53 = bf16[256,1536]{1,0:T(8,128)(2,1)S(1)} collective-permute-done((bf16[256,1536]{1,0:T(8,128)(2,1)S(1)}, bf16[256,1536]{1,0:T(8,128)(2,1)S(1)}, u32[]{:S(2)}, u32[]{:S(2)}) %collective-permute-start.53) | collective-permute-done | bytes 786464 | tf_op jit(solution)/shard_map/ppermute | solution.py:34
  825.6 5.8 collective-permute-done.55
  (338 shorter events, 170.3 us)
Async XLA Ops:
  0.6 13.1 %collective-permute-start = (bf16[1024,512]{1,0:T(8,128)(2,1)}, bf16[1024,512]{1,0:T(8,128)(2,1)S(1)}, u32[]{:S(2)}, u32[]{:S(2)}) collective-permute-start(bf16[1024,512]{1,0:T(8,128)(2,1)} %refs_4_.2), channel_id=1, source_target_pairs={{0,16},{16,0},{1,17},{17,1},{2,18},{18,2},{3,19},{19,3},{4,20},{20... | collective-permute-start | bytes 3145736 | tf_op jit(solution)/shard_map/ppermute | solution.py:34
  1.2 12.6 %collective-permute-start.1 = (bf16[1024,512]{1,0:T(8,128)(2,1)}, bf16[1024,512]{1,0:T(8,128)(2,1)S(1)}, u32[]{:S(2)}, u32[]{:S(2)}) collective-permute-start(bf16[1024,512]{1,0:T(8,128)(2,1)} %refs_5_.1), channel_id=1, source_target_pairs={{0,16},{16,0},{1,17},{17,1},{2,18},{18,2},{3,19},{19,3},{4,20},{20... | collective-permute-start | bytes 3145736 | tf_op jit(solution)/shard_map/ppermute | solution.py:34
  1.3 12.5 %collective-permute-start.2 = (bf16[1024,512]{1,0:T(8,128)(2,1)}, bf16[1024,512]{1,0:T(8,128)(2,1)}, u32[]{:S(2)}, u32[]{:S(2)}) collective-permute-start(bf16[1024,512]{1,0:T(8,128)(2,1)} %refs_6_.1), channel_id=1, source_target_pairs={{0,16},{16,0},{1,17},{17,1},{2,18},{18,2},{3,19},{19,3},{4,20},{20... | collective-permute-start | bytes 3145736 | tf_op jit(solution)/shard_map/ppermute | solution.py:34
  33.3 32.3 %collective-permute-start.6 = (bf16[1408,1024]{1,0:T(8,128)(2,1)S(1)}, bf16[1408,1024]{1,0:T(8,128)(2,1)S(1)}, u32[]{:S(2)}, u32[]{:S(2)}) collective-permute-start(bf16[1408,1024]{1,0:T(8,128)(2,1)S(1)} %copy-done.23), channel_id=1, source_target_pairs={{0,16},{16,0},{1,17},{17,1},{2,18},{18,2},{3,19},{19,3},{4,20},{20... | collective-permute-start | bytes 8650760 | tf_op jit(solution)/shard_map/ppermute | solution.py:34
  33.4 27.9 %collective-permute-start.7 = (bf16[512,1024]{1,0:T(8,128)(2,1)S(1)}, bf16[512,1024]{1,0:T(8,128)(2,1)S(1)}, u32[]{:S(2)}, u32[]{:S(2)}) collective-permute-start(bf16[512,1024]{1,0:T(8,128)(2,1)S(1)} %copy-done), channel_id=1, source_target_pairs={{0,16},{16,0},{1,17},{17,1},{2,18},{18,2},{3,19},{19,3},{4,20},{20... | collective-permute-start | bytes 3145736 | tf_op jit(solution)/shard_map/ppermute | solution.py:34
  43.9 34.1 %collective-permute-start.8 = (bf16[1024,1408]{1,0:T(8,128)(2,1)S(1)}, bf16[1024,1408]{1,0:T(8,128)(2,1)}, u32[]{:S(2)}, u32[]{:S(2)}) collective-permute-start(bf16[1024,1408]{1,0:T(8,128)(2,1)S(1)} %copy-done.27), channel_id=1, source_target_pairs={{0,16},{16,0},{1,17},{17,1},{2,18},{18,2},{3,19},{19,3},{4,20},{20... | collective-permute-start | bytes 8650760 | tf_op jit(solution)/shard_map/ppermute | solution.py:34
  44.0 38.7 %collective-permute-start.9 = (bf16[1024,1408]{1,0:T(8,128)(2,1)S(1)}, bf16[1024,1408]{1,0:T(8,128)(2,1)}, u32[]{:S(2)}, u32[]{:S(2)}) collective-permute-start(bf16[1024,1408]{1,0:T(8,128)(2,1)S(1)} %copy-done.28), channel_id=1, source_target_pairs={{0,16},{16,0},{1,17},{17,1},{2,18},{18,2},{3,19},{19,3},{4,20},{20... | collective-permute-start | bytes 8650760 | tf_op jit(solution)/shard_map/ppermute | solution.py:34
  44.4 43.1 %collective-permute-start.3 = (bf16[1024,384]{1,0:T(8,128)(2,1)}, bf16[1024,384]{1,0:T(8,128)(2,1)}, u32[]{:S(2)}, u32[]{:S(2)}) collective-permute-start(bf16[1024,384]{1,0:T(8,128)(2,1)} %get-tuple-element.137), channel_id=1, source_target_pairs={{0,4},{4,0},{8,12},{12,8},{1,5},{5,1},{9,13},{13,9},{2,6},{6,2},{1... | collective-permute-start | bytes 2359304 | tf_op jit(solution)/shard_map/ppermute | solution.py:34
  61.3 55.2 %collective-permute-start.4 = (bf16[1024,384]{1,0:T(8,128)(2,1)S(1)}, bf16[1024,384]{1,0:T(8,128)(2,1)}, u32[]{:S(2)}, u32[]{:S(2)}) collective-permute-start(bf16[1024,384]{1,0:T(8,128)(2,1)S(1)} %copy-done.48), channel_id=1, source_target_pairs={{0,8},{4,12},{8,0},{12,4},{1,9},{5,13},{9,1},{13,5},{2,10},{6,14},... | collective-permute-start | bytes 2359304 | tf_op jit(solution)/shard_map/ppermute | solution.py:34
  65.6 51.0 %collective-permute-start.5 = (bf16[1024,384]{1,0:T(8,128)(2,1)S(1)}, bf16[1024,384]{1,0:T(8,128)(2,1)S(1)}, u32[]{:S(2)}, u32[]{:S(2)}) collective-permute-start(bf16[1024,384]{1,0:T(8,128)(2,1)S(1)} %copy-done.47), channel_id=1, source_target_pairs={{0,12},{4,8},{8,4},{12,0},{1,13},{5,9},{9,5},{13,1},{2,14},{6,10},... | collective-permute-start | bytes 2359304 | tf_op jit(solution)/shard_map/ppermute | solution.py:34
  151.0 21.1 %collective-permute-start.10 = (bf16[1024,128]{1,0:T(8,128)(2,1)}, bf16[1024,128]{1,0:T(8,128)(2,1)S(1)}, u32[]{:S(2)}, u32[]{:S(2)}) collective-permute-start(bf16[1024,128]{1,0:T(8,128)(2,1)} %get-tuple-element.154), channel_id=1, source_target_pairs={{0,4},{4,0},{8,12},{12,8},{1,5},{5,1},{9,13},{13,9},{2,6},{6,2},{1... | collective-permute-start | bytes 786440 | tf_op jit(solution)/shard_map/ppermute | solution.py:34
  167.6 9.6 %collective-permute-start.11 = (bf16[1024,128]{1,0:T(8,128)(2,1)}, bf16[1024,128]{1,0:T(8,128)(2,1)S(1)}, u32[]{:S(2)}, u32[]{:S(2)}) collective-permute-start(bf16[1024,128]{1,0:T(8,128)(2,1)} %get-tuple-element.155), channel_id=1, source_target_pairs={{0,8},{4,12},{8,0},{12,4},{1,9},{5,13},{9,1},{13,5},{2,10},{6,14},... | collective-permute-start | bytes 786440 | tf_op jit(solution)/shard_map/ppermute | solution.py:34
  168.7 16.2 %collective-permute-start.12 = (bf16[1024,128]{1,0:T(8,128)(2,1)}, bf16[1024,128]{1,0:T(8,128)(2,1)S(1)}, u32[]{:S(2)}, u32[]{:S(2)}) collective-permute-start(bf16[1024,128]{1,0:T(8,128)(2,1)} %get-tuple-element.156), channel_id=1, source_target_pairs={{0,12},{4,8},{8,4},{12,0},{1,13},{5,9},{9,5},{13,1},{2,14},{6,10},... | collective-permute-start | bytes 786440 | tf_op jit(solution)/shard_map/ppermute | solution.py:34
  192.9 20.7 %collective-permute-start.13 = (bf16[256,2048]{1,0:T(8,128)(2,1)}, bf16[256,2048]{1,0:T(8,128)(2,1)}, u32[]{:S(2)}, u32[]{:S(2)}) collective-permute-start(bf16[256,2048]{1,0:T(8,128)(2,1)} %get-tuple-element.158), channel_id=1, source_target_pairs={{0,1},{1,0},{2,3},{3,2},{4,5},{5,4},{6,7},{7,6},{8,9},{9,8},{10,11... | collective-permute-start | bytes 3145736 | tf_op jit(solution)/shard_map/ppermute | solution.py:34
  194.3 21.8 %collective-permute-start.14 = (bf16[256,2048]{1,0:T(8,128)(2,1)}, bf16[256,2048]{1,0:T(8,128)(2,1)}, u32[]{:S(2)}, u32[]{:S(2)}) collective-permute-start(bf16[256,2048]{1,0:T(8,128)(2,1)} %get-tuple-element.159), channel_id=1, source_target_pairs={{0,2},{1,3},{2,0},{3,1},{4,6},{5,7},{6,4},{7,5},{8,10},{9,11},{10,... | collective-permute-start | bytes 3145736 | tf_op jit(solution)/shard_map/ppermute | solution.py:34
  195.9 41.3 %collective-permute-start.15 = (bf16[256,2048]{1,0:T(8,128)(2,1)S(1)}, bf16[256,2048]{1,0:T(8,128)(2,1)}, u32[]{:S(2)}, u32[]{:S(2)}) collective-permute-start(bf16[256,2048]{1,0:T(8,128)(2,1)S(1)} %get-tuple-element.160), channel_id=1, source_target_pairs={{0,3},{1,2},{2,1},{3,0},{4,7},{5,6},{6,5},{7,4},{8,11},{9,10},{10,... | collective-permute-start | bytes 3145736 | tf_op jit(solution)/shard_map/ppermute | solution.py:34
  241.8 21.2 %collective-permute-start.16 = (bf16[256,2048]{1,0:T(8,128)(2,1)S(1)}, bf16[256,2048]{1,0:T(8,128)(2,1)S(1)}, u32[]{:S(2)}, u32[]{:S(2)}) collective-permute-start(bf16[256,2048]{1,0:T(8,128)(2,1)S(1)} %add_convert_fusion.1), channel_id=1, source_target_pairs={{0,1},{1,0},{2,3},{3,2},{4,5},{5,4},{6,7},{7,6},{8,9},{9,8},{10,11... | collective-permute-start | bytes 3145736 | tf_op jit(solution)/shard_map/ppermute | solution.py:34
  243.2 29.7 %collective-permute-start.17 = (bf16[256,2048]{1,0:T(8,128)(2,1)S(1)}, bf16[256,2048]{1,0:T(8,128)(2,1)S(1)}, u32[]{:S(2)}, u32[]{:S(2)}) collective-permute-start(bf16[256,2048]{1,0:T(8,128)(2,1)S(1)} %add_convert_fusion.1), channel_id=1, source_target_pairs={{0,2},{1,3},{2,0},{3,1},{4,6},{5,7},{6,4},{7,5},{8,10},{9,11},{10,... | collective-permute-start | bytes 3145736 | tf_op jit(solution)/shard_map/ppermute | solution.py:34
  243.8 41.0 %collective-permute-start.19 = (bf16[256,2048]{1,0:T(8,128)(2,1)S(1)}, bf16[256,2048]{1,0:T(8,128)(2,1)S(1)}, u32[]{:S(2)}, u32[]{:S(2)}) collective-permute-start(bf16[256,2048]{1,0:T(8,128)(2,1)S(1)} %add_convert_fusion.1), channel_id=1, source_target_pairs={{0,3},{1,2},{2,1},{3,0},{4,7},{5,6},{6,5},{7,4},{8,11},{9,10},{10,... | collective-permute-start | bytes 3145736 | tf_op jit(solution)/shard_map/ppermute | solution.py:34
  317.4 65.0 %collective-permute-start.22 = (bf16[1024,1408]{1,0:T(8,128)(2,1)}, bf16[1024,1408]{1,0:T(8,128)(2,1)}, u32[]{:S(2)}, u32[]{:S(2)}) collective-permute-start(bf16[1024,1408]{1,0:T(8,128)(2,1)} %convolution_convert_fusion.8), channel_id=1, source_target_pairs={{0,16},{16,0},{1,17},{17,1},{2,18},{18,2},{3,19},{19,3},{4,20},{20... | collective-permute-start | bytes 8650760 | tf_op jit(solution)/shard_map/ppermute | solution.py:34
  333.9 48.5 %collective-permute-start.23 = (bf16[1024,1408]{1,0:T(8,128)(2,1)}, bf16[1024,1408]{1,0:T(8,128)(2,1)}, u32[]{:S(2)}, u32[]{:S(2)}) collective-permute-start(bf16[1024,1408]{1,0:T(8,128)(2,1)} %convolution_convert_fusion.7), channel_id=1, source_target_pairs={{0,16},{16,0},{1,17},{17,1},{2,18},{18,2},{3,19},{19,3},{4,20},{20... | collective-permute-start | bytes 8650760 | tf_op jit(solution)/shard_map/ppermute | solution.py:34
  334.1 27.3 %collective-permute-start.21 = (bf16[256,2048]{1,0:T(8,128)(2,1)}, bf16[256,2048]{1,0:T(8,128)(2,1)S(1)}, u32[]{:S(2)}, u32[]{:S(2)}) collective-permute-start(bf16[256,2048]{1,0:T(8,128)(2,1)} %fusion.2), channel_id=1, source_target_pairs={{0,3},{1,2},{2,1},{3,0},{4,7},{5,6},{6,5},{7,4},{8,11},{9,10},{10,... | collective-permute-start | bytes 3145736 | tf_op jit(solution)/shard_map/ppermute | solution.py:34
  334.1 48.3 %collective-permute-start.20 = (bf16[256,2048]{1,0:T(8,128)(2,1)}, bf16[256,2048]{1,0:T(8,128)(2,1)S(1)}, u32[]{:S(2)}, u32[]{:S(2)}) collective-permute-start(bf16[256,2048]{1,0:T(8,128)(2,1)} %fusion.1), channel_id=1, source_target_pairs={{0,2},{1,3},{2,0},{3,1},{4,6},{5,7},{6,4},{7,5},{8,10},{9,11},{10,... | collective-permute-start | bytes 3145736 | tf_op jit(solution)/shard_map/ppermute | solution.py:34
  336.2 46.2 %collective-permute-start.18 = (bf16[256,2048]{1,0:T(8,128)(2,1)}, bf16[256,2048]{1,0:T(8,128)(2,1)S(1)}, u32[]{:S(2)}, u32[]{:S(2)}) collective-permute-start(bf16[256,2048]{1,0:T(8,128)(2,1)} %fusion), channel_id=1, source_target_pairs={{0,1},{1,0},{2,3},{3,2},{4,5},{5,4},{6,7},{7,6},{8,9},{9,8},{10,11... | collective-permute-start | bytes 3145736 | tf_op jit(solution)/shard_map/ppermute | solution.py:34
  386.1 53.7 %collective-permute-start.24 = (bf16[256,2048]{1,0:T(8,128)(2,1)S(1)}, bf16[256,2048]{1,0:T(8,128)(2,1)S(1)}, u32[]{:S(2)}, u32[]{:S(2)}) collective-permute-start(bf16[256,2048]{1,0:T(8,128)(2,1)S(1)} %get-tuple-element.185), channel_id=1, source_target_pairs={{0,1},{1,0},{2,3},{3,2},{4,5},{5,4},{6,7},{7,6},{8,9},{9,8},{10,11... | collective-permute-start | bytes 3145736 | tf_op jit(solution)/shard_map/ppermute | solution.py:34
  387.6 52.3 %collective-permute-start.25 = (bf16[256,2048]{1,0:T(8,128)(2,1)S(1)}, bf16[256,2048]{1,0:T(8,128)(2,1)S(1)}, u32[]{:S(2)}, u32[]{:S(2)}) collective-permute-start(bf16[256,2048]{1,0:T(8,128)(2,1)S(1)} %get-tuple-element.185), channel_id=1, source_target_pairs={{0,2},{1,3},{2,0},{3,1},{4,6},{5,7},{6,4},{7,5},{8,10},{9,11},{10,... | collective-permute-start | bytes 3145736 | tf_op jit(solution)/shard_map/ppermute | solution.py:34
  388.2 51.7 %collective-permute-start.26 = (bf16[256,2048]{1,0:T(8,128)(2,1)S(1)}, bf16[256,2048]{1,0:T(8,128)(2,1)S(1)}, u32[]{:S(2)}, u32[]{:S(2)}) collective-permute-start(bf16[256,2048]{1,0:T(8,128)(2,1)S(1)} %get-tuple-element.185), channel_id=1, source_target_pairs={{0,3},{1,2},{2,1},{3,0},{4,7},{5,6},{6,5},{7,4},{8,11},{9,10},{10,... | collective-permute-start | bytes 3145736 | tf_op jit(solution)/shard_map/ppermute | solution.py:34
  391.3 29.7 %collective-permute-start.35 = (bf16[256,1408]{1,0:T(8,128)(2,1)S(1)}, bf16[256,1408]{1,0:T(8,128)(2,1)S(1)}, u32[]{:S(2)}, u32[]{:S(2)}) collective-permute-start(bf16[256,1408]{1,0:T(8,128)(2,1)S(1)} %get-tuple-element.274), channel_id=1, source_target_pairs={{0,4},{4,0},{8,12},{12,8},{1,5},{5,1},{9,13},{13,9},{2,6},{6,2},{1... | collective-permute-start | bytes 2162696 | tf_op jit(solution)/shard_map/ppermute | solution.py:34
  404.0 32.4 %collective-permute-start.34 = (bf16[256,1408]{1,0:T(8,128)(2,1)S(1)}, bf16[256,1408]{1,0:T(8,128)(2,1)S(1)}, u32[]{:S(2)}, u32[]{:S(2)}) collective-permute-start(bf16[256,1408]{1,0:T(8,128)(2,1)S(1)} %get-tuple-element.275), channel_id=1, source_target_pairs={{0,4},{4,0},{8,12},{12,8},{1,5},{5,1},{9,13},{13,9},{2,6},{6,2},{1... | collective-permute-start | bytes 2162696 | tf_op jit(solution)/shard_map/ppermute | solution.py:34
  421.0 30.9 %collective-permute-start.33 = (bf16[256,1408]{1,0:T(8,128)(2,1)S(1)}, bf16[256,1408]{1,0:T(8,128)(2,1)S(1)}, u32[]{:S(2)}, u32[]{:S(2)}) collective-permute-start(bf16[256,1408]{1,0:T(8,128)(2,1)S(1)} %get-tuple-element.276), channel_id=1, source_target_pairs={{0,4},{4,0},{8,12},{12,8},{1,5},{5,1},{9,13},{13,9},{2,6},{6,2},{1... | collective-permute-start | bytes 2162696 | tf_op jit(solution)/shard_map/ppermute | solution.py:34
  436.5 29.4 %collective-permute-start.32 = (bf16[256,1408]{1,0:T(8,128)(2,1)S(1)}, bf16[256,1408]{1,0:T(8,128)(2,1)S(1)}, u32[]{:S(2)}, u32[]{:S(2)}) collective-permute-start(bf16[256,1408]{1,0:T(8,128)(2,1)S(1)} %get-tuple-element.277), channel_id=1, source_target_pairs={{0,4},{4,0},{8,12},{12,8},{1,5},{5,1},{9,13},{13,9},{2,6},{6,2},{1... | collective-permute-start | bytes 2162696 | tf_op jit(solution)/shard_map/ppermute | solution.py:34
  439.8 50.5 %collective-permute-start.31 = (bf16[1408,1024]{1,0:T(8,128)(2,1)S(1)}, bf16[1408,1024]{1,0:T(8,128)(2,1)S(1)}, u32[]{:S(2)}, u32[]{:S(2)}) collective-permute-start(bf16[1408,1024]{1,0:T(8,128)(2,1)S(1)} %copy-done.43), channel_id=1, source_target_pairs={{0,16},{16,0},{1,17},{17,1},{2,18},{18,2},{3,19},{19,3},{4,20},{20... | collective-permute-start | bytes 8650760 | tf_op jit(solution)/shard_map/ppermute | solution.py:34
  446.8 43.6 %collective-permute-start.30 = (bf16[512,1024]{1,0:T(8,128)(2,1)S(1)}, bf16[512,1024]{1,0:T(8,128)(2,1)}, u32[]{:S(2)}, u32[]{:S(2)}) collective-permute-start(bf16[512,1024]{1,0:T(8,128)(2,1)S(1)} %fusion.19), channel_id=1, source_target_pairs={{0,16},{16,0},{1,17},{17,1},{2,18},{18,2},{3,19},{19,3},{4,20},{20... | collective-permute-start | bytes 3145736 | tf_op jit(solution)/shard_map/ppermute | solution.py:34
  467.3 10.8 %collective-permute-start.27 = (bf16[1024,128]{1,0:T(8,128)(2,1)S(1)}, bf16[1024,128]{1,0:T(8,128)(2,1)S(1)}, u32[]{:S(2)}, u32[]{:S(2)}) collective-permute-start(bf16[1024,128]{1,0:T(8,128)(2,1)S(1)} %get-tuple-element.191), channel_id=1, source_target_pairs={{0,4},{4,0},{8,12},{12,8},{1,5},{5,1},{9,13},{13,9},{2,6},{6,2},{1... | collective-permute-start | bytes 786440 | tf_op jit(solution)/shard_map/ppermute | solution.py:34
  469.1 21.2 %collective-permute-start.28 = (bf16[1024,128]{1,0:T(8,128)(2,1)S(1)}, bf16[1024,128]{1,0:T(8,128)(2,1)S(1)}, u32[]{:S(2)}, u32[]{:S(2)}) collective-permute-start(bf16[1024,128]{1,0:T(8,128)(2,1)S(1)} %get-tuple-element.192), channel_id=1, source_target_pairs={{0,8},{4,12},{8,0},{12,4},{1,9},{5,13},{9,1},{13,5},{2,10},{6,14},... | collective-permute-start | bytes 786440 | tf_op jit(solution)/shard_map/ppermute | solution.py:34
  470.9 19.5 %collective-permute-start.29 = (bf16[1024,128]{1,0:T(8,128)(2,1)S(1)}, bf16[1024,128]{1,0:T(8,128)(2,1)S(1)}, u32[]{:S(2)}, u32[]{:S(2)}) collective-permute-start(bf16[1024,128]{1,0:T(8,128)(2,1)S(1)} %get-tuple-element.193), channel_id=1, source_target_pairs={{0,12},{4,8},{8,4},{12,0},{1,13},{5,9},{9,5},{13,1},{2,14},{6,10},... | collective-permute-start | bytes 786440 | tf_op jit(solution)/shard_map/ppermute | solution.py:34
  492.6 64.8 %collective-permute-start.43 = (bf16[1408,256]{1,0:T(8,128)(2,1)}, bf16[1408,256]{1,0:T(8,128)(2,1)}, u32[]{:S(2)}, u32[]{:S(2)}) collective-permute-start(bf16[1408,256]{1,0:T(8,128)(2,1)} %get-tuple-element.272), channel_id=1, source_target_pairs={{0,4},{4,0},{8,12},{12,8},{1,5},{5,1},{9,13},{13,9},{2,6},{6,2},{1... | collective-permute-start | bytes 2162696 | tf_op jit(solution)/shard_map/ppermute | solution.py:34
  495.9 58.7 %collective-permute-start.42 = (bf16[1408,256]{1,0:T(8,128)(2,1)}, bf16[1408,256]{1,0:T(8,128)(2,1)}, u32[]{:S(2)}, u32[]{:S(2)}) collective-permute-start(bf16[1408,256]{1,0:T(8,128)(2,1)} %get-tuple-element.273), channel_id=1, source_target_pairs={{0,4},{4,0},{8,12},{12,8},{1,5},{5,1},{9,13},{13,9},{2,6},{6,2},{1... | collective-permute-start | bytes 2162696 | tf_op jit(solution)/shard_map/ppermute | solution.py:34
  497.8 93.0 %collective-permute-start.39 = (bf16[256,2048]{1,0:T(8,128)(2,1)}, bf16[256,2048]{1,0:T(8,128)(2,1)}, u32[]{:S(2)}, u32[]{:S(2)}) collective-permute-start(bf16[256,2048]{1,0:T(8,128)(2,1)} %get-tuple-element.280), channel_id=1, source_target_pairs={{0,1},{1,0},{2,3},{3,2},{4,5},{5,4},{6,7},{7,6},{8,9},{9,8},{10,11... | collective-permute-start | bytes 3145736 | tf_op jit(solution)/shard_map/ppermute | solution.py:34
  498.9 93.3 %collective-permute-start.40 = (bf16[256,2048]{1,0:T(8,128)(2,1)}, bf16[256,2048]{1,0:T(8,128)(2,1)}, u32[]{:S(2)}, u32[]{:S(2)}) collective-permute-start(bf16[256,2048]{1,0:T(8,128)(2,1)} %get-tuple-element.279), channel_id=1, source_target_pairs={{0,2},{1,3},{2,0},{3,1},{4,6},{5,7},{6,4},{7,5},{8,10},{9,11},{10,... | collective-permute-start | bytes 3145736 | tf_op jit(solution)/shard_map/ppermute | solution.py:34
  499.2 51.5 %collective-permute-start.63 = (bf16[256,1408]{1,0:T(8,128)(2,1)}, bf16[256,1408]{1,0:T(8,128)(2,1)}, u32[]{:S(2)}, u32[]{:S(2)}) collective-permute-start(bf16[256,1408]{1,0:T(8,128)(2,1)} %convert_add_fusion.8), channel_id=1, source_target_pairs={{0,8},{4,12},{8,0},{12,4},{1,9},{5,13},{9,1},{13,5},{2,10},{6,14},... | collective-permute-start | bytes 2162696 | tf_op jit(solution)/shard_map/ppermute | solution.py:34
  550.7 41.5 %collective-permute-start.41 = (bf16[256,2048]{1,0:T(8,128)(2,1)}, bf16[256,2048]{1,0:T(8,128)(2,1)S(1)}, u32[]{:S(2)}, u32[]{:S(2)}) collective-permute-start(bf16[256,2048]{1,0:T(8,128)(2,1)} %get-tuple-element.278), channel_id=1, source_target_pairs={{0,3},{1,2},{2,1},{3,0},{4,7},{5,6},{6,5},{7,4},{8,11},{9,10},{10,... | collective-permute-start | bytes 3145736 | tf_op jit(solution)/shard_map/ppermute | solution.py:34
  554.6 34.9 %collective-permute-start.62 = (bf16[256,1408]{1,0:T(8,128)(2,1)S(1)}, bf16[256,1408]{1,0:T(8,128)(2,1)S(1)}, u32[]{:S(2)}, u32[]{:S(2)}) collective-permute-start(bf16[256,1408]{1,0:T(8,128)(2,1)S(1)} %copy-done.36), channel_id=1, source_target_pairs={{0,8},{4,12},{8,0},{12,4},{1,9},{5,13},{9,1},{13,5},{2,10},{6,14},... | collective-permute-start | bytes 2162696 | tf_op jit(solution)/shard_map/ppermute | solution.py:34
  557.4 41.0 %collective-permute-start.36 = (bf16[1024,384]{1,0:T(8,128)(2,1)S(1)}, bf16[1024,384]{1,0:T(8,128)(2,1)S(1)}, u32[]{:S(2)}, u32[]{:S(2)}) collective-permute-start(bf16[1024,384]{1,0:T(8,128)(2,1)S(1)} %copy-done.51), channel_id=1, source_target_pairs={{0,4},{4,0},{8,12},{12,8},{1,5},{5,1},{9,13},{13,9},{2,6},{6,2},{1... | collective-permute-start | bytes 2359304 | tf_op jit(solution)/shard_map/ppermute | solution.py:34
  589.6 68.4 %collective-permute-start.37 = (bf16[1024,384]{1,0:T(8,128)(2,1)S(1)}, bf16[1024,384]{1,0:T(8,128)(2,1)S(1)}, u32[]{:S(2)}, u32[]{:S(2)}) collective-permute-start(bf16[1024,384]{1,0:T(8,128)(2,1)S(1)} %copy-done.50), channel_id=1, source_target_pairs={{0,8},{4,12},{8,0},{12,4},{1,9},{5,13},{9,1},{13,5},{2,10},{6,14},... | collective-permute-start | bytes 2359304 | tf_op jit(solution)/shard_map/ppermute | solution.py:34
  590.8 67.2 %collective-permute-start.38 = (bf16[1024,384]{1,0:T(8,128)(2,1)S(1)}, bf16[1024,384]{1,0:T(8,128)(2,1)S(1)}, u32[]{:S(2)}, u32[]{:S(2)}) collective-permute-start(bf16[1024,384]{1,0:T(8,128)(2,1)S(1)} %copy-done.49), channel_id=1, source_target_pairs={{0,12},{4,8},{8,4},{12,0},{1,13},{5,9},{9,5},{13,1},{2,14},{6,10},... | collective-permute-start | bytes 2359304 | tf_op jit(solution)/shard_map/ppermute | solution.py:34
  592.2 136.0 %collective-permute-start.64 = (bf16[1408,256]{1,0:T(8,128)(2,1)}, bf16[1408,256]{1,0:T(8,128)(2,1)}, u32[]{:S(2)}, u32[]{:S(2)}) collective-permute-start(bf16[1408,256]{1,0:T(8,128)(2,1)} %convert_add_fusion.6), channel_id=1, source_target_pairs={{0,8},{4,12},{8,0},{12,4},{1,9},{5,13},{9,1},{13,5},{2,10},{6,14},... | collective-permute-start | bytes 2162696 | tf_op jit(solution)/shard_map/ppermute | solution.py:34
  673.9 18.9 %collective-permute-start.56 = (f32[1,1536]{1,0:T(1,128)S(1)}, f32[1,1536]{1,0:T(1,128)S(1)}, u32[]{:S(2)}, u32[]{:S(2)}) collective-permute-start(f32[1,1536]{1,0:T(1,128)S(1)} %broadcast_in_dim.27), channel_id=1, source_target_pairs={{0,16},{16,0},{1,17},{17,1},{2,18},{18,2},{3,19},{19,3},{4,20},{20... | collective-permute-start | bytes 18440 | tf_op jit(solution)/shard_map/ppermute | solution.py:34
  675.2 33.0 %collective-permute-start.60 = (bf16[512,256]{1,0:T(8,128)(2,1)S(1)}, bf16[512,256]{1,0:T(8,128)(2,1)S(1)}, u32[]{:S(2)}, u32[]{:S(2)}) collective-permute-start(bf16[512,256]{1,0:T(8,128)(2,1)S(1)} %get-tuple-element.294), channel_id=1, source_target_pairs={{0,4},{4,0},{8,12},{12,8},{1,5},{5,1},{9,13},{13,9},{2,6},{6,2},{1... | collective-permute-start | bytes 786440 | tf_op jit(solution)/shard_map/ppermute | solution.py:34
  692.7 23.4 %collective-permute-start.59 = (bf16[512,256]{1,0:T(8,128)(2,1)S(1)}, bf16[512,256]{1,0:T(8,128)(2,1)S(1)}, u32[]{:S(2)}, u32[]{:S(2)}) collective-permute-start(bf16[512,256]{1,0:T(8,128)(2,1)S(1)} %get-tuple-element.293), channel_id=1, source_target_pairs={{0,4},{4,0},{8,12},{12,8},{1,5},{5,1},{9,13},{13,9},{2,6},{6,2},{1... | collective-permute-start | bytes 786440 | tf_op jit(solution)/shard_map/ppermute | solution.py:34
  692.8 12.6 %collective-permute-start.57 = (f32[1,1536]{1,0:T(1,128)S(1)}, f32[1,1536]{1,0:T(1,128)S(1)}, u32[]{:S(2)}, u32[]{:S(2)}) collective-permute-start(f32[1,1536]{1,0:T(1,128)S(1)} %reshape_add_fusion), channel_id=1, source_target_pairs={{0,4},{4,0},{8,12},{12,8},{1,5},{5,1},{9,13},{13,9},{2,6},{6,2},{1... | collective-permute-start | bytes 18440 | tf_op jit(solution)/shard_map/ppermute | solution.py:34
  699.8 75.0 %collective-permute-start.52 = (bf16[1024,1536]{1,0:T(8,128)(2,1)}, bf16[1024,1536]{1,0:T(8,128)(2,1)}, u32[]{:S(2)}, u32[]{:S(2)}) collective-permute-start(bf16[1024,1536]{1,0:T(8,128)(2,1)} %convolution_convert_fusion.1), channel_id=1, source_target_pairs={{0,16},{16,0},{1,17},{17,1},{2,18},{18,2},{3,19},{19,3},{4,20},{20... | collective-permute-start | bytes 9437192 | tf_op jit(solution)/shard_map/ppermute | solution.py:34
  705.4 9.0 %collective-permute-start.58 = (f32[1,1536]{1,0:T(1,128)S(1)}, f32[1,1536]{1,0:T(1,128)S(1)}, u32[]{:S(2)}, u32[]{:S(2)}) collective-permute-start(f32[1,1536]{1,0:T(1,128)S(1)} %add.465), channel_id=1, source_target_pairs={{0,8},{4,12},{8,0},{12,4},{1,9},{5,13},{9,1},{13,5},{2,10},{6,14},... | collective-permute-start | bytes 18440 | tf_op jit(solution)/shard_map/ppermute | solution.py:34
  709.3 14.1 %collective-permute-start.61 = (bf16[512,256]{1,0:T(8,128)(2,1)S(1)}, bf16[512,256]{1,0:T(8,128)(2,1)S(1)}, u32[]{:S(2)}, u32[]{:S(2)}) collective-permute-start(bf16[512,256]{1,0:T(8,128)(2,1)S(1)} %add_convert_fusion.11), channel_id=1, source_target_pairs={{0,8},{4,12},{8,0},{12,4},{1,9},{5,13},{9,1},{13,5},{2,10},{6,14},... | collective-permute-start | bytes 786440 | tf_op jit(solution)/shard_map/ppermute | solution.py:34
  714.4 26.1 %collective-permute-start.44 = (bf16[256,2048]{1,0:T(8,128)(2,1)S(1)}, bf16[256,2048]{1,0:T(8,128)(2,1)}, u32[]{:S(2)}, u32[]{:S(2)}) collective-permute-start(bf16[256,2048]{1,0:T(8,128)(2,1)S(1)} %get-tuple-element.232), channel_id=1, source_target_pairs={{0,1},{1,0},{2,3},{3,2},{4,5},{5,4},{6,7},{7,6},{8,9},{9,8},{10,11... | collective-permute-start | bytes 3145736 | tf_op jit(solution)/shard_map/ppermute | solution.py:34
  716.1 46.8 %collective-permute-start.45 = (bf16[256,2048]{1,0:T(8,128)(2,1)S(1)}, bf16[256,2048]{1,0:T(8,128)(2,1)}, u32[]{:S(2)}, u32[]{:S(2)}) collective-permute-start(bf16[256,2048]{1,0:T(8,128)(2,1)S(1)} %get-tuple-element.233), channel_id=1, source_target_pairs={{0,2},{1,3},{2,0},{3,1},{4,6},{5,7},{6,4},{7,5},{8,10},{9,11},{10,... | collective-permute-start | bytes 3145736 | tf_op jit(solution)/shard_map/ppermute | solution.py:34
  723.4 39.4 %collective-permute-start.46 = (bf16[256,2048]{1,0:T(8,128)(2,1)S(1)}, bf16[256,2048]{1,0:T(8,128)(2,1)}, u32[]{:S(2)}, u32[]{:S(2)}) collective-permute-start(bf16[256,2048]{1,0:T(8,128)(2,1)S(1)} %get-tuple-element.234), channel_id=1, source_target_pairs={{0,3},{1,2},{2,1},{3,0},{4,7},{5,6},{6,5},{7,4},{8,11},{9,10},{10,... | collective-permute-start | bytes 3145736 | tf_op jit(solution)/shard_map/ppermute | solution.py:34
  768.1 4.0 collective-permute-start.48
  772.1 5.9 collective-permute-start.49
  776.6 20.5 %collective-permute-start.54 = (bf16[256,1536]{1,0:T(8,128)(2,1)S(1)}, bf16[256,1536]{1,0:T(8,128)(2,1)S(1)}, u32[]{:S(2)}, u32[]{:S(2)}) collective-permute-start(bf16[256,1536]{1,0:T(8,128)(2,1)S(1)} %get-tuple-element.271), channel_id=1, source_target_pairs={{0,4},{4,0},{8,12},{12,8},{1,5},{5,1},{9,13},{13,9},{2,6},{6,2},{1... | collective-permute-start | bytes 2359304 | tf_op jit(solution)/shard_map/ppermute | solution.py:34
  778.0 4.0 collective-permute-start.50
  782.0 18.6 %collective-permute-start.51 = (f32[4,2048]{1,0:T(4,128)S(1)}, f32[4,2048]{1,0:T(4,128)S(1)}, u32[]{:S(2)}, u32[]{:S(2)}) collective-permute-start(f32[4,2048]{1,0:T(4,128)S(1)} %add.455), channel_id=1, source_target_pairs={{0,2},{1,3},{2,0},{3,1},{4,6},{5,7},{6,4},{7,5},{8,10},{9,11},{10,... | collective-permute-start | bytes 98312 | tf_op jit(solution)/shard_map/ppermute | solution.py:34
  782.5 43.1 %collective-permute-start.53 = (bf16[256,1536]{1,0:T(8,128)(2,1)S(1)}, bf16[256,1536]{1,0:T(8,128)(2,1)S(1)}, u32[]{:S(2)}, u32[]{:S(2)}) collective-permute-start(bf16[256,1536]{1,0:T(8,128)(2,1)S(1)} %get-tuple-element.270), channel_id=1, source_target_pairs={{0,4},{4,0},{8,12},{12,8},{1,5},{5,1},{9,13},{13,9},{2,6},{6,2},{1... | collective-permute-start | bytes 2359304 | tf_op jit(solution)/shard_map/ppermute | solution.py:34
  798.5 33.0 %collective-permute-start.55 = (bf16[256,1536]{1,0:T(8,128)(2,1)S(1)}, bf16[256,1536]{1,0:T(8,128)(2,1)S(1)}, u32[]{:S(2)}, u32[]{:S(2)}) collective-permute-start(bf16[256,1536]{1,0:T(8,128)(2,1)S(1)} %add_convert_fusion.2), channel_id=1, source_target_pairs={{0,8},{4,12},{8,0},{12,4},{1,9},{5,13},{9,1},{13,5},{2,10},{6,14},... | collective-permute-start | bytes 2359304 | tf_op jit(solution)/shard_map/ppermute | solution.py:34
  (65 other events, 1156.4 us)

commit v2 on v1

--- a/solution.py
+++ b/solution.py
@@ -35,12 +35,10 @@
 
 
 def sum_over(x, axis):
-    size = lax.axis_size(axis)
-    bit = 1
-    while bit < size:
-        x = x + swap_with(x, axis, bit)
-        bit *= 2
-    return x
+    terms = [x] + [swap_with(x, axis, i) for i in range(1, lax.axis_size(axis))]
+    while len(terms) > 1:
+        terms = [terms[i] + terms[i + 1] for i in range(0, len(terms), 2)]
+    return terms[0]
 
 
 def rotary_tables(positions):
@@ -644,8 +642,27 @@
         NN,
     )
 
+    mid = share // 2
+
     def send_rows(parts):
         return [swap_with(parts[i].astype(bf16), "tensor", i) for i in range(1, slots)]
+
+    def relay_sums(parts):
+        if slots != 4:
+            return send_rows(parts)
+        one, two, far = (parts[i].astype(bf16) for i in range(1, 4))
+        far_two = swap_with(far[:mid], "tensor", 1)
+        far_one = swap_with(far[mid:], "tensor", 2)
+        first = swap_with(one[:mid], "tensor", 1)
+        last = swap_with(two[mid:], "tensor", 2)
+        two = (two[:mid].astype(f32) + far_two.astype(f32)).astype(bf16)
+        one = (one[mid:].astype(f32) + far_one.astype(f32)).astype(bf16)
+        two = swap_with(two, "tensor", 2)
+        one = swap_with(one, "tensor", 1)
+        return [
+            jnp.concatenate([first, one], axis=0),
+            jnp.concatenate([two, last], axis=0),
+        ]
 
     def add_rows(own, received):
         for part in received:
@@ -653,12 +670,25 @@
         return own
 
     def gather_rows(block):
-        return [block] + [swap_with(block, "tensor", i) for i in range(1, slots)]
+        if slots != 4:
+            return [block] + [swap_with(block, "tensor", i) for i in range(1, slots)]
+        one_last = swap_with(block[mid:], "tensor", 1)
+        two_first = swap_with(block[:mid], "tensor", 2)
+        one_first = swap_with(block[:mid], "tensor", 1)
+        two_last = swap_with(block[mid:], "tensor", 2)
+        far_first = swap_with(two_first, "tensor", 1)
+        far_last = swap_with(one_last, "tensor", 2)
+        return [
+            block,
+            jnp.concatenate([one_first, one_last], axis=0),
+            jnp.concatenate([two_first, two_last], axis=0),
+            jnp.concatenate([far_first, far_last], axis=0),
+        ]
 
     def slot_of(x, i):
         return x[i * share : (i + 1) * share]
 
-    x1 = x_share + add_rows(attn_parts[0], send_rows(attn_parts))
+    x1 = x_share + add_rows(attn_parts[0], relay_sums(attn_parts))
     mean2 = jnp.mean(x1, axis=-1, keepdims=True)
     cent2 = x1 - mean2
     inv2 = lax.rsqrt(jnp.mean(cent2 * cent2, axis=-1, keepdims=True) + EPS)
@@ -709,20 +739,15 @@
         jnp.concatenate(blocks, axis=0) for blocks in (h2, gate_grad, up_grad, hidden)
     )
 
-    norm2_parts, h2_all, gate_all, up_all = hold(norm2_parts, h2_all, gate_all, up_all)
     gate_theirs = dot(h2_all[:, half:], gate_all, TN).astype(bf16)
     up_theirs = dot(h2_all[:, half:], up_all, TN).astype(bf16)
-    h2_all, gate_theirs, up_theirs = hold(h2_all, gate_theirs, up_theirs)
     gate_theirs = other_half(gate_theirs)
     up_theirs = other_half(up_theirs)
     gate_mine = dot(h2_all[:, :half], gate_all, TN).astype(bf16)
     up_mine = dot(h2_all[:, :half], up_all, TN).astype(bf16)
-    dh2_received, norm2_own, gate_mine, up_mine, gate_theirs, up_theirs = hold(
-        dh2_received, norm2_parts[0], gate_mine, up_mine, gate_theirs, up_theirs
-    )
     gate_parts = scatter_step(blocks_of(gate_mine, gate_theirs, 0), 1)
     up_parts = scatter_step(blocks_of(up_mine, up_theirs, 0), 1)
-    dh2 = add_rows(norm2_own, dh2_received)
+    dh2 = add_rows(norm2_parts[0], dh2_received)
     cot_share = slot_of(cot_all, 0).astype(f32)
     e2 = dh2 * gain_two
     dx1 = cot_share + inv2 * (
@@ -732,28 +757,23 @@
     )
     dx1_slots = gather_rows(dx1.astype(bf16))
 
-    hidden_all, cot_all, dx1_own = hold(hidden_all, cot_all, dx1_slots[0])
     down_theirs = dot(hidden_all, cot_all[:, half:], TN).astype(bf16)
     down_mine = dot(hidden_all, cot_all[:, :half], TN).astype(bf16)
     out_all = dot(hidden_all, down_full).astype(bf16)
     down_theirs = other_half(down_theirs)
-    dx1_rest, dx1_own, out_all, down_mine = hold(dx1_slots[1:], dx1_own, out_all, down_mine)
-    dx1b = jnp.concatenate([dx1_own] + dx1_rest, axis=0)
+    dx1b = jnp.concatenate(dx1_slots, axis=0)
     d_attn = dot(dx1b, o_full, NT).astype(bf16)
     d_send = [
         lax.dynamic_slice_in_dim(d_attn, ((ctx & (groups - 1)) ^ s) * PAIR, PAIR, 1)
         for s in range(groups)
     ]
-    d_send, dx1b = hold(d_send, dx1b)
+    d_send, dx1b, out_all = hold(d_send, dx1b, out_all)
     d_pieces = [d_send[0]] + [swap_with(d_send[s % groups], "context", s) for s in range(1, ctxs)]
 
     o_theirs = dot(attn, dx1b[:, half:], TN).astype(bf16)
     o_mine = dot(attn, dx1b[:, :half], TN).astype(bf16)
     o_theirs = other_half(o_theirs)
 
-    d_pieces, out_all, o_mine, o_theirs, down_mine, down_theirs, gate_parts, up_parts = hold(
-        d_pieces, out_all, o_mine, o_theirs, down_mine, down_theirs, gate_parts, up_parts
-    )
     out_received = send_rows([slot_of(out_all, i) for i in range(slots)])
     gate_out = scatter_rest(gate_parts)
     up_out = scatter_rest(up_parts)
@@ -763,23 +783,20 @@
     )
     back_rest = [swap_with(back[s], "context", s) for s in range(1, groups)]
 
-    back_own, out_received, down_parts, o_mine = hold(back[0], out_received, down_parts, o_mine)
-    output = by_shard((x1 + add_rows(slot_of(out_all, 0).astype(f32), out_received)).astype(bf16))[None]
+    output = by_shard(
+        (x1 + add_rows(slot_of(out_all, 0).astype(f32), out_received)).astype(bf16)
+    )[None]
     o_parts = scatter_step(blocks_of(o_mine, o_theirs, 1), 1)
     down_grad = scatter_rest(down_parts)
     o_grad = scatter_rest(o_parts)
-    back_rest, output = hold(back_rest, output)
-
-    d_qkv, norm1_parts = join(ids, [back_own] + back_rest, own_qkv, oth_qkv, slots, NT)
+
+    d_qkv, norm1_parts = join(ids, [back[0]] + back_rest, own_qkv, oth_qkv, slots, NT)
     norm1_parts, d_qkv = hold(norm1_parts, d_qkv)
     dh1_received = send_rows(norm1_parts)
     qkv_theirs = other_half(dot(h1[:, half:], d_qkv, TN).astype(bf16))
     qkv_mine = dot(h1[:, :half], d_qkv, TN).astype(bf16)
     qkv_parts = scatter_step(blocks_of(qkv_mine, qkv_theirs, 0), 1)
     qkv_grad = scatter_rest(qkv_parts)
-    bias = jnp.sum(d_qkv.astype(f32), axis=0, keepdims=True)
-    bias = sum_over(sum_over(bias, "shard"), "context")[0]
-    dh1_received, qkv_mine = hold(dh1_received, qkv_mine)
     dh1 = add_rows(norm1_parts[0], dh1_received)
 
     mean1 = jnp.mean(x_share, axis=-1, keepdims=True)
@@ -794,7 +811,6 @@
     )
     tokens_grad = by_shard(tokens_grad)[None]
 
-    k_bias_grad = bias[inner : 2 * inner].reshape(heads_here, HEAD_DIM)[:, :ROT]
     norms = jnp.stack(
         [
             jnp.sum(dh1 * unit1, axis=0),
@@ -803,9 +819,13 @@
             jnp.sum(dh2, axis=0),
         ]
     )
-    norms = by_shard(norms)
-    for axis in ("shard", "context", "tensor"):
-        norms = sum_over(norms, axis)
+    norms = sum_over(by_shard(norms), "tensor")
+    bias = jnp.sum(d_qkv.astype(f32), axis=0, keepdims=True)
+    sums = sum_over(jnp.concatenate([norms.reshape(1, 4 * width), bias], axis=1), "shard")
+    sums = sum_over(sums, "context")
+    norms = sums[0, : 4 * width].reshape(4, width)
+    bias = sums[0, 4 * width :]
+    k_bias_grad = bias[inner : 2 * inner].reshape(heads_here, HEAD_DIM)[:, :ROT]
     return (
         output,
         tokens_grad,

time: 844 us -> 809 us (0.959)
  other arithmetic: 100 us -> 78.5 us
  waiting for transfers between devices: 346 us -> 328 us
  matrix products: 117 us -> 129 us
    ppermute x65 -> x73, waiting for transfers between devices: 346 us -> 328 us  [swap_with(): return lax.ppermute(x, axis, [(i, i ^ bit) for i in range(size)])]
    concatenate x4 -> x1, other arithmetic: 15.4 us -> 0.61 us  [local(): jnp.concatenate(blocks, axis=0)]
    dot_general x29, matrix products: 105 us -> 118 us  [dot(): return lax.dot_general(a, b, dims, preferred_element_type=f32)]
    add x11 -> x5, other arithmetic: 22.1 us -> 11.6 us  [scatter_step(): parts[d ^ bit]]
    convert_element_type x7 -> x10, other arithmetic: 11.1 us -> 20.1 us  [scatter_step(): parts.pop(d).astype(bf16)]
    ppermute x65 -> x73, starting transfers between devices: 128 us -> 123 us  [swap_with(): return lax.ppermute(x, axis, [(i, i ^ bit) for i in range(size)])]
  transfers between devices with their start and end apart: 65 -> 73, of which waited for: 28 -> 31; matrix products, arithmetic and copies ran while one was open for 22% -> 26% of each run, Pallas kernels for 7% -> 8%
where the time goes in v2:
time: 809 us; the launch traced here: 799 us
  waiting for transfers between devices  328 us (41%)
  matrix products  129 us (16%)
  starting transfers between devices  123 us (15%)
  Pallas kernels  116 us (14%)
  other arithmetic  78.5 us (10%)
  local copies, waits for them, and re-layouts  23.1 us (3%)
    ppermute x73, waiting for transfers between devices, swap_with(): return lax.ppermute(x, axis, [(i, i ^ bit) for i in range(size)])  328 us
    ppermute x73, starting transfers between devices, swap_with(): return lax.ppermute(x, axis, [(i, i ^ bit) for i in range(size)])  123 us
    dot_general x29, matrix products, dot(): return lax.dot_general(a, b, dims, preferred_element_type=f32)  118 us
    pallas_call x1, Pallas kernels, attend_back(): pl.pallas_call(functools.partial(attend_back_kernel, dims), grid_spec=plt...  47.7 us
    pallas_call x1, Pallas kernels, attend(): pl.pallas_call(functools.partial(attend_kernel, dims), grid_spec=pltpu.Pr...  33.5 us
    convert_element_type x10, other arithmetic, scatter_step(): parts.pop(d).astype(bf16)  20.1 us
    pallas_call x2, Pallas kernels, join(): pl.pallas_call(functools.partial(join_kernel, groups, kinds, slots, dims)...  18 us
    pallas_call x1, Pallas kernels, project(): pl.pallas_call(functools.partial(project_kernel, groups), grid_spec=pltpu...  16.3 us
  transfers between devices with their start and end apart: 73, of which 31 were waited for; matrix products, arithmetic and copies ran while one was open for 26% of the time, Pallas kernels for 8%

profile of v2, /device:TPU:0, one launch (start us, length us, event | category | flops | bytes accessed | tf_op | source)
XLA Modules:
  0.0 799.1 jit_solution(14857801873797684014)
XLA Ops:
  15.4 16.3 %project.1 = (bf16[1024,2048]{1,0:T(8,128)(2,1)}, bf16[1024,384]{1,0:T(8,128)(2,1)}, bf16[1024,384]{1,0:T(8,128)(2,1)}, bf16[1024,384]{1,0:T(8,128)(2,1)}, bf16[1024,384]{1,0:T(8,128)(2,1)}) custom-call(s32[12]{0:T(128)} %concatenate.89.ids, bf16[1024,2048]{1,0:T(8,128)(2,1)} %bitcast.77, bf16[1024,2048]{1,0:T(8,128)(2,1)} %bitcast.78, ...), custom_call_target="tpu_custom_call" | custom-call | flops 6442450944 | bytes 17825792 | tf_op jit(solution)/shard_map/project/pallas_call | solution.py:143
  33.8 3.9 collective-permute-start.4
  38.2 3.2 convolution_add_fusion.refs_10_
  42.6 4.8 fusion.28.refs_11_
  50.5 9.1 %maximum_select_fusion = bf16[1024,2048]{1,0:T(8,128)(2,1)S(1)} fusion(bf16[1024,1024]{1,0:T(8,128)(2,1)S(1)} %get-tuple-element.185, bf16[1024,1024]{1,0:T(8,128)(2,1)S(1)} %get-tuple-element.184, pred[]{:T(512)S(6)} %eq.20, bf16[256,2048]{1,0:T(8,128)(2,1)S(1)} %get-tuple-element.187, bf16[256,2048]{1,0:T(8,128)(2,1)S(1)} %get-tuple-element.188, ...), kind=kLoop, calls=%fused_computation.5 | loop fusion | flops 27262976 | bytes 12582913 | tf_op jit(solution)/shard_map/jit(_where)/select_n | solution.py:567
  59.6 3.8 fusion.26
  68.2 10.5 %fusion.72 = f32[1024,1408]{1,0:T(8,128)} fusion(bf16[1024,2048]{1,0:T(8,128)(2,1)S(1)} %maximum_select_fusion, bf16[1408,2048]{1,0:T(8,128)(2,1)} %constant_dynamic-update-slice_fusion), kind=kOutput, calls=%fused_computation.208 | convolution fusion | flops 5905580032 | bytes 15728640 | tf_op jit(solution)/shard_map/dot_general | solution.py:29
  78.7 4.7 pad_maximum_fusion
  83.4 3.0 pad_maximum_fusion.1
  86.4 13.7 %collective-permute-done.3.refs_1_ = bf16[1024,384]{1,0:T(8,128)(2,1)} collective-permute-done((bf16[1024,384]{1,0:T(8,128)(2,1)}, bf16[1024,384]{1,0:T(8,128)(2,1)}, u32[]{:S(2)}, u32[]{:S(2)}) %collective-permute-start.3) | collective-permute-done | bytes 786464 | tf_op jit(solution)/shard_map/ppermute | solution.py:34
  100.1 33.5 %attend.1 = (bf16[1024,128]{1,0:T(8,128)(2,1)}, bf16[1024,128]{1,0:T(8,128)(2,1)}, bf16[1024,128]{1,0:T(8,128)(2,1)}, bf16[1024,128]{1,0:T(8,128)(2,1)}, f32[128,4096]{1,0:T(8,128)}, /*index=5*/f32[8,4096]{1,0:T(8,128)}) custom-call(s32[12]{0:T(128)} %concatenate.89.ids, bf16[1024,384]{1,0:T(8,128)(2,1)} %get-tuple-element.98.refs_0_, ...), custom_call_target="tpu_custom_call" | custom-call | flops 17179869184 | bytes 8388608 | tf_op jit(solution)/shard_map/attend/pallas_call | solution.py:295
  133.7 6.9 collective-permute-start.10
  145.2 3.5 collective-permute-done.11.refs_2_
  148.7 9.4 %collective-permute-done.12.refs_3_ = bf16[1024,128]{1,0:T(8,128)(2,1)S(1)} collective-permute-done((bf16[1024,128]{1,0:T(8,128)(2,1)}, bf16[1024,128]{1,0:T(8,128)(2,1)S(1)}, u32[]{:S(2)}, u32[]{:S(2)}) %collective-permute-start.12) | collective-permute-done | bytes 262176 | tf_op jit(solution)/shard_map/ppermute | solution.py:34
  159.1 5.0 shard_map.297
  170.6 2.8 collective-permute-done.16
  180.2 6.9 collective-permute-done.18
  187.1 11.2 %collective-permute-done.17 = bf16[128,2048]{1,0:T(8,128)(2,1)} collective-permute-done((bf16[128,2048]{1,0:T(8,128)(2,1)}, bf16[128,2048]{1,0:T(8,128)(2,1)}, u32[]{:S(2)}, u32[]{:S(2)}) %collective-permute-start.17) | collective-permute-done | bytes 524320 | tf_op jit(solution)/shard_map/ppermute | solution.py:34
  206.2 4.6 fusion.73
  210.8 4.8 multiply_convert_fusion.11
  219.9 4.0 collective-permute-done.19
  225.7 4.8 multiply_convert_fusion.9
  237.1 4.7 multiply_convert_fusion.7
  250.0 6.4 collective-permute-done.25
  256.4 21.5 %collective-permute-done.24 = bf16[128,2048]{1,0:T(8,128)(2,1)S(1)} collective-permute-done((bf16[128,2048]{1,0:T(8,128)(2,1)S(1)}, bf16[128,2048]{1,0:T(8,128)(2,1)S(1)}, u32[]{:S(2)}, u32[]{:S(2)}) %collective-permute-start.24) | collective-permute-done | bytes 524320 | tf_op jit(solution)/shard_map/ppermute | solution.py:34
  280.5 4.6 multiply_convert_fusion.5
  285.1 3.2 fusion.80
  288.4 4.9 convolution_convert_fusion.3
  293.3 5.0 convolution_convert_fusion.5
  305.0 9.2 %convolution_convert_fusion = bf16[1024,2048]{1,0:T(8,128)(2,1)S(1)} fusion(bf16[1408,2048]{1,0:T(8,128)(2,1)S(1)} %bitcast.76, bf16[256,1408]{1,0:T(8,128)(2,1)} %get-tuple-element.193, bf16[256,1408]{1,0:T(8,128)(2,1)} %get-tuple-element.192, bf16[256,1408]{1,0:T(8,128)(2,1)} %get-tuple-element.191, bf16[256,1408]{1,0:T(8,128)(2,1)} %get-tuple-element.190), kind=kOutput, calls=%fused_computation.7 | convolution fusion | flops 5919211520 | bytes 12845056 | tf_op jit(solution)/shard_map/dot_general | solution.py:29
  314.3 8.1 %convolution_convert_fusion.1 = bf16[1408,1024]{1,0:T(8,128)(2,1)} fusion(bf16[1024,2048]{1,0:T(8,128)(2,1)S(1)} %copy-done.10, bf16[256,1408]{1,0:T(8,128)(2,1)} %get-tuple-element.193, bf16[256,1408]{1,0:T(8,128)(2,1)} %get-tuple-element.192, bf16[256,1408]{1,0:T(8,128)(2,1)} %get-tuple-element.191, bf16[256,1408]{1,0:T(8,128)(2,1)} %get-tuple-element.190), kind=kOutput, calls=%fused_computation.8 | convolution fusion | flops 2965766144 | bytes 7864320 | tf_op jit(solution)/shard_map/dot_general | solution.py:29
  322.4 4.9 convolution_convert_fusion.6
  327.3 4.8 convolution_convert_fusion.2
  332.1 17.5 %collective-permute-done.26 = bf16[256,2048]{1,0:T(8,128)(2,1)S(1)} collective-permute-done((bf16[256,2048]{1,0:T(8,128)(2,1)S(1)}, bf16[256,2048]{1,0:T(8,128)(2,1)S(1)}, u32[]{:S(2)}, u32[]{:S(2)}) %collective-permute-start.26) | collective-permute-done | bytes 1048608 | tf_op jit(solution)/shard_map/ppermute | solution.py:34
  355.3 5.1 convolution_convert_fusion.4
  360.4 6.2 collective-permute-done.28
  368.7 9.2 %collective-permute-done.29 = bf16[128,2048]{1,0:T(8,128)(2,1)S(1)} collective-permute-done((bf16[128,2048]{1,0:T(8,128)(2,1)S(1)}, bf16[128,2048]{1,0:T(8,128)(2,1)S(1)}, u32[]{:S(2)}, u32[]{:S(2)}) %collective-permute-start.29) | collective-permute-done | bytes 524320 | tf_op jit(solution)/shard_map/ppermute | solution.py:34
  379.5 8.8 %collective-permute-done.32 = bf16[128,2048]{1,0:T(8,128)(2,1)S(1)} collective-permute-done((bf16[128,2048]{1,0:T(8,128)(2,1)S(1)}, bf16[128,2048]{1,0:T(8,128)(2,1)S(1)}, u32[]{:S(2)}, u32[]{:S(2)}) %collective-permute-start.32) | collective-permute-done | bytes 524320 | tf_op jit(solution)/shard_map/ppermute | solution.py:34
  393.5 16.6 %collective-permute-start.37 = (bf16[1024,128]{1,0:T(8,128)(2,1)S(1)}, bf16[1024,128]{1,0:T(8,128)(2,1)S(1)}, u32[]{:S(2)}, u32[]{:S(2)}) collective-permute-start(bf16[1024,128]{1,0:T(8,128)(2,1)S(1)} %get-tuple-element.124), channel_id=1, source_target_pairs={{0,4},{4,0},{8,12},{12,8},{1,5},{5,1},{9,13},{13,9},{2,6},{6,2},{1... | collective-permute-start | bytes 786440 | tf_op jit(solution)/shard_map/ppermute | solution.py:34
  419.6 10.9 %collective-permute-done.38.refs_6_ = bf16[1024,128]{1,0:T(8,128)(2,1)S(1)} collective-permute-done((bf16[1024,128]{1,0:T(8,128)(2,1)S(1)}, bf16[1024,128]{1,0:T(8,128)(2,1)S(1)}, u32[]{:S(2)}, u32[]{:S(2)}) %collective-permute-start.38) | collective-permute-done | bytes 262176 | tf_op jit(solution)/shard_map/ppermute | solution.py:34
  434.0 47.7 %attend_back.1 = (bf16[1024,384]{1,0:T(8,128)(2,1)}, bf16[1024,384]{1,0:T(8,128)(2,1)}, bf16[1024,384]{1,0:T(8,128)(2,1)}, bf16[1024,384]{1,0:T(8,128)(2,1)}) custom-call(s32[12]{0:T(128)} %concatenate.89.ids, bf16[1024,384]{1,0:T(8,128)(2,1)} %get-tuple-element.98.refs_0_, bf16[1024,384]{1,0:T(8,128)(2,1)} %collective-permute-done.3.refs_1_, ...), custom_call_target="tpu_custom_call" | custom-call | flops 42949672960 | bytes 8388608 | tf_op jit(solution)/shard_map/attend_back/pallas_call | solution.py:434
  484.6 2.9 add_convert_fusion.10
  487.5 6.5 collective-permute-start.40
  494.0 3.0 add_convert_fusion.7
  507.1 19.9 %collective-permute-done.40.refs_1_ = bf16[1024,384]{1,0:T(8,128)(2,1)S(1)} collective-permute-done((bf16[1024,384]{1,0:T(8,128)(2,1)S(1)}, bf16[1024,384]{1,0:T(8,128)(2,1)S(1)}, u32[]{:S(2)}, u32[]{:S(2)}) %collective-permute-start.40) | collective-permute-done | bytes 786464 | tf_op jit(solution)/shard_map/ppermute | solution.py:34
  527.0 25.0 %collective-permute-done.41.refs_2_ = bf16[1024,384]{1,0:T(8,128)(2,1)S(1)} collective-permute-done((bf16[1024,384]{1,0:T(8,128)(2,1)S(1)}, bf16[1024,384]{1,0:T(8,128)(2,1)S(1)}, u32[]{:S(2)}, u32[]{:S(2)}) %collective-permute-start.41) | collective-permute-done | bytes 786464 | tf_op jit(solution)/shard_map/ppermute | solution.py:34
  552.6 15.9 %collective-permute-start.58 = (bf16[512,256]{1,0:T(8,128)(2,1)S(1)}, bf16[512,256]{1,0:T(8,128)(2,1)S(1)}, u32[]{:S(2)}, u32[]{:S(2)}) collective-permute-start(bf16[512,256]{1,0:T(8,128)(2,1)S(1)} %get-tuple-element.194), channel_id=1, source_target_pairs={{0,4},{4,0},{8,12},{12,8},{1,5},{5,1},{9,13},{13,9},{2,6},{6,2},{1... | collective-permute-start | bytes 786440 | tf_op jit(solution)/shard_map/ppermute | solution.py:34
  568.5 13.0 %shard_map.298 = (bf16[1024,1536]{1,0:T(8,128)(2,1)}, f32[256,2048]{1,0:T(8,128)}, bf16[256,2048]{1,0:T(8,128)(2,1)S(1)}, bf16[256,2048]{1,0:T(8,128)(2,1)S(1)}, bf16[256,2048]{1,0:T(8,128)(2,1)S(1)}) custom-call(s32[12]{0:T(128)S(1)} %copy-done.2, bf16[1024,384]{1,0:T(8,128)(2,1)S(1)} %copy-done.7, bf16[1024,384]{1,0:T(8,128)(2,1)S(1)} %collective-permute-done.40.refs_1_, ...), custom_call_target="tpu_custom_call" | custom-call | flops 6442450944 | bytes 18874368 | tf_op jit(solution)/shard_map/pallas_call | solution.py:500
  581.5 7.8 convolution_convert_fusion.7
  589.3 4.0 convolution_convert_fusion.8
  593.9 4.2 collective-permute-done.59
  606.9 4.1 collective-permute-start.60
  613.7 7.2 collective-permute-done.60
  621.9 3.2 collective-permute-done.45
  625.0 20.6 %collective-permute-done.44 = bf16[256,2048]{1,0:T(8,128)(2,1)S(1)} collective-permute-done((bf16[256,2048]{1,0:T(8,128)(2,1)S(1)}, bf16[256,2048]{1,0:T(8,128)(2,1)S(1)}, u32[]{:S(2)}, u32[]{:S(2)}) %collective-permute-start.44) | collective-permute-done | bytes 1048608 | tf_op jit(solution)/shard_map/ppermute | solution.py:34
  654.7 3.5 collective-permute-start.51
  673.0 37.1 %collective-permute-done.64 = bf16[256,1408]{1,0:T(8,128)(2,1)} collective-permute-done((bf16[256,1408]{1,0:T(8,128)(2,1)}, bf16[256,1408]{1,0:T(8,128)(2,1)}, u32[]{:S(2)}, u32[]{:S(2)}) %collective-permute-start.64) | collective-permute-done | bytes 720928 | tf_op jit(solution)/shard_map/ppermute | solution.py:34
  710.1 3.4 collective-permute-start.72
  713.5 3.2 convert_add_fusion.5
  716.7 41.4 %collective-permute-done.55 = bf16[256,1536]{1,0:T(8,128)(2,1)S(1)} collective-permute-done((bf16[256,1536]{1,0:T(8,128)(2,1)S(1)}, bf16[256,1536]{1,0:T(8,128)(2,1)S(1)}, u32[]{:S(2)}, u32[]{:S(2)}) %collective-permute-start.55) | collective-permute-done | bytes 786464 | tf_op jit(solution)/shard_map/ppermute | solution.py:34
  761.3 3.0 convert_add_fusion.4
  764.2 3.0 convert_add_fusion.3
  767.3 24.0 %collective-permute-done.54 = bf16[256,1536]{1,0:T(8,128)(2,1)S(1)} collective-permute-done((bf16[256,1536]{1,0:T(8,128)(2,1)S(1)}, bf16[256,1536]{1,0:T(8,128)(2,1)S(1)}, u32[]{:S(2)}, u32[]{:S(2)}) %collective-permute-start.54) | collective-permute-done | bytes 786464 | tf_op jit(solution)/shard_map/ppermute | solution.py:34
  791.3 4.7 collective-permute-done.56
  (380 shorter events, 166.4 us)
Async XLA Ops:
  0.6 13.1 %collective-permute-start = (bf16[1024,512]{1,0:T(8,128)(2,1)}, bf16[1024,512]{1,0:T(8,128)(2,1)S(1)}, u32[]{:S(2)}, u32[]{:S(2)}) collective-permute-start(bf16[1024,512]{1,0:T(8,128)(2,1)} %refs_4_.2), channel_id=1, source_target_pairs={{0,16},{16,0},{1,17},{17,1},{2,18},{18,2},{3,19},{19,3},{4,20},{20... | collective-permute-start | bytes 3145736 | tf_op jit(solution)/shard_map/ppermute | solution.py:34
  1.2 12.6 %collective-permute-start.1 = (bf16[1024,512]{1,0:T(8,128)(2,1)}, bf16[1024,512]{1,0:T(8,128)(2,1)S(1)}, u32[]{:S(2)}, u32[]{:S(2)}) collective-permute-start(bf16[1024,512]{1,0:T(8,128)(2,1)} %refs_5_.1), channel_id=1, source_target_pairs={{0,16},{16,0},{1,17},{17,1},{2,18},{18,2},{3,19},{19,3},{4,20},{20... | collective-permute-start | bytes 3145736 | tf_op jit(solution)/shard_map/ppermute | solution.py:34
  1.3 12.5 %collective-permute-start.2 = (bf16[1024,512]{1,0:T(8,128)(2,1)}, bf16[1024,512]{1,0:T(8,128)(2,1)S(1)}, u32[]{:S(2)}, u32[]{:S(2)}) collective-permute-start(bf16[1024,512]{1,0:T(8,128)(2,1)} %refs_6_.1), channel_id=1, source_target_pairs={{0,16},{16,0},{1,17},{17,1},{2,18},{18,2},{3,19},{19,3},{4,20},{20... | collective-permute-start | bytes 3145736 | tf_op jit(solution)/shard_map/ppermute | solution.py:34
  33.7 31.3 %collective-permute-start.6 = (bf16[1408,1024]{1,0:T(8,128)(2,1)S(1)}, bf16[1408,1024]{1,0:T(8,128)(2,1)S(1)}, u32[]{:S(2)}, u32[]{:S(2)}) collective-permute-start(bf16[1408,1024]{1,0:T(8,128)(2,1)S(1)} %copy-done.17), channel_id=1, source_target_pairs={{0,16},{16,0},{1,17},{17,1},{2,18},{18,2},{3,19},{19,3},{4,20},{20... | collective-permute-start | bytes 8650760 | tf_op jit(solution)/shard_map/ppermute | solution.py:34
  33.8 66.3 %collective-permute-start.4 = (bf16[1024,384]{1,0:T(8,128)(2,1)}, bf16[1024,384]{1,0:T(8,128)(2,1)}, u32[]{:S(2)}, u32[]{:S(2)}) collective-permute-start(bf16[1024,384]{1,0:T(8,128)(2,1)} %get-tuple-element.88), channel_id=1, source_target_pairs={{0,8},{4,12},{8,0},{12,4},{1,9},{5,13},{9,1},{13,5},{2,10},{6,14},... | collective-permute-start | bytes 2359304 | tf_op jit(solution)/shard_map/ppermute | solution.py:34
  37.7 25.8 %collective-permute-start.7 = (bf16[512,1024]{1,0:T(8,128)(2,1)S(1)}, bf16[512,1024]{1,0:T(8,128)(2,1)S(1)}, u32[]{:S(2)}, u32[]{:S(2)}) collective-permute-start(bf16[512,1024]{1,0:T(8,128)(2,1)S(1)} %copy-done), channel_id=1, source_target_pairs={{0,16},{16,0},{1,17},{17,1},{2,18},{18,2},{3,19},{19,3},{4,20},{20... | collective-permute-start | bytes 3145736 | tf_op jit(solution)/shard_map/ppermute | solution.py:34
  47.4 52.8 %collective-permute-start.3 = (bf16[1024,384]{1,0:T(8,128)(2,1)}, bf16[1024,384]{1,0:T(8,128)(2,1)}, u32[]{:S(2)}, u32[]{:S(2)}) collective-permute-start(bf16[1024,384]{1,0:T(8,128)(2,1)} %get-tuple-element.87), channel_id=1, source_target_pairs={{0,4},{4,0},{8,12},{12,8},{1,5},{5,1},{9,13},{13,9},{2,6},{6,2},{1... | collective-permute-start | bytes 2359304 | tf_op jit(solution)/shard_map/ppermute | solution.py:34
  49.0 29.7 %collective-permute-start.8 = (bf16[1024,1408]{1,0:T(8,128)(2,1)S(1)}, bf16[1024,1408]{1,0:T(8,128)(2,1)}, u32[]{:S(2)}, u32[]{:S(2)}) collective-permute-start(bf16[1024,1408]{1,0:T(8,128)(2,1)S(1)} %copy-done.18), channel_id=1, source_target_pairs={{0,16},{16,0},{1,17},{17,1},{2,18},{18,2},{3,19},{19,3},{4,20},{20... | collective-permute-start | bytes 8650760 | tf_op jit(solution)/shard_map/ppermute | solution.py:34
  63.4 36.7 %collective-permute-start.5 = (bf16[1024,384]{1,0:T(8,128)(2,1)S(1)}, bf16[1024,384]{1,0:T(8,128)(2,1)}, u32[]{:S(2)}, u32[]{:S(2)}) collective-permute-start(bf16[1024,384]{1,0:T(8,128)(2,1)S(1)} %copy-done.40), channel_id=1, source_target_pairs={{0,12},{4,8},{8,4},{12,0},{1,13},{5,9},{9,5},{13,1},{2,14},{6,10},... | collective-permute-start | bytes 2359304 | tf_op jit(solution)/shard_map/ppermute | solution.py:34
  66.0 17.4 %collective-permute-start.9 = (bf16[1024,1408]{1,0:T(8,128)(2,1)S(1)}, bf16[1024,1408]{1,0:T(8,128)(2,1)S(1)}, u32[]{:S(2)}, u32[]{:S(2)}) collective-permute-start(bf16[1024,1408]{1,0:T(8,128)(2,1)S(1)} %copy-done.19), channel_id=1, source_target_pairs={{0,16},{16,0},{1,17},{17,1},{2,18},{18,2},{3,19},{19,3},{4,20},{20... | collective-permute-start | bytes 8650760 | tf_op jit(solution)/shard_map/ppermute | solution.py:34
  133.7 11.5 %collective-permute-start.10 = (bf16[1024,128]{1,0:T(8,128)(2,1)}, bf16[1024,128]{1,0:T(8,128)(2,1)S(1)}, u32[]{:S(2)}, u32[]{:S(2)}) collective-permute-start(bf16[1024,128]{1,0:T(8,128)(2,1)} %get-tuple-element.103), channel_id=1, source_target_pairs={{0,4},{4,0},{8,12},{12,8},{1,5},{5,1},{9,13},{13,9},{2,6},{6,2},{1... | collective-permute-start | bytes 786440 | tf_op jit(solution)/shard_map/ppermute | solution.py:34
  142.7 15.5 %collective-permute-start.12 = (bf16[1024,128]{1,0:T(8,128)(2,1)}, bf16[1024,128]{1,0:T(8,128)(2,1)S(1)}, u32[]{:S(2)}, u32[]{:S(2)}) collective-permute-start(bf16[1024,128]{1,0:T(8,128)(2,1)} %get-tuple-element.105), channel_id=1, source_target_pairs={{0,12},{4,8},{8,4},{12,0},{1,13},{5,9},{9,5},{13,1},{2,14},{6,10},... | collective-permute-start | bytes 786440 | tf_op jit(solution)/shard_map/ppermute | solution.py:34
  166.4 9.5 %collective-permute-start.14 = (bf16[128,2048]{1,0:T(8,128)(2,1)S(1)}, bf16[128,2048]{1,0:T(8,128)(2,1)S(1)}, u32[]{:S(2)}, u32[]{:S(2)}) collective-permute-start(bf16[128,2048]{1,0:T(8,128)(2,1)S(1)} %get-tuple-element.212), channel_id=1, source_target_pairs={{0,2},{1,3},{2,0},{3,1},{4,6},{5,7},{6,4},{7,5},{8,10},{9,11},{10,... | collective-permute-start | bytes 1572872 | tf_op jit(solution)/shard_map/ppermute | solution.py:34
  168.8 18.3 %collective-permute-start.18 = (bf16[128,2048]{1,0:T(8,128)(2,1)}, bf16[128,2048]{1,0:T(8,128)(2,1)}, u32[]{:S(2)}, u32[]{:S(2)}) collective-permute-start(bf16[128,2048]{1,0:T(8,128)(2,1)} %slice.197), channel_id=1, source_target_pairs={{0,2},{1,3},{2,0},{3,1},{4,6},{5,7},{6,4},{7,5},{8,10},{9,11},{10,... | collective-permute-start | bytes 1572872 | tf_op jit(solution)/shard_map/ppermute | solution.py:34
  170.1 16.9 %collective-permute-start.13 = (bf16[128,2048]{1,0:T(8,128)(2,1)}, bf16[128,2048]{1,0:T(8,128)(2,1)}, u32[]{:S(2)}, u32[]{:S(2)}) collective-permute-start(bf16[128,2048]{1,0:T(8,128)(2,1)} %slice.192), channel_id=1, source_target_pairs={{0,1},{1,0},{2,3},{3,2},{4,5},{5,4},{6,7},{7,6},{8,9},{9,8},{10,11... | collective-permute-start | bytes 1572872 | tf_op jit(solution)/shard_map/ppermute | solution.py:34
  174.4 23.9 %collective-permute-start.17 = (bf16[128,2048]{1,0:T(8,128)(2,1)}, bf16[128,2048]{1,0:T(8,128)(2,1)}, u32[]{:S(2)}, u32[]{:S(2)}) collective-permute-start(bf16[128,2048]{1,0:T(8,128)(2,1)} %add_convert_fusion.14), channel_id=1, source_target_pairs={{0,2},{1,3},{2,0},{3,1},{4,6},{5,7},{6,4},{7,5},{8,10},{9,11},{10,... | collective-permute-start | bytes 1572872 | tf_op jit(solution)/shard_map/ppermute | solution.py:34
  176.9 21.4 %collective-permute-start.15 = (bf16[128,2048]{1,0:T(8,128)(2,1)}, bf16[128,2048]{1,0:T(8,128)(2,1)}, u32[]{:S(2)}, u32[]{:S(2)}) collective-permute-start(bf16[128,2048]{1,0:T(8,128)(2,1)} %add_convert_fusion.15), channel_id=1, source_target_pairs={{0,1},{1,0},{2,3},{3,2},{4,5},{5,4},{6,7},{7,6},{8,9},{9,8},{10,11... | collective-permute-start | bytes 1572872 | tf_op jit(solution)/shard_map/ppermute | solution.py:34
  202.1 17.8 %collective-permute-start.20 = (bf16[128,2048]{1,0:T(8,128)(2,1)S(1)}, bf16[128,2048]{1,0:T(8,128)(2,1)S(1)}, u32[]{:S(2)}, u32[]{:S(2)}) collective-permute-start(bf16[128,2048]{1,0:T(8,128)(2,1)S(1)} %get-tuple-element.211), channel_id=1, source_target_pairs={{0,1},{1,0},{2,3},{3,2},{4,5},{5,4},{6,7},{7,6},{8,9},{9,8},{10,11... | collective-permute-start | bytes 1572872 | tf_op jit(solution)/shard_map/ppermute | solution.py:34
  202.8 32.4 %collective-permute-start.22 = (bf16[128,2048]{1,0:T(8,128)(2,1)S(1)}, bf16[128,2048]{1,0:T(8,128)(2,1)S(1)}, u32[]{:S(2)}, u32[]{:S(2)}) collective-permute-start(bf16[128,2048]{1,0:T(8,128)(2,1)S(1)} %get-tuple-element.211), channel_id=1, source_target_pairs={{0,2},{1,3},{2,0},{3,1},{4,6},{5,7},{6,4},{7,5},{8,10},{9,11},{10,... | collective-permute-start | bytes 1572872 | tf_op jit(solution)/shard_map/ppermute | solution.py:34
  204.2 19.6 %collective-permute-start.19 = (bf16[128,2048]{1,0:T(8,128)(2,1)S(1)}, bf16[128,2048]{1,0:T(8,128)(2,1)S(1)}, u32[]{:S(2)}, u32[]{:S(2)}) collective-permute-start(bf16[128,2048]{1,0:T(8,128)(2,1)S(1)} %get-tuple-element.210), channel_id=1, source_target_pairs={{0,1},{1,0},{2,3},{3,2},{4,5},{5,4},{6,7},{7,6},{8,9},{9,8},{10,11... | collective-permute-start | bytes 1572872 | tf_op jit(solution)/shard_map/ppermute | solution.py:34
  205.7 29.5 %collective-permute-start.21 = (bf16[128,2048]{1,0:T(8,128)(2,1)S(1)}, bf16[128,2048]{1,0:T(8,128)(2,1)S(1)}, u32[]{:S(2)}, u32[]{:S(2)}) collective-permute-start(bf16[128,2048]{1,0:T(8,128)(2,1)S(1)} %get-tuple-element.210), channel_id=1, source_target_pairs={{0,2},{1,3},{2,0},{3,1},{4,6},{5,7},{6,4},{7,5},{8,10},{9,11},{10,... | collective-permute-start | bytes 1572872 | tf_op jit(solution)/shard_map/ppermute | solution.py:34
  243.6 88.5 %collective-permute-start.23 = (bf16[256,2048]{1,0:T(8,128)(2,1)}, bf16[256,2048]{1,0:T(8,128)(2,1)S(1)}, u32[]{:S(2)}, u32[]{:S(2)}) collective-permute-start(bf16[256,2048]{1,0:T(8,128)(2,1)} %fusion), channel_id=1, source_target_pairs={{0,1},{1,0},{2,3},{3,2},{4,5},{5,4},{6,7},{7,6},{8,9},{9,8},{10,11... | collective-permute-start | bytes 3145736 | tf_op jit(solution)/shard_map/ppermute | solution.py:34
  244.4 12.0 %collective-permute-start.25 = (bf16[128,2048]{1,0:T(8,128)(2,1)S(1)}, bf16[128,2048]{1,0:T(8,128)(2,1)S(1)}, u32[]{:S(2)}, u32[]{:S(2)}) collective-permute-start(bf16[128,2048]{1,0:T(8,128)(2,1)S(1)} %collective-permute-done.20), channel_id=1, source_target_pairs={{0,2},{1,3},{2,0},{3,1},{4,6},{5,7},{6,4},{7,5},{8,10},{9,11},{10,... | collective-permute-start | bytes 1572872 | tf_op jit(solution)/shard_map/ppermute | solution.py:34
  245.7 32.2 %collective-permute-start.24 = (bf16[128,2048]{1,0:T(8,128)(2,1)S(1)}, bf16[128,2048]{1,0:T(8,128)(2,1)S(1)}, u32[]{:S(2)}, u32[]{:S(2)}) collective-permute-start(bf16[128,2048]{1,0:T(8,128)(2,1)S(1)} %collective-permute-done.21), channel_id=1, source_target_pairs={{0,1},{1,0},{2,3},{3,2},{4,5},{5,4},{6,7},{7,6},{8,9},{9,8},{10,11... | collective-permute-start | bytes 1572872 | tf_op jit(solution)/shard_map/ppermute | solution.py:34
  300.2 31.9 %collective-permute-start.27 = (bf16[256,2048]{1,0:T(8,128)(2,1)S(1)}, bf16[256,2048]{1,0:T(8,128)(2,1)S(1)}, u32[]{:S(2)}, u32[]{:S(2)}) collective-permute-start(bf16[256,2048]{1,0:T(8,128)(2,1)S(1)} %fusion.2), channel_id=1, source_target_pairs={{0,3},{1,2},{2,1},{3,0},{4,7},{5,6},{6,5},{7,4},{8,11},{9,10},{10,... | collective-permute-start | bytes 3145736 | tf_op jit(solution)/shard_map/ppermute | solution.py:34
  301.8 47.8 %collective-permute-start.26 = (bf16[256,2048]{1,0:T(8,128)(2,1)S(1)}, bf16[256,2048]{1,0:T(8,128)(2,1)S(1)}, u32[]{:S(2)}, u32[]{:S(2)}) collective-permute-start(bf16[256,2048]{1,0:T(8,128)(2,1)S(1)} %copy-done.39), channel_id=1, source_target_pairs={{0,2},{1,3},{2,0},{3,1},{4,6},{5,7},{6,4},{7,5},{8,10},{9,11},{10,... | collective-permute-start | bytes 3145736 | tf_op jit(solution)/shard_map/ppermute | solution.py:34
  302.6 129.7 %collective-permute-start.61 = (bf16[1024,1408]{1,0:T(8,128)(2,1)}, bf16[1024,1408]{1,0:T(8,128)(2,1)}, u32[]{:S(2)}, u32[]{:S(2)}) collective-permute-start(bf16[1024,1408]{1,0:T(8,128)(2,1)} %convolution_convert_fusion.5), channel_id=1, source_target_pairs={{0,16},{16,0},{1,17},{17,1},{2,18},{18,2},{3,19},{19,3},{4,20},{20... | collective-permute-start | bytes 8650760 | tf_op jit(solution)/shard_map/ppermute | solution.py:34
  304.9 179.5 %collective-permute-start.65 = (bf16[1024,1408]{1,0:T(8,128)(2,1)}, bf16[1024,1408]{1,0:T(8,128)(2,1)}, u32[]{:S(2)}, u32[]{:S(2)}) collective-permute-start(bf16[1024,1408]{1,0:T(8,128)(2,1)} %convolution_convert_fusion.3), channel_id=1, source_target_pairs={{0,16},{16,0},{1,17},{17,1},{2,18},{18,2},{3,19},{19,3},{4,20},{20... | collective-permute-start | bytes 8650760 | tf_op jit(solution)/shard_map/ppermute | solution.py:34
  351.8 14.9 %collective-permute-start.28 = (bf16[128,2048]{1,0:T(8,128)(2,1)S(1)}, bf16[128,2048]{1,0:T(8,128)(2,1)S(1)}, u32[]{:S(2)}, u32[]{:S(2)}) collective-permute-start(bf16[128,2048]{1,0:T(8,128)(2,1)S(1)} %get-tuple-element.209), channel_id=1, source_target_pairs={{0,1},{1,0},{2,3},{3,2},{4,5},{5,4},{6,7},{7,6},{8,9},{9,8},{10,11... | collective-permute-start | bytes 1572872 | tf_op jit(solution)/shard_map/ppermute | solution.py:34
  352.8 15.3 %collective-permute-start.30 = (bf16[128,2048]{1,0:T(8,128)(2,1)S(1)}, bf16[128,2048]{1,0:T(8,128)(2,1)S(1)}, u32[]{:S(2)}, u32[]{:S(2)}) collective-permute-start(bf16[128,2048]{1,0:T(8,128)(2,1)S(1)} %get-tuple-element.209), channel_id=1, source_target_pairs={{0,2},{1,3},{2,0},{3,1},{4,6},{5,7},{6,4},{7,5},{8,10},{9,11},{10,... | collective-permute-start | bytes 1572872 | tf_op jit(solution)/shard_map/ppermute | solution.py:34
  353.9 24.0 %collective-permute-start.29 = (bf16[128,2048]{1,0:T(8,128)(2,1)S(1)}, bf16[128,2048]{1,0:T(8,128)(2,1)S(1)}, u32[]{:S(2)}, u32[]{:S(2)}) collective-permute-start(bf16[128,2048]{1,0:T(8,128)(2,1)S(1)} %get-tuple-element.208), channel_id=1, source_target_pairs={{0,1},{1,0},{2,3},{3,2},{4,5},{5,4},{6,7},{7,6},{8,9},{9,8},{10,11... | collective-permute-start | bytes 1572872 | tf_op jit(solution)/shard_map/ppermute | solution.py:34
  366.7 12.7 %collective-permute-start.31 = (bf16[128,2048]{1,0:T(8,128)(2,1)S(1)}, bf16[128,2048]{1,0:T(8,128)(2,1)S(1)}, u32[]{:S(2)}, u32[]{:S(2)}) collective-permute-start(bf16[128,2048]{1,0:T(8,128)(2,1)S(1)} %get-tuple-element.208), channel_id=1, source_target_pairs={{0,2},{1,3},{2,0},{3,1},{4,6},{5,7},{6,4},{7,5},{8,10},{9,11},{10,... | collective-permute-start | bytes 1572872 | tf_op jit(solution)/shard_map/ppermute | solution.py:34
  368.1 20.3 %collective-permute-start.32 = (bf16[128,2048]{1,0:T(8,128)(2,1)S(1)}, bf16[128,2048]{1,0:T(8,128)(2,1)S(1)}, u32[]{:S(2)}, u32[]{:S(2)}) collective-permute-start(bf16[128,2048]{1,0:T(8,128)(2,1)S(1)} %collective-permute-done.30), channel_id=1, source_target_pairs={{0,1},{1,0},{2,3},{3,2},{4,5},{5,4},{6,7},{7,6},{8,9},{9,8},{10,11... | collective-permute-start | bytes 1572872 | tf_op jit(solution)/shard_map/ppermute | solution.py:34
  377.9 12.2 %collective-permute-start.33 = (bf16[128,2048]{1,0:T(8,128)(2,1)S(1)}, bf16[128,2048]{1,0:T(8,128)(2,1)S(1)}, u32[]{:S(2)}, u32[]{:S(2)}) collective-permute-start(bf16[128,2048]{1,0:T(8,128)(2,1)S(1)} %collective-permute-done.29), channel_id=1, source_target_pairs={{0,2},{1,3},{2,0},{3,1},{4,6},{5,7},{6,4},{7,5},{8,10},{9,11},{10,... | collective-permute-start | bytes 1572872 | tf_op jit(solution)/shard_map/ppermute | solution.py:34
  393.5 26.1 %collective-permute-start.37 = (bf16[1024,128]{1,0:T(8,128)(2,1)S(1)}, bf16[1024,128]{1,0:T(8,128)(2,1)S(1)}, u32[]{:S(2)}, u32[]{:S(2)}) collective-permute-start(bf16[1024,128]{1,0:T(8,128)(2,1)S(1)} %get-tuple-element.124), channel_id=1, source_target_pairs={{0,4},{4,0},{8,12},{12,8},{1,5},{5,1},{9,13},{13,9},{2,6},{6,2},{1... | collective-permute-start | bytes 786440 | tf_op jit(solution)/shard_map/ppermute | solution.py:34
  410.1 20.4 %collective-permute-start.38 = (bf16[1024,128]{1,0:T(8,128)(2,1)S(1)}, bf16[1024,128]{1,0:T(8,128)(2,1)S(1)}, u32[]{:S(2)}, u32[]{:S(2)}) collective-permute-start(bf16[1024,128]{1,0:T(8,128)(2,1)S(1)} %get-tuple-element.125), channel_id=1, source_target_pairs={{0,8},{4,12},{8,0},{12,4},{1,9},{5,13},{9,1},{13,5},{2,10},{6,14},... | collective-permute-start | bytes 786440 | tf_op jit(solution)/shard_map/ppermute | solution.py:34
  411.8 20.2 %collective-permute-start.39 = (bf16[1024,128]{1,0:T(8,128)(2,1)S(1)}, bf16[1024,128]{1,0:T(8,128)(2,1)S(1)}, u32[]{:S(2)}, u32[]{:S(2)}) collective-permute-start(bf16[1024,128]{1,0:T(8,128)(2,1)S(1)} %get-tuple-element.126), channel_id=1, source_target_pairs={{0,12},{4,8},{8,4},{12,0},{1,13},{5,9},{9,5},{13,1},{2,14},{6,10},... | collective-permute-start | bytes 786440 | tf_op jit(solution)/shard_map/ppermute | solution.py:34
  419.6 67.9 %collective-permute-start.69 = (bf16[1408,1024]{1,0:T(8,128)(2,1)}, bf16[1408,1024]{1,0:T(8,128)(2,1)}, u32[]{:S(2)}, u32[]{:S(2)}) collective-permute-start(bf16[1408,1024]{1,0:T(8,128)(2,1)} %convolution_convert_fusion.1), channel_id=1, source_target_pairs={{0,16},{16,0},{1,17},{17,1},{2,18},{18,2},{3,19},{19,3},{4,20},{20... | collective-permute-start | bytes 8650760 | tf_op jit(solution)/shard_map/ppermute | solution.py:34
  430.5 66.5 %collective-permute-start.36 = (bf16[256,2048]{1,0:T(8,128)(2,1)}, bf16[256,2048]{1,0:T(8,128)(2,1)S(1)}, u32[]{:S(2)}, u32[]{:S(2)}) collective-permute-start(bf16[256,2048]{1,0:T(8,128)(2,1)} %get-tuple-element.180), channel_id=1, source_target_pairs={{0,3},{1,2},{2,1},{3,0},{4,7},{5,6},{6,5},{7,4},{8,11},{9,10},{10,... | collective-permute-start | bytes 3145736 | tf_op jit(solution)/shard_map/ppermute | solution.py:34
  432.0 67.0 %collective-permute-start.35 = (bf16[256,2048]{1,0:T(8,128)(2,1)}, bf16[256,2048]{1,0:T(8,128)(2,1)}, u32[]{:S(2)}, u32[]{:S(2)}) collective-permute-start(bf16[256,2048]{1,0:T(8,128)(2,1)} %get-tuple-element.181), channel_id=1, source_target_pairs={{0,2},{1,3},{2,0},{3,1},{4,6},{5,7},{6,4},{7,5},{8,10},{9,11},{10,... | collective-permute-start | bytes 3145736 | tf_op jit(solution)/shard_map/ppermute | solution.py:34
  432.3 68.1 %collective-permute-start.34 = (bf16[256,2048]{1,0:T(8,128)(2,1)}, bf16[256,2048]{1,0:T(8,128)(2,1)}, u32[]{:S(2)}, u32[]{:S(2)}) collective-permute-start(bf16[256,2048]{1,0:T(8,128)(2,1)} %get-tuple-element.179), channel_id=1, source_target_pairs={{0,1},{1,0},{2,3},{3,2},{4,5},{5,4},{6,7},{7,6},{8,9},{9,8},{10,11... | collective-permute-start | bytes 3145736 | tf_op jit(solution)/shard_map/ppermute | solution.py:34
  484.5 19.3 %collective-permute-start.57 = (bf16[512,1024]{1,0:T(8,128)(2,1)S(1)}, bf16[512,1024]{1,0:T(8,128)(2,1)S(1)}, u32[]{:S(2)}, u32[]{:S(2)}) collective-permute-start(bf16[512,1024]{1,0:T(8,128)(2,1)S(1)} %copy-done.38), channel_id=1, source_target_pairs={{0,16},{16,0},{1,17},{17,1},{2,18},{18,2},{3,19},{19,3},{4,20},{20... | collective-permute-start | bytes 3145736 | tf_op jit(solution)/shard_map/ppermute | solution.py:34
  487.5 39.5 %collective-permute-start.40 = (bf16[1024,384]{1,0:T(8,128)(2,1)S(1)}, bf16[1024,384]{1,0:T(8,128)(2,1)S(1)}, u32[]{:S(2)}, u32[]{:S(2)}) collective-permute-start(bf16[1024,384]{1,0:T(8,128)(2,1)S(1)} %copy-done.43), channel_id=1, source_target_pairs={{0,4},{4,0},{8,12},{12,8},{1,5},{5,1},{9,13},{13,9},{2,6},{6,2},{1... | collective-permute-start | bytes 2359304 | tf_op jit(solution)/shard_map/ppermute | solution.py:34
  497.0 55.1 %collective-permute-start.41 = (bf16[1024,384]{1,0:T(8,128)(2,1)S(1)}, bf16[1024,384]{1,0:T(8,128)(2,1)S(1)}, u32[]{:S(2)}, u32[]{:S(2)}) collective-permute-start(bf16[1024,384]{1,0:T(8,128)(2,1)S(1)} %copy-done.42), channel_id=1, source_target_pairs={{0,8},{4,12},{8,0},{12,4},{1,9},{5,13},{9,1},{13,5},{2,10},{6,14},... | collective-permute-start | bytes 2359304 | tf_op jit(solution)/shard_map/ppermute | solution.py:34
  499.0 53.6 %collective-permute-start.42 = (bf16[1024,384]{1,0:T(8,128)(2,1)S(1)}, bf16[1024,384]{1,0:T(8,128)(2,1)S(1)}, u32[]{:S(2)}, u32[]{:S(2)}) collective-permute-start(bf16[1024,384]{1,0:T(8,128)(2,1)S(1)} %copy-done.41), channel_id=1, source_target_pairs={{0,12},{4,8},{8,4},{12,0},{1,13},{5,9},{9,5},{13,1},{2,14},{6,10},... | collective-permute-start | bytes 2359304 | tf_op jit(solution)/shard_map/ppermute | solution.py:34
  500.5 99.3 %collective-permute-start.63 = (bf16[256,1408]{1,0:T(8,128)(2,1)S(1)}, bf16[256,1408]{1,0:T(8,128)(2,1)}, u32[]{:S(2)}, u32[]{:S(2)}) collective-permute-start(bf16[256,1408]{1,0:T(8,128)(2,1)S(1)} %get-tuple-element.178), channel_id=1, source_target_pairs={{0,4},{4,0},{8,12},{12,8},{1,5},{5,1},{9,13},{13,9},{2,6},{6,2},{1... | collective-permute-start | bytes 2162696 | tf_op jit(solution)/shard_map/ppermute | solution.py:34
  503.8 99.1 %collective-permute-start.67 = (bf16[256,1408]{1,0:T(8,128)(2,1)}, bf16[256,1408]{1,0:T(8,128)(2,1)S(1)}, u32[]{:S(2)}, u32[]{:S(2)}) collective-permute-start(bf16[256,1408]{1,0:T(8,128)(2,1)} %get-tuple-element.176), channel_id=1, source_target_pairs={{0,4},{4,0},{8,12},{12,8},{1,5},{5,1},{9,13},{13,9},{2,6},{6,2},{1... | collective-permute-start | bytes 2162696 | tf_op jit(solution)/shard_map/ppermute | solution.py:34
  527.0 79.9 %collective-permute-start.71 = (bf16[1408,256]{1,0:T(8,128)(2,1)}, bf16[1408,256]{1,0:T(8,128)(2,1)}, u32[]{:S(2)}, u32[]{:S(2)}) collective-permute-start(bf16[1408,256]{1,0:T(8,128)(2,1)} %get-tuple-element.174), channel_id=1, source_target_pairs={{0,4},{4,0},{8,12},{12,8},{1,5},{5,1},{9,13},{13,9},{2,6},{6,2},{1... | collective-permute-start | bytes 2162696 | tf_op jit(solution)/shard_map/ppermute | solution.py:34
  552.1 46.0 %collective-permute-start.59 = (bf16[512,256]{1,0:T(8,128)(2,1)S(1)}, bf16[512,256]{1,0:T(8,128)(2,1)S(1)}, u32[]{:S(2)}, u32[]{:S(2)}) collective-permute-start(bf16[512,256]{1,0:T(8,128)(2,1)S(1)} %get-tuple-element.195), channel_id=1, source_target_pairs={{0,4},{4,0},{8,12},{12,8},{1,5},{5,1},{9,13},{13,9},{2,6},{6,2},{1... | collective-permute-start | bytes 786440 | tf_op jit(solution)/shard_map/ppermute | solution.py:34
  552.6 61.1 %collective-permute-start.58 = (bf16[512,256]{1,0:T(8,128)(2,1)S(1)}, bf16[512,256]{1,0:T(8,128)(2,1)S(1)}, u32[]{:S(2)}, u32[]{:S(2)}) collective-permute-start(bf16[512,256]{1,0:T(8,128)(2,1)S(1)} %get-tuple-element.194), channel_id=1, source_target_pairs={{0,4},{4,0},{8,12},{12,8},{1,5},{5,1},{9,13},{13,9},{2,6},{6,2},{1... | collective-permute-start | bytes 786440 | tf_op jit(solution)/shard_map/ppermute | solution.py:34
  598.1 27.0 %collective-permute-start.45 = (bf16[256,2048]{1,0:T(8,128)(2,1)S(1)}, bf16[256,2048]{1,0:T(8,128)(2,1)S(1)}, u32[]{:S(2)}, u32[]{:S(2)}) collective-permute-start(bf16[256,2048]{1,0:T(8,128)(2,1)S(1)} %get-tuple-element.143), channel_id=1, source_target_pairs={{0,3},{1,2},{2,1},{3,0},{4,7},{5,6},{6,5},{7,4},{8,11},{9,10},{10,... | collective-permute-start | bytes 3145736 | tf_op jit(solution)/shard_map/ppermute | solution.py:34
  599.8 45.8 %collective-permute-start.44 = (bf16[256,2048]{1,0:T(8,128)(2,1)S(1)}, bf16[256,2048]{1,0:T(8,128)(2,1)S(1)}, u32[]{:S(2)}, u32[]{:S(2)}) collective-permute-start(bf16[256,2048]{1,0:T(8,128)(2,1)S(1)} %get-tuple-element.142), channel_id=1, source_target_pairs={{0,2},{1,3},{2,0},{3,1},{4,6},{5,7},{6,4},{7,5},{8,10},{9,11},{10,... | collective-permute-start | bytes 3145736 | tf_op jit(solution)/shard_map/ppermute | solution.py:34
  602.9 42.7 %collective-permute-start.43 = (bf16[256,2048]{1,0:T(8,128)(2,1)S(1)}, bf16[256,2048]{1,0:T(8,128)(2,1)S(1)}, u32[]{:S(2)}, u32[]{:S(2)}) collective-permute-start(bf16[256,2048]{1,0:T(8,128)(2,1)S(1)} %get-tuple-element.141), channel_id=1, source_target_pairs={{0,1},{1,0},{2,3},{3,2},{4,5},{5,4},{6,7},{7,6},{8,9},{9,8},{10,11... | collective-permute-start | bytes 3145736 | tf_op jit(solution)/shard_map/ppermute | solution.py:34
  606.9 14.0 %collective-permute-start.60 = (bf16[512,256]{1,0:T(8,128)(2,1)S(1)}, bf16[512,256]{1,0:T(8,128)(2,1)S(1)}, u32[]{:S(2)}, u32[]{:S(2)}) collective-permute-start(bf16[512,256]{1,0:T(8,128)(2,1)S(1)} %add_convert_fusion.16), channel_id=1, source_target_pairs={{0,8},{4,12},{8,0},{12,4},{1,9},{5,13},{9,1},{13,5},{2,10},{6,14},... | collective-permute-start | bytes 786440 | tf_op jit(solution)/shard_map/ppermute | solution.py:34
  613.7 57.0 %collective-permute-start.62 = (bf16[256,1408]{1,0:T(8,128)(2,1)}, bf16[256,1408]{1,0:T(8,128)(2,1)}, u32[]{:S(2)}, u32[]{:S(2)}) collective-permute-start(bf16[256,1408]{1,0:T(8,128)(2,1)} %get-tuple-element.177), channel_id=1, source_target_pairs={{0,4},{4,0},{8,12},{12,8},{1,5},{5,1},{9,13},{13,9},{2,6},{6,2},{1... | collective-permute-start | bytes 2162696 | tf_op jit(solution)/shard_map/ppermute | solution.py:34
  620.9 46.7 %collective-permute-start.53 = (bf16[1024,1536]{1,0:T(8,128)(2,1)}, bf16[1024,1536]{1,0:T(8,128)(2,1)}, u32[]{:S(2)}, u32[]{:S(2)}) collective-permute-start(bf16[1024,1536]{1,0:T(8,128)(2,1)} %convolution_convert_fusion.7), channel_id=1, source_target_pairs={{0,16},{16,0},{1,17},{17,1},{2,18},{18,2},{3,19},{19,3},{4,20},{20... | collective-permute-start | bytes 9437192 | tf_op jit(solution)/shard_map/ppermute | solution.py:34
  661.2 98.3 %collective-permute-start.66 = (bf16[256,1408]{1,0:T(8,128)(2,1)}, bf16[256,1408]{1,0:T(8,128)(2,1)}, u32[]{:S(2)}, u32[]{:S(2)}) collective-permute-start(bf16[256,1408]{1,0:T(8,128)(2,1)} %get-tuple-element.175), channel_id=1, source_target_pairs={{0,4},{4,0},{8,12},{12,8},{1,5},{5,1},{9,13},{13,9},{2,6},{6,2},{1... | collective-permute-start | bytes 2162696 | tf_op jit(solution)/shard_map/ppermute | solution.py:34
  664.1 100.1 %collective-permute-start.70 = (bf16[1408,256]{1,0:T(8,128)(2,1)}, bf16[1408,256]{1,0:T(8,128)(2,1)}, u32[]{:S(2)}, u32[]{:S(2)}) collective-permute-start(bf16[1408,256]{1,0:T(8,128)(2,1)} %get-tuple-element.173), channel_id=1, source_target_pairs={{0,4},{4,0},{8,12},{12,8},{1,5},{5,1},{9,13},{13,9},{2,6},{6,2},{1... | collective-permute-start | bytes 2162696 | tf_op jit(solution)/shard_map/ppermute | solution.py:34
  664.1 46.0 %collective-permute-start.64 = (bf16[256,1408]{1,0:T(8,128)(2,1)}, bf16[256,1408]{1,0:T(8,128)(2,1)}, u32[]{:S(2)}, u32[]{:S(2)}) collective-permute-start(bf16[256,1408]{1,0:T(8,128)(2,1)} %add_convert_fusion.11), channel_id=1, source_target_pairs={{0,8},{4,12},{8,0},{12,4},{1,9},{5,13},{9,1},{13,5},{2,10},{6,14},... | collective-permute-start | bytes 2162696 | tf_op jit(solution)/shard_map/ppermute | solution.py:34
  669.5 88.6 %collective-permute-start.55 = (bf16[256,1536]{1,0:T(8,128)(2,1)S(1)}, bf16[256,1536]{1,0:T(8,128)(2,1)S(1)}, u32[]{:S(2)}, u32[]{:S(2)}) collective-permute-start(bf16[256,1536]{1,0:T(8,128)(2,1)S(1)} %get-tuple-element.172), channel_id=1, source_target_pairs={{0,4},{4,0},{8,12},{12,8},{1,5},{5,1},{9,13},{13,9},{2,6},{6,2},{1... | collective-permute-start | bytes 2359304 | tf_op jit(solution)/shard_map/ppermute | solution.py:34
  670.7 90.6 %collective-permute-start.68 = (bf16[256,1408]{1,0:T(8,128)(2,1)S(1)}, bf16[256,1408]{1,0:T(8,128)(2,1)S(1)}, u32[]{:S(2)}, u32[]{:S(2)}) collective-permute-start(bf16[256,1408]{1,0:T(8,128)(2,1)S(1)} %copy-done.27), channel_id=1, source_target_pairs={{0,8},{4,12},{8,0},{12,4},{1,9},{5,13},{9,1},{13,5},{2,10},{6,14},... | collective-permute-start | bytes 2162696 | tf_op jit(solution)/shard_map/ppermute | solution.py:34
  710.1 54.1 %collective-permute-start.72 = (bf16[1408,256]{1,0:T(8,128)(2,1)S(1)}, bf16[1408,256]{1,0:T(8,128)(2,1)S(1)}, u32[]{:S(2)}, u32[]{:S(2)}) collective-permute-start(bf16[1408,256]{1,0:T(8,128)(2,1)S(1)} %copy-done.26), channel_id=1, source_target_pairs={{0,8},{4,12},{8,0},{12,4},{1,9},{5,13},{9,1},{13,5},{2,10},{6,14},... | collective-permute-start | bytes 2162696 | tf_op jit(solution)/shard_map/ppermute | solution.py:34
  758.1 33.2 %collective-permute-start.54 = (bf16[256,1536]{1,0:T(8,128)(2,1)S(1)}, bf16[256,1536]{1,0:T(8,128)(2,1)S(1)}, u32[]{:S(2)}, u32[]{:S(2)}) collective-permute-start(bf16[256,1536]{1,0:T(8,128)(2,1)S(1)} %get-tuple-element.171), channel_id=1, source_target_pairs={{0,4},{4,0},{8,12},{12,8},{1,5},{5,1},{9,13},{13,9},{2,6},{6,2},{1... | collective-permute-start | bytes 2359304 | tf_op jit(solution)/shard_map/ppermute | solution.py:34
  759.5 36.5 %collective-permute-start.56 = (bf16[256,1536]{1,0:T(8,128)(2,1)S(1)}, bf16[256,1536]{1,0:T(8,128)(2,1)S(1)}, u32[]{:S(2)}, u32[]{:S(2)}) collective-permute-start(bf16[256,1536]{1,0:T(8,128)(2,1)S(1)} %add_convert_fusion.2), channel_id=1, source_target_pairs={{0,8},{4,12},{8,0},{12,4},{1,9},{5,13},{9,1},{13,5},{2,10},{6,14},... | collective-permute-start | bytes 2359304 | tf_op jit(solution)/shard_map/ppermute | solution.py:34
  (85 other events, 1334.4 us)

commit v3 on v2

--- a/solution.py
+++ b/solution.py
@@ -15,6 +15,10 @@
 LOW = -1e30
 LOWER = -2e30
 SCALE = HEAD_DIM ** (-0.5)
+
+SHARD = "shard"
+CONTEXT = "context"
+TENSOR = "tensor"
 
 f32 = jnp.float32
 bf16 = jnp.bfloat16
@@ -247,15 +251,18 @@
             if masked:
                 p = j * bk + lax.broadcasted_iota(jnp.int32, (bk, bq), 0)
                 ok = (p >= lo) & (p < hi)
+            scores = [dot(k, heads[h], NT) for h in range(2)]
+            if masked:
+                scores = [jnp.where(ok, s, LOWER) for s in scores]
+            old = [m_ref[h, 0:1] for h in range(2)]
+            tops = [jnp.max(s, axis=0, keepdims=True) for s in scores]
+            new = [jnp.maximum(a, b) for a, b in zip(old, tops)]
+            fade = [jnp.exp(a - b) for a, b in zip(old, new)]
+            ws = [jnp.exp(s - n).astype(bf16) for s, n in zip(scores, new)]
+            sums = [dot(vx[h, :, keys], ws[h]) for h in range(2)]
             for h in range(2):
-                s = dot(k, heads[h], NT)
-                if masked:
-                    s = jnp.where(ok, s, LOWER)
-                old = m_ref[h, 0:1]
-                new = jnp.maximum(old, jnp.max(s, axis=0, keepdims=True))
-                w = jnp.exp(s - new).astype(bf16)
-                acc[h] = acc[h] * jnp.exp(old - new) + dot(vx[h, :, keys], w)
-                m_ref[h, 0:1] = new
+                acc[h] = acc[h] * fade[h] + sums[h]
+                m_ref[h, 0:1] = new[h]
             return 0
 
         lax.fori_loop(begin, full_begin, functools.partial(visit, True), 0)
@@ -543,11 +550,11 @@
     doc_lengths,
     picture_starts,
 ):
-    me = lax.axis_index("shard")
-    ctx = lax.axis_index("context")
-    ctxs = lax.axis_size("context")
-    ten = lax.axis_index("tensor")
-    slots = lax.axis_size("tensor")
+    me = lax.axis_index(SHARD)
+    ctx = lax.axis_index(CONTEXT)
+    ctxs = lax.axis_size(CONTEXT)
+    ten = lax.axis_index(TENSOR)
+    slots = lax.axis_size(TENSOR)
     rows, width = tokens.shape[1:]
     half = width // 2
     share = rows // slots
@@ -570,7 +577,7 @@
         return lax.dynamic_slice_in_dim(x, (ten ^ i) * share, share, 0)
 
     def other_half(x):
-        return swap_with(x, "shard", 1)
+        return swap_with(x, SHARD, 1)
 
     own_qkv = (q_weight, k_weight, v_weight)
     oth_qkv = tuple(other_half(w) for w in own_qkv)
@@ -612,7 +619,7 @@
         ),
     )
     o_weight, gate_weight, up_weight, down_weight, cot_rows, x_rows, positions = later
-    pieces = [send[0]] + [swap_with(send[s % groups], "context", s) for s in range(1, ctxs)]
+    pieces = [send[0]] + [swap_with(send[s % groups], CONTEXT, s) for s in range(1, ctxs)]
     down_oth, o_oth, gate_oth, up_oth = map(
         other_half, (down_weight, o_weight, gate_weight, up_weight)
     )
@@ -635,7 +642,7 @@
     attn_send, o_t, lse = attend(ids, pieces, groups, slots, docs, pics, bq, bk)
     attn, attn_parts = join(
         ids,
-        [attn_send[0]] + [swap_with(attn_send[s], "context", s) for s in range(1, groups)],
+        [attn_send[0]] + [swap_with(attn_send[s], CONTEXT, s) for s in range(1, groups)],
         (o_weight,),
         (o_oth,),
         slots,
@@ -645,20 +652,20 @@
     mid = share // 2
 
     def send_rows(parts):
-        return [swap_with(parts[i].astype(bf16), "tensor", i) for i in range(1, slots)]
+        return [swap_with(parts[i].astype(bf16), TENSOR, i) for i in range(1, slots)]
 
     def relay_sums(parts):
         if slots != 4:
             return send_rows(parts)
         one, two, far = (parts[i].astype(bf16) for i in range(1, 4))
-        far_two = swap_with(far[:mid], "tensor", 1)
-        far_one = swap_with(far[mid:], "tensor", 2)
-        first = swap_with(one[:mid], "tensor", 1)
-        last = swap_with(two[mid:], "tensor", 2)
+        far_two = swap_with(far[:mid], TENSOR, 1)
+        far_one = swap_with(far[mid:], TENSOR, 2)
+        first = swap_with(one[:mid], TENSOR, 1)
+        last = swap_with(two[mid:], TENSOR, 2)
         two = (two[:mid].astype(f32) + far_two.astype(f32)).astype(bf16)
         one = (one[mid:].astype(f32) + far_one.astype(f32)).astype(bf16)
-        two = swap_with(two, "tensor", 2)
-        one = swap_with(one, "tensor", 1)
+        two = swap_with(two, TENSOR, 2)
+        one = swap_with(one, TENSOR, 1)
         return [
             jnp.concatenate([first, one], axis=0),
             jnp.concatenate([two, last], axis=0),
@@ -671,13 +678,13 @@
 
     def gather_rows(block):
         if slots != 4:
-            return [block] + [swap_with(block, "tensor", i) for i in range(1, slots)]
-        one_last = swap_with(block[mid:], "tensor", 1)
-        two_first = swap_with(block[:mid], "tensor", 2)
-        one_first = swap_with(block[:mid], "tensor", 1)
-        two_last = swap_with(block[mid:], "tensor", 2)
-        far_first = swap_with(two_first, "tensor", 1)
-        far_last = swap_with(one_last, "tensor", 2)
+            return [block] + [swap_with(block, TENSOR, i) for i in range(1, slots)]
+        one_last = swap_with(block[mid:], TENSOR, 1)
+        two_first = swap_with(block[:mid], TENSOR, 2)
+        one_first = swap_with(block[:mid], TENSOR, 1)
+        two_last = swap_with(block[mid:], TENSOR, 2)
+        far_first = swap_with(two_first, TENSOR, 1)
+        far_last = swap_with(one_last, TENSOR, 2)
         return [
             block,
             jnp.concatenate([one_first, one_last], axis=0),
@@ -714,7 +721,7 @@
         if i + 1 < slots:
             norm2_parts[i], h2[i + 1] = hold(norm2_parts[i], h2[i + 1])
         if i > 0:
-            dh2_received.append(swap_with(norm2_parts[i], "tensor", i))
+            dh2_received.append(swap_with(norm2_parts[i], TENSOR, i))
 
     def blocks_of(mine, theirs, axis):
         def block(x, d):
@@ -725,7 +732,7 @@
     def scatter_step(parts, bit):
         parts = dict(parts)
         for d in sorted((d for d in parts if d & bit), reverse=True):
-            parts[d ^ bit] += swap_with(parts.pop(d).astype(bf16), "context", bit).astype(f32)
+            parts[d ^ bit] += swap_with(parts.pop(d).astype(bf16), CONTEXT, bit).astype(f32)
         return parts
 
     def scatter_rest(parts):
@@ -768,7 +775,9 @@
         for s in range(groups)
     ]
     d_send, dx1b, out_all = hold(d_send, dx1b, out_all)
-    d_pieces = [d_send[0]] + [swap_with(d_send[s % groups], "context", s) for s in range(1, ctxs)]
+    d_pieces = [d_send[0]] + [
+        swap_with(d_send[s % groups], CONTEXT, s) for s in range(1, ctxs)
+    ]
 
     o_theirs = dot(attn, dx1b[:, half:], TN).astype(bf16)
     o_mine = dot(attn, dx1b[:, :half], TN).astype(bf16)
@@ -781,7 +790,7 @@
     back = attend_back(
         ids, pieces, d_pieces, o_t, lse, full_tables, groups, slots, docs, pics, bq, bk
     )
-    back_rest = [swap_with(back[s], "context", s) for s in range(1, groups)]
+    back_rest = [swap_with(back[s], CONTEXT, s) for s in range(1, groups)]
 
     output = by_shard(
         (x1 + add_rows(slot_of(out_all, 0).astype(f32), out_received)).astype(bf16)
@@ -819,10 +828,10 @@
             jnp.sum(dh2, axis=0),
         ]
     )
-    norms = sum_over(by_shard(norms), "tensor")
+    norms = sum_over(by_shard(norms), TENSOR)
     bias = jnp.sum(d_qkv.astype(f32), axis=0, keepdims=True)
-    sums = sum_over(jnp.concatenate([norms.reshape(1, 4 * width), bias], axis=1), "shard")
-    sums = sum_over(sums, "context")
+    sums = sum_over(jnp.concatenate([norms.reshape(1, 4 * width), bias], axis=1), SHARD)
+    sums = sum_over(sums, CONTEXT)
     norms = sums[0, : 4 * width].reshape(4, width)
     bias = sums[0, 4 * width :]
     k_bias_grad = bias[inner : 2 * inner].reshape(heads_here, HEAD_DIM)[:, :ROT]
@@ -847,10 +856,10 @@
 
 
 def solution(mesh):
-    tokens = P("shard", "context", None)
-    inward = P("shard", "tensor")
-    outward = P("tensor", "shard")
-    vector = P("tensor")
+    tokens = P(SHARD, CONTEXT, None)
+    inward = P(SHARD, TENSOR)
+    outward = P(TENSOR, SHARD)
+    vector = P(TENSOR)
     placed = (
         tokens,
         P(),
@@ -868,12 +877,12 @@
         inward,
         outward,
         tokens,
-        P("shard", None),
-        P("shard", None),
-    )
-    share = P("shard", ("context", "tensor"), None)
-    grad_in = P(("shard", "context"), "tensor")
-    grad_out = P("tensor", ("shard", "context"))
+        P(SHARD, None),
+        P(SHARD, None),
+    )
+    share = P(SHARD, (CONTEXT, TENSOR), None)
+    grad_in = P((SHARD, CONTEXT), TENSOR)
+    grad_out = P(TENSOR, (SHARD, CONTEXT))
 
     return jax.shard_map(
         local,

time: 809 us -> 805 us (level)
  no operation moved by 1% of the time
where the time goes in v3:
time: 805 us; the launch traced here: 795 us
  waiting for transfers between devices  330 us (41%)
  matrix products  129 us (16%)
  starting transfers between devices  120 us (15%)
  Pallas kernels  112 us (14%)
  other arithmetic  78.5 us (10%)
  local copies, waits for them, and re-layouts  23.1 us (3%)
    ppermute x73, waiting for transfers between devices, swap_with(): return lax.ppermute(x, axis, [(i, i ^ bit) for i in range(size)])  330 us
    ppermute x73, starting transfers between devices, swap_with(): return lax.ppermute(x, axis, [(i, i ^ bit) for i in range(size)])  120 us
    dot_general x29, matrix products, dot(): return lax.dot_general(a, b, dims, preferred_element_type=f32)  118 us
    pallas_call x1, Pallas kernels, attend_back(): pl.pallas_call(functools.partial(attend_back_kernel, dims), grid_spec=plt...  47.7 us
    pallas_call x1, Pallas kernels, attend(): pl.pallas_call(functools.partial(attend_kernel, dims), grid_spec=pltpu.Pr...  29.8 us
    convert_element_type x10, other arithmetic, scatter_step(): parts.pop(d).astype(bf16)  20.1 us
    pallas_call x2, Pallas kernels, join(): pl.pallas_call(functools.partial(join_kernel, groups, kinds, slots, dims)...  18 us
    pallas_call x1, Pallas kernels, project(): pl.pallas_call(functools.partial(project_kernel, groups), grid_spec=pltpu...  16.3 us
  transfers between devices with their start and end apart: 73, of which 31 were waited for; matrix products, arithmetic and copies ran while one was open for 26% of the time, Pallas kernels for 8%

profile of v3, /device:TPU:0, one launch (start us, length us, event | category | flops | bytes accessed | tf_op | source)
XLA Modules:
  0.0 795.3 jit_solution(15389793663477284733)
XLA Ops:
  15.4 16.3 %project.1 = (bf16[1024,2048]{1,0:T(8,128)(2,1)}, bf16[1024,384]{1,0:T(8,128)(2,1)}, bf16[1024,384]{1,0:T(8,128)(2,1)}, bf16[1024,384]{1,0:T(8,128)(2,1)}, bf16[1024,384]{1,0:T(8,128)(2,1)}) custom-call(s32[12]{0:T(128)} %concatenate.89.ids, bf16[1024,2048]{1,0:T(8,128)(2,1)} %bitcast.77, bf16[1024,2048]{1,0:T(8,128)(2,1)} %bitcast.78, ...), custom_call_target="tpu_custom_call" | custom-call | flops 6442450944 | bytes 17825792 | tf_op jit(solution)/shard_map/project/pallas_call | solution.py:147
  33.8 3.9 collective-permute-start.4
  38.2 3.2 convolution_add_fusion.refs_10_
  42.6 4.8 fusion.28.refs_11_
  50.5 9.1 %maximum_select_fusion = bf16[1024,2048]{1,0:T(8,128)(2,1)S(1)} fusion(bf16[1024,1024]{1,0:T(8,128)(2,1)S(1)} %get-tuple-element.185, bf16[1024,1024]{1,0:T(8,128)(2,1)S(1)} %get-tuple-element.184, pred[]{:T(512)S(6)} %eq.20, bf16[256,2048]{1,0:T(8,128)(2,1)S(1)} %get-tuple-element.187, bf16[256,2048]{1,0:T(8,128)(2,1)S(1)} %get-tuple-element.188, ...), kind=kLoop, calls=%fused_computation.5 | loop fusion | flops 27262976 | bytes 12582913 | tf_op jit(solution)/shard_map/jit(_where)/select_n | solution.py:574
  59.6 3.8 fusion.26
  68.2 10.5 %fusion.72 = f32[1024,1408]{1,0:T(8,128)} fusion(bf16[1024,2048]{1,0:T(8,128)(2,1)S(1)} %maximum_select_fusion, bf16[1408,2048]{1,0:T(8,128)(2,1)} %constant_dynamic-update-slice_fusion), kind=kOutput, calls=%fused_computation.208 | convolution fusion | flops 5905580032 | bytes 15728640 | tf_op jit(solution)/shard_map/dot_general | solution.py:33
  78.7 4.7 pad_maximum_fusion
  83.4 3.0 pad_maximum_fusion.1
  86.4 13.7 %collective-permute-done.3.refs_1_ = bf16[1024,384]{1,0:T(8,128)(2,1)} collective-permute-done((bf16[1024,384]{1,0:T(8,128)(2,1)}, bf16[1024,384]{1,0:T(8,128)(2,1)}, u32[]{:S(2)}, u32[]{:S(2)}) %collective-permute-start.3) | collective-permute-done | bytes 786464 | tf_op jit(solution)/shard_map/ppermute | solution.py:38
  100.1 29.8 %attend.1 = (bf16[1024,128]{1,0:T(8,128)(2,1)}, bf16[1024,128]{1,0:T(8,128)(2,1)}, bf16[1024,128]{1,0:T(8,128)(2,1)}, bf16[1024,128]{1,0:T(8,128)(2,1)}, f32[128,4096]{1,0:T(8,128)}, /*index=5*/f32[8,4096]{1,0:T(8,128)}) custom-call(s32[12]{0:T(128)} %concatenate.89.ids, bf16[1024,384]{1,0:T(8,128)(2,1)} %get-tuple-element.98.refs_0_, ...), custom_call_target="tpu_custom_call" | custom-call | flops 17179869184 | bytes 8388608 | tf_op jit(solution)/shard_map/attend/pallas_call | solution.py:302
  129.9 6.9 collective-permute-start.10
  141.4 4.1 collective-permute-done.11.refs_2_
  145.5 9.5 %collective-permute-done.12.refs_3_ = bf16[1024,128]{1,0:T(8,128)(2,1)S(1)} collective-permute-done((bf16[1024,128]{1,0:T(8,128)(2,1)}, bf16[1024,128]{1,0:T(8,128)(2,1)S(1)}, u32[]{:S(2)}, u32[]{:S(2)}) %collective-permute-start.12) | collective-permute-done | bytes 262176 | tf_op jit(solution)/shard_map/ppermute | solution.py:38
  155.9 5.0 shard_map.297
  167.4 3.4 collective-permute-done.16
  177.4 7.0 collective-permute-done.18
  184.4 11.2 %collective-permute-done.17 = bf16[128,2048]{1,0:T(8,128)(2,1)} collective-permute-done((bf16[128,2048]{1,0:T(8,128)(2,1)}, bf16[128,2048]{1,0:T(8,128)(2,1)}, u32[]{:S(2)}, u32[]{:S(2)}) %collective-permute-start.17) | collective-permute-done | bytes 524320 | tf_op jit(solution)/shard_map/ppermute | solution.py:38
  203.5 4.6 fusion.73
  208.2 4.8 multiply_convert_fusion.11
  217.2 4.5 collective-permute-done.19
  223.6 4.8 multiply_convert_fusion.9
  235.0 4.7 multiply_convert_fusion.7
  248.0 7.1 collective-permute-done.25
  255.1 21.4 %collective-permute-done.24 = bf16[128,2048]{1,0:T(8,128)(2,1)S(1)} collective-permute-done((bf16[128,2048]{1,0:T(8,128)(2,1)S(1)}, bf16[128,2048]{1,0:T(8,128)(2,1)S(1)}, u32[]{:S(2)}, u32[]{:S(2)}) %collective-permute-start.24) | collective-permute-done | bytes 524320 | tf_op jit(solution)/shard_map/ppermute | solution.py:38
  279.0 4.6 multiply_convert_fusion.5
  283.6 3.2 fusion.80
  286.8 4.9 convolution_convert_fusion.3
  291.8 5.0 convolution_convert_fusion.5
  303.0 9.2 %convolution_convert_fusion = bf16[1024,2048]{1,0:T(8,128)(2,1)S(1)} fusion(bf16[1408,2048]{1,0:T(8,128)(2,1)S(1)} %bitcast.76, bf16[256,1408]{1,0:T(8,128)(2,1)} %get-tuple-element.193, bf16[256,1408]{1,0:T(8,128)(2,1)} %get-tuple-element.192, bf16[256,1408]{1,0:T(8,128)(2,1)} %get-tuple-element.191, bf16[256,1408]{1,0:T(8,128)(2,1)} %get-tuple-element.190), kind=kOutput, calls=%fused_computation.7 | convolution fusion | flops 5919211520 | bytes 12845056 | tf_op jit(solution)/shard_map/dot_general | solution.py:33
  312.3 8.1 %convolution_convert_fusion.1 = bf16[1408,1024]{1,0:T(8,128)(2,1)} fusion(bf16[1024,2048]{1,0:T(8,128)(2,1)S(1)} %copy-done.10, bf16[256,1408]{1,0:T(8,128)(2,1)} %get-tuple-element.193, bf16[256,1408]{1,0:T(8,128)(2,1)} %get-tuple-element.192, bf16[256,1408]{1,0:T(8,128)(2,1)} %get-tuple-element.191, bf16[256,1408]{1,0:T(8,128)(2,1)} %get-tuple-element.190), kind=kOutput, calls=%fused_computation.8 | convolution fusion | flops 2965766144 | bytes 7864320 | tf_op jit(solution)/shard_map/dot_general | solution.py:33
  320.3 4.9 convolution_convert_fusion.6
  325.3 4.8 convolution_convert_fusion.2
  330.1 17.9 %collective-permute-done.26 = bf16[256,2048]{1,0:T(8,128)(2,1)S(1)} collective-permute-done((bf16[256,2048]{1,0:T(8,128)(2,1)S(1)}, bf16[256,2048]{1,0:T(8,128)(2,1)S(1)}, u32[]{:S(2)}, u32[]{:S(2)}) %collective-permute-start.26) | collective-permute-done | bytes 1048608 | tf_op jit(solution)/shard_map/ppermute | solution.py:38
  354.0 5.1 convolution_convert_fusion.4
  359.1 6.0 collective-permute-done.28
  367.2 9.1 %collective-permute-done.29 = bf16[128,2048]{1,0:T(8,128)(2,1)S(1)} collective-permute-done((bf16[128,2048]{1,0:T(8,128)(2,1)S(1)}, bf16[128,2048]{1,0:T(8,128)(2,1)S(1)}, u32[]{:S(2)}, u32[]{:S(2)}) %collective-permute-start.29) | collective-permute-done | bytes 524320 | tf_op jit(solution)/shard_map/ppermute | solution.py:38
  378.1 8.6 %collective-permute-done.32 = bf16[128,2048]{1,0:T(8,128)(2,1)S(1)} collective-permute-done((bf16[128,2048]{1,0:T(8,128)(2,1)S(1)}, bf16[128,2048]{1,0:T(8,128)(2,1)S(1)}, u32[]{:S(2)}, u32[]{:S(2)}) %collective-permute-start.32) | collective-permute-done | bytes 524320 | tf_op jit(solution)/shard_map/ppermute | solution.py:38
  391.9 14.4 %collective-permute-start.37 = (bf16[1024,128]{1,0:T(8,128)(2,1)S(1)}, bf16[1024,128]{1,0:T(8,128)(2,1)S(1)}, u32[]{:S(2)}, u32[]{:S(2)}) collective-permute-start(bf16[1024,128]{1,0:T(8,128)(2,1)S(1)} %get-tuple-element.124), channel_id=1, source_target_pairs={{0,4},{4,0},{8,12},{12,8},{1,5},{5,1},{9,13},{13,9},{2,6},{6,2},{1... | collective-permute-start | bytes 786440 | tf_op jit(solution)/shard_map/ppermute | solution.py:38
  415.8 10.9 %collective-permute-done.38.refs_6_ = bf16[1024,128]{1,0:T(8,128)(2,1)S(1)} collective-permute-done((bf16[1024,128]{1,0:T(8,128)(2,1)S(1)}, bf16[1024,128]{1,0:T(8,128)(2,1)S(1)}, u32[]{:S(2)}, u32[]{:S(2)}) %collective-permute-start.38) | collective-permute-done | bytes 262176 | tf_op jit(solution)/shard_map/ppermute | solution.py:38
  430.2 47.7 %attend_back.1 = (bf16[1024,384]{1,0:T(8,128)(2,1)}, bf16[1024,384]{1,0:T(8,128)(2,1)}, bf16[1024,384]{1,0:T(8,128)(2,1)}, bf16[1024,384]{1,0:T(8,128)(2,1)}) custom-call(s32[12]{0:T(128)} %concatenate.89.ids, bf16[1024,384]{1,0:T(8,128)(2,1)} %get-tuple-element.98.refs_0_, bf16[1024,384]{1,0:T(8,128)(2,1)} %collective-permute-done.3.refs_1_, ...), custom_call_target="tpu_custom_call" | custom-call | flops 42949672960 | bytes 8388608 | tf_op jit(solution)/shard_map/attend_back/pallas_call | solution.py:441
  480.8 2.9 add_convert_fusion.10
  483.7 6.5 collective-permute-start.40
  490.2 3.0 add_convert_fusion.7
  503.3 19.9 %collective-permute-done.40.refs_1_ = bf16[1024,384]{1,0:T(8,128)(2,1)S(1)} collective-permute-done((bf16[1024,384]{1,0:T(8,128)(2,1)S(1)}, bf16[1024,384]{1,0:T(8,128)(2,1)S(1)}, u32[]{:S(2)}, u32[]{:S(2)}) %collective-permute-start.40) | collective-permute-done | bytes 786464 | tf_op jit(solution)/shard_map/ppermute | solution.py:38
  523.2 25.0 %collective-permute-done.41.refs_2_ = bf16[1024,384]{1,0:T(8,128)(2,1)S(1)} collective-permute-done((bf16[1024,384]{1,0:T(8,128)(2,1)S(1)}, bf16[1024,384]{1,0:T(8,128)(2,1)S(1)}, u32[]{:S(2)}, u32[]{:S(2)}) %collective-permute-start.41) | collective-permute-done | bytes 786464 | tf_op jit(solution)/shard_map/ppermute | solution.py:38
  548.8 15.9 %collective-permute-start.58 = (bf16[512,256]{1,0:T(8,128)(2,1)S(1)}, bf16[512,256]{1,0:T(8,128)(2,1)S(1)}, u32[]{:S(2)}, u32[]{:S(2)}) collective-permute-start(bf16[512,256]{1,0:T(8,128)(2,1)S(1)} %get-tuple-element.194), channel_id=1, source_target_pairs={{0,4},{4,0},{8,12},{12,8},{1,5},{5,1},{9,13},{13,9},{2,6},{6,2},{1... | collective-permute-start | bytes 786440 | tf_op jit(solution)/shard_map/ppermute | solution.py:38
  564.7 13.0 %shard_map.298 = (bf16[1024,1536]{1,0:T(8,128)(2,1)}, f32[256,2048]{1,0:T(8,128)}, bf16[256,2048]{1,0:T(8,128)(2,1)S(1)}, bf16[256,2048]{1,0:T(8,128)(2,1)S(1)}, bf16[256,2048]{1,0:T(8,128)(2,1)S(1)}) custom-call(s32[12]{0:T(128)S(1)} %copy-done.2, bf16[1024,384]{1,0:T(8,128)(2,1)S(1)} %copy-done.7, bf16[1024,384]{1,0:T(8,128)(2,1)S(1)} %collective-permute-done.40.refs_1_, ...), custom_call_target="tpu_custom_call" | custom-call | flops 6442450944 | bytes 18874368 | tf_op jit(solution)/shard_map/pallas_call | solution.py:507
  577.7 7.8 convolution_convert_fusion.7
  585.6 4.0 convolution_convert_fusion.8
  590.1 4.2 collective-permute-done.59
  603.2 4.1 collective-permute-start.60
  609.9 7.2 collective-permute-done.60
  618.1 3.2 collective-permute-done.45
  621.3 20.6 %collective-permute-done.44 = bf16[256,2048]{1,0:T(8,128)(2,1)S(1)} collective-permute-done((bf16[256,2048]{1,0:T(8,128)(2,1)S(1)}, bf16[256,2048]{1,0:T(8,128)(2,1)S(1)}, u32[]{:S(2)}, u32[]{:S(2)}) %collective-permute-start.44) | collective-permute-done | bytes 1048608 | tf_op jit(solution)/shard_map/ppermute | solution.py:38
  650.9 3.5 collective-permute-start.51
  669.2 37.1 %collective-permute-done.64 = bf16[256,1408]{1,0:T(8,128)(2,1)} collective-permute-done((bf16[256,1408]{1,0:T(8,128)(2,1)}, bf16[256,1408]{1,0:T(8,128)(2,1)}, u32[]{:S(2)}, u32[]{:S(2)}) %collective-permute-start.64) | collective-permute-done | bytes 720928 | tf_op jit(solution)/shard_map/ppermute | solution.py:38
  706.3 3.4 collective-permute-start.72
  709.7 3.2 convert_add_fusion.5
  712.9 41.4 %collective-permute-done.55 = bf16[256,1536]{1,0:T(8,128)(2,1)S(1)} collective-permute-done((bf16[256,1536]{1,0:T(8,128)(2,1)S(1)}, bf16[256,1536]{1,0:T(8,128)(2,1)S(1)}, u32[]{:S(2)}, u32[]{:S(2)}) %collective-permute-start.55) | collective-permute-done | bytes 786464 | tf_op jit(solution)/shard_map/ppermute | solution.py:38
  757.4 3.0 convert_add_fusion.4
  760.4 3.0 convert_add_fusion.3
  763.5 24.0 %collective-permute-done.54 = bf16[256,1536]{1,0:T(8,128)(2,1)S(1)} collective-permute-done((bf16[256,1536]{1,0:T(8,128)(2,1)S(1)}, bf16[256,1536]{1,0:T(8,128)(2,1)S(1)}, u32[]{:S(2)}, u32[]{:S(2)}) %collective-permute-start.54) | collective-permute-done | bytes 786464 | tf_op jit(solution)/shard_map/ppermute | solution.py:38
  787.5 4.7 collective-permute-done.56
  (380 shorter events, 166.1 us)
Async XLA Ops:
  0.6 13.1 %collective-permute-start = (bf16[1024,512]{1,0:T(8,128)(2,1)}, bf16[1024,512]{1,0:T(8,128)(2,1)S(1)}, u32[]{:S(2)}, u32[]{:S(2)}) collective-permute-start(bf16[1024,512]{1,0:T(8,128)(2,1)} %refs_4_.2), channel_id=1, source_target_pairs={{0,16},{16,0},{1,17},{17,1},{2,18},{18,2},{3,19},{19,3},{4,20},{20... | collective-permute-start | bytes 3145736 | tf_op jit(solution)/shard_map/ppermute | solution.py:38
  1.2 12.6 %collective-permute-start.1 = (bf16[1024,512]{1,0:T(8,128)(2,1)}, bf16[1024,512]{1,0:T(8,128)(2,1)S(1)}, u32[]{:S(2)}, u32[]{:S(2)}) collective-permute-start(bf16[1024,512]{1,0:T(8,128)(2,1)} %refs_5_.1), channel_id=1, source_target_pairs={{0,16},{16,0},{1,17},{17,1},{2,18},{18,2},{3,19},{19,3},{4,20},{20... | collective-permute-start | bytes 3145736 | tf_op jit(solution)/shard_map/ppermute | solution.py:38
  1.3 12.5 %collective-permute-start.2 = (bf16[1024,512]{1,0:T(8,128)(2,1)}, bf16[1024,512]{1,0:T(8,128)(2,1)S(1)}, u32[]{:S(2)}, u32[]{:S(2)}) collective-permute-start(bf16[1024,512]{1,0:T(8,128)(2,1)} %refs_6_.1), channel_id=1, source_target_pairs={{0,16},{16,0},{1,17},{17,1},{2,18},{18,2},{3,19},{19,3},{4,20},{20... | collective-permute-start | bytes 3145736 | tf_op jit(solution)/shard_map/ppermute | solution.py:38
  33.7 31.3 %collective-permute-start.6 = (bf16[1408,1024]{1,0:T(8,128)(2,1)S(1)}, bf16[1408,1024]{1,0:T(8,128)(2,1)S(1)}, u32[]{:S(2)}, u32[]{:S(2)}) collective-permute-start(bf16[1408,1024]{1,0:T(8,128)(2,1)S(1)} %copy-done.17), channel_id=1, source_target_pairs={{0,16},{16,0},{1,17},{17,1},{2,18},{18,2},{3,19},{19,3},{4,20},{20... | collective-permute-start | bytes 8650760 | tf_op jit(solution)/shard_map/ppermute | solution.py:38
  33.8 66.3 %collective-permute-start.4 = (bf16[1024,384]{1,0:T(8,128)(2,1)}, bf16[1024,384]{1,0:T(8,128)(2,1)}, u32[]{:S(2)}, u32[]{:S(2)}) collective-permute-start(bf16[1024,384]{1,0:T(8,128)(2,1)} %get-tuple-element.88), channel_id=1, source_target_pairs={{0,8},{4,12},{8,0},{12,4},{1,9},{5,13},{9,1},{13,5},{2,10},{6,14},... | collective-permute-start | bytes 2359304 | tf_op jit(solution)/shard_map/ppermute | solution.py:38
  37.7 25.8 %collective-permute-start.7 = (bf16[512,1024]{1,0:T(8,128)(2,1)S(1)}, bf16[512,1024]{1,0:T(8,128)(2,1)S(1)}, u32[]{:S(2)}, u32[]{:S(2)}) collective-permute-start(bf16[512,1024]{1,0:T(8,128)(2,1)S(1)} %copy-done), channel_id=1, source_target_pairs={{0,16},{16,0},{1,17},{17,1},{2,18},{18,2},{3,19},{19,3},{4,20},{20... | collective-permute-start | bytes 3145736 | tf_op jit(solution)/shard_map/ppermute | solution.py:38
  47.4 52.8 %collective-permute-start.3 = (bf16[1024,384]{1,0:T(8,128)(2,1)}, bf16[1024,384]{1,0:T(8,128)(2,1)}, u32[]{:S(2)}, u32[]{:S(2)}) collective-permute-start(bf16[1024,384]{1,0:T(8,128)(2,1)} %get-tuple-element.87), channel_id=1, source_target_pairs={{0,4},{4,0},{8,12},{12,8},{1,5},{5,1},{9,13},{13,9},{2,6},{6,2},{1... | collective-permute-start | bytes 2359304 | tf_op jit(solution)/shard_map/ppermute | solution.py:38
  49.0 29.7 %collective-permute-start.8 = (bf16[1024,1408]{1,0:T(8,128)(2,1)S(1)}, bf16[1024,1408]{1,0:T(8,128)(2,1)}, u32[]{:S(2)}, u32[]{:S(2)}) collective-permute-start(bf16[1024,1408]{1,0:T(8,128)(2,1)S(1)} %copy-done.18), channel_id=1, source_target_pairs={{0,16},{16,0},{1,17},{17,1},{2,18},{18,2},{3,19},{19,3},{4,20},{20... | collective-permute-start | bytes 8650760 | tf_op jit(solution)/shard_map/ppermute | solution.py:38
  63.4 36.7 %collective-permute-start.5 = (bf16[1024,384]{1,0:T(8,128)(2,1)S(1)}, bf16[1024,384]{1,0:T(8,128)(2,1)}, u32[]{:S(2)}, u32[]{:S(2)}) collective-permute-start(bf16[1024,384]{1,0:T(8,128)(2,1)S(1)} %copy-done.40), channel_id=1, source_target_pairs={{0,12},{4,8},{8,4},{12,0},{1,13},{5,9},{9,5},{13,1},{2,14},{6,10},... | collective-permute-start | bytes 2359304 | tf_op jit(solution)/shard_map/ppermute | solution.py:38
  66.0 17.4 %collective-permute-start.9 = (bf16[1024,1408]{1,0:T(8,128)(2,1)S(1)}, bf16[1024,1408]{1,0:T(8,128)(2,1)S(1)}, u32[]{:S(2)}, u32[]{:S(2)}) collective-permute-start(bf16[1024,1408]{1,0:T(8,128)(2,1)S(1)} %copy-done.19), channel_id=1, source_target_pairs={{0,16},{16,0},{1,17},{17,1},{2,18},{18,2},{3,19},{19,3},{4,20},{20... | collective-permute-start | bytes 8650760 | tf_op jit(solution)/shard_map/ppermute | solution.py:38
  129.9 11.5 %collective-permute-start.10 = (bf16[1024,128]{1,0:T(8,128)(2,1)}, bf16[1024,128]{1,0:T(8,128)(2,1)S(1)}, u32[]{:S(2)}, u32[]{:S(2)}) collective-permute-start(bf16[1024,128]{1,0:T(8,128)(2,1)} %get-tuple-element.103), channel_id=1, source_target_pairs={{0,4},{4,0},{8,12},{12,8},{1,5},{5,1},{9,13},{13,9},{2,6},{6,2},{1... | collective-permute-start | bytes 786440 | tf_op jit(solution)/shard_map/ppermute | solution.py:38
  138.9 16.0 %collective-permute-start.12 = (bf16[1024,128]{1,0:T(8,128)(2,1)}, bf16[1024,128]{1,0:T(8,128)(2,1)S(1)}, u32[]{:S(2)}, u32[]{:S(2)}) collective-permute-start(bf16[1024,128]{1,0:T(8,128)(2,1)} %get-tuple-element.105), channel_id=1, source_target_pairs={{0,12},{4,8},{8,4},{12,0},{1,13},{5,9},{9,5},{13,1},{2,14},{6,10},... | collective-permute-start | bytes 786440 | tf_op jit(solution)/shard_map/ppermute | solution.py:38
  163.2 9.9 %collective-permute-start.14 = (bf16[128,2048]{1,0:T(8,128)(2,1)S(1)}, bf16[128,2048]{1,0:T(8,128)(2,1)S(1)}, u32[]{:S(2)}, u32[]{:S(2)}) collective-permute-start(bf16[128,2048]{1,0:T(8,128)(2,1)S(1)} %get-tuple-element.212), channel_id=1, source_target_pairs={{0,2},{1,3},{2,0},{3,1},{4,6},{5,7},{6,4},{7,5},{8,10},{9,11},{10,... | collective-permute-start | bytes 1572872 | tf_op jit(solution)/shard_map/ppermute | solution.py:38
  165.6 18.8 %collective-permute-start.18 = (bf16[128,2048]{1,0:T(8,128)(2,1)}, bf16[128,2048]{1,0:T(8,128)(2,1)}, u32[]{:S(2)}, u32[]{:S(2)}) collective-permute-start(bf16[128,2048]{1,0:T(8,128)(2,1)} %slice.197), channel_id=1, source_target_pairs={{0,2},{1,3},{2,0},{3,1},{4,6},{5,7},{6,4},{7,5},{8,10},{9,11},{10,... | collective-permute-start | bytes 1572872 | tf_op jit(solution)/shard_map/ppermute | solution.py:38
  166.9 17.5 %collective-permute-start.13 = (bf16[128,2048]{1,0:T(8,128)(2,1)}, bf16[128,2048]{1,0:T(8,128)(2,1)}, u32[]{:S(2)}, u32[]{:S(2)}) collective-permute-start(bf16[128,2048]{1,0:T(8,128)(2,1)} %slice.192), channel_id=1, source_target_pairs={{0,1},{1,0},{2,3},{3,2},{4,5},{5,4},{6,7},{7,6},{8,9},{9,8},{10,11... | collective-permute-start | bytes 1572872 | tf_op jit(solution)/shard_map/ppermute | solution.py:38
  171.8 23.9 %collective-permute-start.17 = (bf16[128,2048]{1,0:T(8,128)(2,1)}, bf16[128,2048]{1,0:T(8,128)(2,1)}, u32[]{:S(2)}, u32[]{:S(2)}) collective-permute-start(bf16[128,2048]{1,0:T(8,128)(2,1)} %add_convert_fusion.14), channel_id=1, source_target_pairs={{0,2},{1,3},{2,0},{3,1},{4,6},{5,7},{6,4},{7,5},{8,10},{9,11},{10,... | collective-permute-start | bytes 1572872 | tf_op jit(solution)/shard_map/ppermute | solution.py:38
  174.1 21.6 %collective-permute-start.15 = (bf16[128,2048]{1,0:T(8,128)(2,1)}, bf16[128,2048]{1,0:T(8,128)(2,1)}, u32[]{:S(2)}, u32[]{:S(2)}) collective-permute-start(bf16[128,2048]{1,0:T(8,128)(2,1)} %add_convert_fusion.15), channel_id=1, source_target_pairs={{0,1},{1,0},{2,3},{3,2},{4,5},{5,4},{6,7},{7,6},{8,9},{9,8},{10,11... | collective-permute-start | bytes 1572872 | tf_op jit(solution)/shard_map/ppermute | solution.py:38
  199.4 17.8 %collective-permute-start.20 = (bf16[128,2048]{1,0:T(8,128)(2,1)S(1)}, bf16[128,2048]{1,0:T(8,128)(2,1)S(1)}, u32[]{:S(2)}, u32[]{:S(2)}) collective-permute-start(bf16[128,2048]{1,0:T(8,128)(2,1)S(1)} %get-tuple-element.211), channel_id=1, source_target_pairs={{0,1},{1,0},{2,3},{3,2},{4,5},{5,4},{6,7},{7,6},{8,9},{9,8},{10,11... | collective-permute-start | bytes 1572872 | tf_op jit(solution)/shard_map/ppermute | solution.py:38
  200.2 32.9 %collective-permute-start.22 = (bf16[128,2048]{1,0:T(8,128)(2,1)S(1)}, bf16[128,2048]{1,0:T(8,128)(2,1)S(1)}, u32[]{:S(2)}, u32[]{:S(2)}) collective-permute-start(bf16[128,2048]{1,0:T(8,128)(2,1)S(1)} %get-tuple-element.211), channel_id=1, source_target_pairs={{0,2},{1,3},{2,0},{3,1},{4,6},{5,7},{6,4},{7,5},{8,10},{9,11},{10,... | collective-permute-start | bytes 1572872 | tf_op jit(solution)/shard_map/ppermute | solution.py:38
  201.6 20.2 %collective-permute-start.19 = (bf16[128,2048]{1,0:T(8,128)(2,1)S(1)}, bf16[128,2048]{1,0:T(8,128)(2,1)S(1)}, u32[]{:S(2)}, u32[]{:S(2)}) collective-permute-start(bf16[128,2048]{1,0:T(8,128)(2,1)S(1)} %get-tuple-element.210), channel_id=1, source_target_pairs={{0,1},{1,0},{2,3},{3,2},{4,5},{5,4},{6,7},{7,6},{8,9},{9,8},{10,11... | collective-permute-start | bytes 1572872 | tf_op jit(solution)/shard_map/ppermute | solution.py:38
  203.1 30.0 %collective-permute-start.21 = (bf16[128,2048]{1,0:T(8,128)(2,1)S(1)}, bf16[128,2048]{1,0:T(8,128)(2,1)S(1)}, u32[]{:S(2)}, u32[]{:S(2)}) collective-permute-start(bf16[128,2048]{1,0:T(8,128)(2,1)S(1)} %get-tuple-element.210), channel_id=1, source_target_pairs={{0,2},{1,3},{2,0},{3,1},{4,6},{5,7},{6,4},{7,5},{8,10},{9,11},{10,... | collective-permute-start | bytes 1572872 | tf_op jit(solution)/shard_map/ppermute | solution.py:38
  241.5 88.6 %collective-permute-start.23 = (bf16[256,2048]{1,0:T(8,128)(2,1)}, bf16[256,2048]{1,0:T(8,128)(2,1)S(1)}, u32[]{:S(2)}, u32[]{:S(2)}) collective-permute-start(bf16[256,2048]{1,0:T(8,128)(2,1)} %fusion), channel_id=1, source_target_pairs={{0,1},{1,0},{2,3},{3,2},{4,5},{5,4},{6,7},{7,6},{8,9},{9,8},{10,11... | collective-permute-start | bytes 3145736 | tf_op jit(solution)/shard_map/ppermute | solution.py:38
  242.4 12.6 %collective-permute-start.25 = (bf16[128,2048]{1,0:T(8,128)(2,1)S(1)}, bf16[128,2048]{1,0:T(8,128)(2,1)S(1)}, u32[]{:S(2)}, u32[]{:S(2)}) collective-permute-start(bf16[128,2048]{1,0:T(8,128)(2,1)S(1)} %collective-permute-done.20), channel_id=1, source_target_pairs={{0,2},{1,3},{2,0},{3,1},{4,6},{5,7},{6,4},{7,5},{8,10},{9,11},{10,... | collective-permute-start | bytes 1572872 | tf_op jit(solution)/shard_map/ppermute | solution.py:38
  243.6 32.8 %collective-permute-start.24 = (bf16[128,2048]{1,0:T(8,128)(2,1)S(1)}, bf16[128,2048]{1,0:T(8,128)(2,1)S(1)}, u32[]{:S(2)}, u32[]{:S(2)}) collective-permute-start(bf16[128,2048]{1,0:T(8,128)(2,1)S(1)} %collective-permute-done.21), channel_id=1, source_target_pairs={{0,1},{1,0},{2,3},{3,2},{4,5},{5,4},{6,7},{7,6},{8,9},{9,8},{10,11... | collective-permute-start | bytes 1572872 | tf_op jit(solution)/shard_map/ppermute | solution.py:38
  298.7 31.4 %collective-permute-start.27 = (bf16[256,2048]{1,0:T(8,128)(2,1)S(1)}, bf16[256,2048]{1,0:T(8,128)(2,1)S(1)}, u32[]{:S(2)}, u32[]{:S(2)}) collective-permute-start(bf16[256,2048]{1,0:T(8,128)(2,1)S(1)} %fusion.2), channel_id=1, source_target_pairs={{0,3},{1,2},{2,1},{3,0},{4,7},{5,6},{6,5},{7,4},{8,11},{9,10},{10,... | collective-permute-start | bytes 3145736 | tf_op jit(solution)/shard_map/ppermute | solution.py:38
  300.3 47.8 %collective-permute-start.26 = (bf16[256,2048]{1,0:T(8,128)(2,1)S(1)}, bf16[256,2048]{1,0:T(8,128)(2,1)S(1)}, u32[]{:S(2)}, u32[]{:S(2)}) collective-permute-start(bf16[256,2048]{1,0:T(8,128)(2,1)S(1)} %copy-done.39), channel_id=1, source_target_pairs={{0,2},{1,3},{2,0},{3,1},{4,6},{5,7},{6,4},{7,5},{8,10},{9,11},{10,... | collective-permute-start | bytes 3145736 | tf_op jit(solution)/shard_map/ppermute | solution.py:38
  301.2 127.3 %collective-permute-start.61 = (bf16[1024,1408]{1,0:T(8,128)(2,1)}, bf16[1024,1408]{1,0:T(8,128)(2,1)}, u32[]{:S(2)}, u32[]{:S(2)}) collective-permute-start(bf16[1024,1408]{1,0:T(8,128)(2,1)} %convolution_convert_fusion.5), channel_id=1, source_target_pairs={{0,16},{16,0},{1,17},{17,1},{2,18},{18,2},{3,19},{19,3},{4,20},{20... | collective-permute-start | bytes 8650760 | tf_op jit(solution)/shard_map/ppermute | solution.py:38
  302.9 177.7 %collective-permute-start.65 = (bf16[1024,1408]{1,0:T(8,128)(2,1)}, bf16[1024,1408]{1,0:T(8,128)(2,1)}, u32[]{:S(2)}, u32[]{:S(2)}) collective-permute-start(bf16[1024,1408]{1,0:T(8,128)(2,1)} %convolution_convert_fusion.3), channel_id=1, source_target_pairs={{0,16},{16,0},{1,17},{17,1},{2,18},{18,2},{3,19},{19,3},{4,20},{20... | collective-permute-start | bytes 8650760 | tf_op jit(solution)/shard_map/ppermute | solution.py:38
  350.3 14.9 %collective-permute-start.28 = (bf16[128,2048]{1,0:T(8,128)(2,1)S(1)}, bf16[128,2048]{1,0:T(8,128)(2,1)S(1)}, u32[]{:S(2)}, u32[]{:S(2)}) collective-permute-start(bf16[128,2048]{1,0:T(8,128)(2,1)S(1)} %get-tuple-element.209), channel_id=1, source_target_pairs={{0,1},{1,0},{2,3},{3,2},{4,5},{5,4},{6,7},{7,6},{8,9},{9,8},{10,11... | collective-permute-start | bytes 1572872 | tf_op jit(solution)/shard_map/ppermute | solution.py:38
  351.4 15.3 %collective-permute-start.30 = (bf16[128,2048]{1,0:T(8,128)(2,1)S(1)}, bf16[128,2048]{1,0:T(8,128)(2,1)S(1)}, u32[]{:S(2)}, u32[]{:S(2)}) collective-permute-start(bf16[128,2048]{1,0:T(8,128)(2,1)S(1)} %get-tuple-element.209), channel_id=1, source_target_pairs={{0,2},{1,3},{2,0},{3,1},{4,6},{5,7},{6,4},{7,5},{8,10},{9,11},{10,... | collective-permute-start | bytes 1572872 | tf_op jit(solution)/shard_map/ppermute | solution.py:38
  352.4 23.9 %collective-permute-start.29 = (bf16[128,2048]{1,0:T(8,128)(2,1)S(1)}, bf16[128,2048]{1,0:T(8,128)(2,1)S(1)}, u32[]{:S(2)}, u32[]{:S(2)}) collective-permute-start(bf16[128,2048]{1,0:T(8,128)(2,1)S(1)} %get-tuple-element.208), channel_id=1, source_target_pairs={{0,1},{1,0},{2,3},{3,2},{4,5},{5,4},{6,7},{7,6},{8,9},{9,8},{10,11... | collective-permute-start | bytes 1572872 | tf_op jit(solution)/shard_map/ppermute | solution.py:38
  365.1 12.9 %collective-permute-start.31 = (bf16[128,2048]{1,0:T(8,128)(2,1)S(1)}, bf16[128,2048]{1,0:T(8,128)(2,1)S(1)}, u32[]{:S(2)}, u32[]{:S(2)}) collective-permute-start(bf16[128,2048]{1,0:T(8,128)(2,1)S(1)} %get-tuple-element.208), channel_id=1, source_target_pairs={{0,2},{1,3},{2,0},{3,1},{4,6},{5,7},{6,4},{7,5},{8,10},{9,11},{10,... | collective-permute-start | bytes 1572872 | tf_op jit(solution)/shard_map/ppermute | solution.py:38
  366.7 20.0 %collective-permute-start.32 = (bf16[128,2048]{1,0:T(8,128)(2,1)S(1)}, bf16[128,2048]{1,0:T(8,128)(2,1)S(1)}, u32[]{:S(2)}, u32[]{:S(2)}) collective-permute-start(bf16[128,2048]{1,0:T(8,128)(2,1)S(1)} %collective-permute-done.30), channel_id=1, source_target_pairs={{0,1},{1,0},{2,3},{3,2},{4,5},{5,4},{6,7},{7,6},{8,9},{9,8},{10,11... | collective-permute-start | bytes 1572872 | tf_op jit(solution)/shard_map/ppermute | solution.py:38
  376.4 12.2 %collective-permute-start.33 = (bf16[128,2048]{1,0:T(8,128)(2,1)S(1)}, bf16[128,2048]{1,0:T(8,128)(2,1)S(1)}, u32[]{:S(2)}, u32[]{:S(2)}) collective-permute-start(bf16[128,2048]{1,0:T(8,128)(2,1)S(1)} %collective-permute-done.29), channel_id=1, source_target_pairs={{0,2},{1,3},{2,0},{3,1},{4,6},{5,7},{6,4},{7,5},{8,10},{9,11},{10,... | collective-permute-start | bytes 1572872 | tf_op jit(solution)/shard_map/ppermute | solution.py:38
  391.9 23.8 %collective-permute-start.37 = (bf16[1024,128]{1,0:T(8,128)(2,1)S(1)}, bf16[1024,128]{1,0:T(8,128)(2,1)S(1)}, u32[]{:S(2)}, u32[]{:S(2)}) collective-permute-start(bf16[1024,128]{1,0:T(8,128)(2,1)S(1)} %get-tuple-element.124), channel_id=1, source_target_pairs={{0,4},{4,0},{8,12},{12,8},{1,5},{5,1},{9,13},{13,9},{2,6},{6,2},{1... | collective-permute-start | bytes 786440 | tf_op jit(solution)/shard_map/ppermute | solution.py:38
  406.3 20.4 %collective-permute-start.38 = (bf16[1024,128]{1,0:T(8,128)(2,1)S(1)}, bf16[1024,128]{1,0:T(8,128)(2,1)S(1)}, u32[]{:S(2)}, u32[]{:S(2)}) collective-permute-start(bf16[1024,128]{1,0:T(8,128)(2,1)S(1)} %get-tuple-element.125), channel_id=1, source_target_pairs={{0,8},{4,12},{8,0},{12,4},{1,9},{5,13},{9,1},{13,5},{2,10},{6,14},... | collective-permute-start | bytes 786440 | tf_op jit(solution)/shard_map/ppermute | solution.py:38
  408.0 20.2 %collective-permute-start.39 = (bf16[1024,128]{1,0:T(8,128)(2,1)S(1)}, bf16[1024,128]{1,0:T(8,128)(2,1)S(1)}, u32[]{:S(2)}, u32[]{:S(2)}) collective-permute-start(bf16[1024,128]{1,0:T(8,128)(2,1)S(1)} %get-tuple-element.126), channel_id=1, source_target_pairs={{0,12},{4,8},{8,4},{12,0},{1,13},{5,9},{9,5},{13,1},{2,14},{6,10},... | collective-permute-start | bytes 786440 | tf_op jit(solution)/shard_map/ppermute | solution.py:38
  415.8 68.0 %collective-permute-start.69 = (bf16[1408,1024]{1,0:T(8,128)(2,1)}, bf16[1408,1024]{1,0:T(8,128)(2,1)}, u32[]{:S(2)}, u32[]{:S(2)}) collective-permute-start(bf16[1408,1024]{1,0:T(8,128)(2,1)} %convolution_convert_fusion.1), channel_id=1, source_target_pairs={{0,16},{16,0},{1,17},{17,1},{2,18},{18,2},{3,19},{19,3},{4,20},{20... | collective-permute-start | bytes 8650760 | tf_op jit(solution)/shard_map/ppermute | solution.py:38
  426.7 66.5 %collective-permute-start.36 = (bf16[256,2048]{1,0:T(8,128)(2,1)}, bf16[256,2048]{1,0:T(8,128)(2,1)S(1)}, u32[]{:S(2)}, u32[]{:S(2)}) collective-permute-start(bf16[256,2048]{1,0:T(8,128)(2,1)} %get-tuple-element.180), channel_id=1, source_target_pairs={{0,3},{1,2},{2,1},{3,0},{4,7},{5,6},{6,5},{7,4},{8,11},{9,10},{10,... | collective-permute-start | bytes 3145736 | tf_op jit(solution)/shard_map/ppermute | solution.py:38
  428.2 67.0 %collective-permute-start.35 = (bf16[256,2048]{1,0:T(8,128)(2,1)}, bf16[256,2048]{1,0:T(8,128)(2,1)}, u32[]{:S(2)}, u32[]{:S(2)}) collective-permute-start(bf16[256,2048]{1,0:T(8,128)(2,1)} %get-tuple-element.181), channel_id=1, source_target_pairs={{0,2},{1,3},{2,0},{3,1},{4,6},{5,7},{6,4},{7,5},{8,10},{9,11},{10,... | collective-permute-start | bytes 3145736 | tf_op jit(solution)/shard_map/ppermute | solution.py:38
  428.5 68.2 %collective-permute-start.34 = (bf16[256,2048]{1,0:T(8,128)(2,1)}, bf16[256,2048]{1,0:T(8,128)(2,1)}, u32[]{:S(2)}, u32[]{:S(2)}) collective-permute-start(bf16[256,2048]{1,0:T(8,128)(2,1)} %get-tuple-element.179), channel_id=1, source_target_pairs={{0,1},{1,0},{2,3},{3,2},{4,5},{5,4},{6,7},{7,6},{8,9},{9,8},{10,11... | collective-permute-start | bytes 3145736 | tf_op jit(solution)/shard_map/ppermute | solution.py:38
  480.7 19.3 %collective-permute-start.57 = (bf16[512,1024]{1,0:T(8,128)(2,1)S(1)}, bf16[512,1024]{1,0:T(8,128)(2,1)S(1)}, u32[]{:S(2)}, u32[]{:S(2)}) collective-permute-start(bf16[512,1024]{1,0:T(8,128)(2,1)S(1)} %copy-done.38), channel_id=1, source_target_pairs={{0,16},{16,0},{1,17},{17,1},{2,18},{18,2},{3,19},{19,3},{4,20},{20... | collective-permute-start | bytes 3145736 | tf_op jit(solution)/shard_map/ppermute | solution.py:38
  483.7 39.5 %collective-permute-start.40 = (bf16[1024,384]{1,0:T(8,128)(2,1)S(1)}, bf16[1024,384]{1,0:T(8,128)(2,1)S(1)}, u32[]{:S(2)}, u32[]{:S(2)}) collective-permute-start(bf16[1024,384]{1,0:T(8,128)(2,1)S(1)} %copy-done.43), channel_id=1, source_target_pairs={{0,4},{4,0},{8,12},{12,8},{1,5},{5,1},{9,13},{13,9},{2,6},{6,2},{1... | collective-permute-start | bytes 2359304 | tf_op jit(solution)/shard_map/ppermute | solution.py:38
  493.2 55.1 %collective-permute-start.41 = (bf16[1024,384]{1,0:T(8,128)(2,1)S(1)}, bf16[1024,384]{1,0:T(8,128)(2,1)S(1)}, u32[]{:S(2)}, u32[]{:S(2)}) collective-permute-start(bf16[1024,384]{1,0:T(8,128)(2,1)S(1)} %copy-done.42), channel_id=1, source_target_pairs={{0,8},{4,12},{8,0},{12,4},{1,9},{5,13},{9,1},{13,5},{2,10},{6,14},... | collective-permute-start | bytes 2359304 | tf_op jit(solution)/shard_map/ppermute | solution.py:38
  495.3 53.6 %collective-permute-start.42 = (bf16[1024,384]{1,0:T(8,128)(2,1)S(1)}, bf16[1024,384]{1,0:T(8,128)(2,1)S(1)}, u32[]{:S(2)}, u32[]{:S(2)}) collective-permute-start(bf16[1024,384]{1,0:T(8,128)(2,1)S(1)} %copy-done.41), channel_id=1, source_target_pairs={{0,12},{4,8},{8,4},{12,0},{1,13},{5,9},{9,5},{13,1},{2,14},{6,10},... | collective-permute-start | bytes 2359304 | tf_op jit(solution)/shard_map/ppermute | solution.py:38
  496.7 99.3 %collective-permute-start.63 = (bf16[256,1408]{1,0:T(8,128)(2,1)S(1)}, bf16[256,1408]{1,0:T(8,128)(2,1)}, u32[]{:S(2)}, u32[]{:S(2)}) collective-permute-start(bf16[256,1408]{1,0:T(8,128)(2,1)S(1)} %get-tuple-element.178), channel_id=1, source_target_pairs={{0,4},{4,0},{8,12},{12,8},{1,5},{5,1},{9,13},{13,9},{2,6},{6,2},{1... | collective-permute-start | bytes 2162696 | tf_op jit(solution)/shard_map/ppermute | solution.py:38
  500.0 99.0 %collective-permute-start.67 = (bf16[256,1408]{1,0:T(8,128)(2,1)}, bf16[256,1408]{1,0:T(8,128)(2,1)S(1)}, u32[]{:S(2)}, u32[]{:S(2)}) collective-permute-start(bf16[256,1408]{1,0:T(8,128)(2,1)} %get-tuple-element.176), channel_id=1, source_target_pairs={{0,4},{4,0},{8,12},{12,8},{1,5},{5,1},{9,13},{13,9},{2,6},{6,2},{1... | collective-permute-start | bytes 2162696 | tf_op jit(solution)/shard_map/ppermute | solution.py:38
  523.2 79.9 %collective-permute-start.71 = (bf16[1408,256]{1,0:T(8,128)(2,1)}, bf16[1408,256]{1,0:T(8,128)(2,1)}, u32[]{:S(2)}, u32[]{:S(2)}) collective-permute-start(bf16[1408,256]{1,0:T(8,128)(2,1)} %get-tuple-element.174), channel_id=1, source_target_pairs={{0,4},{4,0},{8,12},{12,8},{1,5},{5,1},{9,13},{13,9},{2,6},{6,2},{1... | collective-permute-start | bytes 2162696 | tf_op jit(solution)/shard_map/ppermute | solution.py:38
  548.3 46.0 %collective-permute-start.59 = (bf16[512,256]{1,0:T(8,128)(2,1)S(1)}, bf16[512,256]{1,0:T(8,128)(2,1)S(1)}, u32[]{:S(2)}, u32[]{:S(2)}) collective-permute-start(bf16[512,256]{1,0:T(8,128)(2,1)S(1)} %get-tuple-element.195), channel_id=1, source_target_pairs={{0,4},{4,0},{8,12},{12,8},{1,5},{5,1},{9,13},{13,9},{2,6},{6,2},{1... | collective-permute-start | bytes 786440 | tf_op jit(solution)/shard_map/ppermute | solution.py:38
  548.8 61.1 %collective-permute-start.58 = (bf16[512,256]{1,0:T(8,128)(2,1)S(1)}, bf16[512,256]{1,0:T(8,128)(2,1)S(1)}, u32[]{:S(2)}, u32[]{:S(2)}) collective-permute-start(bf16[512,256]{1,0:T(8,128)(2,1)S(1)} %get-tuple-element.194), channel_id=1, source_target_pairs={{0,4},{4,0},{8,12},{12,8},{1,5},{5,1},{9,13},{13,9},{2,6},{6,2},{1... | collective-permute-start | bytes 786440 | tf_op jit(solution)/shard_map/ppermute | solution.py:38
  594.3 27.0 %collective-permute-start.45 = (bf16[256,2048]{1,0:T(8,128)(2,1)S(1)}, bf16[256,2048]{1,0:T(8,128)(2,1)S(1)}, u32[]{:S(2)}, u32[]{:S(2)}) collective-permute-start(bf16[256,2048]{1,0:T(8,128)(2,1)S(1)} %get-tuple-element.143), channel_id=1, source_target_pairs={{0,3},{1,2},{2,1},{3,0},{4,7},{5,6},{6,5},{7,4},{8,11},{9,10},{10,... | collective-permute-start | bytes 3145736 | tf_op jit(solution)/shard_map/ppermute | solution.py:38
  596.0 45.8 %collective-permute-start.44 = (bf16[256,2048]{1,0:T(8,128)(2,1)S(1)}, bf16[256,2048]{1,0:T(8,128)(2,1)S(1)}, u32[]{:S(2)}, u32[]{:S(2)}) collective-permute-start(bf16[256,2048]{1,0:T(8,128)(2,1)S(1)} %get-tuple-element.142), channel_id=1, source_target_pairs={{0,2},{1,3},{2,0},{3,1},{4,6},{5,7},{6,4},{7,5},{8,10},{9,11},{10,... | collective-permute-start | bytes 3145736 | tf_op jit(solution)/shard_map/ppermute | solution.py:38
  599.0 42.8 %collective-permute-start.43 = (bf16[256,2048]{1,0:T(8,128)(2,1)S(1)}, bf16[256,2048]{1,0:T(8,128)(2,1)S(1)}, u32[]{:S(2)}, u32[]{:S(2)}) collective-permute-start(bf16[256,2048]{1,0:T(8,128)(2,1)S(1)} %get-tuple-element.141), channel_id=1, source_target_pairs={{0,1},{1,0},{2,3},{3,2},{4,5},{5,4},{6,7},{7,6},{8,9},{9,8},{10,11... | collective-permute-start | bytes 3145736 | tf_op jit(solution)/shard_map/ppermute | solution.py:38
  603.2 14.0 %collective-permute-start.60 = (bf16[512,256]{1,0:T(8,128)(2,1)S(1)}, bf16[512,256]{1,0:T(8,128)(2,1)S(1)}, u32[]{:S(2)}, u32[]{:S(2)}) collective-permute-start(bf16[512,256]{1,0:T(8,128)(2,1)S(1)} %add_convert_fusion.16), channel_id=1, source_target_pairs={{0,8},{4,12},{8,0},{12,4},{1,9},{5,13},{9,1},{13,5},{2,10},{6,14},... | collective-permute-start | bytes 786440 | tf_op jit(solution)/shard_map/ppermute | solution.py:38
  609.9 56.9 %collective-permute-start.62 = (bf16[256,1408]{1,0:T(8,128)(2,1)}, bf16[256,1408]{1,0:T(8,128)(2,1)}, u32[]{:S(2)}, u32[]{:S(2)}) collective-permute-start(bf16[256,1408]{1,0:T(8,128)(2,1)} %get-tuple-element.177), channel_id=1, source_target_pairs={{0,4},{4,0},{8,12},{12,8},{1,5},{5,1},{9,13},{13,9},{2,6},{6,2},{1... | collective-permute-start | bytes 2162696 | tf_op jit(solution)/shard_map/ppermute | solution.py:38
  617.1 46.7 %collective-permute-start.53 = (bf16[1024,1536]{1,0:T(8,128)(2,1)}, bf16[1024,1536]{1,0:T(8,128)(2,1)}, u32[]{:S(2)}, u32[]{:S(2)}) collective-permute-start(bf16[1024,1536]{1,0:T(8,128)(2,1)} %convolution_convert_fusion.7), channel_id=1, source_target_pairs={{0,16},{16,0},{1,17},{17,1},{2,18},{18,2},{3,19},{19,3},{4,20},{20... | collective-permute-start | bytes 9437192 | tf_op jit(solution)/shard_map/ppermute | solution.py:38
  657.4 98.3 %collective-permute-start.66 = (bf16[256,1408]{1,0:T(8,128)(2,1)}, bf16[256,1408]{1,0:T(8,128)(2,1)}, u32[]{:S(2)}, u32[]{:S(2)}) collective-permute-start(bf16[256,1408]{1,0:T(8,128)(2,1)} %get-tuple-element.175), channel_id=1, source_target_pairs={{0,4},{4,0},{8,12},{12,8},{1,5},{5,1},{9,13},{13,9},{2,6},{6,2},{1... | collective-permute-start | bytes 2162696 | tf_op jit(solution)/shard_map/ppermute | solution.py:38
  660.3 100.1 %collective-permute-start.70 = (bf16[1408,256]{1,0:T(8,128)(2,1)}, bf16[1408,256]{1,0:T(8,128)(2,1)}, u32[]{:S(2)}, u32[]{:S(2)}) collective-permute-start(bf16[1408,256]{1,0:T(8,128)(2,1)} %get-tuple-element.173), channel_id=1, source_target_pairs={{0,4},{4,0},{8,12},{12,8},{1,5},{5,1},{9,13},{13,9},{2,6},{6,2},{1... | collective-permute-start | bytes 2162696 | tf_op jit(solution)/shard_map/ppermute | solution.py:38
  660.3 46.0 %collective-permute-start.64 = (bf16[256,1408]{1,0:T(8,128)(2,1)}, bf16[256,1408]{1,0:T(8,128)(2,1)}, u32[]{:S(2)}, u32[]{:S(2)}) collective-permute-start(bf16[256,1408]{1,0:T(8,128)(2,1)} %add_convert_fusion.11), channel_id=1, source_target_pairs={{0,8},{4,12},{8,0},{12,4},{1,9},{5,13},{9,1},{13,5},{2,10},{6,14},... | collective-permute-start | bytes 2162696 | tf_op jit(solution)/shard_map/ppermute | solution.py:38
  665.7 88.6 %collective-permute-start.55 = (bf16[256,1536]{1,0:T(8,128)(2,1)S(1)}, bf16[256,1536]{1,0:T(8,128)(2,1)S(1)}, u32[]{:S(2)}, u32[]{:S(2)}) collective-permute-start(bf16[256,1536]{1,0:T(8,128)(2,1)S(1)} %get-tuple-element.172), channel_id=1, source_target_pairs={{0,4},{4,0},{8,12},{12,8},{1,5},{5,1},{9,13},{13,9},{2,6},{6,2},{1... | collective-permute-start | bytes 2359304 | tf_op jit(solution)/shard_map/ppermute | solution.py:38
  666.8 90.6 %collective-permute-start.68 = (bf16[256,1408]{1,0:T(8,128)(2,1)S(1)}, bf16[256,1408]{1,0:T(8,128)(2,1)S(1)}, u32[]{:S(2)}, u32[]{:S(2)}) collective-permute-start(bf16[256,1408]{1,0:T(8,128)(2,1)S(1)} %copy-done.27), channel_id=1, source_target_pairs={{0,8},{4,12},{8,0},{12,4},{1,9},{5,13},{9,1},{13,5},{2,10},{6,14},... | collective-permute-start | bytes 2162696 | tf_op jit(solution)/shard_map/ppermute | solution.py:38
  706.3 54.1 %collective-permute-start.72 = (bf16[1408,256]{1,0:T(8,128)(2,1)S(1)}, bf16[1408,256]{1,0:T(8,128)(2,1)S(1)}, u32[]{:S(2)}, u32[]{:S(2)}) collective-permute-start(bf16[1408,256]{1,0:T(8,128)(2,1)S(1)} %copy-done.26), channel_id=1, source_target_pairs={{0,8},{4,12},{8,0},{12,4},{1,9},{5,13},{9,1},{13,5},{2,10},{6,14},... | collective-permute-start | bytes 2162696 | tf_op jit(solution)/shard_map/ppermute | solution.py:38
  754.3 33.2 %collective-permute-start.54 = (bf16[256,1536]{1,0:T(8,128)(2,1)S(1)}, bf16[256,1536]{1,0:T(8,128)(2,1)S(1)}, u32[]{:S(2)}, u32[]{:S(2)}) collective-permute-start(bf16[256,1536]{1,0:T(8,128)(2,1)S(1)} %get-tuple-element.171), channel_id=1, source_target_pairs={{0,4},{4,0},{8,12},{12,8},{1,5},{5,1},{9,13},{13,9},{2,6},{6,2},{1... | collective-permute-start | bytes 2359304 | tf_op jit(solution)/shard_map/ppermute | solution.py:38
  755.7 36.5 %collective-permute-start.56 = (bf16[256,1536]{1,0:T(8,128)(2,1)S(1)}, bf16[256,1536]{1,0:T(8,128)(2,1)S(1)}, u32[]{:S(2)}, u32[]{:S(2)}) collective-permute-start(bf16[256,1536]{1,0:T(8,128)(2,1)S(1)} %add_convert_fusion.2), channel_id=1, source_target_pairs={{0,8},{4,12},{8,0},{12,4},{1,9},{5,13},{9,1},{13,5},{2,10},{6,14},... | collective-permute-start | bytes 2359304 | tf_op jit(solution)/shard_map/ppermute | solution.py:38
  (85 other events, 1332.4 us)

commit v4 on v3

--- a/solution.py
+++ b/solution.py
@@ -474,19 +474,18 @@
     pieces = refs[:groups]
     own = refs[groups : groups + kinds]
     oth = refs[groups + kinds : groups + 2 * kinds]
-    joined = refs[groups + 2 * kinds]
-    parts = refs[groups + 2 * kinds + 1 :]
-    inner = groups * PAIR
+    joined = refs[groups + 2 * kinds : groups + 3 * kinds]
+    parts = refs[groups + 3 * kinds :]
     half = parts[0].shape[1] // 2
     for s in range(groups):
         group = (ids[1] & (groups - 1)) ^ s
         for j in range(kinds):
-            cols = pl.ds(pl.multiple_of(j * inner + group * PAIR, PAIR), PAIR)
-            joined[:, cols] = pieces[s][:, j * PAIR : (j + 1) * PAIR]
+            cols = pl.ds(pl.multiple_of(group * PAIR, PAIR), PAIR)
+            joined[j][:, cols] = pieces[s][:, j * PAIR : (j + 1) * PAIR]
     for side, weights in enumerate((own, oth)):
         total = None
         for j, w in enumerate(weights):
-            term = dot(joined[:, j * inner : (j + 1) * inner], w[...], dims)
+            term = dot(joined[j][...], w[...], dims)
             total = term if total is None else total + term
         for i in range(slots):
 
@@ -511,10 +510,10 @@
             grid=(slots,),
             in_specs=[pl.BlockSpec((share, kinds * PAIR), by_row)] * groups
             + [pl.BlockSpec(own[0].shape, whole)] * (2 * kinds),
-            out_specs=[pl.BlockSpec((share, kinds * inner), by_row)]
+            out_specs=[pl.BlockSpec((share, inner), by_row)] * kinds
             + [pl.BlockSpec((share, width), whole)] * slots,
         ),
-        out_shape=[jax.ShapeDtypeStruct((rows, kinds * inner), bf16)]
+        out_shape=[jax.ShapeDtypeStruct((rows, inner), bf16)] * kinds
         + [jax.ShapeDtypeStruct((share, width), f32 if i == 0 else bf16) for i in range(slots)],
         compiler_params=pltpu.CompilerParams(vmem_limit_bytes=44 << 20),
         cost_estimate=pl.CostEstimate(
@@ -523,7 +522,7 @@
             transcendentals=0,
         ),
     )(ids, *pieces, *own, *oth)
-    return out[0], out[1:]
+    return out[:kinds], out[kinds:]
 
 
 def hold(*groups):
@@ -640,7 +639,7 @@
     down_full, o_full, gate_full, up_full, cot_all, dm_all, full_tables, x_share = ready
 
     attn_send, o_t, lse = attend(ids, pieces, groups, slots, docs, pics, bq, bk)
-    attn, attn_parts = join(
+    (attn,), attn_parts = join(
         ids,
         [attn_send[0]] + [swap_with(attn_send[s], CONTEXT, s) for s in range(1, groups)],
         (o_weight,),
@@ -802,10 +801,15 @@
     d_qkv, norm1_parts = join(ids, [back[0]] + back_rest, own_qkv, oth_qkv, slots, NT)
     norm1_parts, d_qkv = hold(norm1_parts, d_qkv)
     dh1_received = send_rows(norm1_parts)
-    qkv_theirs = other_half(dot(h1[:, half:], d_qkv, TN).astype(bf16))
-    qkv_mine = dot(h1[:, :half], d_qkv, TN).astype(bf16)
-    qkv_parts = scatter_step(blocks_of(qkv_mine, qkv_theirs, 0), 1)
-    qkv_grad = scatter_rest(qkv_parts)
+    qkv_theirs = []
+    qkv_mine = []
+    qkv_parts = []
+    qkv_grad = []
+    for j in range(3):
+        qkv_theirs.append(other_half(dot(h1[:, half:], d_qkv[j], TN).astype(bf16)))
+        qkv_mine.append(dot(h1[:, :half], d_qkv[j], TN).astype(bf16))
+        qkv_parts.append(scatter_step(blocks_of(qkv_mine[j], qkv_theirs[j], 0), 1))
+        qkv_grad.append(scatter_rest(qkv_parts[j]))
     dh1 = add_rows(norm1_parts[0], dh1_received)
 
     mean1 = jnp.mean(x_share, axis=-1, keepdims=True)
@@ -829,7 +833,9 @@
         ]
     )
     norms = sum_over(by_shard(norms), TENSOR)
-    bias = jnp.sum(d_qkv.astype(f32), axis=0, keepdims=True)
+    bias = jnp.concatenate(
+        [jnp.sum(d.astype(f32), axis=0, keepdims=True) for d in d_qkv], axis=1
+    )
     sums = sum_over(jnp.concatenate([norms.reshape(1, 4 * width), bias], axis=1), SHARD)
     sums = sum_over(sums, CONTEXT)
     norms = sums[0, : 4 * width].reshape(4, width)
@@ -840,9 +846,7 @@
         tokens_grad,
         norms[0],
         norms[1],
-        qkv_grad[:, :inner],
-        qkv_grad[:, inner : 2 * inner],
-        qkv_grad[:, 2 * inner :],
+        *qkv_grad,
         bias[:inner],
         k_bias_grad.reshape(heads_here * ROT),
         bias[2 * inner :],

time: 805 us -> 829 us (1.030)
  waiting for transfers between devices: 330 us -> 355 us
    ppermute x73 -> x81, waiting for transfers between devices: 330 us -> 355 us  [swap_with(): return lax.ppermute(x, axis, [(i, i ^ bit) for i in range(size)])]
    ppermute x73 -> x81, starting transfers between devices: 120 us -> 117 us  [swap_with(): return lax.ppermute(x, axis, [(i, i ^ bit) for i in range(size)])]
    dot_general x29 -> x33, matrix products: 118 us -> 115 us  [dot(): return lax.dot_general(a, b, dims, preferred_element_type=f32)]
    convert_element_type x10 -> x14, other arithmetic: 20.1 us -> 20 us  [scatter_step(): parts.pop(d).astype(bf16)]
  transfers between devices with their start and end apart: 73 -> 81, of which waited for: 31 -> 36; matrix products, arithmetic and copies ran while one was open for 26% -> 26% of each run, Pallas kernels for 8% -> 7%
where the time goes in v4:
time: 829 us; the launch traced here: 820 us
  waiting for transfers between devices  355 us (43%)
  matrix products  127 us (15%)
  starting transfers between devices  117 us (14%)
  Pallas kernels  112 us (14%)
  other arithmetic  81.5 us (10%)
  local copies, waits for them, and re-layouts  25.1 us (3%)
    ppermute x81, waiting for transfers between devices, swap_with(): return lax.ppermute(x, axis, [(i, i ^ bit) for i in range(size)])  355 us
    ppermute x81, starting transfers between devices, swap_with(): return lax.ppermute(x, axis, [(i, i ^ bit) for i in range(size)])  117 us
    dot_general x33, matrix products, dot(): return lax.dot_general(a, b, dims, preferred_element_type=f32)  115 us
    pallas_call x1, Pallas kernels, attend_back(): pl.pallas_call(functools.partial(attend_back_kernel, dims), grid_spec=plt...  47.8 us
    pallas_call x1, Pallas kernels, attend(): pl.pallas_call(functools.partial(attend_kernel, dims), grid_spec=pltpu.Pr...  29.7 us
    convert_element_type x14, other arithmetic, scatter_step(): parts.pop(d).astype(bf16)  20 us
    pallas_call x2, Pallas kernels, join(): pl.pallas_call(functools.partial(join_kernel, groups, kinds, slots, dims)...  18.3 us
  transfers between devices with their start and end apart: 81, of which 36 were waited for; matrix products, arithmetic and copies ran while one was open for 26% of the time, Pallas kernels for 7%

profile of v4, /device:TPU:0, one launch (start us, length us, event | category | flops | bytes accessed | tf_op | source)
XLA Modules:
  0.0 819.7 jit_solution(7679791392776665786)
XLA Ops:
  15.4 16.3 %project.1 = (bf16[1024,2048]{1,0:T(8,128)(2,1)}, bf16[1024,384]{1,0:T(8,128)(2,1)}, bf16[1024,384]{1,0:T(8,128)(2,1)}, bf16[1024,384]{1,0:T(8,128)(2,1)}, bf16[1024,384]{1,0:T(8,128)(2,1)}) custom-call(s32[12]{0:T(128)} %concatenate.89.ids, bf16[1024,2048]{1,0:T(8,128)(2,1)} %bitcast.84, bf16[1024,2048]{1,0:T(8,128)(2,1)} %bitcast.85, ...), custom_call_target="tpu_custom_call" | custom-call | flops 6442450944 | bytes 17825792 | tf_op jit(solution)/shard_map/project/pallas_call | solution.py:147
  33.8 3.9 collective-permute-start.4
  38.2 3.1 convolution_add_fusion.refs_10_
  42.8 4.8 fusion.56.refs_11_
  50.8 9.1 %maximum_select_fusion = bf16[1024,2048]{1,0:T(8,128)(2,1)S(1)} fusion(bf16[1024,1024]{1,0:T(8,128)(2,1)S(1)} %get-tuple-element.191, bf16[1024,1024]{1,0:T(8,128)(2,1)S(1)} %get-tuple-element.190, pred[]{:T(512)S(6)} %eq.20, bf16[256,2048]{1,0:T(8,128)(2,1)S(1)} %get-tuple-element.193, bf16[256,2048]{1,0:T(8,128)(2,1)S(1)} %get-tuple-element.194, ...), kind=kLoop, calls=%fused_computation.4 | loop fusion | flops 27262976 | bytes 12582913 | tf_op jit(solution)/shard_map/jit(_where)/select_n | solution.py:573
  59.9 3.8 fusion.54
  68.4 10.5 %fusion.99 = f32[1024,1408]{1,0:T(8,128)} fusion(bf16[1024,2048]{1,0:T(8,128)(2,1)S(1)} %maximum_select_fusion, bf16[1408,2048]{1,0:T(8,128)(2,1)} %constant_dynamic-update-slice_fusion), kind=kOutput, calls=%fused_computation.230 | convolution fusion | flops 5905580032 | bytes 15728640 | tf_op jit(solution)/shard_map/dot_general | solution.py:33
  78.9 4.7 pad_maximum_fusion
  83.6 3.0 pad_maximum_fusion.1
  86.6 13.5 %collective-permute-done.3.refs_1_ = bf16[1024,384]{1,0:T(8,128)(2,1)S(1)} collective-permute-done((bf16[1024,384]{1,0:T(8,128)(2,1)S(1)}, bf16[1024,384]{1,0:T(8,128)(2,1)S(1)}, u32[]{:S(2)}, u32[]{:S(2)}) %collective-permute-start.3) | collective-permute-done | bytes 786464 | tf_op jit(solution)/shard_map/ppermute | solution.py:38
  102.1 29.7 %attend.1 = (bf16[1024,128]{1,0:T(8,128)(2,1)}, bf16[1024,128]{1,0:T(8,128)(2,1)}, bf16[1024,128]{1,0:T(8,128)(2,1)}, bf16[1024,128]{1,0:T(8,128)(2,1)}, f32[128,4096]{1,0:T(8,128)}, /*index=5*/f32[8,4096]{1,0:T(8,128)}) custom-call(s32[12]{0:T(128)} %concatenate.89.ids, bf16[1024,384]{1,0:T(8,128)(2,1)} %get-tuple-element.102.refs_0_, ...), custom_call_target="tpu_custom_call" | custom-call | flops 17179869184 | bytes 8388608 | tf_op jit(solution)/shard_map/attend/pallas_call | solution.py:302
  131.8 5.8 collective-permute-start.10
  142.2 4.1 collective-permute-done.11.refs_2_
  146.3 9.3 %collective-permute-done.12.refs_3_ = bf16[1024,128]{1,0:T(8,128)(2,1)S(1)} collective-permute-done((bf16[1024,128]{1,0:T(8,128)(2,1)}, bf16[1024,128]{1,0:T(8,128)(2,1)S(1)}, u32[]{:S(2)}, u32[]{:S(2)}) %collective-permute-start.12) | collective-permute-done | bytes 262176 | tf_op jit(solution)/shard_map/ppermute | solution.py:38
  156.6 5.0 shard_map.297
  168.2 3.3 collective-permute-done.16
  178.1 7.0 collective-permute-done.18
  185.1 11.2 %collective-permute-done.17 = bf16[128,2048]{1,0:T(8,128)(2,1)} collective-permute-done((bf16[128,2048]{1,0:T(8,128)(2,1)}, bf16[128,2048]{1,0:T(8,128)(2,1)}, u32[]{:S(2)}, u32[]{:S(2)}) %collective-permute-start.17) | collective-permute-done | bytes 524320 | tf_op jit(solution)/shard_map/ppermute | solution.py:38
  204.3 4.6 fusion.100
  208.9 4.7 multiply_convert_fusion.11
  217.9 4.6 collective-permute-done.19
  224.4 4.8 multiply_convert_fusion.9
  234.8 4.6 multiply_convert_fusion.7
  246.7 6.9 collective-permute-done.25
  253.6 22.4 %collective-permute-done.24 = bf16[128,2048]{1,0:T(8,128)(2,1)S(1)} collective-permute-done((bf16[128,2048]{1,0:T(8,128)(2,1)S(1)}, bf16[128,2048]{1,0:T(8,128)(2,1)S(1)}, u32[]{:S(2)}, u32[]{:S(2)}) %collective-permute-start.24) | collective-permute-done | bytes 524320 | tf_op jit(solution)/shard_map/ppermute | solution.py:38
  278.8 4.6 multiply_convert_fusion.5
  284.3 3.2 fusion.107
  287.4 6.3 convolution_convert_fusion.3
  293.8 5.0 convolution_convert_fusion.5
  304.5 9.1 %convolution_convert_fusion = bf16[1024,2048]{1,0:T(8,128)(2,1)S(1)} fusion(bf16[1408,2048]{1,0:T(8,128)(2,1)S(1)} %bitcast.83, bf16[256,1408]{1,0:T(8,128)(2,1)} %get-tuple-element.199, bf16[256,1408]{1,0:T(8,128)(2,1)} %get-tuple-element.198, bf16[256,1408]{1,0:T(8,128)(2,1)} %get-tuple-element.197, bf16[256,1408]{1,0:T(8,128)(2,1)} %get-tuple-element.196), kind=kOutput, calls=%fused_computation.6 | convolution fusion | flops 5919211520 | bytes 12845056 | tf_op jit(solution)/shard_map/dot_general | solution.py:33
  313.6 8.1 convolution_convert_fusion.1
  321.8 5.5 convolution_convert_fusion.6
  327.3 4.8 convolution_convert_fusion.2
  332.2 17.6 %collective-permute-done.26 = bf16[256,2048]{1,0:T(8,128)(2,1)S(1)} collective-permute-done((bf16[256,2048]{1,0:T(8,128)(2,1)S(1)}, bf16[256,2048]{1,0:T(8,128)(2,1)S(1)}, u32[]{:S(2)}, u32[]{:S(2)}) %collective-permute-start.26) | collective-permute-done | bytes 1048608 | tf_op jit(solution)/shard_map/ppermute | solution.py:38
  354.3 5.1 convolution_convert_fusion.4
  359.4 7.5 collective-permute-done.28
  368.5 9.7 %collective-permute-done.29 = bf16[128,2048]{1,0:T(8,128)(2,1)S(1)} collective-permute-done((bf16[128,2048]{1,0:T(8,128)(2,1)S(1)}, bf16[128,2048]{1,0:T(8,128)(2,1)S(1)}, u32[]{:S(2)}, u32[]{:S(2)}) %collective-permute-start.29) | collective-permute-done | bytes 524320 | tf_op jit(solution)/shard_map/ppermute | solution.py:38
  379.2 9.3 %collective-permute-done.32 = bf16[128,2048]{1,0:T(8,128)(2,1)S(1)} collective-permute-done((bf16[128,2048]{1,0:T(8,128)(2,1)S(1)}, bf16[128,2048]{1,0:T(8,128)(2,1)S(1)}, u32[]{:S(2)}, u32[]{:S(2)}) %collective-permute-start.32) | collective-permute-done | bytes 524320 | tf_op jit(solution)/shard_map/ppermute | solution.py:38
  393.8 14.5 %collective-permute-start.37 = (bf16[1024,128]{1,0:T(8,128)(2,1)S(1)}, bf16[1024,128]{1,0:T(8,128)(2,1)S(1)}, u32[]{:S(2)}, u32[]{:S(2)}) collective-permute-start(bf16[1024,128]{1,0:T(8,128)(2,1)S(1)} %get-tuple-element.128), channel_id=1, source_target_pairs={{0,4},{4,0},{8,12},{12,8},{1,5},{5,1},{9,13},{13,9},{2,6},{6,2},{1... | collective-permute-start | bytes 786440 | tf_op jit(solution)/shard_map/ppermute | solution.py:38
  417.9 10.8 %collective-permute-done.38.refs_6_ = bf16[1024,128]{1,0:T(8,128)(2,1)S(1)} collective-permute-done((bf16[1024,128]{1,0:T(8,128)(2,1)S(1)}, bf16[1024,128]{1,0:T(8,128)(2,1)S(1)}, u32[]{:S(2)}, u32[]{:S(2)}) %collective-permute-start.38) | collective-permute-done | bytes 262176 | tf_op jit(solution)/shard_map/ppermute | solution.py:38
  432.2 47.8 %attend_back.1 = (bf16[1024,384]{1,0:T(8,128)(2,1)}, bf16[1024,384]{1,0:T(8,128)(2,1)}, bf16[1024,384]{1,0:T(8,128)(2,1)}, bf16[1024,384]{1,0:T(8,128)(2,1)}) custom-call(s32[12]{0:T(128)} %concatenate.89.ids, bf16[1024,384]{1,0:T(8,128)(2,1)} %get-tuple-element.102.refs_0_, bf16[1024,384]{1,0:T(8,128)(2,1)} %copy-done.48, bf16[1024,384]{1,0:T(8,128)(2,1)} %copy-done.47, ...), custom_call_target="tpu_custom_call" | custom-call | flops 42949672960 | bytes 8388608 | tf_op jit(solution)/shard_map/attend_back/pallas_call | solution.py:441
  483.0 3.0 add_convert_fusion.7
  486.0 6.6 collective-permute-start.40
  492.7 3.0 add_convert_fusion.4
  499.7 3.0 add_convert_fusion
  506.1 19.6 %collective-permute-done.40.refs_1_ = bf16[1024,384]{1,0:T(8,128)(2,1)S(1)} collective-permute-done((bf16[1024,384]{1,0:T(8,128)(2,1)S(1)}, bf16[1024,384]{1,0:T(8,128)(2,1)S(1)}, u32[]{:S(2)}, u32[]{:S(2)}) %collective-permute-start.40) | collective-permute-done | bytes 786464 | tf_op jit(solution)/shard_map/ppermute | solution.py:38
  525.7 25.1 %collective-permute-done.41.refs_2_ = bf16[1024,384]{1,0:T(8,128)(2,1)S(1)} collective-permute-done((bf16[1024,384]{1,0:T(8,128)(2,1)S(1)}, bf16[1024,384]{1,0:T(8,128)(2,1)S(1)}, u32[]{:S(2)}, u32[]{:S(2)}) %collective-permute-start.41) | collective-permute-done | bytes 786464 | tf_op jit(solution)/shard_map/ppermute | solution.py:38
  551.3 15.8 %collective-permute-start.66 = (bf16[512,256]{1,0:T(8,128)(2,1)S(1)}, bf16[512,256]{1,0:T(8,128)(2,1)S(1)}, u32[]{:S(2)}, u32[]{:S(2)}) collective-permute-start(bf16[512,256]{1,0:T(8,128)(2,1)S(1)} %get-tuple-element.200), channel_id=1, source_target_pairs={{0,4},{4,0},{8,12},{12,8},{1,5},{5,1},{9,13},{13,9},{2,6},{6,2},{1... | collective-permute-start | bytes 786440 | tf_op jit(solution)/shard_map/ppermute | solution.py:38
  567.2 13.3 %shard_map.298 = (bf16[1024,512]{1,0:T(8,128)(2,1)S(1)}, bf16[1024,512]{1,0:T(8,128)(2,1)S(1)}, bf16[1024,512]{1,0:T(8,128)(2,1)S(1)}, f32[256,2048]{1,0:T(8,128...) custom-call(s32[12]{0:T(128)S(1)} %copy-done.2, ...), custom_call_target="tpu_custom_call" | custom-call | flops 6442450944 | bytes 18874368 | tf_op jit(solution)/shard_map/pallas_call | solution.py:506
  580.5 3.0 fusion.35
  590.7 6.0 collective-permute-done.67
  605.6 4.1 collective-permute-start.68
  612.2 7.3 collective-permute-done.68
  623.7 20.5 %collective-permute-done.44 = bf16[256,2048]{1,0:T(8,128)(2,1)S(1)} collective-permute-done((bf16[256,2048]{1,0:T(8,128)(2,1)S(1)}, bf16[256,2048]{1,0:T(8,128)(2,1)S(1)}, u32[]{:S(2)}, u32[]{:S(2)}) %collective-permute-start.44) | collective-permute-done | bytes 1048608 | tf_op jit(solution)/shard_map/ppermute | solution.py:38
  657.1 3.5 collective-permute-start.51
  672.0 61.3 %collective-permute-done.72 = bf16[256,1408]{1,0:T(8,128)(2,1)} collective-permute-done((bf16[256,1408]{1,0:T(8,128)(2,1)}, bf16[256,1408]{1,0:T(8,128)(2,1)}, u32[]{:S(2)}, u32[]{:S(2)}) %collective-permute-start.72) | collective-permute-done | bytes 720928 | tf_op jit(solution)/shard_map/ppermute | solution.py:38
  733.4 3.2 convert_add_fusion.4
  738.6 10.3 %collective-permute-done.76 = bf16[256,1408]{1,0:T(8,128)(2,1)} collective-permute-done((bf16[256,1408]{1,0:T(8,128)(2,1)}, bf16[256,1408]{1,0:T(8,128)(2,1)}, u32[]{:S(2)}, u32[]{:S(2)}) %collective-permute-start.76) | collective-permute-done | bytes 720928 | tf_op jit(solution)/shard_map/ppermute | solution.py:38
  748.9 3.2 convert_add_fusion.3
  754.2 7.9 collective-permute-done.80
  767.6 11.1 %collective-permute-done.59 = bf16[256,512]{1,0:T(8,128)(2,1)S(1)} collective-permute-done((bf16[256,512]{1,0:T(8,128)(2,1)S(1)}, bf16[256,512]{1,0:T(8,128)(2,1)S(1)}, u32[]{:S(2)}, u32[]{:S(2)}) %collective-permute-start.59) | collective-permute-done | bytes 262176 | tf_op jit(solution)/shard_map/ppermute | solution.py:38
  778.8 14.0 %collective-permute-done.63 = bf16[256,512]{1,0:T(8,128)(2,1)S(1)} collective-permute-done((bf16[256,512]{1,0:T(8,128)(2,1)S(1)}, bf16[256,512]{1,0:T(8,128)(2,1)S(1)}, u32[]{:S(2)}, u32[]{:S(2)}) %collective-permute-start.63) | collective-permute-done | bytes 262176 | tf_op jit(solution)/shard_map/ppermute | solution.py:38
  796.9 17.3 %collective-permute-done.60 = bf16[256,512]{1,0:T(8,128)(2,1)S(1)} collective-permute-done((bf16[256,512]{1,0:T(8,128)(2,1)S(1)}, bf16[256,512]{1,0:T(8,128)(2,1)S(1)}, u32[]{:S(2)}, u32[]{:S(2)}) %collective-permute-start.60) | collective-permute-done | bytes 262176 | tf_op jit(solution)/shard_map/ppermute | solution.py:38
  815.1 3.3 collective-permute-done.64
  (432 shorter events, 181.9 us)
Async XLA Ops:
  0.6 13.1 %collective-permute-start = (bf16[1024,512]{1,0:T(8,128)(2,1)}, bf16[1024,512]{1,0:T(8,128)(2,1)S(1)}, u32[]{:S(2)}, u32[]{:S(2)}) collective-permute-start(bf16[1024,512]{1,0:T(8,128)(2,1)} %refs_4_.2), channel_id=1, source_target_pairs={{0,16},{16,0},{1,17},{17,1},{2,18},{18,2},{3,19},{19,3},{4,20},{20... | collective-permute-start | bytes 3145736 | tf_op jit(solution)/shard_map/ppermute | solution.py:38
  1.2 12.5 %collective-permute-start.1 = (bf16[1024,512]{1,0:T(8,128)(2,1)}, bf16[1024,512]{1,0:T(8,128)(2,1)S(1)}, u32[]{:S(2)}, u32[]{:S(2)}) collective-permute-start(bf16[1024,512]{1,0:T(8,128)(2,1)} %refs_5_.1), channel_id=1, source_target_pairs={{0,16},{16,0},{1,17},{17,1},{2,18},{18,2},{3,19},{19,3},{4,20},{20... | collective-permute-start | bytes 3145736 | tf_op jit(solution)/shard_map/ppermute | solution.py:38
  33.7 31.6 %collective-permute-start.6 = (bf16[1408,1024]{1,0:T(8,128)(2,1)S(1)}, bf16[1408,1024]{1,0:T(8,128)(2,1)S(1)}, u32[]{:S(2)}, u32[]{:S(2)}) collective-permute-start(bf16[1408,1024]{1,0:T(8,128)(2,1)S(1)} %copy-done.13), channel_id=1, source_target_pairs={{0,16},{16,0},{1,17},{17,1},{2,18},{18,2},{3,19},{19,3},{4,20},{20... | collective-permute-start | bytes 8650760 | tf_op jit(solution)/shard_map/ppermute | solution.py:38
  33.8 66.3 %collective-permute-start.4 = (bf16[1024,384]{1,0:T(8,128)(2,1)}, bf16[1024,384]{1,0:T(8,128)(2,1)S(1)}, u32[]{:S(2)}, u32[]{:S(2)}) collective-permute-start(bf16[1024,384]{1,0:T(8,128)(2,1)} %get-tuple-element.92), channel_id=1, source_target_pairs={{0,8},{4,12},{8,0},{12,4},{1,9},{5,13},{9,1},{13,5},{2,10},{6,14},... | collective-permute-start | bytes 2359304 | tf_op jit(solution)/shard_map/ppermute | solution.py:38
  37.6 26.0 %collective-permute-start.7 = (bf16[512,1024]{1,0:T(8,128)(2,1)S(1)}, bf16[512,1024]{1,0:T(8,128)(2,1)S(1)}, u32[]{:S(2)}, u32[]{:S(2)}) collective-permute-start(bf16[512,1024]{1,0:T(8,128)(2,1)S(1)} %copy-done), channel_id=1, source_target_pairs={{0,16},{16,0},{1,17},{17,1},{2,18},{18,2},{3,19},{19,3},{4,20},{20... | collective-permute-start | bytes 3145736 | tf_op jit(solution)/shard_map/ppermute | solution.py:38
  47.6 52.5 %collective-permute-start.3 = (bf16[1024,384]{1,0:T(8,128)(2,1)S(1)}, bf16[1024,384]{1,0:T(8,128)(2,1)S(1)}, u32[]{:S(2)}, u32[]{:S(2)}) collective-permute-start(bf16[1024,384]{1,0:T(8,128)(2,1)S(1)} %copy-done.51), channel_id=1, source_target_pairs={{0,4},{4,0},{8,12},{12,8},{1,5},{5,1},{9,13},{13,9},{2,6},{6,2},{1... | collective-permute-start | bytes 2359304 | tf_op jit(solution)/shard_map/ppermute | solution.py:38
  49.3 29.7 %collective-permute-start.8 = (bf16[1024,1408]{1,0:T(8,128)(2,1)S(1)}, bf16[1024,1408]{1,0:T(8,128)(2,1)}, u32[]{:S(2)}, u32[]{:S(2)}) collective-permute-start(bf16[1024,1408]{1,0:T(8,128)(2,1)S(1)} %copy-done.14), channel_id=1, source_target_pairs={{0,16},{16,0},{1,17},{17,1},{2,18},{18,2},{3,19},{19,3},{4,20},{20... | collective-permute-start | bytes 8650760 | tf_op jit(solution)/shard_map/ppermute | solution.py:38
  63.7 36.4 %collective-permute-start.5 = (bf16[1024,384]{1,0:T(8,128)(2,1)S(1)}, bf16[1024,384]{1,0:T(8,128)(2,1)S(1)}, u32[]{:S(2)}, u32[]{:S(2)}) collective-permute-start(bf16[1024,384]{1,0:T(8,128)(2,1)S(1)} %copy-done.50), channel_id=1, source_target_pairs={{0,12},{4,8},{8,4},{12,0},{1,13},{5,9},{9,5},{13,1},{2,14},{6,10},... | collective-permute-start | bytes 2359304 | tf_op jit(solution)/shard_map/ppermute | solution.py:38
  66.2 17.4 %collective-permute-start.9 = (bf16[1024,1408]{1,0:T(8,128)(2,1)S(1)}, bf16[1024,1408]{1,0:T(8,128)(2,1)S(1)}, u32[]{:S(2)}, u32[]{:S(2)}) collective-permute-start(bf16[1024,1408]{1,0:T(8,128)(2,1)S(1)} %copy-done.15), channel_id=1, source_target_pairs={{0,16},{16,0},{1,17},{17,1},{2,18},{18,2},{3,19},{19,3},{4,20},{20... | collective-permute-start | bytes 8650760 | tf_op jit(solution)/shard_map/ppermute | solution.py:38
  139.6 16.0 %collective-permute-start.12 = (bf16[1024,128]{1,0:T(8,128)(2,1)}, bf16[1024,128]{1,0:T(8,128)(2,1)S(1)}, u32[]{:S(2)}, u32[]{:S(2)}) collective-permute-start(bf16[1024,128]{1,0:T(8,128)(2,1)} %get-tuple-element.109), channel_id=1, source_target_pairs={{0,12},{4,8},{8,4},{12,0},{1,13},{5,9},{9,5},{13,1},{2,14},{6,10},... | collective-permute-start | bytes 786440 | tf_op jit(solution)/shard_map/ppermute | solution.py:38
  166.3 18.8 %collective-permute-start.18 = (bf16[128,2048]{1,0:T(8,128)(2,1)}, bf16[128,2048]{1,0:T(8,128)(2,1)}, u32[]{:S(2)}, u32[]{:S(2)}) collective-permute-start(bf16[128,2048]{1,0:T(8,128)(2,1)} %slice.192), channel_id=1, source_target_pairs={{0,2},{1,3},{2,0},{3,1},{4,6},{5,7},{6,4},{7,5},{8,10},{9,11},{10,... | collective-permute-start | bytes 1572872 | tf_op jit(solution)/shard_map/ppermute | solution.py:38
  167.6 17.5 %collective-permute-start.13 = (bf16[128,2048]{1,0:T(8,128)(2,1)}, bf16[128,2048]{1,0:T(8,128)(2,1)}, u32[]{:S(2)}, u32[]{:S(2)}) collective-permute-start(bf16[128,2048]{1,0:T(8,128)(2,1)} %slice.187), channel_id=1, source_target_pairs={{0,1},{1,0},{2,3},{3,2},{4,5},{5,4},{6,7},{7,6},{8,9},{9,8},{10,11... | collective-permute-start | bytes 1572872 | tf_op jit(solution)/shard_map/ppermute | solution.py:38
  172.4 24.0 %collective-permute-start.17 = (bf16[128,2048]{1,0:T(8,128)(2,1)}, bf16[128,2048]{1,0:T(8,128)(2,1)}, u32[]{:S(2)}, u32[]{:S(2)}) collective-permute-start(bf16[128,2048]{1,0:T(8,128)(2,1)} %add_convert_fusion.11), channel_id=1, source_target_pairs={{0,2},{1,3},{2,0},{3,1},{4,6},{5,7},{6,4},{7,5},{8,10},{9,11},{10,... | collective-permute-start | bytes 1572872 | tf_op jit(solution)/shard_map/ppermute | solution.py:38
  174.8 21.6 %collective-permute-start.15 = (bf16[128,2048]{1,0:T(8,128)(2,1)}, bf16[128,2048]{1,0:T(8,128)(2,1)}, u32[]{:S(2)}, u32[]{:S(2)}) collective-permute-start(bf16[128,2048]{1,0:T(8,128)(2,1)} %add_convert_fusion.12), channel_id=1, source_target_pairs={{0,1},{1,0},{2,3},{3,2},{4,5},{5,4},{6,7},{7,6},{8,9},{9,8},{10,11... | collective-permute-start | bytes 1572872 | tf_op jit(solution)/shard_map/ppermute | solution.py:38
  200.2 17.7 %collective-permute-start.20 = (bf16[128,2048]{1,0:T(8,128)(2,1)S(1)}, bf16[128,2048]{1,0:T(8,128)(2,1)S(1)}, u32[]{:S(2)}, u32[]{:S(2)}) collective-permute-start(bf16[128,2048]{1,0:T(8,128)(2,1)S(1)} %get-tuple-element.220), channel_id=1, source_target_pairs={{0,1},{1,0},{2,3},{3,2},{4,5},{5,4},{6,7},{7,6},{8,9},{9,8},{10,11... | collective-permute-start | bytes 1572872 | tf_op jit(solution)/shard_map/ppermute | solution.py:38
  200.5 32.4 %collective-permute-start.22 = (bf16[128,2048]{1,0:T(8,128)(2,1)S(1)}, bf16[128,2048]{1,0:T(8,128)(2,1)S(1)}, u32[]{:S(2)}, u32[]{:S(2)}) collective-permute-start(bf16[128,2048]{1,0:T(8,128)(2,1)S(1)} %get-tuple-element.220), channel_id=1, source_target_pairs={{0,2},{1,3},{2,0},{3,1},{4,6},{5,7},{6,4},{7,5},{8,10},{9,11},{10,... | collective-permute-start | bytes 1572872 | tf_op jit(solution)/shard_map/ppermute | solution.py:38
  202.1 20.4 %collective-permute-start.19 = (bf16[128,2048]{1,0:T(8,128)(2,1)S(1)}, bf16[128,2048]{1,0:T(8,128)(2,1)S(1)}, u32[]{:S(2)}, u32[]{:S(2)}) collective-permute-start(bf16[128,2048]{1,0:T(8,128)(2,1)S(1)} %get-tuple-element.219), channel_id=1, source_target_pairs={{0,1},{1,0},{2,3},{3,2},{4,5},{5,4},{6,7},{7,6},{8,9},{9,8},{10,11... | collective-permute-start | bytes 1572872 | tf_op jit(solution)/shard_map/ppermute | solution.py:38
  203.8 29.1 %collective-permute-start.21 = (bf16[128,2048]{1,0:T(8,128)(2,1)S(1)}, bf16[128,2048]{1,0:T(8,128)(2,1)S(1)}, u32[]{:S(2)}, u32[]{:S(2)}) collective-permute-start(bf16[128,2048]{1,0:T(8,128)(2,1)S(1)} %get-tuple-element.219), channel_id=1, source_target_pairs={{0,2},{1,3},{2,0},{3,1},{4,6},{5,7},{6,4},{7,5},{8,10},{9,11},{10,... | collective-permute-start | bytes 1572872 | tf_op jit(solution)/shard_map/ppermute | solution.py:38
  241.3 90.9 %collective-permute-start.23 = (bf16[256,2048]{1,0:T(8,128)(2,1)S(1)}, bf16[256,2048]{1,0:T(8,128)(2,1)S(1)}, u32[]{:S(2)}, u32[]{:S(2)}) collective-permute-start(bf16[256,2048]{1,0:T(8,128)(2,1)S(1)} %fusion), channel_id=1, source_target_pairs={{0,1},{1,0},{2,3},{3,2},{4,5},{5,4},{6,7},{7,6},{8,9},{9,8},{10,11... | collective-permute-start | bytes 3145736 | tf_op jit(solution)/shard_map/ppermute | solution.py:38
  243.0 33.0 %collective-permute-start.24 = (bf16[128,2048]{1,0:T(8,128)(2,1)S(1)}, bf16[128,2048]{1,0:T(8,128)(2,1)S(1)}, u32[]{:S(2)}, u32[]{:S(2)}) collective-permute-start(bf16[128,2048]{1,0:T(8,128)(2,1)S(1)} %collective-permute-done.21), channel_id=1, source_target_pairs={{0,1},{1,0},{2,3},{3,2},{4,5},{5,4},{6,7},{7,6},{8,9},{9,8},{10,11... | collective-permute-start | bytes 1572872 | tf_op jit(solution)/shard_map/ppermute | solution.py:38
  300.6 31.6 %collective-permute-start.27 = (bf16[256,2048]{1,0:T(8,128)(2,1)S(1)}, bf16[256,2048]{1,0:T(8,128)(2,1)S(1)}, u32[]{:S(2)}, u32[]{:S(2)}) collective-permute-start(bf16[256,2048]{1,0:T(8,128)(2,1)S(1)} %fusion.2), channel_id=1, source_target_pairs={{0,3},{1,2},{2,1},{3,0},{4,7},{5,6},{6,5},{7,4},{8,11},{9,10},{10,... | collective-permute-start | bytes 3145736 | tf_op jit(solution)/shard_map/ppermute | solution.py:38
  301.4 48.3 %collective-permute-start.26 = (bf16[256,2048]{1,0:T(8,128)(2,1)S(1)}, bf16[256,2048]{1,0:T(8,128)(2,1)S(1)}, u32[]{:S(2)}, u32[]{:S(2)}) collective-permute-start(bf16[256,2048]{1,0:T(8,128)(2,1)S(1)} %fusion.1), channel_id=1, source_target_pairs={{0,2},{1,3},{2,0},{3,1},{4,6},{5,7},{6,4},{7,5},{8,10},{9,11},{10,... | collective-permute-start | bytes 3145736 | tf_op jit(solution)/shard_map/ppermute | solution.py:38
  302.3 128.9 %collective-permute-start.69 = (bf16[1024,1408]{1,0:T(8,128)(2,1)}, bf16[1024,1408]{1,0:T(8,128)(2,1)}, u32[]{:S(2)}, u32[]{:S(2)}) collective-permute-start(bf16[1024,1408]{1,0:T(8,128)(2,1)} %convolution_convert_fusion.5), channel_id=1, source_target_pairs={{0,16},{16,0},{1,17},{17,1},{2,18},{18,2},{3,19},{19,3},{4,20},{20... | collective-permute-start | bytes 8650760 | tf_op jit(solution)/shard_map/ppermute | solution.py:38
  304.4 178.5 %collective-permute-start.73 = (bf16[1024,1408]{1,0:T(8,128)(2,1)}, bf16[1024,1408]{1,0:T(8,128)(2,1)}, u32[]{:S(2)}, u32[]{:S(2)}) collective-permute-start(bf16[1024,1408]{1,0:T(8,128)(2,1)} %convolution_convert_fusion.3), channel_id=1, source_target_pairs={{0,16},{16,0},{1,17},{17,1},{2,18},{18,2},{3,19},{19,3},{4,20},{20... | collective-permute-start | bytes 8650760 | tf_op jit(solution)/shard_map/ppermute | solution.py:38
  352.1 14.9 %collective-permute-start.28 = (bf16[128,2048]{1,0:T(8,128)(2,1)S(1)}, bf16[128,2048]{1,0:T(8,128)(2,1)S(1)}, u32[]{:S(2)}, u32[]{:S(2)}) collective-permute-start(bf16[128,2048]{1,0:T(8,128)(2,1)S(1)} %get-tuple-element.218), channel_id=1, source_target_pairs={{0,1},{1,0},{2,3},{3,2},{4,5},{5,4},{6,7},{7,6},{8,9},{9,8},{10,11... | collective-permute-start | bytes 1572872 | tf_op jit(solution)/shard_map/ppermute | solution.py:38
  352.4 14.6 %collective-permute-start.30 = (bf16[128,2048]{1,0:T(8,128)(2,1)S(1)}, bf16[128,2048]{1,0:T(8,128)(2,1)S(1)}, u32[]{:S(2)}, u32[]{:S(2)}) collective-permute-start(bf16[128,2048]{1,0:T(8,128)(2,1)S(1)} %get-tuple-element.218), channel_id=1, source_target_pairs={{0,2},{1,3},{2,0},{3,1},{4,6},{5,7},{6,4},{7,5},{8,10},{9,11},{10,... | collective-permute-start | bytes 1572872 | tf_op jit(solution)/shard_map/ppermute | solution.py:38
  353.7 24.5 %collective-permute-start.29 = (bf16[128,2048]{1,0:T(8,128)(2,1)S(1)}, bf16[128,2048]{1,0:T(8,128)(2,1)S(1)}, u32[]{:S(2)}, u32[]{:S(2)}) collective-permute-start(bf16[128,2048]{1,0:T(8,128)(2,1)S(1)} %get-tuple-element.217), channel_id=1, source_target_pairs={{0,1},{1,0},{2,3},{3,2},{4,5},{5,4},{6,7},{7,6},{8,9},{9,8},{10,11... | collective-permute-start | bytes 1572872 | tf_op jit(solution)/shard_map/ppermute | solution.py:38
  367.1 21.5 %collective-permute-start.32 = (bf16[128,2048]{1,0:T(8,128)(2,1)S(1)}, bf16[128,2048]{1,0:T(8,128)(2,1)S(1)}, u32[]{:S(2)}, u32[]{:S(2)}) collective-permute-start(bf16[128,2048]{1,0:T(8,128)(2,1)S(1)} %collective-permute-done.30), channel_id=1, source_target_pairs={{0,1},{1,0},{2,3},{3,2},{4,5},{5,4},{6,7},{7,6},{8,9},{9,8},{10,11... | collective-permute-start | bytes 1572872 | tf_op jit(solution)/shard_map/ppermute | solution.py:38
  393.8 24.1 %collective-permute-start.37 = (bf16[1024,128]{1,0:T(8,128)(2,1)S(1)}, bf16[1024,128]{1,0:T(8,128)(2,1)S(1)}, u32[]{:S(2)}, u32[]{:S(2)}) collective-permute-start(bf16[1024,128]{1,0:T(8,128)(2,1)S(1)} %get-tuple-element.128), channel_id=1, source_target_pairs={{0,4},{4,0},{8,12},{12,8},{1,5},{5,1},{9,13},{13,9},{2,6},{6,2},{1... | collective-permute-start | bytes 786440 | tf_op jit(solution)/shard_map/ppermute | solution.py:38
  408.3 20.4 %collective-permute-start.38 = (bf16[1024,128]{1,0:T(8,128)(2,1)S(1)}, bf16[1024,128]{1,0:T(8,128)(2,1)S(1)}, u32[]{:S(2)}, u32[]{:S(2)}) collective-permute-start(bf16[1024,128]{1,0:T(8,128)(2,1)S(1)} %get-tuple-element.129), channel_id=1, source_target_pairs={{0,8},{4,12},{8,0},{12,4},{1,9},{5,13},{9,1},{13,5},{2,10},{6,14},... | collective-permute-start | bytes 786440 | tf_op jit(solution)/shard_map/ppermute | solution.py:38
  410.1 19.9 %collective-permute-start.39 = (bf16[1024,128]{1,0:T(8,128)(2,1)S(1)}, bf16[1024,128]{1,0:T(8,128)(2,1)S(1)}, u32[]{:S(2)}, u32[]{:S(2)}) collective-permute-start(bf16[1024,128]{1,0:T(8,128)(2,1)S(1)} %get-tuple-element.130), channel_id=1, source_target_pairs={{0,12},{4,8},{8,4},{12,0},{1,13},{5,9},{9,5},{13,1},{2,14},{6,10},... | collective-permute-start | bytes 786440 | tf_op jit(solution)/shard_map/ppermute | solution.py:38
  417.9 68.1 %collective-permute-start.77 = (bf16[1408,1024]{1,0:T(8,128)(2,1)}, bf16[1408,1024]{1,0:T(8,128)(2,1)}, u32[]{:S(2)}, u32[]{:S(2)}) collective-permute-start(bf16[1408,1024]{1,0:T(8,128)(2,1)} %convolution_convert_fusion.1), channel_id=1, source_target_pairs={{0,16},{16,0},{1,17},{17,1},{2,18},{18,2},{3,19},{19,3},{4,20},{20... | collective-permute-start | bytes 8650760 | tf_op jit(solution)/shard_map/ppermute | solution.py:38
  428.7 67.0 %collective-permute-start.36 = (bf16[256,2048]{1,0:T(8,128)(2,1)}, bf16[256,2048]{1,0:T(8,128)(2,1)}, u32[]{:S(2)}, u32[]{:S(2)}) collective-permute-start(bf16[256,2048]{1,0:T(8,128)(2,1)} %get-tuple-element.186), channel_id=1, source_target_pairs={{0,3},{1,2},{2,1},{3,0},{4,7},{5,6},{6,5},{7,4},{8,11},{9,10},{10,... | collective-permute-start | bytes 3145736 | tf_op jit(solution)/shard_map/ppermute | solution.py:38
  430.0 67.8 %collective-permute-start.35 = (bf16[256,2048]{1,0:T(8,128)(2,1)}, bf16[256,2048]{1,0:T(8,128)(2,1)}, u32[]{:S(2)}, u32[]{:S(2)}) collective-permute-start(bf16[256,2048]{1,0:T(8,128)(2,1)} %get-tuple-element.187), channel_id=1, source_target_pairs={{0,2},{1,3},{2,0},{3,1},{4,6},{5,7},{6,4},{7,5},{8,10},{9,11},{10,... | collective-permute-start | bytes 3145736 | tf_op jit(solution)/shard_map/ppermute | solution.py:38
  431.1 68.1 %collective-permute-start.34 = (bf16[256,2048]{1,0:T(8,128)(2,1)}, bf16[256,2048]{1,0:T(8,128)(2,1)}, u32[]{:S(2)}, u32[]{:S(2)}) collective-permute-start(bf16[256,2048]{1,0:T(8,128)(2,1)} %get-tuple-element.185), channel_id=1, source_target_pairs={{0,1},{1,0},{2,3},{3,2},{4,5},{5,4},{6,7},{7,6},{8,9},{9,8},{10,11... | collective-permute-start | bytes 3145736 | tf_op jit(solution)/shard_map/ppermute | solution.py:38
  483.0 19.8 %collective-permute-start.65 = (bf16[512,1024]{1,0:T(8,128)(2,1)S(1)}, bf16[512,1024]{1,0:T(8,128)(2,1)S(1)}, u32[]{:S(2)}, u32[]{:S(2)}) collective-permute-start(bf16[512,1024]{1,0:T(8,128)(2,1)S(1)} %copy-done.46), channel_id=1, source_target_pairs={{0,16},{16,0},{1,17},{17,1},{2,18},{18,2},{3,19},{19,3},{4,20},{20... | collective-permute-start | bytes 3145736 | tf_op jit(solution)/shard_map/ppermute | solution.py:38
  486.0 39.6 %collective-permute-start.40 = (bf16[1024,384]{1,0:T(8,128)(2,1)S(1)}, bf16[1024,384]{1,0:T(8,128)(2,1)S(1)}, u32[]{:S(2)}, u32[]{:S(2)}) collective-permute-start(bf16[1024,384]{1,0:T(8,128)(2,1)S(1)} %copy-done.54), channel_id=1, source_target_pairs={{0,4},{4,0},{8,12},{12,8},{1,5},{5,1},{9,13},{13,9},{2,6},{6,2},{1... | collective-permute-start | bytes 2359304 | tf_op jit(solution)/shard_map/ppermute | solution.py:38
  495.7 55.1 %collective-permute-start.41 = (bf16[1024,384]{1,0:T(8,128)(2,1)S(1)}, bf16[1024,384]{1,0:T(8,128)(2,1)S(1)}, u32[]{:S(2)}, u32[]{:S(2)}) collective-permute-start(bf16[1024,384]{1,0:T(8,128)(2,1)S(1)} %copy-done.53), channel_id=1, source_target_pairs={{0,8},{4,12},{8,0},{12,4},{1,9},{5,13},{9,1},{13,5},{2,10},{6,14},... | collective-permute-start | bytes 2359304 | tf_op jit(solution)/shard_map/ppermute | solution.py:38
  497.8 53.6 %collective-permute-start.42 = (bf16[1024,384]{1,0:T(8,128)(2,1)S(1)}, bf16[1024,384]{1,0:T(8,128)(2,1)S(1)}, u32[]{:S(2)}, u32[]{:S(2)}) collective-permute-start(bf16[1024,384]{1,0:T(8,128)(2,1)S(1)} %copy-done.52), channel_id=1, source_target_pairs={{0,12},{4,8},{8,4},{12,0},{1,13},{5,9},{9,5},{13,1},{2,14},{6,10},... | collective-permute-start | bytes 2359304 | tf_op jit(solution)/shard_map/ppermute | solution.py:38
  499.2 99.2 %collective-permute-start.71 = (bf16[256,1408]{1,0:T(8,128)(2,1)}, bf16[256,1408]{1,0:T(8,128)(2,1)}, u32[]{:S(2)}, u32[]{:S(2)}) collective-permute-start(bf16[256,1408]{1,0:T(8,128)(2,1)} %get-tuple-element.184), channel_id=1, source_target_pairs={{0,4},{4,0},{8,12},{12,8},{1,5},{5,1},{9,13},{13,9},{2,6},{6,2},{1... | collective-permute-start | bytes 2162696 | tf_op jit(solution)/shard_map/ppermute | solution.py:38
  502.8 98.7 %collective-permute-start.75 = (bf16[256,1408]{1,0:T(8,128)(2,1)}, bf16[256,1408]{1,0:T(8,128)(2,1)}, u32[]{:S(2)}, u32[]{:S(2)}) collective-permute-start(bf16[256,1408]{1,0:T(8,128)(2,1)} %get-tuple-element.182), channel_id=1, source_target_pairs={{0,4},{4,0},{8,12},{12,8},{1,5},{5,1},{9,13},{13,9},{2,6},{6,2},{1... | collective-permute-start | bytes 2162696 | tf_op jit(solution)/shard_map/ppermute | solution.py:38
  525.7 79.9 %collective-permute-start.79 = (bf16[1408,256]{1,0:T(8,128)(2,1)}, bf16[1408,256]{1,0:T(8,128)(2,1)}, u32[]{:S(2)}, u32[]{:S(2)}) collective-permute-start(bf16[1408,256]{1,0:T(8,128)(2,1)} %get-tuple-element.180), channel_id=1, source_target_pairs={{0,4},{4,0},{8,12},{12,8},{1,5},{5,1},{9,13},{13,9},{2,6},{6,2},{1... | collective-permute-start | bytes 2162696 | tf_op jit(solution)/shard_map/ppermute | solution.py:38
  550.8 46.0 %collective-permute-start.67 = (bf16[512,256]{1,0:T(8,128)(2,1)S(1)}, bf16[512,256]{1,0:T(8,128)(2,1)S(1)}, u32[]{:S(2)}, u32[]{:S(2)}) collective-permute-start(bf16[512,256]{1,0:T(8,128)(2,1)S(1)} %get-tuple-element.201), channel_id=1, source_target_pairs={{0,4},{4,0},{8,12},{12,8},{1,5},{5,1},{9,13},{13,9},{2,6},{6,2},{1... | collective-permute-start | bytes 786440 | tf_op jit(solution)/shard_map/ppermute | solution.py:38
  551.3 60.9 %collective-permute-start.66 = (bf16[512,256]{1,0:T(8,128)(2,1)S(1)}, bf16[512,256]{1,0:T(8,128)(2,1)S(1)}, u32[]{:S(2)}, u32[]{:S(2)}) collective-permute-start(bf16[512,256]{1,0:T(8,128)(2,1)S(1)} %get-tuple-element.200), channel_id=1, source_target_pairs={{0,4},{4,0},{8,12},{12,8},{1,5},{5,1},{9,13},{13,9},{2,6},{6,2},{1... | collective-permute-start | bytes 786440 | tf_op jit(solution)/shard_map/ppermute | solution.py:38
  596.7 27.0 %collective-permute-start.45 = (bf16[256,2048]{1,0:T(8,128)(2,1)S(1)}, bf16[256,2048]{1,0:T(8,128)(2,1)S(1)}, u32[]{:S(2)}, u32[]{:S(2)}) collective-permute-start(bf16[256,2048]{1,0:T(8,128)(2,1)S(1)} %get-tuple-element.149), channel_id=1, source_target_pairs={{0,3},{1,2},{2,1},{3,0},{4,7},{5,6},{6,5},{7,4},{8,11},{9,10},{10,... | collective-permute-start | bytes 3145736 | tf_op jit(solution)/shard_map/ppermute | solution.py:38
  598.4 45.8 %collective-permute-start.44 = (bf16[256,2048]{1,0:T(8,128)(2,1)S(1)}, bf16[256,2048]{1,0:T(8,128)(2,1)S(1)}, u32[]{:S(2)}, u32[]{:S(2)}) collective-permute-start(bf16[256,2048]{1,0:T(8,128)(2,1)S(1)} %get-tuple-element.148), channel_id=1, source_target_pairs={{0,2},{1,3},{2,0},{3,1},{4,6},{5,7},{6,4},{7,5},{8,10},{9,11},{10,... | collective-permute-start | bytes 3145736 | tf_op jit(solution)/shard_map/ppermute | solution.py:38
  601.5 42.8 %collective-permute-start.43 = (bf16[256,2048]{1,0:T(8,128)(2,1)S(1)}, bf16[256,2048]{1,0:T(8,128)(2,1)S(1)}, u32[]{:S(2)}, u32[]{:S(2)}) collective-permute-start(bf16[256,2048]{1,0:T(8,128)(2,1)S(1)} %get-tuple-element.147), channel_id=1, source_target_pairs={{0,1},{1,0},{2,3},{3,2},{4,5},{5,4},{6,7},{7,6},{8,9},{9,8},{10,11... | collective-permute-start | bytes 3145736 | tf_op jit(solution)/shard_map/ppermute | solution.py:38
  605.6 14.0 %collective-permute-start.68 = (bf16[512,256]{1,0:T(8,128)(2,1)S(1)}, bf16[512,256]{1,0:T(8,128)(2,1)S(1)}, u32[]{:S(2)}, u32[]{:S(2)}) collective-permute-start(bf16[512,256]{1,0:T(8,128)(2,1)S(1)} %add_convert_fusion.13), channel_id=1, source_target_pairs={{0,8},{4,12},{8,0},{12,4},{1,9},{5,13},{9,1},{13,5},{2,10},{6,14},... | collective-permute-start | bytes 786440 | tf_op jit(solution)/shard_map/ppermute | solution.py:38
  612.2 59.4 %collective-permute-start.70 = (bf16[256,1408]{1,0:T(8,128)(2,1)}, bf16[256,1408]{1,0:T(8,128)(2,1)}, u32[]{:S(2)}, u32[]{:S(2)}) collective-permute-start(bf16[256,1408]{1,0:T(8,128)(2,1)} %get-tuple-element.183), channel_id=1, source_target_pairs={{0,4},{4,0},{8,12},{12,8},{1,5},{5,1},{9,13},{13,9},{2,6},{6,2},{1... | collective-permute-start | bytes 2162696 | tf_op jit(solution)/shard_map/ppermute | solution.py:38
  619.6 117.0 %collective-permute-start.74 = (bf16[256,1408]{1,0:T(8,128)(2,1)}, bf16[256,1408]{1,0:T(8,128)(2,1)}, u32[]{:S(2)}, u32[]{:S(2)}) collective-permute-start(bf16[256,1408]{1,0:T(8,128)(2,1)} %get-tuple-element.181), channel_id=1, source_target_pairs={{0,4},{4,0},{8,12},{12,8},{1,5},{5,1},{9,13},{13,9},{2,6},{6,2},{1... | collective-permute-start | bytes 2162696 | tf_op jit(solution)/shard_map/ppermute | solution.py:38
  623.7 26.9 %collective-permute-start.53 = (bf16[1024,512]{1,0:T(8,128)(2,1)S(1)}, bf16[1024,512]{1,0:T(8,128)(2,1)S(1)}, u32[]{:S(2)}, u32[]{:S(2)}) collective-permute-start(bf16[1024,512]{1,0:T(8,128)(2,1)S(1)} %fusion.35), channel_id=1, source_target_pairs={{0,16},{16,0},{1,17},{17,1},{2,18},{18,2},{3,19},{19,3},{4,20},{20... | collective-permute-start | bytes 3145736 | tf_op jit(solution)/shard_map/ppermute | solution.py:38
  663.4 88.8 %collective-permute-start.78 = (bf16[1408,256]{1,0:T(8,128)(2,1)}, bf16[1408,256]{1,0:T(8,128)(2,1)}, u32[]{:S(2)}, u32[]{:S(2)}) collective-permute-start(bf16[1408,256]{1,0:T(8,128)(2,1)} %get-tuple-element.179), channel_id=1, source_target_pairs={{0,4},{4,0},{8,12},{12,8},{1,5},{5,1},{9,13},{13,9},{2,6},{6,2},{1... | collective-permute-start | bytes 2162696 | tf_op jit(solution)/shard_map/ppermute | solution.py:38
  666.8 66.6 %collective-permute-start.72 = (bf16[256,1408]{1,0:T(8,128)(2,1)}, bf16[256,1408]{1,0:T(8,128)(2,1)}, u32[]{:S(2)}, u32[]{:S(2)}) collective-permute-start(bf16[256,1408]{1,0:T(8,128)(2,1)} %add_convert_fusion.8), channel_id=1, source_target_pairs={{0,8},{4,12},{8,0},{12,4},{1,9},{5,13},{9,1},{13,5},{2,10},{6,14},... | collective-permute-start | bytes 2162696 | tf_op jit(solution)/shard_map/ppermute | solution.py:38
  667.1 81.8 %collective-permute-start.76 = (bf16[256,1408]{1,0:T(8,128)(2,1)}, bf16[256,1408]{1,0:T(8,128)(2,1)}, u32[]{:S(2)}, u32[]{:S(2)}) collective-permute-start(bf16[256,1408]{1,0:T(8,128)(2,1)} %add_convert_fusion.5), channel_id=1, source_target_pairs={{0,8},{4,12},{8,0},{12,4},{1,9},{5,13},{9,1},{13,5},{2,10},{6,14},... | collective-permute-start | bytes 2162696 | tf_op jit(solution)/shard_map/ppermute | solution.py:38
  671.7 90.4 %collective-permute-start.80 = (bf16[1408,256]{1,0:T(8,128)(2,1)}, bf16[1408,256]{1,0:T(8,128)(2,1)S(1)}, u32[]{:S(2)}, u32[]{:S(2)}) collective-permute-start(bf16[1408,256]{1,0:T(8,128)(2,1)} %add_convert_fusion.2), channel_id=1, source_target_pairs={{0,8},{4,12},{8,0},{12,4},{1,9},{5,13},{9,1},{13,5},{2,10},{6,14},... | collective-permute-start | bytes 2162696 | tf_op jit(solution)/shard_map/ppermute | solution.py:38
  733.4 34.1 %collective-permute-start.55 = (bf16[256,512]{1,0:T(8,128)(2,1)}, bf16[256,512]{1,0:T(8,128)(2,1)S(1)}, u32[]{:S(2)}, u32[]{:S(2)}) collective-permute-start(bf16[256,512]{1,0:T(8,128)(2,1)} %get-tuple-element.207), channel_id=1, source_target_pairs={{0,4},{4,0},{8,12},{12,8},{1,5},{5,1},{9,13},{13,9},{2,6},{6,2},{1... | collective-permute-start | bytes 786440 | tf_op jit(solution)/shard_map/ppermute | solution.py:38
  736.6 58.6 %collective-permute-start.54 = (bf16[256,512]{1,0:T(8,128)(2,1)S(1)}, bf16[256,512]{1,0:T(8,128)(2,1)S(1)}, u32[]{:S(2)}, u32[]{:S(2)}) collective-permute-start(bf16[256,512]{1,0:T(8,128)(2,1)S(1)} %get-tuple-element.206), channel_id=1, source_target_pairs={{0,4},{4,0},{8,12},{12,8},{1,5},{5,1},{9,13},{13,9},{2,6},{6,2},{1... | collective-permute-start | bytes 786440 | tf_op jit(solution)/shard_map/ppermute | solution.py:38
  748.9 29.8 %collective-permute-start.59 = (bf16[256,512]{1,0:T(8,128)(2,1)S(1)}, bf16[256,512]{1,0:T(8,128)(2,1)S(1)}, u32[]{:S(2)}, u32[]{:S(2)}) collective-permute-start(bf16[256,512]{1,0:T(8,128)(2,1)S(1)} %copy-done.34), channel_id=1, source_target_pairs={{0,4},{4,0},{8,12},{12,8},{1,5},{5,1},{9,13},{13,9},{2,6},{6,2},{1... | collective-permute-start | bytes 786440 | tf_op jit(solution)/shard_map/ppermute | solution.py:38
  752.2 44.7 %collective-permute-start.58 = (bf16[256,512]{1,0:T(8,128)(2,1)S(1)}, bf16[256,512]{1,0:T(8,128)(2,1)S(1)}, u32[]{:S(2)}, u32[]{:S(2)}) collective-permute-start(bf16[256,512]{1,0:T(8,128)(2,1)S(1)} %get-tuple-element.204), channel_id=1, source_target_pairs={{0,4},{4,0},{8,12},{12,8},{1,5},{5,1},{9,13},{13,9},{2,6},{6,2},{1... | collective-permute-start | bytes 786440 | tf_op jit(solution)/shard_map/ppermute | solution.py:38
  762.1 30.8 %collective-permute-start.63 = (bf16[256,512]{1,0:T(8,128)(2,1)S(1)}, bf16[256,512]{1,0:T(8,128)(2,1)S(1)}, u32[]{:S(2)}, u32[]{:S(2)}) collective-permute-start(bf16[256,512]{1,0:T(8,128)(2,1)S(1)} %copy-done.35), channel_id=1, source_target_pairs={{0,4},{4,0},{8,12},{12,8},{1,5},{5,1},{9,13},{13,9},{2,6},{6,2},{1... | collective-permute-start | bytes 786440 | tf_op jit(solution)/shard_map/ppermute | solution.py:38
  767.5 47.6 %collective-permute-start.62 = (bf16[256,512]{1,0:T(8,128)(2,1)S(1)}, bf16[256,512]{1,0:T(8,128)(2,1)S(1)}, u32[]{:S(2)}, u32[]{:S(2)}) collective-permute-start(bf16[256,512]{1,0:T(8,128)(2,1)S(1)} %copy-done.33), channel_id=1, source_target_pairs={{0,4},{4,0},{8,12},{12,8},{1,5},{5,1},{9,13},{13,9},{2,6},{6,2},{1... | collective-permute-start | bytes 786440 | tf_op jit(solution)/shard_map/ppermute | solution.py:38
  778.7 17.3 %collective-permute-start.56 = (bf16[256,512]{1,0:T(8,128)(2,1)S(1)}, bf16[256,512]{1,0:T(8,128)(2,1)S(1)}, u32[]{:S(2)}, u32[]{:S(2)}) collective-permute-start(bf16[256,512]{1,0:T(8,128)(2,1)S(1)} %add_convert_fusion.22), channel_id=1, source_target_pairs={{0,8},{4,12},{8,0},{12,4},{1,9},{5,13},{9,1},{13,5},{2,10},{6,14},... | collective-permute-start | bytes 786440 | tf_op jit(solution)/shard_map/ppermute | solution.py:38
  792.8 21.3 %collective-permute-start.60 = (bf16[256,512]{1,0:T(8,128)(2,1)S(1)}, bf16[256,512]{1,0:T(8,128)(2,1)S(1)}, u32[]{:S(2)}, u32[]{:S(2)}) collective-permute-start(bf16[256,512]{1,0:T(8,128)(2,1)S(1)} %add_convert_fusion.19), channel_id=1, source_target_pairs={{0,8},{4,12},{8,0},{12,4},{1,9},{5,13},{9,1},{13,5},{2,10},{6,14},... | collective-permute-start | bytes 786440 | tf_op jit(solution)/shard_map/ppermute | solution.py:38
  795.2 23.1 %collective-permute-start.64 = (bf16[256,512]{1,0:T(8,128)(2,1)S(1)}, bf16[256,512]{1,0:T(8,128)(2,1)S(1)}, u32[]{:S(2)}, u32[]{:S(2)}) collective-permute-start(bf16[256,512]{1,0:T(8,128)(2,1)S(1)} %add_convert_fusion.16), channel_id=1, source_target_pairs={{0,8},{4,12},{8,0},{12,4},{1,9},{5,13},{9,1},{13,5},{2,10},{6,14},... | collective-permute-start | bytes 786440 | tf_op jit(solution)/shard_map/ppermute | solution.py:38
  (106 other events, 1425.1 us)

commit v5 on v4

--- a/solution.py
+++ b/solution.py
@@ -122,7 +122,7 @@
         pieces[s][:, 2 * PAIR :] = vs[:, cols].astype(bf16)
 
 
-def project(ids, tokens, gain, shift, own, other, biases, tables, groups, slots):
+def project(ids, tokens, vectors, own, other, tables, groups, slots):
     rows, width = tokens.shape
     half = width // 2
     share = rows // slots
@@ -133,16 +133,19 @@
 
     whole = lambda i, ids: (0, 0)
     weight = pl.BlockSpec((half, inner), whole)
-    bias = pl.BlockSpec((1, inner), whole)
+    first_bias = 2 * width // inner
     in_specs = [
         pl.BlockSpec((share, half), lambda i, ids: (row_block(i, ids), ids[0])),
         pl.BlockSpec((share, half), lambda i, ids: (row_block(i, ids), 1 - ids[0])),
         pl.BlockSpec((1, half), lambda i, ids: (0, ids[0])),
         pl.BlockSpec((1, half), lambda i, ids: (0, 1 - ids[0])),
-        pl.BlockSpec((1, half), lambda i, ids: (0, ids[0])),
-        pl.BlockSpec((1, half), lambda i, ids: (0, 1 - ids[0])),
+        pl.BlockSpec((1, half), lambda i, ids: (0, 2 + ids[0])),
+        pl.BlockSpec((1, half), lambda i, ids: (0, 3 - ids[0])),
     ]
-    in_specs += [weight] * 6 + [bias] * 3
+    in_specs += [weight] * 6
+    in_specs += [
+        pl.BlockSpec((1, inner), lambda i, ids, j=j: (0, first_bias + j)) for j in range(3)
+    ]
     in_specs += [pl.BlockSpec((share, PAIR), lambda i, ids: (row_block(i, ids), 0))] * 2
     out = pl.pallas_call(
         functools.partial(project_kernel, groups),
@@ -163,7 +166,7 @@
             transcendentals=rows,
         ),
         name="project",
-    )(ids, tokens, tokens, gain, gain, shift, shift, *own, *other, *biases, *tables)
+    )(ids, tokens, tokens, *[vectors] * 4, *own, *other, *[vectors] * 3, *tables)
     return out[0], out[1:]
 
 
@@ -590,20 +593,13 @@
     )
     local_tables = rotary_tables(ctx * rows + jnp.arange(rows, dtype=jnp.int32))
     k_bias_wide = jnp.pad(
-        k_bias.astype(f32).reshape(heads_here, ROT), ((0, 0), (0, HEAD_DIM - ROT))
-    ).reshape(1, inner)
-    h1, send = project(
-        ids,
-        tokens[0],
-        ln1_gain.reshape(1, width),
-        ln1_shift.reshape(1, width),
-        own_qkv,
-        oth_qkv,
-        (q_bias.astype(f32).reshape(1, inner), k_bias_wide, v_bias.astype(f32).reshape(1, inner)),
-        local_tables,
-        groups,
-        slots,
-    )
+        k_bias.reshape(heads_here, ROT), ((0, 0), (0, HEAD_DIM - ROT))
+    ).reshape(inner)
+    assert 2 * width % inner == 0
+    vectors = jnp.concatenate(
+        [ln1_gain, ln1_shift, q_bias, k_bias_wide, v_bias], axis=0
+    ).astype(f32)[None]
+    h1, send = project(ids, tokens[0], vectors, own_qkv, oth_qkv, local_tables, groups, slots)
 
     (send, later) = hold(
         send,

time: 829 us -> 827 us (level)
  no operation moved by 1% of the time
where the time goes in v5:
time: 827 us; the launch traced here: 817 us
  waiting for transfers between devices  356 us (43%)
  matrix products  127 us (15%)
  starting transfers between devices  116 us (14%)
  Pallas kernels  112 us (14%)
  other arithmetic  79.6 us (10%)
  local copies, waits for them, and re-layouts  24.8 us (3%)
    ppermute x81, waiting for transfers between devices, swap_with(): return lax.ppermute(x, axis, [(i, i ^ bit) for i in range(size)])  356 us
    ppermute x81, starting transfers between devices, swap_with(): return lax.ppermute(x, axis, [(i, i ^ bit) for i in range(size)])  116 us
    dot_general x33, matrix products, dot(): return lax.dot_general(a, b, dims, preferred_element_type=f32)  115 us
    pallas_call x1, Pallas kernels, attend_back(): pl.pallas_call(functools.partial(attend_back_kernel, dims), grid_spec=plt...  47.8 us
    pallas_call x1, Pallas kernels, attend(): pl.pallas_call(functools.partial(attend_kernel, dims), grid_spec=pltpu.Pr...  29.7 us
    convert_element_type x14, other arithmetic, scatter_step(): parts.pop(d).astype(bf16)  20 us
    pallas_call x2, Pallas kernels, join(): pl.pallas_call(functools.partial(join_kernel, groups, kinds, slots, dims)...  18.3 us
  transfers between devices with their start and end apart: 81, of which 36 were waited for; matrix products, arithmetic and copies ran while one was open for 26% of the time, Pallas kernels for 7%

profile of v5, /device:TPU:0, one launch (start us, length us, event | category | flops | bytes accessed | tf_op | source)
XLA Modules:
  0.0 817.5 jit_solution(6543908182765977813)
XLA Ops:
  13.2 16.4 %project.1 = (bf16[1024,2048]{1,0:T(8,128)(2,1)}, bf16[1024,384]{1,0:T(8,128)(2,1)}, bf16[1024,384]{1,0:T(8,128)(2,1)}, bf16[1024,384]{1,0:T(8,128)(2,1)}, bf16[1024,384]{1,0:T(8,128)(2,1)}) custom-call(s32[12]{0:T(128)} %concatenate.109.ids, bf16[1024,2048]{1,0:T(8,128)(2,1)} %bitcast.82, bf16[1024,2048]{1,0:T(8,128)(2,1)} %bitcast.83, ...), custom_call_target="tpu_custom_call" | custom-call | flops 6442450944 | bytes 17825792 | tf_op jit(solution)/shard_map/project/pallas_call | solution.py:150
  31.6 3.8 collective-permute-start.4
  36.0 3.1 convolution_add_fusion.refs_10_
  40.6 4.8 fusion.56.refs_11_
  48.6 9.1 %maximum_select_fusion = bf16[1024,2048]{1,0:T(8,128)(2,1)S(1)} fusion(bf16[1024,1024]{1,0:T(8,128)(2,1)S(1)} %get-tuple-element.191, bf16[1024,1024]{1,0:T(8,128)(2,1)S(1)} %get-tuple-element.190, pred[]{:T(512)S(6)} %eq.20, bf16[256,2048]{1,0:T(8,128)(2,1)S(1)} %get-tuple-element.193, bf16[256,2048]{1,0:T(8,128)(2,1)S(1)} %get-tuple-element.194, ...), kind=kLoop, calls=%fused_computation.4 | loop fusion | flops 27262976 | bytes 12582913 | tf_op jit(solution)/shard_map/jit(_where)/select_n | solution.py:576
  57.7 3.8 fusion.54
  66.2 10.5 %fusion.99 = f32[1024,1408]{1,0:T(8,128)} fusion(bf16[1024,2048]{1,0:T(8,128)(2,1)S(1)} %maximum_select_fusion, bf16[1408,2048]{1,0:T(8,128)(2,1)} %constant_dynamic-update-slice_fusion.5), kind=kOutput, calls=%fused_computation.234 | convolution fusion | flops 5905580032 | bytes 15728640 | tf_op jit(solution)/shard_map/dot_general | solution.py:33
  76.7 4.7 pad_maximum_fusion
  81.4 3.0 pad_maximum_fusion.1
  84.4 13.4 %collective-permute-done.3.refs_1_ = bf16[1024,384]{1,0:T(8,128)(2,1)S(1)} collective-permute-done((bf16[1024,384]{1,0:T(8,128)(2,1)S(1)}, bf16[1024,384]{1,0:T(8,128)(2,1)S(1)}, u32[]{:S(2)}, u32[]{:S(2)}) %collective-permute-start.3) | collective-permute-done | bytes 786464 | tf_op jit(solution)/shard_map/ppermute | solution.py:38
  99.9 29.7 %attend.1 = (bf16[1024,128]{1,0:T(8,128)(2,1)}, bf16[1024,128]{1,0:T(8,128)(2,1)}, bf16[1024,128]{1,0:T(8,128)(2,1)}, bf16[1024,128]{1,0:T(8,128)(2,1)}, f32[128,4096]{1,0:T(8,128)}, /*index=5*/f32[8,4096]{1,0:T(8,128)}) custom-call(s32[12]{0:T(128)} %concatenate.109.ids, bf16[1024,384]{1,0:T(8,128)(2,1)} %get-tuple-element.102.refs_0_, ...), custom_call_target="tpu_custom_call" | custom-call | flops 17179869184 | bytes 8388608 | tf_op jit(solution)/shard_map/attend/pallas_call | solution.py:305
  129.6 5.8 collective-permute-start.10
  140.0 4.1 collective-permute-done.11.refs_2_
  144.1 9.3 %collective-permute-done.12.refs_3_ = bf16[1024,128]{1,0:T(8,128)(2,1)S(1)} collective-permute-done((bf16[1024,128]{1,0:T(8,128)(2,1)}, bf16[1024,128]{1,0:T(8,128)(2,1)S(1)}, u32[]{:S(2)}, u32[]{:S(2)}) %collective-permute-start.12) | collective-permute-done | bytes 262176 | tf_op jit(solution)/shard_map/ppermute | solution.py:38
  154.4 5.0 shard_map.297
  166.0 3.3 collective-permute-done.16
  175.9 7.1 collective-permute-done.18
  182.9 11.2 %collective-permute-done.17 = bf16[128,2048]{1,0:T(8,128)(2,1)} collective-permute-done((bf16[128,2048]{1,0:T(8,128)(2,1)}, bf16[128,2048]{1,0:T(8,128)(2,1)}, u32[]{:S(2)}, u32[]{:S(2)}) %collective-permute-start.17) | collective-permute-done | bytes 524320 | tf_op jit(solution)/shard_map/ppermute | solution.py:38
  202.1 4.6 fusion.100
  206.7 4.7 multiply_convert_fusion.11
  215.6 4.6 collective-permute-done.19
  222.1 4.8 multiply_convert_fusion.9
  232.6 4.6 multiply_convert_fusion.7
  244.5 6.9 collective-permute-done.25
  251.4 22.4 %collective-permute-done.24 = bf16[128,2048]{1,0:T(8,128)(2,1)S(1)} collective-permute-done((bf16[128,2048]{1,0:T(8,128)(2,1)S(1)}, bf16[128,2048]{1,0:T(8,128)(2,1)S(1)}, u32[]{:S(2)}, u32[]{:S(2)}) %collective-permute-start.24) | collective-permute-done | bytes 524320 | tf_op jit(solution)/shard_map/ppermute | solution.py:38
  276.5 4.6 multiply_convert_fusion.5
  282.0 3.2 fusion.107
  285.2 6.3 convolution_convert_fusion.3
  291.6 5.0 convolution_convert_fusion.5
  302.2 9.1 %convolution_convert_fusion = bf16[1024,2048]{1,0:T(8,128)(2,1)S(1)} fusion(bf16[1408,2048]{1,0:T(8,128)(2,1)S(1)} %bitcast.81, bf16[256,1408]{1,0:T(8,128)(2,1)} %get-tuple-element.199, bf16[256,1408]{1,0:T(8,128)(2,1)} %get-tuple-element.198, bf16[256,1408]{1,0:T(8,128)(2,1)} %get-tuple-element.197, bf16[256,1408]{1,0:T(8,128)(2,1)} %get-tuple-element.196), kind=kOutput, calls=%fused_computation.6 | convolution fusion | flops 5919211520 | bytes 12845056 | tf_op jit(solution)/shard_map/dot_general | solution.py:33
  311.4 8.1 convolution_convert_fusion.1
  319.5 5.5 convolution_convert_fusion.6
  325.0 4.8 convolution_convert_fusion.2
  329.9 17.7 %collective-permute-done.26 = bf16[256,2048]{1,0:T(8,128)(2,1)S(1)} collective-permute-done((bf16[256,2048]{1,0:T(8,128)(2,1)S(1)}, bf16[256,2048]{1,0:T(8,128)(2,1)S(1)}, u32[]{:S(2)}, u32[]{:S(2)}) %collective-permute-start.26) | collective-permute-done | bytes 1048608 | tf_op jit(solution)/shard_map/ppermute | solution.py:38
  352.0 5.1 convolution_convert_fusion.4
  357.2 7.6 collective-permute-done.28
  366.3 9.7 %collective-permute-done.29 = bf16[128,2048]{1,0:T(8,128)(2,1)S(1)} collective-permute-done((bf16[128,2048]{1,0:T(8,128)(2,1)S(1)}, bf16[128,2048]{1,0:T(8,128)(2,1)S(1)}, u32[]{:S(2)}, u32[]{:S(2)}) %collective-permute-start.29) | collective-permute-done | bytes 524320 | tf_op jit(solution)/shard_map/ppermute | solution.py:38
  377.1 9.3 %collective-permute-done.32 = bf16[128,2048]{1,0:T(8,128)(2,1)S(1)} collective-permute-done((bf16[128,2048]{1,0:T(8,128)(2,1)S(1)}, bf16[128,2048]{1,0:T(8,128)(2,1)S(1)}, u32[]{:S(2)}, u32[]{:S(2)}) %collective-permute-start.32) | collective-permute-done | bytes 524320 | tf_op jit(solution)/shard_map/ppermute | solution.py:38
  391.6 14.5 %collective-permute-start.37 = (bf16[1024,128]{1,0:T(8,128)(2,1)S(1)}, bf16[1024,128]{1,0:T(8,128)(2,1)S(1)}, u32[]{:S(2)}, u32[]{:S(2)}) collective-permute-start(bf16[1024,128]{1,0:T(8,128)(2,1)S(1)} %get-tuple-element.128), channel_id=1, source_target_pairs={{0,4},{4,0},{8,12},{12,8},{1,5},{5,1},{9,13},{13,9},{2,6},{6,2},{1... | collective-permute-start | bytes 786440 | tf_op jit(solution)/shard_map/ppermute | solution.py:38
  415.6 10.9 %collective-permute-done.38.refs_6_ = bf16[1024,128]{1,0:T(8,128)(2,1)S(1)} collective-permute-done((bf16[1024,128]{1,0:T(8,128)(2,1)S(1)}, bf16[1024,128]{1,0:T(8,128)(2,1)S(1)}, u32[]{:S(2)}, u32[]{:S(2)}) %collective-permute-start.38) | collective-permute-done | bytes 262176 | tf_op jit(solution)/shard_map/ppermute | solution.py:38
  430.0 47.8 %attend_back.1 = (bf16[1024,384]{1,0:T(8,128)(2,1)}, bf16[1024,384]{1,0:T(8,128)(2,1)}, bf16[1024,384]{1,0:T(8,128)(2,1)}, bf16[1024,384]{1,0:T(8,128)(2,1)}) custom-call(s32[12]{0:T(128)} %concatenate.109.ids, bf16[1024,384]{1,0:T(8,128)(2,1)} %get-tuple-element.102.refs_0_, bf16[1024,384]{1,0:T(8,128)(2,1)} %copy-done.48, bf16[1024,384]{1,0:T(8,128)(2,1)} %copy-done.47, ...), custom_call_target="tpu_custom_call" | custom-call | flops 42949672960 | bytes 8388608 | tf_op jit(solution)/shard_map/attend_back/pallas_call | solution.py:444
  480.8 3.0 add_convert_fusion.7
  483.8 6.6 collective-permute-start.40
  490.4 3.0 add_convert_fusion.4
  497.5 3.0 add_convert_fusion
  503.8 19.6 %collective-permute-done.40.refs_1_ = bf16[1024,384]{1,0:T(8,128)(2,1)S(1)} collective-permute-done((bf16[1024,384]{1,0:T(8,128)(2,1)S(1)}, bf16[1024,384]{1,0:T(8,128)(2,1)S(1)}, u32[]{:S(2)}, u32[]{:S(2)}) %collective-permute-start.40) | collective-permute-done | bytes 786464 | tf_op jit(solution)/shard_map/ppermute | solution.py:38
  523.4 25.1 %collective-permute-done.41.refs_2_ = bf16[1024,384]{1,0:T(8,128)(2,1)S(1)} collective-permute-done((bf16[1024,384]{1,0:T(8,128)(2,1)S(1)}, bf16[1024,384]{1,0:T(8,128)(2,1)S(1)}, u32[]{:S(2)}, u32[]{:S(2)}) %collective-permute-start.41) | collective-permute-done | bytes 786464 | tf_op jit(solution)/shard_map/ppermute | solution.py:38
  549.1 15.8 %collective-permute-start.66 = (bf16[512,256]{1,0:T(8,128)(2,1)S(1)}, bf16[512,256]{1,0:T(8,128)(2,1)S(1)}, u32[]{:S(2)}, u32[]{:S(2)}) collective-permute-start(bf16[512,256]{1,0:T(8,128)(2,1)S(1)} %get-tuple-element.200), channel_id=1, source_target_pairs={{0,4},{4,0},{8,12},{12,8},{1,5},{5,1},{9,13},{13,9},{2,6},{6,2},{1... | collective-permute-start | bytes 786440 | tf_op jit(solution)/shard_map/ppermute | solution.py:38
  564.9 13.3 %shard_map.298 = (bf16[1024,512]{1,0:T(8,128)(2,1)S(1)}, bf16[1024,512]{1,0:T(8,128)(2,1)S(1)}, bf16[1024,512]{1,0:T(8,128)(2,1)S(1)}, f32[256,2048]{1,0:T(8,128...) custom-call(s32[12]{0:T(128)S(1)} %copy-done.2, ...), custom_call_target="tpu_custom_call" | custom-call | flops 6442450944 | bytes 18874368 | tf_op jit(solution)/shard_map/pallas_call | solution.py:509
  578.3 3.0 fusion.35
  588.5 6.0 collective-permute-done.67
  603.4 4.1 collective-permute-start.68
  610.0 7.3 collective-permute-done.68
  621.5 20.5 %collective-permute-done.44 = bf16[256,2048]{1,0:T(8,128)(2,1)S(1)} collective-permute-done((bf16[256,2048]{1,0:T(8,128)(2,1)S(1)}, bf16[256,2048]{1,0:T(8,128)(2,1)S(1)}, u32[]{:S(2)}, u32[]{:S(2)}) %collective-permute-start.44) | collective-permute-done | bytes 1048608 | tf_op jit(solution)/shard_map/ppermute | solution.py:38
  654.9 3.5 collective-permute-start.51
  669.8 61.3 %collective-permute-done.72 = bf16[256,1408]{1,0:T(8,128)(2,1)} collective-permute-done((bf16[256,1408]{1,0:T(8,128)(2,1)}, bf16[256,1408]{1,0:T(8,128)(2,1)}, u32[]{:S(2)}, u32[]{:S(2)}) %collective-permute-start.72) | collective-permute-done | bytes 720928 | tf_op jit(solution)/shard_map/ppermute | solution.py:38
  731.1 3.2 convert_add_fusion.4
  736.3 10.3 %collective-permute-done.76 = bf16[256,1408]{1,0:T(8,128)(2,1)} collective-permute-done((bf16[256,1408]{1,0:T(8,128)(2,1)}, bf16[256,1408]{1,0:T(8,128)(2,1)}, u32[]{:S(2)}, u32[]{:S(2)}) %collective-permute-start.76) | collective-permute-done | bytes 720928 | tf_op jit(solution)/shard_map/ppermute | solution.py:38
  746.7 3.2 convert_add_fusion.3
  751.9 7.9 collective-permute-done.80
  765.3 11.1 %collective-permute-done.59 = bf16[256,512]{1,0:T(8,128)(2,1)S(1)} collective-permute-done((bf16[256,512]{1,0:T(8,128)(2,1)S(1)}, bf16[256,512]{1,0:T(8,128)(2,1)S(1)}, u32[]{:S(2)}, u32[]{:S(2)}) %collective-permute-start.59) | collective-permute-done | bytes 262176 | tf_op jit(solution)/shard_map/ppermute | solution.py:38
  776.6 14.0 %collective-permute-done.63 = bf16[256,512]{1,0:T(8,128)(2,1)S(1)} collective-permute-done((bf16[256,512]{1,0:T(8,128)(2,1)S(1)}, bf16[256,512]{1,0:T(8,128)(2,1)S(1)}, u32[]{:S(2)}, u32[]{:S(2)}) %collective-permute-start.63) | collective-permute-done | bytes 262176 | tf_op jit(solution)/shard_map/ppermute | solution.py:38
  794.6 17.3 %collective-permute-done.60 = bf16[256,512]{1,0:T(8,128)(2,1)S(1)} collective-permute-done((bf16[256,512]{1,0:T(8,128)(2,1)S(1)}, bf16[256,512]{1,0:T(8,128)(2,1)S(1)}, u32[]{:S(2)}, u32[]{:S(2)}) %collective-permute-start.60) | collective-permute-done | bytes 262176 | tf_op jit(solution)/shard_map/ppermute | solution.py:38
  812.8 3.3 collective-permute-done.64
  (434 shorter events, 179.4 us)
Async XLA Ops:
  31.5 31.6 %collective-permute-start.6 = (bf16[1408,1024]{1,0:T(8,128)(2,1)S(1)}, bf16[1408,1024]{1,0:T(8,128)(2,1)S(1)}, u32[]{:S(2)}, u32[]{:S(2)}) collective-permute-start(bf16[1408,1024]{1,0:T(8,128)(2,1)S(1)} %copy-done.13), channel_id=1, source_target_pairs={{0,16},{16,0},{1,17},{17,1},{2,18},{18,2},{3,19},{19,3},{4,20},{20... | collective-permute-start | bytes 8650760 | tf_op jit(solution)/shard_map/ppermute | solution.py:38
  31.6 66.3 %collective-permute-start.4 = (bf16[1024,384]{1,0:T(8,128)(2,1)}, bf16[1024,384]{1,0:T(8,128)(2,1)S(1)}, u32[]{:S(2)}, u32[]{:S(2)}) collective-permute-start(bf16[1024,384]{1,0:T(8,128)(2,1)} %get-tuple-element.92), channel_id=1, source_target_pairs={{0,8},{4,12},{8,0},{12,4},{1,9},{5,13},{9,1},{13,5},{2,10},{6,14},... | collective-permute-start | bytes 2359304 | tf_op jit(solution)/shard_map/ppermute | solution.py:38
  35.4 26.1 %collective-permute-start.7 = (bf16[512,1024]{1,0:T(8,128)(2,1)S(1)}, bf16[512,1024]{1,0:T(8,128)(2,1)S(1)}, u32[]{:S(2)}, u32[]{:S(2)}) collective-permute-start(bf16[512,1024]{1,0:T(8,128)(2,1)S(1)} %copy-done), channel_id=1, source_target_pairs={{0,16},{16,0},{1,17},{17,1},{2,18},{18,2},{3,19},{19,3},{4,20},{20... | collective-permute-start | bytes 3145736 | tf_op jit(solution)/shard_map/ppermute | solution.py:38
  45.4 52.4 %collective-permute-start.3 = (bf16[1024,384]{1,0:T(8,128)(2,1)S(1)}, bf16[1024,384]{1,0:T(8,128)(2,1)S(1)}, u32[]{:S(2)}, u32[]{:S(2)}) collective-permute-start(bf16[1024,384]{1,0:T(8,128)(2,1)S(1)} %copy-done.51), channel_id=1, source_target_pairs={{0,4},{4,0},{8,12},{12,8},{1,5},{5,1},{9,13},{13,9},{2,6},{6,2},{1... | collective-permute-start | bytes 2359304 | tf_op jit(solution)/shard_map/ppermute | solution.py:38
  47.1 29.7 %collective-permute-start.8 = (bf16[1024,1408]{1,0:T(8,128)(2,1)S(1)}, bf16[1024,1408]{1,0:T(8,128)(2,1)}, u32[]{:S(2)}, u32[]{:S(2)}) collective-permute-start(bf16[1024,1408]{1,0:T(8,128)(2,1)S(1)} %copy-done.14), channel_id=1, source_target_pairs={{0,16},{16,0},{1,17},{17,1},{2,18},{18,2},{3,19},{19,3},{4,20},{20... | collective-permute-start | bytes 8650760 | tf_op jit(solution)/shard_map/ppermute | solution.py:38
  61.5 36.4 %collective-permute-start.5 = (bf16[1024,384]{1,0:T(8,128)(2,1)S(1)}, bf16[1024,384]{1,0:T(8,128)(2,1)S(1)}, u32[]{:S(2)}, u32[]{:S(2)}) collective-permute-start(bf16[1024,384]{1,0:T(8,128)(2,1)S(1)} %copy-done.50), channel_id=1, source_target_pairs={{0,12},{4,8},{8,4},{12,0},{1,13},{5,9},{9,5},{13,1},{2,14},{6,10},... | collective-permute-start | bytes 2359304 | tf_op jit(solution)/shard_map/ppermute | solution.py:38
  64.1 17.4 %collective-permute-start.9 = (bf16[1024,1408]{1,0:T(8,128)(2,1)S(1)}, bf16[1024,1408]{1,0:T(8,128)(2,1)S(1)}, u32[]{:S(2)}, u32[]{:S(2)}) collective-permute-start(bf16[1024,1408]{1,0:T(8,128)(2,1)S(1)} %copy-done.15), channel_id=1, source_target_pairs={{0,16},{16,0},{1,17},{17,1},{2,18},{18,2},{3,19},{19,3},{4,20},{20... | collective-permute-start | bytes 8650760 | tf_op jit(solution)/shard_map/ppermute | solution.py:38
  137.4 16.0 %collective-permute-start.12 = (bf16[1024,128]{1,0:T(8,128)(2,1)}, bf16[1024,128]{1,0:T(8,128)(2,1)S(1)}, u32[]{:S(2)}, u32[]{:S(2)}) collective-permute-start(bf16[1024,128]{1,0:T(8,128)(2,1)} %get-tuple-element.109), channel_id=1, source_target_pairs={{0,12},{4,8},{8,4},{12,0},{1,13},{5,9},{9,5},{13,1},{2,14},{6,10},... | collective-permute-start | bytes 786440 | tf_op jit(solution)/shard_map/ppermute | solution.py:38
  164.1 18.8 %collective-permute-start.18 = (bf16[128,2048]{1,0:T(8,128)(2,1)}, bf16[128,2048]{1,0:T(8,128)(2,1)}, u32[]{:S(2)}, u32[]{:S(2)}) collective-permute-start(bf16[128,2048]{1,0:T(8,128)(2,1)} %slice.192), channel_id=1, source_target_pairs={{0,2},{1,3},{2,0},{3,1},{4,6},{5,7},{6,4},{7,5},{8,10},{9,11},{10,... | collective-permute-start | bytes 1572872 | tf_op jit(solution)/shard_map/ppermute | solution.py:38
  165.4 17.5 %collective-permute-start.13 = (bf16[128,2048]{1,0:T(8,128)(2,1)}, bf16[128,2048]{1,0:T(8,128)(2,1)}, u32[]{:S(2)}, u32[]{:S(2)}) collective-permute-start(bf16[128,2048]{1,0:T(8,128)(2,1)} %slice.187), channel_id=1, source_target_pairs={{0,1},{1,0},{2,3},{3,2},{4,5},{5,4},{6,7},{7,6},{8,9},{9,8},{10,11... | collective-permute-start | bytes 1572872 | tf_op jit(solution)/shard_map/ppermute | solution.py:38
  170.2 24.0 %collective-permute-start.17 = (bf16[128,2048]{1,0:T(8,128)(2,1)}, bf16[128,2048]{1,0:T(8,128)(2,1)}, u32[]{:S(2)}, u32[]{:S(2)}) collective-permute-start(bf16[128,2048]{1,0:T(8,128)(2,1)} %add_convert_fusion.11), channel_id=1, source_target_pairs={{0,2},{1,3},{2,0},{3,1},{4,6},{5,7},{6,4},{7,5},{8,10},{9,11},{10,... | collective-permute-start | bytes 1572872 | tf_op jit(solution)/shard_map/ppermute | solution.py:38
  172.6 21.6 %collective-permute-start.15 = (bf16[128,2048]{1,0:T(8,128)(2,1)}, bf16[128,2048]{1,0:T(8,128)(2,1)}, u32[]{:S(2)}, u32[]{:S(2)}) collective-permute-start(bf16[128,2048]{1,0:T(8,128)(2,1)} %add_convert_fusion.12), channel_id=1, source_target_pairs={{0,1},{1,0},{2,3},{3,2},{4,5},{5,4},{6,7},{7,6},{8,9},{9,8},{10,11... | collective-permute-start | bytes 1572872 | tf_op jit(solution)/shard_map/ppermute | solution.py:38
  197.9 17.7 %collective-permute-start.20 = (bf16[128,2048]{1,0:T(8,128)(2,1)S(1)}, bf16[128,2048]{1,0:T(8,128)(2,1)S(1)}, u32[]{:S(2)}, u32[]{:S(2)}) collective-permute-start(bf16[128,2048]{1,0:T(8,128)(2,1)S(1)} %get-tuple-element.220), channel_id=1, source_target_pairs={{0,1},{1,0},{2,3},{3,2},{4,5},{5,4},{6,7},{7,6},{8,9},{9,8},{10,11... | collective-permute-start | bytes 1572872 | tf_op jit(solution)/shard_map/ppermute | solution.py:38
  198.3 32.3 %collective-permute-start.22 = (bf16[128,2048]{1,0:T(8,128)(2,1)S(1)}, bf16[128,2048]{1,0:T(8,128)(2,1)S(1)}, u32[]{:S(2)}, u32[]{:S(2)}) collective-permute-start(bf16[128,2048]{1,0:T(8,128)(2,1)S(1)} %get-tuple-element.220), channel_id=1, source_target_pairs={{0,2},{1,3},{2,0},{3,1},{4,6},{5,7},{6,4},{7,5},{8,10},{9,11},{10,... | collective-permute-start | bytes 1572872 | tf_op jit(solution)/shard_map/ppermute | solution.py:38
  199.8 20.4 %collective-permute-start.19 = (bf16[128,2048]{1,0:T(8,128)(2,1)S(1)}, bf16[128,2048]{1,0:T(8,128)(2,1)S(1)}, u32[]{:S(2)}, u32[]{:S(2)}) collective-permute-start(bf16[128,2048]{1,0:T(8,128)(2,1)S(1)} %get-tuple-element.219), channel_id=1, source_target_pairs={{0,1},{1,0},{2,3},{3,2},{4,5},{5,4},{6,7},{7,6},{8,9},{9,8},{10,11... | collective-permute-start | bytes 1572872 | tf_op jit(solution)/shard_map/ppermute | solution.py:38
  201.5 29.1 %collective-permute-start.21 = (bf16[128,2048]{1,0:T(8,128)(2,1)S(1)}, bf16[128,2048]{1,0:T(8,128)(2,1)S(1)}, u32[]{:S(2)}, u32[]{:S(2)}) collective-permute-start(bf16[128,2048]{1,0:T(8,128)(2,1)S(1)} %get-tuple-element.219), channel_id=1, source_target_pairs={{0,2},{1,3},{2,0},{3,1},{4,6},{5,7},{6,4},{7,5},{8,10},{9,11},{10,... | collective-permute-start | bytes 1572872 | tf_op jit(solution)/shard_map/ppermute | solution.py:38
  239.1 90.8 %collective-permute-start.23 = (bf16[256,2048]{1,0:T(8,128)(2,1)S(1)}, bf16[256,2048]{1,0:T(8,128)(2,1)S(1)}, u32[]{:S(2)}, u32[]{:S(2)}) collective-permute-start(bf16[256,2048]{1,0:T(8,128)(2,1)S(1)} %fusion), channel_id=1, source_target_pairs={{0,1},{1,0},{2,3},{3,2},{4,5},{5,4},{6,7},{7,6},{8,9},{9,8},{10,11... | collective-permute-start | bytes 3145736 | tf_op jit(solution)/shard_map/ppermute | solution.py:38
  240.7 33.0 %collective-permute-start.24 = (bf16[128,2048]{1,0:T(8,128)(2,1)S(1)}, bf16[128,2048]{1,0:T(8,128)(2,1)S(1)}, u32[]{:S(2)}, u32[]{:S(2)}) collective-permute-start(bf16[128,2048]{1,0:T(8,128)(2,1)S(1)} %collective-permute-done.21), channel_id=1, source_target_pairs={{0,1},{1,0},{2,3},{3,2},{4,5},{5,4},{6,7},{7,6},{8,9},{9,8},{10,11... | collective-permute-start | bytes 1572872 | tf_op jit(solution)/shard_map/ppermute | solution.py:38
  298.3 31.5 %collective-permute-start.27 = (bf16[256,2048]{1,0:T(8,128)(2,1)S(1)}, bf16[256,2048]{1,0:T(8,128)(2,1)S(1)}, u32[]{:S(2)}, u32[]{:S(2)}) collective-permute-start(bf16[256,2048]{1,0:T(8,128)(2,1)S(1)} %fusion.2), channel_id=1, source_target_pairs={{0,3},{1,2},{2,1},{3,0},{4,7},{5,6},{6,5},{7,4},{8,11},{9,10},{10,... | collective-permute-start | bytes 3145736 | tf_op jit(solution)/shard_map/ppermute | solution.py:38
  299.2 48.3 %collective-permute-start.26 = (bf16[256,2048]{1,0:T(8,128)(2,1)S(1)}, bf16[256,2048]{1,0:T(8,128)(2,1)S(1)}, u32[]{:S(2)}, u32[]{:S(2)}) collective-permute-start(bf16[256,2048]{1,0:T(8,128)(2,1)S(1)} %fusion.1), channel_id=1, source_target_pairs={{0,2},{1,3},{2,0},{3,1},{4,6},{5,7},{6,4},{7,5},{8,10},{9,11},{10,... | collective-permute-start | bytes 3145736 | tf_op jit(solution)/shard_map/ppermute | solution.py:38
  300.0 128.9 %collective-permute-start.69 = (bf16[1024,1408]{1,0:T(8,128)(2,1)}, bf16[1024,1408]{1,0:T(8,128)(2,1)}, u32[]{:S(2)}, u32[]{:S(2)}) collective-permute-start(bf16[1024,1408]{1,0:T(8,128)(2,1)} %convolution_convert_fusion.5), channel_id=1, source_target_pairs={{0,16},{16,0},{1,17},{17,1},{2,18},{18,2},{3,19},{19,3},{4,20},{20... | collective-permute-start | bytes 8650760 | tf_op jit(solution)/shard_map/ppermute | solution.py:38
  302.2 178.6 %collective-permute-start.73 = (bf16[1024,1408]{1,0:T(8,128)(2,1)}, bf16[1024,1408]{1,0:T(8,128)(2,1)}, u32[]{:S(2)}, u32[]{:S(2)}) collective-permute-start(bf16[1024,1408]{1,0:T(8,128)(2,1)} %convolution_convert_fusion.3), channel_id=1, source_target_pairs={{0,16},{16,0},{1,17},{17,1},{2,18},{18,2},{3,19},{19,3},{4,20},{20... | collective-permute-start | bytes 8650760 | tf_op jit(solution)/shard_map/ppermute | solution.py:38
  349.9 14.9 %collective-permute-start.28 = (bf16[128,2048]{1,0:T(8,128)(2,1)S(1)}, bf16[128,2048]{1,0:T(8,128)(2,1)S(1)}, u32[]{:S(2)}, u32[]{:S(2)}) collective-permute-start(bf16[128,2048]{1,0:T(8,128)(2,1)S(1)} %get-tuple-element.218), channel_id=1, source_target_pairs={{0,1},{1,0},{2,3},{3,2},{4,5},{5,4},{6,7},{7,6},{8,9},{9,8},{10,11... | collective-permute-start | bytes 1572872 | tf_op jit(solution)/shard_map/ppermute | solution.py:38
  350.2 14.6 %collective-permute-start.30 = (bf16[128,2048]{1,0:T(8,128)(2,1)S(1)}, bf16[128,2048]{1,0:T(8,128)(2,1)S(1)}, u32[]{:S(2)}, u32[]{:S(2)}) collective-permute-start(bf16[128,2048]{1,0:T(8,128)(2,1)S(1)} %get-tuple-element.218), channel_id=1, source_target_pairs={{0,2},{1,3},{2,0},{3,1},{4,6},{5,7},{6,4},{7,5},{8,10},{9,11},{10,... | collective-permute-start | bytes 1572872 | tf_op jit(solution)/shard_map/ppermute | solution.py:38
  351.5 24.5 %collective-permute-start.29 = (bf16[128,2048]{1,0:T(8,128)(2,1)S(1)}, bf16[128,2048]{1,0:T(8,128)(2,1)S(1)}, u32[]{:S(2)}, u32[]{:S(2)}) collective-permute-start(bf16[128,2048]{1,0:T(8,128)(2,1)S(1)} %get-tuple-element.217), channel_id=1, source_target_pairs={{0,1},{1,0},{2,3},{3,2},{4,5},{5,4},{6,7},{7,6},{8,9},{9,8},{10,11... | collective-permute-start | bytes 1572872 | tf_op jit(solution)/shard_map/ppermute | solution.py:38
  364.8 12.2 %collective-permute-start.31 = (bf16[128,2048]{1,0:T(8,128)(2,1)S(1)}, bf16[128,2048]{1,0:T(8,128)(2,1)S(1)}, u32[]{:S(2)}, u32[]{:S(2)}) collective-permute-start(bf16[128,2048]{1,0:T(8,128)(2,1)S(1)} %get-tuple-element.217), channel_id=1, source_target_pairs={{0,2},{1,3},{2,0},{3,1},{4,6},{5,7},{6,4},{7,5},{8,10},{9,11},{10,... | collective-permute-start | bytes 1572872 | tf_op jit(solution)/shard_map/ppermute | solution.py:38
  364.8 21.6 %collective-permute-start.32 = (bf16[128,2048]{1,0:T(8,128)(2,1)S(1)}, bf16[128,2048]{1,0:T(8,128)(2,1)S(1)}, u32[]{:S(2)}, u32[]{:S(2)}) collective-permute-start(bf16[128,2048]{1,0:T(8,128)(2,1)S(1)} %collective-permute-done.30), channel_id=1, source_target_pairs={{0,1},{1,0},{2,3},{3,2},{4,5},{5,4},{6,7},{7,6},{8,9},{9,8},{10,11... | collective-permute-start | bytes 1572872 | tf_op jit(solution)/shard_map/ppermute | solution.py:38
  376.0 12.2 %collective-permute-start.33 = (bf16[128,2048]{1,0:T(8,128)(2,1)S(1)}, bf16[128,2048]{1,0:T(8,128)(2,1)S(1)}, u32[]{:S(2)}, u32[]{:S(2)}) collective-permute-start(bf16[128,2048]{1,0:T(8,128)(2,1)S(1)} %collective-permute-done.29), channel_id=1, source_target_pairs={{0,2},{1,3},{2,0},{3,1},{4,6},{5,7},{6,4},{7,5},{8,10},{9,11},{10,... | collective-permute-start | bytes 1572872 | tf_op jit(solution)/shard_map/ppermute | solution.py:38
  391.6 24.0 %collective-permute-start.37 = (bf16[1024,128]{1,0:T(8,128)(2,1)S(1)}, bf16[1024,128]{1,0:T(8,128)(2,1)S(1)}, u32[]{:S(2)}, u32[]{:S(2)}) collective-permute-start(bf16[1024,128]{1,0:T(8,128)(2,1)S(1)} %get-tuple-element.128), channel_id=1, source_target_pairs={{0,4},{4,0},{8,12},{12,8},{1,5},{5,1},{9,13},{13,9},{2,6},{6,2},{1... | collective-permute-start | bytes 786440 | tf_op jit(solution)/shard_map/ppermute | solution.py:38
  406.1 20.4 %collective-permute-start.38 = (bf16[1024,128]{1,0:T(8,128)(2,1)S(1)}, bf16[1024,128]{1,0:T(8,128)(2,1)S(1)}, u32[]{:S(2)}, u32[]{:S(2)}) collective-permute-start(bf16[1024,128]{1,0:T(8,128)(2,1)S(1)} %get-tuple-element.129), channel_id=1, source_target_pairs={{0,8},{4,12},{8,0},{12,4},{1,9},{5,13},{9,1},{13,5},{2,10},{6,14},... | collective-permute-start | bytes 786440 | tf_op jit(solution)/shard_map/ppermute | solution.py:38
  407.9 20.0 %collective-permute-start.39 = (bf16[1024,128]{1,0:T(8,128)(2,1)S(1)}, bf16[1024,128]{1,0:T(8,128)(2,1)S(1)}, u32[]{:S(2)}, u32[]{:S(2)}) collective-permute-start(bf16[1024,128]{1,0:T(8,128)(2,1)S(1)} %get-tuple-element.130), channel_id=1, source_target_pairs={{0,12},{4,8},{8,4},{12,0},{1,13},{5,9},{9,5},{13,1},{2,14},{6,10},... | collective-permute-start | bytes 786440 | tf_op jit(solution)/shard_map/ppermute | solution.py:38
  415.6 68.2 %collective-permute-start.77 = (bf16[1408,1024]{1,0:T(8,128)(2,1)}, bf16[1408,1024]{1,0:T(8,128)(2,1)}, u32[]{:S(2)}, u32[]{:S(2)}) collective-permute-start(bf16[1408,1024]{1,0:T(8,128)(2,1)} %convolution_convert_fusion.1), channel_id=1, source_target_pairs={{0,16},{16,0},{1,17},{17,1},{2,18},{18,2},{3,19},{19,3},{4,20},{20... | collective-permute-start | bytes 8650760 | tf_op jit(solution)/shard_map/ppermute | solution.py:38
  426.5 67.0 %collective-permute-start.36 = (bf16[256,2048]{1,0:T(8,128)(2,1)}, bf16[256,2048]{1,0:T(8,128)(2,1)}, u32[]{:S(2)}, u32[]{:S(2)}) collective-permute-start(bf16[256,2048]{1,0:T(8,128)(2,1)} %get-tuple-element.186), channel_id=1, source_target_pairs={{0,3},{1,2},{2,1},{3,0},{4,7},{5,6},{6,5},{7,4},{8,11},{9,10},{10,... | collective-permute-start | bytes 3145736 | tf_op jit(solution)/shard_map/ppermute | solution.py:38
  427.8 67.7 %collective-permute-start.35 = (bf16[256,2048]{1,0:T(8,128)(2,1)}, bf16[256,2048]{1,0:T(8,128)(2,1)}, u32[]{:S(2)}, u32[]{:S(2)}) collective-permute-start(bf16[256,2048]{1,0:T(8,128)(2,1)} %get-tuple-element.187), channel_id=1, source_target_pairs={{0,2},{1,3},{2,0},{3,1},{4,6},{5,7},{6,4},{7,5},{8,10},{9,11},{10,... | collective-permute-start | bytes 3145736 | tf_op jit(solution)/shard_map/ppermute | solution.py:38
  428.9 68.1 %collective-permute-start.34 = (bf16[256,2048]{1,0:T(8,128)(2,1)}, bf16[256,2048]{1,0:T(8,128)(2,1)}, u32[]{:S(2)}, u32[]{:S(2)}) collective-permute-start(bf16[256,2048]{1,0:T(8,128)(2,1)} %get-tuple-element.185), channel_id=1, source_target_pairs={{0,1},{1,0},{2,3},{3,2},{4,5},{5,4},{6,7},{7,6},{8,9},{9,8},{10,11... | collective-permute-start | bytes 3145736 | tf_op jit(solution)/shard_map/ppermute | solution.py:38
  480.8 19.8 %collective-permute-start.65 = (bf16[512,1024]{1,0:T(8,128)(2,1)S(1)}, bf16[512,1024]{1,0:T(8,128)(2,1)S(1)}, u32[]{:S(2)}, u32[]{:S(2)}) collective-permute-start(bf16[512,1024]{1,0:T(8,128)(2,1)S(1)} %copy-done.46), channel_id=1, source_target_pairs={{0,16},{16,0},{1,17},{17,1},{2,18},{18,2},{3,19},{19,3},{4,20},{20... | collective-permute-start | bytes 3145736 | tf_op jit(solution)/shard_map/ppermute | solution.py:38
  483.8 39.6 %collective-permute-start.40 = (bf16[1024,384]{1,0:T(8,128)(2,1)S(1)}, bf16[1024,384]{1,0:T(8,128)(2,1)S(1)}, u32[]{:S(2)}, u32[]{:S(2)}) collective-permute-start(bf16[1024,384]{1,0:T(8,128)(2,1)S(1)} %copy-done.54), channel_id=1, source_target_pairs={{0,4},{4,0},{8,12},{12,8},{1,5},{5,1},{9,13},{13,9},{2,6},{6,2},{1... | collective-permute-start | bytes 2359304 | tf_op jit(solution)/shard_map/ppermute | solution.py:38
  493.5 55.1 %collective-permute-start.41 = (bf16[1024,384]{1,0:T(8,128)(2,1)S(1)}, bf16[1024,384]{1,0:T(8,128)(2,1)S(1)}, u32[]{:S(2)}, u32[]{:S(2)}) collective-permute-start(bf16[1024,384]{1,0:T(8,128)(2,1)S(1)} %copy-done.53), channel_id=1, source_target_pairs={{0,8},{4,12},{8,0},{12,4},{1,9},{5,13},{9,1},{13,5},{2,10},{6,14},... | collective-permute-start | bytes 2359304 | tf_op jit(solution)/shard_map/ppermute | solution.py:38
  495.5 53.6 %collective-permute-start.42 = (bf16[1024,384]{1,0:T(8,128)(2,1)S(1)}, bf16[1024,384]{1,0:T(8,128)(2,1)S(1)}, u32[]{:S(2)}, u32[]{:S(2)}) collective-permute-start(bf16[1024,384]{1,0:T(8,128)(2,1)S(1)} %copy-done.52), channel_id=1, source_target_pairs={{0,12},{4,8},{8,4},{12,0},{1,13},{5,9},{9,5},{13,1},{2,14},{6,10},... | collective-permute-start | bytes 2359304 | tf_op jit(solution)/shard_map/ppermute | solution.py:38
  496.9 99.2 %collective-permute-start.71 = (bf16[256,1408]{1,0:T(8,128)(2,1)}, bf16[256,1408]{1,0:T(8,128)(2,1)}, u32[]{:S(2)}, u32[]{:S(2)}) collective-permute-start(bf16[256,1408]{1,0:T(8,128)(2,1)} %get-tuple-element.184), channel_id=1, source_target_pairs={{0,4},{4,0},{8,12},{12,8},{1,5},{5,1},{9,13},{13,9},{2,6},{6,2},{1... | collective-permute-start | bytes 2162696 | tf_op jit(solution)/shard_map/ppermute | solution.py:38
  500.5 98.7 %collective-permute-start.75 = (bf16[256,1408]{1,0:T(8,128)(2,1)}, bf16[256,1408]{1,0:T(8,128)(2,1)}, u32[]{:S(2)}, u32[]{:S(2)}) collective-permute-start(bf16[256,1408]{1,0:T(8,128)(2,1)} %get-tuple-element.182), channel_id=1, source_target_pairs={{0,4},{4,0},{8,12},{12,8},{1,5},{5,1},{9,13},{13,9},{2,6},{6,2},{1... | collective-permute-start | bytes 2162696 | tf_op jit(solution)/shard_map/ppermute | solution.py:38
  523.4 79.9 %collective-permute-start.79 = (bf16[1408,256]{1,0:T(8,128)(2,1)}, bf16[1408,256]{1,0:T(8,128)(2,1)}, u32[]{:S(2)}, u32[]{:S(2)}) collective-permute-start(bf16[1408,256]{1,0:T(8,128)(2,1)} %get-tuple-element.180), channel_id=1, source_target_pairs={{0,4},{4,0},{8,12},{12,8},{1,5},{5,1},{9,13},{13,9},{2,6},{6,2},{1... | collective-permute-start | bytes 2162696 | tf_op jit(solution)/shard_map/ppermute | solution.py:38
  548.5 46.0 %collective-permute-start.67 = (bf16[512,256]{1,0:T(8,128)(2,1)S(1)}, bf16[512,256]{1,0:T(8,128)(2,1)S(1)}, u32[]{:S(2)}, u32[]{:S(2)}) collective-permute-start(bf16[512,256]{1,0:T(8,128)(2,1)S(1)} %get-tuple-element.201), channel_id=1, source_target_pairs={{0,4},{4,0},{8,12},{12,8},{1,5},{5,1},{9,13},{13,9},{2,6},{6,2},{1... | collective-permute-start | bytes 786440 | tf_op jit(solution)/shard_map/ppermute | solution.py:38
  549.1 60.9 %collective-permute-start.66 = (bf16[512,256]{1,0:T(8,128)(2,1)S(1)}, bf16[512,256]{1,0:T(8,128)(2,1)S(1)}, u32[]{:S(2)}, u32[]{:S(2)}) collective-permute-start(bf16[512,256]{1,0:T(8,128)(2,1)S(1)} %get-tuple-element.200), channel_id=1, source_target_pairs={{0,4},{4,0},{8,12},{12,8},{1,5},{5,1},{9,13},{13,9},{2,6},{6,2},{1... | collective-permute-start | bytes 786440 | tf_op jit(solution)/shard_map/ppermute | solution.py:38
  594.5 27.0 %collective-permute-start.45 = (bf16[256,2048]{1,0:T(8,128)(2,1)S(1)}, bf16[256,2048]{1,0:T(8,128)(2,1)S(1)}, u32[]{:S(2)}, u32[]{:S(2)}) collective-permute-start(bf16[256,2048]{1,0:T(8,128)(2,1)S(1)} %get-tuple-element.149), channel_id=1, source_target_pairs={{0,3},{1,2},{2,1},{3,0},{4,7},{5,6},{6,5},{7,4},{8,11},{9,10},{10,... | collective-permute-start | bytes 3145736 | tf_op jit(solution)/shard_map/ppermute | solution.py:38
  596.1 45.9 %collective-permute-start.44 = (bf16[256,2048]{1,0:T(8,128)(2,1)S(1)}, bf16[256,2048]{1,0:T(8,128)(2,1)S(1)}, u32[]{:S(2)}, u32[]{:S(2)}) collective-permute-start(bf16[256,2048]{1,0:T(8,128)(2,1)S(1)} %get-tuple-element.148), channel_id=1, source_target_pairs={{0,2},{1,3},{2,0},{3,1},{4,6},{5,7},{6,4},{7,5},{8,10},{9,11},{10,... | collective-permute-start | bytes 3145736 | tf_op jit(solution)/shard_map/ppermute | solution.py:38
  599.2 42.8 %collective-permute-start.43 = (bf16[256,2048]{1,0:T(8,128)(2,1)S(1)}, bf16[256,2048]{1,0:T(8,128)(2,1)S(1)}, u32[]{:S(2)}, u32[]{:S(2)}) collective-permute-start(bf16[256,2048]{1,0:T(8,128)(2,1)S(1)} %get-tuple-element.147), channel_id=1, source_target_pairs={{0,1},{1,0},{2,3},{3,2},{4,5},{5,4},{6,7},{7,6},{8,9},{9,8},{10,11... | collective-permute-start | bytes 3145736 | tf_op jit(solution)/shard_map/ppermute | solution.py:38
  603.4 14.0 %collective-permute-start.68 = (bf16[512,256]{1,0:T(8,128)(2,1)S(1)}, bf16[512,256]{1,0:T(8,128)(2,1)S(1)}, u32[]{:S(2)}, u32[]{:S(2)}) collective-permute-start(bf16[512,256]{1,0:T(8,128)(2,1)S(1)} %add_convert_fusion.13), channel_id=1, source_target_pairs={{0,8},{4,12},{8,0},{12,4},{1,9},{5,13},{9,1},{13,5},{2,10},{6,14},... | collective-permute-start | bytes 786440 | tf_op jit(solution)/shard_map/ppermute | solution.py:38
  610.0 59.4 %collective-permute-start.70 = (bf16[256,1408]{1,0:T(8,128)(2,1)}, bf16[256,1408]{1,0:T(8,128)(2,1)}, u32[]{:S(2)}, u32[]{:S(2)}) collective-permute-start(bf16[256,1408]{1,0:T(8,128)(2,1)} %get-tuple-element.183), channel_id=1, source_target_pairs={{0,4},{4,0},{8,12},{12,8},{1,5},{5,1},{9,13},{13,9},{2,6},{6,2},{1... | collective-permute-start | bytes 2162696 | tf_op jit(solution)/shard_map/ppermute | solution.py:38
  617.3 117.0 %collective-permute-start.74 = (bf16[256,1408]{1,0:T(8,128)(2,1)}, bf16[256,1408]{1,0:T(8,128)(2,1)}, u32[]{:S(2)}, u32[]{:S(2)}) collective-permute-start(bf16[256,1408]{1,0:T(8,128)(2,1)} %get-tuple-element.181), channel_id=1, source_target_pairs={{0,4},{4,0},{8,12},{12,8},{1,5},{5,1},{9,13},{13,9},{2,6},{6,2},{1... | collective-permute-start | bytes 2162696 | tf_op jit(solution)/shard_map/ppermute | solution.py:38
  621.5 26.9 %collective-permute-start.53 = (bf16[1024,512]{1,0:T(8,128)(2,1)S(1)}, bf16[1024,512]{1,0:T(8,128)(2,1)S(1)}, u32[]{:S(2)}, u32[]{:S(2)}) collective-permute-start(bf16[1024,512]{1,0:T(8,128)(2,1)S(1)} %fusion.35), channel_id=1, source_target_pairs={{0,16},{16,0},{1,17},{17,1},{2,18},{18,2},{3,19},{19,3},{4,20},{20... | collective-permute-start | bytes 3145736 | tf_op jit(solution)/shard_map/ppermute | solution.py:38
  661.1 88.8 %collective-permute-start.78 = (bf16[1408,256]{1,0:T(8,128)(2,1)}, bf16[1408,256]{1,0:T(8,128)(2,1)}, u32[]{:S(2)}, u32[]{:S(2)}) collective-permute-start(bf16[1408,256]{1,0:T(8,128)(2,1)} %get-tuple-element.179), channel_id=1, source_target_pairs={{0,4},{4,0},{8,12},{12,8},{1,5},{5,1},{9,13},{13,9},{2,6},{6,2},{1... | collective-permute-start | bytes 2162696 | tf_op jit(solution)/shard_map/ppermute | solution.py:38
  664.5 66.6 %collective-permute-start.72 = (bf16[256,1408]{1,0:T(8,128)(2,1)}, bf16[256,1408]{1,0:T(8,128)(2,1)}, u32[]{:S(2)}, u32[]{:S(2)}) collective-permute-start(bf16[256,1408]{1,0:T(8,128)(2,1)} %add_convert_fusion.8), channel_id=1, source_target_pairs={{0,8},{4,12},{8,0},{12,4},{1,9},{5,13},{9,1},{13,5},{2,10},{6,14},... | collective-permute-start | bytes 2162696 | tf_op jit(solution)/shard_map/ppermute | solution.py:38
  664.9 81.8 %collective-permute-start.76 = (bf16[256,1408]{1,0:T(8,128)(2,1)}, bf16[256,1408]{1,0:T(8,128)(2,1)}, u32[]{:S(2)}, u32[]{:S(2)}) collective-permute-start(bf16[256,1408]{1,0:T(8,128)(2,1)} %add_convert_fusion.5), channel_id=1, source_target_pairs={{0,8},{4,12},{8,0},{12,4},{1,9},{5,13},{9,1},{13,5},{2,10},{6,14},... | collective-permute-start | bytes 2162696 | tf_op jit(solution)/shard_map/ppermute | solution.py:38
  669.4 90.4 %collective-permute-start.80 = (bf16[1408,256]{1,0:T(8,128)(2,1)}, bf16[1408,256]{1,0:T(8,128)(2,1)S(1)}, u32[]{:S(2)}, u32[]{:S(2)}) collective-permute-start(bf16[1408,256]{1,0:T(8,128)(2,1)} %add_convert_fusion.2), channel_id=1, source_target_pairs={{0,8},{4,12},{8,0},{12,4},{1,9},{5,13},{9,1},{13,5},{2,10},{6,14},... | collective-permute-start | bytes 2162696 | tf_op jit(solution)/shard_map/ppermute | solution.py:38
  731.1 34.1 %collective-permute-start.55 = (bf16[256,512]{1,0:T(8,128)(2,1)}, bf16[256,512]{1,0:T(8,128)(2,1)S(1)}, u32[]{:S(2)}, u32[]{:S(2)}) collective-permute-start(bf16[256,512]{1,0:T(8,128)(2,1)} %get-tuple-element.207), channel_id=1, source_target_pairs={{0,4},{4,0},{8,12},{12,8},{1,5},{5,1},{9,13},{13,9},{2,6},{6,2},{1... | collective-permute-start | bytes 786440 | tf_op jit(solution)/shard_map/ppermute | solution.py:38
  734.4 58.6 %collective-permute-start.54 = (bf16[256,512]{1,0:T(8,128)(2,1)S(1)}, bf16[256,512]{1,0:T(8,128)(2,1)S(1)}, u32[]{:S(2)}, u32[]{:S(2)}) collective-permute-start(bf16[256,512]{1,0:T(8,128)(2,1)S(1)} %get-tuple-element.206), channel_id=1, source_target_pairs={{0,4},{4,0},{8,12},{12,8},{1,5},{5,1},{9,13},{13,9},{2,6},{6,2},{1... | collective-permute-start | bytes 786440 | tf_op jit(solution)/shard_map/ppermute | solution.py:38
  746.7 29.8 %collective-permute-start.59 = (bf16[256,512]{1,0:T(8,128)(2,1)S(1)}, bf16[256,512]{1,0:T(8,128)(2,1)S(1)}, u32[]{:S(2)}, u32[]{:S(2)}) collective-permute-start(bf16[256,512]{1,0:T(8,128)(2,1)S(1)} %copy-done.34), channel_id=1, source_target_pairs={{0,4},{4,0},{8,12},{12,8},{1,5},{5,1},{9,13},{13,9},{2,6},{6,2},{1... | collective-permute-start | bytes 786440 | tf_op jit(solution)/shard_map/ppermute | solution.py:38
  749.9 44.7 %collective-permute-start.58 = (bf16[256,512]{1,0:T(8,128)(2,1)S(1)}, bf16[256,512]{1,0:T(8,128)(2,1)S(1)}, u32[]{:S(2)}, u32[]{:S(2)}) collective-permute-start(bf16[256,512]{1,0:T(8,128)(2,1)S(1)} %get-tuple-element.204), channel_id=1, source_target_pairs={{0,4},{4,0},{8,12},{12,8},{1,5},{5,1},{9,13},{13,9},{2,6},{6,2},{1... | collective-permute-start | bytes 786440 | tf_op jit(solution)/shard_map/ppermute | solution.py:38
  759.8 30.8 %collective-permute-start.63 = (bf16[256,512]{1,0:T(8,128)(2,1)S(1)}, bf16[256,512]{1,0:T(8,128)(2,1)S(1)}, u32[]{:S(2)}, u32[]{:S(2)}) collective-permute-start(bf16[256,512]{1,0:T(8,128)(2,1)S(1)} %copy-done.35), channel_id=1, source_target_pairs={{0,4},{4,0},{8,12},{12,8},{1,5},{5,1},{9,13},{13,9},{2,6},{6,2},{1... | collective-permute-start | bytes 786440 | tf_op jit(solution)/shard_map/ppermute | solution.py:38
  765.2 47.6 %collective-permute-start.62 = (bf16[256,512]{1,0:T(8,128)(2,1)S(1)}, bf16[256,512]{1,0:T(8,128)(2,1)S(1)}, u32[]{:S(2)}, u32[]{:S(2)}) collective-permute-start(bf16[256,512]{1,0:T(8,128)(2,1)S(1)} %copy-done.33), channel_id=1, source_target_pairs={{0,4},{4,0},{8,12},{12,8},{1,5},{5,1},{9,13},{13,9},{2,6},{6,2},{1... | collective-permute-start | bytes 786440 | tf_op jit(solution)/shard_map/ppermute | solution.py:38
  776.4 17.3 %collective-permute-start.56 = (bf16[256,512]{1,0:T(8,128)(2,1)S(1)}, bf16[256,512]{1,0:T(8,128)(2,1)S(1)}, u32[]{:S(2)}, u32[]{:S(2)}) collective-permute-start(bf16[256,512]{1,0:T(8,128)(2,1)S(1)} %add_convert_fusion.22), channel_id=1, source_target_pairs={{0,8},{4,12},{8,0},{12,4},{1,9},{5,13},{9,1},{13,5},{2,10},{6,14},... | collective-permute-start | bytes 786440 | tf_op jit(solution)/shard_map/ppermute | solution.py:38
  790.6 21.3 %collective-permute-start.60 = (bf16[256,512]{1,0:T(8,128)(2,1)S(1)}, bf16[256,512]{1,0:T(8,128)(2,1)S(1)}, u32[]{:S(2)}, u32[]{:S(2)}) collective-permute-start(bf16[256,512]{1,0:T(8,128)(2,1)S(1)} %add_convert_fusion.19), channel_id=1, source_target_pairs={{0,8},{4,12},{8,0},{12,4},{1,9},{5,13},{9,1},{13,5},{2,10},{6,14},... | collective-permute-start | bytes 786440 | tf_op jit(solution)/shard_map/ppermute | solution.py:38
  793.0 23.1 %collective-permute-start.64 = (bf16[256,512]{1,0:T(8,128)(2,1)S(1)}, bf16[256,512]{1,0:T(8,128)(2,1)S(1)}, u32[]{:S(2)}, u32[]{:S(2)}) collective-permute-start(bf16[256,512]{1,0:T(8,128)(2,1)S(1)} %add_convert_fusion.16), channel_id=1, source_target_pairs={{0,8},{4,12},{8,0},{12,4},{1,9},{5,13},{9,1},{13,5},{2,10},{6,14},... | collective-permute-start | bytes 786440 | tf_op jit(solution)/shard_map/ppermute | solution.py:38
  (106 other events, 1419.1 us)
